TPU v7x, 32 devices: a whole 2x2x4 slice. The times are simulated.
32 devices in a mesh: dp: 2 (over x), row: 4 (over y, core), col: 4 (over z).
Axes of the slice: x: 2, y: 2, z: 4, core: 2. Of those that a mesh axis runs over, the one named last changes fastest.
Arguments:
- layer_input: bfloat16 [8192, 2560], P('dp', ('row', 'col')), may hold values from -6 to 6
- attn_gain: float32 [2560], P(('row', 'col')), may hold values from 0.5 to 1.5
- mlp_gain: float32 [2560], P(('row', 'col')), may hold values from 0.5 to 1.5
- query_weight: bfloat16 [2560, 2560], P('row', 'col'), may hold values from -0.125 to 0.125
- key_weight: bfloat16 [2560, 640], P('row', 'col'), may hold values from -0.125 to 0.125
- value_weight: bfloat16 [2560, 640], P('row', 'col'), may hold values from -0.125 to 0.125
- mix_weight: bfloat16 [2560, 2560], P('col', 'row'), may hold values from -1.5 to 1.5
- gate_weight: bfloat16 [2560, 6912], P('row', 'col'), may hold values from -0.125 to 0.125
- up_weight: bfloat16 [2560, 6912], P('row', 'col'), may hold values from -0.125 to 0.125
- down_weight: bfloat16 [6912, 2560], P('col', 'row'), may hold values from -0.078125 to 0.078125
- output_grad: bfloat16 [8192, 2560], P('dp', ('row', 'col')), may hold values from -6 to 6
- segment_ids: int32 [8192], P(('dp', 'row')), may hold values from 0 to 8, as said below
- position_ids: int32 [8192], P(('dp', 'row')), may hold values from 0 to 4095, as said below
Outputs:
- layer_output: bfloat16 [8192, 2560], P('dp', ('row', 'col'))
- input_grad: float32 [8192, 2560], P('dp', ('row', 'col'))
- attn_gain_grad: float32 [2560], P(('row', 'col'))
- mlp_gain_grad: float32 [2560], P(('row', 'col'))
- query_grad: float32 [2560, 2560], P('row', 'col')
- key_grad: float32 [2560, 640], P('row', 'col')
- value_grad: float32 [2560, 640], P('row', 'col')
- mix_grad: float32 [2560, 2560], P('col', 'row')
- gate_grad: float32 [2560, 6912], P('row', 'col')
- up_grad: float32 [2560, 6912], P('row', 'col')
- down_grad: float32 [6912, 2560], P('col', 'row')
Inputs may be any that keep to these rules, and one draw needn't show every extreme that they name: `segment_ids`: tokens come in groups of 2048: the first 1024 have id 0, the rest are 8 runs of consecutive tokens with ids 1 to 8 in order, each run one token or more. `position_ids`: each group has an offset: its prompt's positions are the offset plus 0 to 1023, a continuation's the offset plus 1024 plus the token's place within that continuation; some group has offset 0 and some group's largest position is 4095.
All inputs are finite; a program needn't handle non-finite values.
Results may differ from a plain program's by a relative error of at most 0.017.
Values may be sent and summed in bfloat16 or wider, within the bound.
No kernel may reach another device: no remote copies, remote signals or barrier semaphores. Data moves between devices by JAX's collectives and lax.ppermute only.
A program may use at most 320 MiB of HBM per device.

v0:
```python
import jax
import jax.numpy as jnp
from jax import lax
from jax.sharding import PartitionSpec as P

D = 2560
HEAD = 80


EPS = 1e-05
THETA = 10000.0
NEG = -1e30


def passed_along(block, axis, distance):
    devices = range(lax.axis_size(axis))
    route = [(i - distance, i) for i in devices if i - distance in devices]
    return lax.ppermute(block, axis, route)


def rope_parts(positions, width):
    half = width // 2
    freq = THETA ** (-jnp.arange(half, dtype=jnp.float32) * 2.0 / width)
    angle = positions.astype(jnp.float32)[:, None] * freq[None, :]
    return (jnp.cos(angle), jnp.sin(angle))


def rotate(value, cos_part, sin_part):
    half = value.shape[-1] // 2
    first = value[..., :half]
    second = value[..., half:]
    cosine = cos_part[:, None, :]
    sine = sin_part[:, None, :]
    return jnp.concatenate(
        [first * cosine - second * sine, second * cosine + first * sine], axis=-1
    )


def unrotate(grad, cos_part, sin_part):
    half = grad.shape[-1] // 2
    first = grad[..., :half]
    second = grad[..., half:]
    cosine = cos_part[:, None, :]
    sine = sin_part[:, None, :]
    return jnp.concatenate(
        [first * cosine + second * sine, second * cosine - first * sine], axis=-1
    )


def norm_scale(value):
    local = jnp.sum(value * value, axis=1)
    total = lax.psum(local, ("row", "col"))
    return lax.rsqrt(total / D + EPS)


def spread_normed(value, scale, gain):
    normed = (value * scale[:, None] * gain[None, :]).astype(jnp.bfloat16)
    return lax.all_gather(normed, "col", axis=1, tiled=True)


def row_products(gathered, weight):
    return lax.psum_scatter(
        jnp.dot(gathered, weight, preferred_element_type=jnp.float32),
        "row",
        scatter_dimension=0,
        tiled=True,
    )


def token_gather(value):
    return lax.all_gather(value, "row", axis=0, tiled=True)


def col_sum(partial_value):
    return lax.psum_scatter(partial_value, "col", scatter_dimension=1, tiled=True)


def grad_gather(value):
    return lax.all_gather(value, "col", axis=1, tiled=True)


def grad_rows(cols, weight):
    return lax.psum_scatter(
        lax.dot_general(cols, weight, (((1,), (1,)), ((), ())), preferred_element_type=jnp.float32),
        "row",
        scatter_dimension=0,
        tiled=True,
    )


def grad_fold(grads, weight, cols):
    piece = lax.all_gather(grads, "row", axis=0, tiled=True)
    part = lax.dot_general(
        piece, weight, (((1,), (1,)), ((), ())), preferred_element_type=jnp.float32
    )
    wgrad = lax.dot_general(
        cols, piece, (((0,), (0,)), ((), ())), preferred_element_type=jnp.float32
    )
    return (part, wgrad)


def grad_col_sum(partial_value):
    return lax.psum_scatter(partial_value, "col", scatter_dimension=1, tiled=True)


def norm_backward(value, scale, gain, grad):
    weighted = grad * gain[None, :]
    local = jnp.sum(weighted * value, axis=1)
    total = lax.psum(local, ("row", "col"))
    value_grad = scale[:, None] * weighted - value * (scale * scale * scale * total / D)[:, None]
    gain_grad = jnp.sum(grad * value * scale[:, None], axis=0)
    return (value_grad, gain_grad)


def visible_mask(parity, seg_ids, start, count, rows):
    query_index = parity * rows + start + jnp.arange(count, dtype=jnp.int32)
    query_seg = lax.dynamic_slice_in_dim(seg_ids, start, count, 0)
    key_index = jnp.arange(2 * rows, dtype=jnp.int32)
    filler = jnp.full((rows,), -1, jnp.int32)
    key_seg = jnp.where(
        parity == 1, jnp.concatenate([filler, seg_ids]), jnp.concatenate([seg_ids, filler])
    )
    same = (key_seg[None, :] == -1) | (key_seg[None, :] == query_seg[:, None])
    return (key_index[None, :] <= query_index[:, None]) & same


def attend_forward(queries, keys, values, parity, seg_ids, block, scale):
    rows = queries.shape[0]

    def step(carry, index):
        start = index * block
        q_block = lax.dynamic_slice_in_dim(queries, start, block, 0)
        mask = visible_mask(parity, seg_ids, start, block, rows)
        scores = (
            jnp.einsum("bgrd,kgd->grbk", q_block, keys, preferred_element_type=jnp.float32) * scale
        )
        scores = jnp.where(mask[None, None], scores, NEG)
        peak = jnp.max(scores, axis=-1, keepdims=True)
        weights = jnp.exp(scores - peak)
        total = jnp.sum(weights, axis=-1, keepdims=True)
        weights = (weights / total).astype(jnp.bfloat16)
        out = jnp.einsum("grbk,kgd->bgrd", weights, values, preferred_element_type=jnp.float32)
        return (carry, (out, peak[..., 0] + jnp.log(total[..., 0])))

    _, (outs, lse) = lax.scan(step, 0, jnp.arange(rows // block, dtype=jnp.int32))
    return (outs, lse)


def attend_backward(queries, keys, values, grad_out, lse, parity, seg_ids, block, scale):
    rows = queries.shape[0]
    init = (jnp.zeros(keys.shape, jnp.float32), jnp.zeros(values.shape, jnp.float32))

    def step(carry, inputs):
        key_acc, value_acc = carry
        index, lse_block = inputs
        start = index * block
        q_block = lax.dynamic_slice_in_dim(queries, start, block, 0)
        g_block = lax.dynamic_slice_in_dim(grad_out, start, block, 0)
        mask = visible_mask(parity, seg_ids, start, block, rows)
        scores = (
            jnp.einsum("bgrd,kgd->grbk", q_block, keys, preferred_element_type=jnp.float32) * scale
        )
        scores = jnp.where(mask[None, None], scores, NEG)
        weights = jnp.exp(scores - lse_block[..., None])
        weights_low = weights.astype(jnp.bfloat16)
        dprod = jnp.einsum("bgrd,kgd->grbk", g_block, values, preferred_element_type=jnp.float32)
        delta = jnp.sum(weights * dprod, axis=-1, keepdims=True)
        dscore = (weights * (dprod - delta)).astype(jnp.bfloat16)
        q_grad = (
            jnp.einsum("grbk,kgd->bgrd", dscore, keys, preferred_element_type=jnp.float32) * scale
        )
        key_acc = (
            key_acc
            + jnp.einsum("grbk,bgrd->kgd", dscore, q_block, preferred_element_type=jnp.float32)
            * scale
        )
        value_acc = value_acc + jnp.einsum(
            "grbk,bgrd->kgd", weights_low, g_block, preferred_element_type=jnp.float32
        )
        return ((key_acc, value_acc), q_grad)

    (key_all, value_all), q_grads = lax.scan(
        step, init, (jnp.arange(rows // block, dtype=jnp.int32), lse)
    )
    return (key_all, value_all, q_grads)


def body(
    layer_input,
    attn_gain,
    mlp_gain,
    query_weight,
    key_weight,
    value_weight,
    mix_weight,
    gate_weight,
    up_weight,
    down_weight,
    output_grad,
    segment_ids,
    position_ids,
):
    rows = segment_ids.shape[0]
    parity = lax.axis_index("row") % 2
    odd = parity == 1
    q_width = query_weight.shape[1]
    kv_width = key_weight.shape[1]
    kv_local = kv_width // HEAD
    repeat = q_width // kv_width
    block = min(512, rows)
    scale = HEAD ** (-0.5)
    ff_width = gate_weight.shape[1]
    cos_part, sin_part = rope_parts(position_ids, HEAD)
    qkv_weight = jnp.concatenate([query_weight, key_weight, value_weight], axis=1)
    gate_up_weight = jnp.concatenate([gate_weight, up_weight], axis=1)
    source = layer_input.astype(jnp.float32)
    first_scale = norm_scale(source)
    first_cols = spread_normed(source, first_scale, attn_gain)
    qkv = row_products(first_cols, qkv_weight)
    query_raw = qkv[:, :q_width].reshape(rows, q_width // HEAD, HEAD)
    key_raw = qkv[:, q_width : q_width + kv_width].reshape(rows, kv_local, HEAD)
    value_raw = qkv[:, q_width + kv_width :].reshape(rows, kv_local, HEAD)
    queries = (
        rotate(query_raw, cos_part, sin_part)
        .astype(jnp.bfloat16)
        .reshape(rows, kv_local, repeat, HEAD)
    )
    keys_own = rotate(key_raw, cos_part, sin_part).astype(jnp.bfloat16)
    values_own = value_raw.astype(jnp.bfloat16)
    other_keys, other_values = passed_along((keys_own, values_own), "row", 1)
    keys = jnp.where(
        odd, jnp.concatenate([other_keys, keys_own]), jnp.concatenate([keys_own, other_keys])
    )
    values = jnp.where(
        odd,
        jnp.concatenate([other_values, values_own]),
        jnp.concatenate([values_own, other_values]),
    )
    attn_out, lse = attend_forward(queries, keys, values, parity, segment_ids, block, scale)
    attn_low = attn_out.reshape(rows, q_width).astype(jnp.bfloat16)
    attn_full = token_gather(attn_low)
    attn_part = jnp.dot(attn_full, mix_weight, preferred_element_type=jnp.float32)
    residual = source + col_sum(attn_part)
    second_scale = norm_scale(residual)
    second_cols = spread_normed(residual, second_scale, mlp_gain)
    gate_up = row_products(second_cols, gate_up_weight)
    gate = gate_up[:, :ff_width]
    up = gate_up[:, ff_width:]
    sigma = jax.nn.sigmoid(gate)
    act_low = (gate * sigma * up).astype(jnp.bfloat16)
    act_full = token_gather(act_low)
    ff_part = jnp.dot(act_full, down_weight, preferred_element_type=jnp.float32)
    layer_output = (residual + col_sum(ff_part)).astype(jnp.bfloat16)
    out_cols = grad_gather(output_grad)
    act_grad = grad_rows(out_cols, down_weight)
    down_grad = lax.dot_general(
        act_full, out_cols, (((0,), (0,)), ((), ())), preferred_element_type=jnp.float32
    )
    gate_part = act_grad * up * sigma * (1.0 + gate * (1.0 - sigma))
    up_part = act_grad * gate * sigma
    gate_up_grad = jnp.concatenate([gate_part, up_part], axis=1).astype(jnp.bfloat16)
    second_back, gate_up_wgrad = grad_fold(gate_up_grad, gate_up_weight, second_cols)
    second_normed = grad_col_sum(second_back)
    residual_grad, mlp_gain_grad = norm_backward(residual, second_scale, mlp_gain, second_normed)
    residual_grad = residual_grad + output_grad.astype(jnp.float32)
    mix_cols = grad_gather(residual_grad.astype(jnp.bfloat16))
    attn_grad = (
        grad_rows(mix_cols, mix_weight).astype(jnp.bfloat16).reshape(rows, kv_local, repeat, HEAD)
    )
    mix_grad = lax.dot_general(
        attn_full, mix_cols, (((0,), (0,)), ((), ())), preferred_element_type=jnp.float32
    )
    key_all, value_all, q_grads = attend_backward(
        queries, keys, values, attn_grad, lse, parity, segment_ids, block, scale
    )
    key_mine = jnp.where(odd, key_all[rows:], key_all[:rows])
    value_mine = jnp.where(odd, value_all[rows:], value_all[:rows])
    got_keys, got_values = (
        passed_along(key_all[:rows].astype(jnp.bfloat16), "row", -1).astype(jnp.float32),
        passed_along(value_all[:rows].astype(jnp.bfloat16), "row", -1).astype(jnp.float32),
    )
    key_total = key_mine + jnp.where(odd, 0.0, got_keys)
    value_total = value_mine + jnp.where(odd, 0.0, got_values)
    query_back = unrotate(q_grads.reshape(rows, q_width // HEAD, HEAD), cos_part, sin_part).reshape(
        rows, q_width
    )
    key_back = unrotate(key_total, cos_part, sin_part).reshape(rows, kv_width)
    value_back = value_total.reshape(rows, kv_width)
    qkv_grad = jnp.concatenate([query_back, key_back, value_back], axis=1).astype(jnp.bfloat16)
    first_back, qkv_wgrad = grad_fold(qkv_grad, qkv_weight, first_cols)
    first_normed = grad_col_sum(first_back)
    input_part, attn_gain_grad = norm_backward(source, first_scale, attn_gain, first_normed)
    input_grad = residual_grad + input_part
    summed = (
        lax.psum(attn_gain_grad.astype(jnp.bfloat16), "dp").astype(jnp.float32),
        lax.psum(mlp_gain_grad.astype(jnp.bfloat16), "dp").astype(jnp.float32),
        lax.psum(qkv_wgrad.astype(jnp.bfloat16), "dp").astype(jnp.float32),
        lax.psum(mix_grad.astype(jnp.bfloat16), "dp").astype(jnp.float32),
        lax.psum(gate_up_wgrad.astype(jnp.bfloat16), "dp").astype(jnp.float32),
        lax.psum(down_grad.astype(jnp.bfloat16), "dp").astype(jnp.float32),
    )
    gain_one, gain_two, qkv_total, mix_total, gate_up_total, down_total = summed
    return (
        layer_output,
        input_grad,
        gain_one,
        gain_two,
        qkv_total[:, :q_width],
        qkv_total[:, q_width : q_width + kv_width],
        qkv_total[:, q_width + kv_width :],
        mix_total,
        gate_up_total[:, :ff_width],
        gate_up_total[:, ff_width:],
        down_total,
    )


def solution(mesh):
    return jax.shard_map(
        body,
        mesh=mesh,
        in_specs=(
            P("dp", ("row", "col")),
            P(("row", "col")),
            P(("row", "col")),
            P("row", "col"),
            P("row", "col"),
            P("row", "col"),
            P("col", "row"),
            P("row", "col"),
            P("row", "col"),
            P("col", "row"),
            P("dp", ("row", "col")),
            P(("dp", "row")),
            P(("dp", "row")),
        ),
        out_specs=(
            P("dp", ("row", "col")),
            P("dp", ("row", "col")),
            P(("row", "col")),
            P(("row", "col")),
            P("row", "col"),
            P("row", "col"),
            P("row", "col"),
            P("col", "row"),
            P("row", "col"),
            P("row", "col"),
            P("col", "row"),
        ),
        check_vma=False,
    )
```

profile of v0, /device:TPU:0, one launch (start us, length us, event | category | flops | bytes accessed | tf_op | source)
XLA Modules:
  0.0 3041.6 jit_solution(16044881706502954316)
XLA Ops:
  9.0 63.3 %psum.70 = f32[4096]{0:T(1024)S(1)} all-reduce(f32[4096]{0:T(1024)S(1)} %fusion.47), channel_id=1, replica_groups=mesh['dp'=2,'row'=4,'col'=4] {'row','col'}, use_global_device_ids=true, to_apply=%region_1.2 | all-reduce | flops 4096 | bytes 32768 | tf_op jit(solution)/shard_map/psum | solution.py:52
  76.2 95.0 %all-gather.9.cloned.1.call-done = bf16[4096,640]{0,1:T(8,128)(2,1)} async-done(((bf16[4096,160]{0,1:T(8,128)(2,1)}), bf16[4096,640]{0,1:T(8,128)(2,1)}) %all-gather.9.cloned.1.call-update) | async-done | bytes 5242896 | tf_op jit(solution)/shard_map/all_gather | solution.py:58
  184.8 117.0 %reduce-scatter.9.cloned.1.call-done = f32[1024,960]{0,1:T(8,128)} async-done(((f32[4096,960]{0,1:T(8,128)}), f32[1024,960]{0,1:T(8,128)}) %reduce-scatter.9.cloned.1.call-update) | async-done | bytes 3932176 | tf_op jit(solution)/shard_map/reduce_scatter | solution.py:62
  312.7 97.9 %while.31 = (s32[]{:T(128)}, bf16[2,512,2,4,80]{1,4,3,2,0:T(8,128)(2,1)}, f32[2,2,4,512]{3,2,1,0:T(4,128)S(1)}, s32[2]{0:T(128)S(1)}, s32[]{:T(128)}, /*index=5*...) while((s32[]{:T(128)}, ...), condition=%wide.region_6.7_spmd, body=%wide.region_3.6_spmd.sunk | while | flops 2789214720 | bytes 108304616 | solution.py:145
  415.1 43.4 %all-gather.11.cloned.1.call-done = bf16[4096,640]{0,1:T(8,128)(2,1)} async-done(((bf16[1024,640]{0,1:T(8,128)(2,1)}), bf16[4096,640]{0,1:T(8,128)(2,1)}) %all-gather.11.cloned.1.call-update) | async-done | bytes 5242896 | tf_op jit(solution)/shard_map/all_gather | solution.py:71
  470.1 177.5 %reduce-scatter.11.cloned.1.call-done = f32[4096,160]{0,1:T(8,128)} async-done(((f32[4096,640]{0,1:T(8,128)}), f32[4096,160]{0,1:T(8,128)}) %reduce-scatter.11.cloned.1.call-update) | async-done | bytes 2621456 | tf_op jit(solution)/shard_map/reduce_scatter | solution.py:75
  651.3 70.9 %psum.71 = f32[4096]{0:T(1024)S(1)} all-reduce(f32[4096]{0:T(1024)S(1)} %get-tuple-element.405), channel_id=1, replica_groups=mesh['dp'=2,'row'=4,'col'=4] {'row','col'}, use_global_device_ids=true, to_apply=%region_9.10 | all-reduce | flops 4096 | bytes 32768 | tf_op jit(solution)/shard_map/psum | solution.py:52
  725.4 24.7 all-gather.17.cloned.1.call-done
  750.1 19.0 fusion.69
  774.2 74.6 %all-gather.13.cloned.1.call-done = bf16[4096,640]{0,1:T(8,128)(2,1)} async-done(((bf16[4096,160]{0,1:T(8,128)(2,1)}), bf16[4096,640]{0,1:T(8,128)(2,1)}) %all-gather.13.cloned.1.call-update) | async-done | bytes 5242896 | tf_op jit(solution)/shard_map/all_gather | solution.py:58
  848.8 40.5 %fusion.67 = f32[4096,3456]{1,0:T(8,128)} fusion(bf16[4096,640]{0,1:T(8,128)(2,1)} %all-gather.13.cloned.1.call-done, bf16[640,3456]{0,1:T(8,128)(2,1)} %constant_dynamic-update-slice_fusion), kind=kOutput, calls=%fused_computation.132 | convolution fusion | flops 18119393280 | bytes 66289664 | tf_op jit(solution)/shard_map/dot_general | solution.py:63
  889.3 168.3 %reduce-scatter.17.cloned.1.call-done = f32[1024,1728]{1,0:T(8,128)} async-done(((f32[4096,1728]{1,0:T(8,128)}), f32[1024,1728]{1,0:T(8,128)}) %reduce-scatter.17.cloned.1.call-update) | async-done | bytes 7077904 | tf_op jit(solution)/shard_map/reduce_scatter | solution.py:83
  1057.7 386.9 %reduce-scatter.13.cloned.1.call-done = f32[1024,3456]{1,0:T(8,128)} async-done(((f32[4096,3456]{1,0:T(8,128)}), f32[1024,3456]{1,0:T(8,128)}) %reduce-scatter.13.cloned.1.call-update) | async-done | bytes 14155792 | tf_op jit(solution)/shard_map/reduce_scatter | solution.py:62
  1463.4 171.9 %all-gather.19.cloned.1.call-done = bf16[4096,3456]{1,0:T(8,128)(2,1)} async-done(((bf16[1024,3456]{1,0:T(8,128)(2,1)}), bf16[4096,3456]{1,0:T(8,128)(2,1)}) %all-gather.19.cloned.1.call-update) | async-done | bytes 28311568 | tf_op jit(solution)/shard_map/all_gather | solution.py:92
  1635.3 25.6 fusion.70
  1660.9 178.1 %reduce-scatter.19.cloned.1.call-done = f32[4096,160]{0,1:T(8,128)} async-done(((f32[4096,640]{0,1:T(8,128)}), f32[4096,160]{0,1:T(8,128)}) %reduce-scatter.19.cloned.1.call-update) | async-done | bytes 2621456 | tf_op jit(solution)/shard_map/reduce_scatter | solution.py:103
  1843.6 61.6 %psum.72 = f32[4096]{0:T(1024)} all-reduce(f32[4096]{0:T(1024)} %get-tuple-element.350), channel_id=1, replica_groups=mesh['dp'=2,'row'=4,'col'=4] {'row','col'}, use_global_device_ids=true, to_apply=%region_15.16 | all-reduce | flops 4096 | bytes 32768 | tf_op jit(solution)/shard_map/psum | solution.py:109
  1911.0 96.7 %all-gather.21.cloned.1.call-done = bf16[4096,640]{0,1:T(8,128)(2,1)} async-done(((bf16[4096,160]{0,1:T(8,128)(2,1)}), bf16[4096,640]{0,1:T(8,128)(2,1)}) %all-gather.21.cloned.1.call-update) | async-done | bytes 5242896 | tf_op jit(solution)/shard_map/all_gather | solution.py:79
  2017.8 83.0 %reduce-scatter.21.cloned.1.call-done = f32[1024,640]{1,0:T(8,128)} async-done(((f32[4096,640]{1,0:T(8,128)}), f32[1024,640]{1,0:T(8,128)}) %reduce-scatter.21.cloned.1.call-update) | async-done | bytes 2621456 | tf_op jit(solution)/shard_map/reduce_scatter | solution.py:83
  2104.2 265.6 %while.32 = (s32[]{:T(128)}, f32[2048,2,80]{0,2,1:T(8,128)}, f32[2048,2,80]{0,2,1:T(8,128)}, f32[2,512,2,4,80]{1,0,4,3,2:T(2,128)}, s32[2]{0:T(128)S(1)}, /*inde...) while((s32[]{:T(128)}, f32[2048,2,80]{0,2,1:T(8,128)}, ...), condition=%wide.region_19.20_spmd.clone, body=%wide.region_17.19_spmd.clone.sunk | while | flops 6842878464 | bytes 349985152 | solution.py:182
  2107.8 20.0 fusion.127
  2143.3 23.9 fusion.129
  2167.2 27.6 fusion.130
  2213.9 24.3 dynamic_update_slice.25
  2274.3 23.9 fusion.129
  2298.2 27.7 fusion.130
  2345.1 24.3 dynamic_update_slice.25
  2401.4 27.5 convolution_convert_fusion
  2483.4 178.9 %all-reduce.8.cloned.1.call-done = (bf16[640,960]{0,1:T(8,128)(2,1)}, bf16[640,3456]{1,0:T(8,128)(2,1)}, bf16[640,640]{1,0:T(8,128)(2,1)}, bf16[1728,640]{1,0:T(8,128)(2,1)}) async-done(((bf16[640,960]{0,1:T(8,128)(2,1)}, bf16[640,3456]{1,0:T(8,128)(2,1)}, bf16[640,640]{1,0:T(8,128)(2,1)}, bf16[1728,640]{1,0:T(8,128)(2,1)}), (bf16[640,960]{0,1:T(8,128)(2,1)}, bf16[640,3456]{1,0:T(8,128)(2,1)}, ...) | async-done | bytes 8683536 | tf_op jit(solution)/shard_map/psum | solution.py:297
  2690.2 152.7 %reduce-scatter.23.cloned.1.call-done = f32[4096,160]{0,1:T(8,128)} async-done(((f32[4096,640]{0,1:T(8,128)}), f32[4096,160]{0,1:T(8,128)}) %reduce-scatter.23.cloned.1.call-update) | async-done | bytes 2621456 | tf_op jit(solution)/shard_map/reduce_scatter | solution.py:103
  2854.2 67.7 %psum.73 = f32[4096]{0:T(1024)} all-reduce(f32[4096]{0:T(1024)} %get-tuple-element.352), channel_id=1, replica_groups=mesh['dp'=2,'row'=4,'col'=4] {'row','col'}, use_global_device_ids=true, to_apply=%region_22.23 | all-reduce | flops 4096 | bytes 32768 | tf_op jit(solution)/shard_map/psum | solution.py:109
  2923.2 103.7 %reduce-scatter.15.cloned.1.call-done = f32[4096,160]{0,1:T(8,128)} async-done(((f32[4096,640]{0,1:T(8,128)}), f32[4096,160]{0,1:T(8,128)}) %reduce-scatter.15.cloned.1.call-update) | async-done | bytes 2621456 | tf_op jit(solution)/shard_map/reduce_scatter | solution.py:75
  (249 shorter events, 422.9 us)
Async XLA Ops:
  7.2 742.9 %copy-start = (bf16[1728,640]{1,0:T(8,128)(2,1)S(1)}, bf16[1728,640]{1,0:T(8,128)(2,1)}, u32[]{:S(2)}) copy-start(bf16[1728,640]{1,0:T(8,128)(2,1)} %param.26) | copy-start | bytes 6635524
  7.2 164.0 %all-gather.9.cloned.1.call-start = ((), (), s32[]{:S(2)}) async-start(), calls=%async_computation.8 | async-start | bytes 6553600 | tf_op jit(solution)/shard_map/all_gather | solution.py:58
  75.7 226.1 %reduce-scatter.9.cloned.1.call-start = ((), (), s32[]{:S(2)}) async-start(), calls=%async_computation.9 | async-start | bytes 19660800 | tf_op jit(solution)/shard_map/reduce_scatter | solution.py:62
  76.0 107.4 %copy-start.21 = (bf16[640,160]{1,0:T(8,128)(2,1)}, bf16[640,160]{1,0:T(8,128)(2,1)S(1)}, u32[]{:S(2)}) copy-start(bf16[640,160]{1,0:T(8,128)(2,1)S(1)} %copy.31) | copy-start | bytes 614404
  76.2 107.2 %copy-start.23 = (bf16[640,160]{1,0:T(8,128)(2,1)}, bf16[640,160]{1,0:T(8,128)(2,1)S(1)}, u32[]{:S(2)}) copy-start(bf16[640,160]{1,0:T(8,128)(2,1)S(1)} %copy.32) | copy-start | bytes 614404
  183.5 275.1 %all-gather.11.cloned.1.call-start = ((), (), s32[]{:S(2)}) async-start(), calls=%async_computation.10 | async-start | bytes 6553600 | tf_op jit(solution)/shard_map/all_gather | solution.py:71
  184.8 124.0 %copy-start.9 = (f32[1024,40]{0,1:T(8,128)}, f32[1024,40]{0,1:T(8,128)S(1)}, u32[]{:S(2)}) copy-start(f32[1024,40]{0,1:T(8,128)S(1)} %get-tuple-element.428) | copy-start | bytes 491524
  184.8 124.0 %copy-start.11 = (f32[1024,40]{0,1:T(8,128)}, f32[1024,40]{0,1:T(8,128)S(1)}, u32[]{:S(2)}) copy-start(f32[1024,40]{0,1:T(8,128)S(1)} %get-tuple-element.429) | copy-start | bytes 491524
  303.0 7.5 collective-permute-start.1
  306.0 5.5 collective-permute-start
  414.7 232.9 %reduce-scatter.11.cloned.1.call-start = ((), (), s32[]{:S(2)}) async-start(), calls=%async_computation.11 | async-start | bytes 13107200 | tf_op jit(solution)/shard_map/reduce_scatter | solution.py:75
  469.4 178.2 %copy-start.4 = (bf16[4096,160]{0,1:T(8,128)(2,1)S(1)}, bf16[4096,160]{0,1:T(8,128)(2,1)}, u32[]{:S(2)}) copy-start(bf16[4096,160]{0,1:T(8,128)(2,1)} %param.17) | copy-start | bytes 3932164
  469.4 280.6 %all-gather.17.cloned.1.call-start = ((), (), s32[]{:S(2)}) async-start(), calls=%async_computation.16 | async-start | bytes 6553600 | tf_op jit(solution)/shard_map/all_gather | solution.py:79
  470.0 378.8 %all-gather.13.cloned.1.call-start = ((), (), s32[]{:S(2)}) async-start(), calls=%async_computation.12 | async-start | bytes 6553600 | tf_op jit(solution)/shard_map/all_gather | solution.py:58
  722.2 1183.8 %copy-start.19 = (f32[4096]{0:T(1024)}, f32[4096]{0:T(1024)S(1)}, u32[]{:S(2)}) copy-start(f32[4096]{0:T(1024)S(1)} %add_rsqrt_fusion) | copy-start | bytes 49156
  725.4 332.3 %reduce-scatter.17.cloned.1.call-start = ((), (), s32[]{:S(2)}) async-start(), calls=%async_computation.17 | async-start | bytes 36700160 | tf_op jit(solution)/shard_map/reduce_scatter | solution.py:83
  769.1 675.5 %reduce-scatter.13.cloned.1.call-start = ((), (), s32[]{:S(2)}) async-start(), calls=%async_computation.13 | async-start | bytes 70778880 | tf_op jit(solution)/shard_map/reduce_scatter | solution.py:62
  889.3 746.0 %all-gather.19.cloned.1.call-start = ((), (), s32[]{:S(2)}) async-start(), calls=%async_computation.18 | async-start | bytes 35389440 | tf_op jit(solution)/shard_map/all_gather | solution.py:92
  1462.9 376.2 %reduce-scatter.19.cloned.1.call-start = ((), (), s32[]{:S(2)}) async-start(), calls=%async_computation.19 | async-start | bytes 13107200 | tf_op jit(solution)/shard_map/reduce_scatter | solution.py:103
  1660.9 245.7 %copy-start.8 = (bf16[4096,160]{0,1:T(8,128)(2,1)S(1)}, bf16[4096,160]{0,1:T(8,128)(2,1)}, u32[]{:S(2)}) copy-start(bf16[4096,160]{0,1:T(8,128)(2,1)} %param.27) | copy-start | bytes 3932164
  1660.9 346.7 %all-gather.21.cloned.1.call-start = ((), (), s32[]{:S(2)}) async-start(), calls=%async_computation.20 | async-start | bytes 6553600 | tf_op jit(solution)/shard_map/all_gather | solution.py:79
  1910.9 189.9 %reduce-scatter.21.cloned.1.call-start = ((), (), s32[]{:S(2)}) async-start(), calls=%async_computation.21 | async-start | bytes 13107200 | tf_op jit(solution)/shard_map/reduce_scatter | solution.py:83
  2017.0 366.9 %all-gather.15.cloned.1.call-start = ((), (), s32[]{:S(2)}) async-start(), calls=%async_computation.14 | async-start | bytes 18350080 | tf_op jit(solution)/shard_map/all_gather | solution.py:71
  2017.8 427.4 %all-gather.23.cloned.1.call-start = ((), (), s32[]{:S(2)}) async-start(), calls=%async_computation.22 | async-start | bytes 9830400 | tf_op jit(solution)/shard_map/all_gather | solution.py:92
  2375.9 5.9 collective-permute-start.3
  2377.2 4.2 collective-permute-start.2
  2383.9 278.5 %all-reduce.8.cloned.1.call-start = ((), (), s32[]{:S(2)}) async-start(), calls=%async_computation.24 | async-start | bytes 17367040 | tf_op jit(solution)/shard_map/psum | solution.py:297
  2456.2 386.7 %reduce-scatter.23.cloned.1.call-start = ((), (), s32[]{:S(2)}) async-start(), calls=%async_computation.23 | async-start | bytes 13107200 | tf_op jit(solution)/shard_map/reduce_scatter | solution.py:103
  2467.8 559.1 %reduce-scatter.15.cloned.1.call-start = ((), (), s32[]{:S(2)}) async-start(), calls=%async_computation.15 | async-start | bytes 13107200 | tf_op jit(solution)/shard_map/reduce_scatter | solution.py:75
  2682.5 160.5 %copy-start.5 = (bf16[4096,160]{0,1:T(8,128)(2,1)S(1)}, bf16[4096,160]{0,1:T(8,128)(2,1)}, u32[]{:S(2)}) copy-start(bf16[4096,160]{0,1:T(8,128)(2,1)} %param.17) | copy-start | bytes 3932164
  2682.5 160.5 %copy-start.26 = (f32[4096]{0:T(1024)S(1)}, f32[4096]{0:T(1024)}, u32[]{:S(2)}) copy-start(f32[4096]{0:T(1024)} %copy-done.25) | copy-start | bytes 49156
  2688.2 338.7 %copy-start.20 = (f32[4096]{0:T(1024)S(1)}, f32[4096]{0:T(1024)}, u32[]{:S(2)}) copy-start(f32[4096]{0:T(1024)} %copy-done.19) | copy-start | bytes 49156
  (34 other events, 580.3 us)
Sparse Core Ops, SparseCore 0:
  75.9 95.3 all-gather.8
  183.6 118.2 reduce-scatter.8
  414.8 43.7 all-gather.10
  469.5 178.0 reduce-scatter.10
  649.0 101.0 all-gather.16
  752.1 96.6 all-gather.12
  851.4 206.2 reduce-scatter.16
  1060.4 384.1 reduce-scatter.12
  1463.0 172.2 all-gather.18
  1661.0 178.0 reduce-scatter.18
  1911.0 96.5 all-gather.20
  2017.1 83.6 reduce-scatter.20
  2103.0 94.0 all-gather.14
  2384.0 61.1 all-gather.22
  2456.3 205.9 all-reduce.7
  2664.5 178.3 reduce-scatter.22
  2845.1 181.6 reduce-scatter.14
where the time goes:
time: 3050 us; the launch traced here: 3040 us
  waiting for transfers between devices  2070 us (68%)
  matrix products  414 us (14%)
  blocking collectives  269 us (9%)
  other arithmetic  160 us (5%)
  local copies, waits for them, and re-layouts  106 us (3%)
    reduce_scatter x2, waiting for transfers between devices, row_products(): lax.psum_scatter(jnp.dot(gathered, weight, preferred_element_type=jnp.flo...  504 us
    reduce_scatter x2, waiting for transfers between devices, grad_col_sum(): lax.psum_scatter(partial_value, 'col', scatter_dimension=1, tiled=True)  331 us
    reduce_scatter x2, waiting for transfers between devices, col_sum(): lax.psum_scatter(partial_value, 'col', scatter_dimension=1, tiled=True)  281 us
    reduce_scatter x2, waiting for transfers between devices, grad_rows(): lax.psum_scatter(lax.dot_general(cols, weight, (((1,), (1,)), ((), ())),...  251 us
    all_gather x2, waiting for transfers between devices, grad_fold(): piece = lax.all_gather(grads, 'row', axis=0, tiled=True)  183 us
    psum x1, waiting for transfers between devices, body(): lax.psum(qkv_wgrad.astype(jnp.bfloat16), 'dp').astype(jnp.float32)  179 us
    all_gather x2, waiting for transfers between devices, spread_normed(): return lax.all_gather(normed, 'col', axis=1, tiled=True)  170 us
    psum x2, blocking collectives, norm_scale(): total = lax.psum(local, ('row', 'col'))  134 us
  transfers between devices with their start and end apart: 21, of which 17 were waited for; matrix products, arithmetic and copies ran while one was open for 15% of the time, Pallas kernels for 0%

commit v1 on v0

v1 whole, which is shorter than its diff:
```python
import functools

import jax
import jax.numpy as jnp
from jax import lax
from jax.experimental import pallas as pl
from jax.experimental.pallas import tpu as pltpu
from jax.sharding import PartitionSpec as P

D = 2560
HEAD = 80
EPS = 1e-05
THETA = 10000.0
NEG = -1e30
LOG2E = 1.4426950408889634
LN2 = 0.6931471805599453
BF = jnp.bfloat16
F32 = jnp.float32
TN = (((0,), (0,)), ((), ()))
NT = (((1,), (1,)), ((), ()))


def dot(left, right, dims=(((1,), (0,)), ((), ()))):
    return lax.dot_general(left, right, dims, preferred_element_type=F32)


def swapped(value, axis, mask):
    size = lax.axis_size(axis)
    return lax.ppermute(value, axis, [(i, i ^ mask) for i in range(size)])


def bit_order(size):
    bits = [1 << i for i in range(size.bit_length() - 1)]
    return bits[1:] + bits[:1]


def gather_blocks(own, axis):
    size = lax.axis_size(axis)
    blocks = {0: own}
    for bit in bit_order(size):
        for k in list(blocks):
            blocks[k | bit] = swapped(blocks[k], axis, bit)
    return [blocks[k] for k in range(size)]


def reduce_blocks(blocks, axis, low=True):
    size = lax.axis_size(axis)
    held = {k: blocks[k] for k in range(size)}
    for bit in reversed(bit_order(size)):
        for k in [k for k in held if k & bit]:
            other = swapped(held.pop(k), axis, bit)
            total = held[k ^ bit].astype(F32) + other.astype(F32)
            held[k ^ bit] = total.astype(BF) if low else total
    return held[0]


def exchange_blocks(blocks, axis):
    return [blocks[0]] + [swapped(blocks[k], axis, k) for k in range(1, len(blocks))]


def by_xor(value, index, axis):
    parts = [
        lax.dynamic_index_in_dim(value, index ^ k, axis, keepdims=True)
        for k in range(value.shape[axis])
    ]
    return jnp.concatenate(parts, axis=axis)


def grant(mib):
    return pltpu.CompilerParams(vmem_limit_bytes=mib * 1024 * 1024)


def project_kernel(count, *refs):
    weights, x_ref, out_ref = refs[:count], refs[count], refs[count + 1]
    total = None
    for k in range(count):
        part = dot(weights[k][...], x_ref[k], TN)
        total = part if total is None else total + part
    out_ref[...] = total.astype(out_ref.dtype)


def project(weights, x, tile, dtype):
    count, depth, tokens = x.shape
    width = weights[0].shape[1]
    return pl.pallas_call(
        functools.partial(project_kernel, count),
        out_shape=jax.ShapeDtypeStruct((width, tokens), dtype),
        grid=(pl.cdiv(width, tile),),
        in_specs=[pl.BlockSpec((depth, tile), lambda n: (0, n))] * count
        + [pl.BlockSpec((count, depth, tokens), lambda n: (0, 0, 0))],
        out_specs=pl.BlockSpec((tile, tokens), lambda n: (n, 0)),
        compiler_params=grant(56),
        name="project",
    )(*weights, x)


def fan_kernel(count, cols, *refs):
    weights, x_ref, out_ref = refs[:count], refs[count], refs[count + 1]
    piece = out_ref.shape[2]
    for k in range(count):
        part = dot(weights[k][...], x_ref[...], TN)
        for c in range(cols):
            out_ref[c, k] = part[c * piece : (c + 1) * piece].astype(out_ref.dtype)


def fan_out(weights, x, cols):
    count = len(weights)
    piece = weights[0].shape[1] // cols
    return pl.pallas_call(
        functools.partial(fan_kernel, count, cols),
        out_shape=jax.ShapeDtypeStruct((cols, count, piece, x.shape[1]), BF),
        compiler_params=grant(56),
        name="fan_out",
    )(*weights, x)


def pull_kernel(count, *refs):
    weights, x_ref, out_ref = refs[:count], refs[count], refs[count + 1]
    total = None
    for k in range(count):
        part = dot(weights[k][...], x_ref[k])
        total = part if total is None else total + part
    out_ref[...] = total.astype(out_ref.dtype)


def pull(weights, x, tile, dtype):
    count, depth, tokens = x.shape
    width = weights[0].shape[0]
    return pl.pallas_call(
        functools.partial(pull_kernel, count),
        out_shape=jax.ShapeDtypeStruct((width, tokens), dtype),
        grid=(width // tile,),
        in_specs=[pl.BlockSpec((tile, depth), lambda n: (n, 0))] * count
        + [pl.BlockSpec((count, depth, tokens), lambda n: (0, 0, 0))],
        out_specs=pl.BlockSpec((tile, tokens), lambda n: (n, 0)),
        compiler_params=grant(56),
        name="pull",
    )(*weights, x)


def tile_masks(seg_q, seg_k, start_q, start_k, size_q, size_k):
    rows = lax.broadcasted_iota(jnp.int32, (size_k, size_q), 0) + start_k
    cols = lax.broadcasted_iota(jnp.int32, (size_k, size_q), 1) + start_q
    seen = rows <= cols
    if seg_q is not None:
        seen = seen & (seg_k == seg_q)
    return seen


def attend_kernel(tile, q_ref, k_ref, v_ref, seg_row, seg_col, out_ref, lse_ref):
    tokens = q_ref.shape[-1]
    for half in range(2):
        for i in range(tokens // tile):
            at = i * tile
            span = slice(at, at + tile)
            query = q_ref[half, 0, :, span]
            ends = at + tile
            pieces = []
            if half == 1:
                pieces.append((0, 0, tokens, None))
                pieces.append((1, 0, ends, (seg_row[:, span], seg_col[:ends])))
            else:
                if at:
                    pieces.append((0, 0, at, None))
                pieces.append((0, at, ends, (None, None)))
            scores = []
            for which, begin, end, segs in pieces:
                part = dot(k_ref[which, begin:end, :], query)
                if segs is not None:
                    seen = tile_masks(segs[0], segs[1], at, begin, tile, end - begin)
                    part = jnp.where(seen, part, NEG)
                scores.append(part)
            peak = functools.reduce(
                jnp.maximum, [jnp.max(s, axis=0, keepdims=True) for s in scores]
            )
            total = None
            out = None
            for (which, begin, end, _), part in zip(pieces, scores):
                weights = jnp.exp2(part - peak)
                mass = jnp.sum(weights, axis=0, keepdims=True)
                value = dot(v_ref[which, :, begin:end], weights.astype(BF))
                total = mass if total is None else total + mass
                out = value if out is None else out + value
            out_ref[half, 0, :, span] = (out / total).astype(BF)
            lse_ref[half, 0, :, span] = peak + jnp.log2(total)


def attend(q, k, v, seg):
    _, heads, width, tokens = q.shape
    tile = min(256, tokens)
    head_block = pl.BlockSpec((2, 1, width, tokens), lambda h: (0, h, 0, 0))
    whole = lambda a: pl.BlockSpec(a.shape, lambda h: (0,) * a.ndim)
    seg_row, seg_col = seg[None, :], seg[:, None]
    return pl.pallas_call(
        functools.partial(attend_kernel, tile),
        out_shape=(
            jax.ShapeDtypeStruct(q.shape, BF),
            jax.ShapeDtypeStruct((2, heads, 1, tokens), F32),
        ),
        grid=(heads,),
        in_specs=[head_block, whole(k), whole(v), whole(seg_row), whole(seg_col)],
        out_specs=(head_block, pl.BlockSpec((2, 1, 1, tokens), lambda h: (0, h, 0, 0))),
        compiler_params=grant(56),
        name="attend",
    )(q, k, v, seg_row, seg_col)


def attend_back_kernel(
    tile,
    q_ref,
    g_ref,
    qn_ref,
    gn_ref,
    o_ref,
    k_ref,
    kt_ref,
    v_ref,
    lse_ref,
    seg_row,
    seg_col,
    dq_ref,
    dk_ref,
    dv_ref,
):
    tokens = q_ref.shape[-1]

    @pl.when(pl.program_id(0) == 0)
    def _():
        dk_ref[...] = jnp.zeros_like(dk_ref)
        dv_ref[...] = jnp.zeros_like(dv_ref)

    for half in range(2):
        for i in range(tokens // tile):
            at = i * tile
            span = slice(at, at + tile)
            ends = at + tile
            query = q_ref[half, 0, :, span]
            grad = g_ref[half, 0, :, span]
            lse = lse_ref[half, 0, :, span]
            delta = jnp.sum(
                grad.astype(F32) * o_ref[half, 0, :, span].astype(F32), axis=0, keepdims=True
            )
            query_rows = qn_ref[half, 0, span, :]
            grad_rows = gn_ref[half, 0, span, :]
            pieces = []
            if half == 1:
                pieces.append((0, 0, tokens, None))
                pieces.append((1, 0, ends, (seg_row[:, span], seg_col[:ends])))
            else:
                if at:
                    pieces.append((0, 0, at, None))
                pieces.append((0, at, ends, (None, None)))
            dq = None
            for which, begin, end, segs in pieces:
                part = dot(k_ref[which, begin:end, :], query)
                if segs is not None:
                    seen = tile_masks(segs[0], segs[1], at, begin, tile, end - begin)
                    part = jnp.where(seen, part, NEG)
                weights = jnp.exp2(part - lse)
                dprod = dot(v_ref[which, begin:end, :], grad)
                dscore = (weights * (dprod - delta)).astype(BF)
                dv_ref[which, begin:end, :] += dot(weights.astype(BF), grad_rows)
                dk_ref[which, begin:end, :] += dot(dscore, query_rows)
                more = dot(kt_ref[which, :, begin:end], dscore)
                dq = more if dq is None else dq + more
            dq_ref[half, 0, :, span] = dq


def attend_back(q, g, out, k, v, lse, seg):
    _, heads, width, tokens = q.shape
    tile = min(256, tokens)
    head_block = pl.BlockSpec((2, 1, width, tokens), lambda h: (0, h, 0, 0))
    row_block = pl.BlockSpec((2, 1, tokens, width), lambda h: (0, h, 0, 0))
    whole = lambda a: pl.BlockSpec(a.shape, lambda h: (0,) * a.ndim)
    seg_row, seg_col = seg[None, :], seg[:, None]
    k_rows, v_rows = k.swapaxes(1, 2), v.swapaxes(1, 2)
    fixed = pl.BlockSpec((2, tokens, width), lambda h: (0, 0, 0))
    return pl.pallas_call(
        functools.partial(attend_back_kernel, tile),
        out_shape=(
            jax.ShapeDtypeStruct(q.shape, F32),
            jax.ShapeDtypeStruct((2, tokens, width), F32),
            jax.ShapeDtypeStruct((2, tokens, width), F32),
        ),
        grid=(heads,),
        in_specs=[
            head_block,
            head_block,
            row_block,
            row_block,
            head_block,
            whole(k_rows),
            whole(k),
            whole(v_rows),
            pl.BlockSpec((2, 1, 1, tokens), lambda h: (0, h, 0, 0)),
            whole(seg_row),
            whole(seg_col),
        ],
        out_specs=(head_block, fixed, fixed),
        compiler_params=grant(56),
        name="attend_back",
    )(q, g, q.swapaxes(2, 3), g.swapaxes(2, 3), out, k_rows, k, v_rows, lse, seg_row, seg_col)


def rope_parts(positions, width):
    half = width // 2
    freq = THETA ** (-jnp.arange(half, dtype=F32) * 2.0 / width)
    angle = freq[:, None] * positions.astype(F32)[None, :]
    return (jnp.cos(angle), jnp.sin(angle))


def rotate(value, cosine, sine):
    half = value.shape[-2] // 2
    first, second = value[..., :half, :], value[..., half:, :]
    return jnp.concatenate(
        [first * cosine - second * sine, second * cosine + first * sine], axis=-2
    )


def normed(gathered, gain):
    cols, count, piece, tokens = gathered.shape
    value = gathered.astype(F32)
    scale = lax.rsqrt(jnp.sum(value * value, axis=(0, 1, 2)) / D + EPS)
    low = (value * scale * gain[..., None]).astype(BF)
    return by_row(low), scale


def by_row(value):
    cols, count, piece, tokens = value.shape
    return value.swapaxes(0, 1).reshape(count, cols * piece, tokens)


def norm_back(partials, gathered, gain, scale, inner):
    cols, count, piece, tokens = gathered.shape
    grads = jnp.stack(partials).reshape(count, cols, piece, tokens).swapaxes(0, 1)
    value = gathered.astype(F32)
    gain_share = jnp.sum(grads * (value * scale), axis=3)
    share = scale * (gain[..., None] * grads) - value * (scale * scale * inner / D)
    return share.astype(BF), gain_share


def spread_cols(value):
    return lax.all_gather(value, "col", axis=0, tiled=False)


def sum_cols(value):
    return lax.psum_scatter(value, "col", scatter_dimension=0, tiled=False)


def over_dp(value):
    low = value.astype(BF)
    total = low.astype(F32)
    size = lax.axis_size("dp")
    for step in range(1, size):
        other = lax.ppermute(low, "dp", [(i, (i + step) % size) for i in range(size)])
        total = total + other.astype(F32)
    return total


def gain_total(share):
    cols, count, piece = share.shape
    mine = lax.psum_scatter(share, "col", scatter_dimension=0, tiled=False)
    mine = reduce_blocks([mine[k] for k in range(count)], "row", low=False)
    return over_dp(mine)


def weight_total(blocks):
    return over_dp(reduce_blocks(blocks, "row"))


def body(
    layer_input,
    attn_gain,
    mlp_gain,
    query_weight,
    key_weight,
    value_weight,
    mix_weight,
    gate_weight,
    up_weight,
    down_weight,
    output_grad,
    segment_ids,
    position_ids,
):
    rows = segment_ids.shape[0]
    count = lax.axis_size("row")
    cols = lax.axis_size("col")
    piece = layer_input.shape[1]
    row = lax.axis_index("row")
    first_core = row % 2 == 0
    q_width = query_weight.shape[1]
    kv_width = key_weight.shape[1]
    kv_local = kv_width // HEAD
    q_half = q_width // 2
    own_kv = kv_local % 2 == 0
    kv_half = kv_width // 2 if own_kv else kv_width
    assert kv_half == HEAD
    heads = q_half // HEAD
    ff_width = gate_weight.shape[1]

    halves = []
    for h in range(2):
        halves.append(query_weight[:, h * q_half : (h + 1) * q_half])
        at = h * kv_half if own_kv else 0
        if own_kv or h == 0:
            halves.append(key_weight[:, at : at + kv_half])
            halves.append(value_weight[:, at : at + kv_half])
    qkv_width = q_width + 2 * kv_width
    padded = -(-qkv_width // 256) * 256
    halves.append(jnp.zeros((query_weight.shape[0], padded - qkv_width), BF))
    qkv_weight = jnp.concatenate(halves, axis=1)
    gate_up_weight = jnp.concatenate([gate_weight, up_weight], axis=1)

    both = jnp.concatenate([layer_input.T, output_grad.T], axis=0)
    both = both.reshape(2 * piece, count, rows)
    outgoing = [
        lax.dynamic_index_in_dim(both, row ^ k, axis=1, keepdims=False) for k in range(count)
    ]
    incoming = exchange_blocks(outgoing, "row")
    source_own = jnp.stack([b[:piece] for b in incoming])
    grad_own = jnp.stack([b[piece:] for b in incoming])

    qkv_blocks = gather_blocks(qkv_weight, "row")
    mix_blocks = gather_blocks(mix_weight, "row")
    gate_up_blocks = gather_blocks(gate_up_weight, "row")
    down_blocks = gather_blocks(down_weight, "row")

    gains = lax.all_gather(jnp.stack([attn_gain, mlp_gain]), ("row", "col"), axis=1, tiled=True)
    gains = gains.reshape(2, count, cols, piece)
    gains = by_xor(gains, row, 1).swapaxes(1, 2)
    gain_one, gain_two = gains[0], gains[1]

    cosine, sine = rope_parts(position_ids, HEAD)
    other_seg = swapped(segment_ids, "row", 1)
    seg = jnp.where(first_core, other_seg, segment_ids)

    source = spread_cols(source_own)
    norm_one, scale_one = normed(source, gain_one)
    qkv = project(qkv_blocks, norm_one, 256, F32)
    scale = HEAD ** (-0.5) * LOG2E

    def half_of(values, at, factor):
        queries = values[at : at + q_half].reshape(heads, HEAD, rows)
        return (rotate(queries, cosine, sine) * factor).astype(BF).reshape(q_half, rows)

    def kv_of(values, at):
        key = rotate(values[at : at + HEAD], cosine, sine).astype(BF)
        return key, values[at + HEAD : at + 2 * HEAD].astype(BF)

    step = q_half + 2 * kv_half
    low_q = [half_of(qkv, 0, scale), half_of(qkv, step, scale)]
    low_k0, low_v0 = kv_of(qkv, q_half)
    low_k1, low_v1 = kv_of(qkv, step + q_half) if own_kv else (low_k0, low_v0)
    sets = [
        jnp.concatenate([low_q[0], low_k0, low_v0]),
        jnp.concatenate([low_q[1], low_k1, low_v1]),
    ]

    def trade(pair):
        mine = jnp.where(first_core, pair[0], pair[1])
        other = swapped(jnp.where(first_core, pair[1], pair[0]), "row", 1)
        return jnp.stack([jnp.where(first_core, mine, other), jnp.where(first_core, other, mine)])

    def trade_back(pair):
        mine = jnp.where(first_core, pair[0], pair[1])
        other = swapped(jnp.where(first_core, pair[1], pair[0]), "row", 1)
        return jnp.where(first_core, mine, other), jnp.where(first_core, other, mine)

    traded = trade(sets)
    queries = traded[:, :q_half].reshape(2, heads, HEAD, rows)
    keys = traded[:, q_half : q_half + HEAD]
    values = traded[:, q_half + HEAD : q_half + 2 * HEAD]
    attn_half, lse = attend(queries, keys.swapaxes(1, 2), values, seg)
    attn_low = jnp.concatenate(trade_back(attn_half.reshape(2, q_half, rows)))
    attn_sum = sum_cols(fan_out(mix_blocks, attn_low, cols))
    residual_own = source_own.astype(F32) + attn_sum.astype(F32)

    residual = spread_cols(residual_own.astype(BF))
    norm_two, scale_two = normed(residual, gain_two)
    gate_up = project(gate_up_blocks, norm_two, 384 if 2 * ff_width % 384 == 0 else 128, BF)
    gate = gate_up[:ff_width].astype(F32)
    up = gate_up[ff_width:].astype(F32)
    sigma = jax.nn.sigmoid(gate)
    act_low = (gate * sigma * up).astype(BF)
    ff_sum = sum_cols(fan_out(down_blocks, act_low, cols))
    output_own = (residual_own + ff_sum.astype(F32)).astype(BF)

    out_grad = by_row(spread_cols(grad_own))
    act_grad = pull(down_blocks, out_grad, 432 if ff_width % 432 == 0 else ff_width, F32)
    gate_part = act_grad * up * sigma * (1.0 + gate * (1.0 - sigma))
    up_part = act_grad * gate * sigma
    inner = jnp.sum(gate_part * gate + up_part * up, axis=0)
    gate_up_grad = jnp.concatenate([gate_part, up_part]).astype(BF)
    share, gain_share = norm_back(
        [dot(w, gate_up_grad) for w in gate_up_blocks], residual, gain_two, scale_two, inner
    )
    residual_grad_own = grad_own.astype(F32) + sum_cols(share).astype(F32)
    mlp_gain_grad = gain_total(gain_share)
    down_grad = weight_total([dot(act_low, out_grad[k], NT).astype(BF) for k in range(count)])
    gate_up_wgrad = weight_total(
        [dot(norm_two[k], gate_up_grad, NT).astype(BF) for k in range(count)]
    )

    mix_cols = by_row(spread_cols(residual_grad_own.astype(BF)))
    attn_grad = pull(mix_blocks, mix_cols, q_width, BF)
    mix_grad = weight_total([dot(attn_low, mix_cols[k], NT).astype(BF) for k in range(count)])
    grad_half = trade([attn_grad[:q_half], attn_grad[q_half:]]).reshape(2, heads, HEAD, rows)
    dq, dk, dv = attend_back(queries, grad_half, attn_half, keys, values, lse, seg)
    dq = (dq * HEAD ** (-0.5)).astype(BF).reshape(2, q_half, rows)
    dk = (dk * LN2).astype(BF).swapaxes(1, 2)
    dv = dv.astype(BF).swapaxes(1, 2)
    back0, back1 = trade_back(jnp.concatenate([dq, dk, dv], axis=1))

    def unturned(values, heads_in):
        turned = rotate(values.astype(F32).reshape(heads_in, HEAD, rows), cosine, -sine)
        return turned.reshape(heads_in * HEAD, rows).astype(BF)

    back = [unturned(back0[:q_half], heads)]
    kv0, kv1 = back0[q_half:], back1[q_half:]
    if own_kv:
        back += [unturned(kv0[:HEAD], 1), kv0[HEAD:]]
        back += [unturned(back1[:q_half], heads), unturned(kv1[:HEAD], 1), kv1[HEAD:]]
    else:
        kv = kv0.astype(F32) + kv1.astype(F32)
        back += [unturned(kv[:HEAD], 1), kv[HEAD:].astype(BF), unturned(back1[:q_half], heads)]
    back.append(jnp.zeros((padded - qkv_width, rows), BF))
    qkv_grad = jnp.concatenate(back)
    raw_low = qkv
    inner = jnp.sum(qkv_grad.astype(F32) * raw_low, axis=0)
    share, gain_share = norm_back(
        [dot(w, qkv_grad) for w in qkv_blocks], source, gain_one, scale_one, inner
    )
    input_grad_own = residual_grad_own + sum_cols(share).astype(F32)
    attn_gain_grad = gain_total(gain_share)
    qkv_wgrad = weight_total([dot(norm_one[k], qkv_grad, NT).astype(BF) for k in range(count)])

    def all_tokens(value):
        got = exchange_blocks([value[k] for k in range(count)], "row")
        placed = by_xor(jnp.stack(got), row, 0)
        return placed.transpose(0, 2, 1).reshape(count * rows, piece)

    layer_output = all_tokens(output_own)
    input_grad = all_tokens(input_grad_own)

    q_grad = [qkv_wgrad[:, :q_half], qkv_wgrad[:, step : step + q_half]]
    if own_kv:
        at = step + q_half
        k_grad = [qkv_wgrad[:, q_half : q_half + HEAD], qkv_wgrad[:, at : at + HEAD]]
        v_grad = [
            qkv_wgrad[:, q_half + HEAD : q_half + 2 * HEAD],
            qkv_wgrad[:, at + HEAD : at + 2 * HEAD],
        ]
    else:
        k_grad = [qkv_wgrad[:, q_half : q_half + HEAD]]
        v_grad = [qkv_wgrad[:, q_half + HEAD : q_half + 2 * HEAD]]
    return (
        layer_output,
        input_grad,
        attn_gain_grad,
        mlp_gain_grad,
        jnp.concatenate(q_grad, axis=1),
        jnp.concatenate(k_grad, axis=1),
        jnp.concatenate(v_grad, axis=1),
        mix_grad,
        gate_up_wgrad[:, :ff_width],
        gate_up_wgrad[:, ff_width:],
        down_grad,
    )


def solution(mesh):
    return jax.shard_map(
        body,
        mesh=mesh,
        in_specs=(
            P("dp", ("row", "col")),
            P(("row", "col")),
            P(("row", "col")),
            P("row", "col"),
            P("row", "col"),
            P("row", "col"),
            P("col", "row"),
            P("row", "col"),
            P("row", "col"),
            P("col", "row"),
            P("dp", ("row", "col")),
            P(("dp", "row")),
            P(("dp", "row")),
        ),
        out_specs=(
            P("dp", ("row", "col")),
            P("dp", ("row", "col")),
            P(("row", "col")),
            P(("row", "col")),
            P("row", "col"),
            P("row", "col"),
            P("row", "col"),
            P("col", "row"),
            P("row", "col"),
            P("row", "col"),
            P("col", "row"),
        ),
        check_vma=False,
    )
```

time: 3050 us -> 1190 us (0.39)
  waiting for transfers between devices: 2070 us -> 548 us
  matrix products: 414 us -> 116 us
  blocking collectives: 269 us -> 52.1 us
  Pallas kernels: 0 us -> 142 us
  local copies, waits for them, and re-layouts: 106 us -> 148 us
  other arithmetic: 160 us -> 127 us
    reduce_scatter x8 -> x4, waiting for transfers between devices: 1370 us -> 170 us  [sum_cols(): return lax.psum_scatter(value, 'col', scatter_dimension=0, tiled=False)]
    all_gather x8 -> x4, waiting for transfers between devices: 517 us -> 84.9 us  [spread_cols(): return lax.all_gather(value, 'col', axis=0, tiled=False)]
    dot_general x26 -> x24, matrix products: 414 us -> 116 us  [dot(): return lax.dot_general(left, right, dims, preferred_element_type=F32)]
    ppermute x4 -> x50, waiting for transfers between devices: 0.54 us -> 293 us  [the longest x44 233 us: swapped(): return lax.ppermute(value, axis, [(i, i ^ mask) for i in range(size)])]
    psum x5 -> x0, blocking collectives: 269 us -> none  [the longest x2 134 us: norm_scale(): total = lax.psum(local, ('row', 'col'))]
    psum x1 -> x0, waiting for transfers between devices: 179 us -> none  [body(): lax.psum(qkv_wgrad.astype(jnp.bfloat16), 'dp').astype(jnp.float32)]
    pallas_call x0 -> x8, Pallas kernels: none -> 142 us  [the longest x2 39.5 us: project(): pl.pallas_call(functools.partial(project_kernel, count), out_shape=jax.Sh...]
    dynamic_update_slice x4 -> x0, local copies, waits for them, and re-layouts: 53.4 us -> none  [attend_forward(): lax.scan(step, 0, jnp.arange(rows // block, dtype=jnp.int32))]
  transfers between devices with their start and end apart: 21 -> 58, of which waited for: 17 -> 24; matrix products, arithmetic and copies ran while one was open for 15% -> 24% of each run, Pallas kernels for 0% -> 8%
where the time goes in v1:
time: 1190 us; the launch traced here: 1180 us
  waiting for transfers between devices  548 us (46%)
  local copies, waits for them, and re-layouts  148 us (12%)
  Pallas kernels  142 us (12%)
  other arithmetic  127 us (11%)
  matrix products  116 us (10%)
  blocking collectives  52.1 us (4%)
  starting transfers between devices  31.5 us (3%)
  between operations  16.3 us (1%)
    ppermute x44, waiting for transfers between devices, swapped(): return lax.ppermute(value, axis, [(i, i ^ mask) for i in range(size)])  233 us
    reduce_scatter x4, waiting for transfers between devices, sum_cols(): return lax.psum_scatter(value, 'col', scatter_dimension=0, tiled=False)  170 us
    dot_general x24, matrix products, dot(): return lax.dot_general(left, right, dims, preferred_element_type=F32)  116 us
    all_gather x4, waiting for transfers between devices, spread_cols(): return lax.all_gather(value, 'col', axis=0, tiled=False)  84.9 us
    ppermute x6, waiting for transfers between devices, over_dp(): lax.ppermute(low, 'dp', [(i, (i + step) % size) for i in range(size)])  59.5 us
    unnamed x221, local copies, waits for them, and re-layouts  42.8 us
    pallas_call x2, Pallas kernels, project(): pl.pallas_call(functools.partial(project_kernel, count), out_shape=jax.Sh...  39.5 us
    all_gather x1, blocking collectives, body(): lax.all_gather(jnp.stack([attn_gain, mlp_gain]), ('row', 'col'), axis=1,...  33.4 us
  transfers between devices with their start and end apart: 58, of which 24 were waited for; matrix products, arithmetic and copies ran while one was open for 24% of the time, Pallas kernels for 8%

profile of v1, /device:TPU:0, one launch (start us, length us, event | category | flops | bytes accessed | tf_op | source)
XLA Modules:
  0.0 1180.8 jit_solution(9059891168525660678)
XLA Ops:
  29.9 10.2 collective-permute-done.1
  42.2 11.6 collective-permute-done.2
  64.2 33.4 %all-gather.2 = f32[16,160,2]{1,2,0:T(2,128)S(1)} all-gather(f32[1,160,2]{1,2,0:T(2,128)S(1)} %maximum_bitcast_fusion.7), channel_id=1, replica_groups=mesh['dp'=2,'row'=4,'col'=4] {'row','col'}, dimensions={0}, use_global_device_ids=true | all-gather | bytes 21760 | tf_op jit(solution)/shard_map/all_gather | solution.py:429
  98.7 59.0 %all-gather.12.cloned.1.call-done = bf16[16,160,1024]{2,1,0:T(8,128)(2,1)} async-done(((bf16[4,160,1024]{2,1,0:T(8,128)(2,1)}), bf16[16,160,1024]{2,1,0:T(8,128)(2,1)}) %all-gather.12.cloned.1.call-update) | async-done | bytes 5242896 | tf_op jit(solution)/shard_map/all_gather | solution.py:343
  167.0 11.4 project.2
  217.1 20.9 %attend.1 = (bf16[2,4,80,1024]{3,2,1,0:T(8,128)(2,1)}, f32[2,4,1,1024]{3,2,1,0:T(1,128)}) custom-call(bf16[2,4,80,1024]{3,2,1,0:T(8,128)(2,1)} %bitcast.270, bf16[2,1024,80]{2,1,0:T(8,128)(2,1)} %bitcast.273, bf16[2,80,1024]{2,1,0:T(8,128)(2,1)} %copy.222.v_ref, s32[1,1024]{1,0:T(1,128)} %bitcast.329, s32[1024,1]{1,0:T(8,128)} %copy.223.seg_col), custom_call_target="tpu_custom_call" | custom-call | tf_op jit(solution)/shard_map/attend/pallas_call | solution.py:194
  245.8 9.0 fan_out.2
  264.9 82.4 %reduce-scatter.5.cloned.1.call-done = bf16[1,4,160,1024]{3,2,1,0:T(8,128)(2,1)} async-done(((bf16[4,4,160,1024]{3,2,1,0:T(8,128)(2,1)}), bf16[1,4,160,1024]{3,2,1,0:T(8,128)(2,1)}) %reduce-scatter.5.cloned.1.call-update) | async-done | bytes 1310736 | tf_op jit(solution)/shard_map/reduce_scatter | solution.py:347
  357.4 96.7 %collective-permute-done.16.refs_2_ = bf16[640,3456]{1,0:T(8,128)(2,1)} collective-permute-done((bf16[640,3456]{1,0:T(8,128)(2,1)}, bf16[640,3456]{1,0:T(8,128)(2,1)}, u32[]{:S(2)}, u32[]{:S(2)}) %collective-permute-start.16) | collective-permute-done | bytes 4423712 | tf_op jit(solution)/shard_map/ppermute | solution.py:29
  454.6 45.7 %collective-permute-done.13.refs_2_ = bf16[1728,640]{1,0:T(8,128)(2,1)S(1)} collective-permute-done((bf16[1728,640]{1,0:T(8,128)(2,1)}, bf16[1728,640]{1,0:T(8,128)(2,1)S(1)}, u32[]{:S(2)}, u32[]{:S(2)}) %collective-permute-start.13) | collective-permute-done | bytes 2211872 | tf_op jit(solution)/shard_map/ppermute | solution.py:29
  506.7 16.7 %pull.2 = f32[1728,1024]{1,0:T(8,128)} custom-call(bf16[1728,640]{1,0:T(8,128)(2,1)} %refs_0_.6, bf16[1728,640]{1,0:T(8,128)(2,1)} %collective-permute-done.12.refs_1_, bf16[1728,640]{1,0:T(8,128)(2,1)} %copy-done.10, bf16[1728,640]{1,0:T(8,128)(2,1)} %collective-permute-done.14.refs_3_, bf16[4,640,1024]{2,1,0:T(8,128)(2,1)} %bitcast.259), custom_call_target="tpu_custom_call" | custom-call | tf_op jit(solution)/shard_map/pull/pallas_call | solution.py:129
  523.4 22.6 %all-gather.8.cloned.1.call-done = bf16[4,4,160,1024]{3,2,1,0:T(8,128)(2,1)} async-done(((bf16[1,4,160,1024]{3,2,1,0:T(8,128)(2,1)}), bf16[4,4,160,1024]{3,2,1,0:T(8,128)(2,1)}) %all-gather.8.cloned.1.call-update) | async-done | bytes 5242896 | tf_op jit(solution)/shard_map/all_gather | solution.py:343
  555.1 28.1 %project.3 = bf16[3456,1024]{1,0:T(8,128)(2,1)} custom-call(bf16[640,3456]{1,0:T(8,128)(2,1)} %pad_maximum_fusion.1.refs_0_, bf16[640,3456]{1,0:T(8,128)(2,1)} %collective-permute-done.15.refs_1_, bf16[640,3456]{1,0:T(8,128)(2,1)} %collective-permute-done.16.refs_2_, bf16[640,3456]{1,0:T(8,128)(2,1)} %collective-permute-done.17.refs_3_, ...), custom_call_target="tpu_custom_call" | custom-call | tf_op jit(solution)/shard_map/project/pallas_call | solution.py:85
  583.2 10.2 fusion.18
  593.4 9.8 fusion.80
  603.2 7.3 fusion.79
  610.5 7.3 fusion.78
  635.7 87.4 %reduce-scatter.9.cloned.1.call-done = bf16[1,4,160,1024]{3,2,1,0:T(8,128)(2,1)} async-done(((bf16[4,4,160,1024]{3,2,1,0:T(8,128)(2,1)}), bf16[1,4,160,1024]{3,2,1,0:T(8,128)(2,1)}) %reduce-scatter.9.cloned.1.call-update) | async-done | bytes 1310736 | tf_op jit(solution)/shard_map/reduce_scatter | solution.py:347
  726.1 10.6 convolution_convert_fusion
  749.2 9.4 convolution_convert_fusion.2
  771.8 11.9 %add_convert_fusion.1 = bf16[640,3456]{1,0:T(8,128)(2,1)} fusion(bf16[640,3456]{1,0:T(8,128)(2,1)} %collective-permute-done.43, bf16[640,1024]{1,0:T(8,128)(2,1)} %bitcast.310, bf16[1728,1024]{1,0:T(8,128)(2,1)} %copy-done.30, bf16[1728,1024]{1,0:T(8,128)(2,1)} %copy-done.27), kind=kOutput, calls=%fused_computation.32 | convolution fusion | flops 4555063296 | bytes 17235968 | tf_op jit(solution)/shard_map/dot_general | solution.py:24
  787.5 16.7 %fan_out.3 = bf16[4,4,160,1024]{3,2,1,0:T(8,128)(2,1)} custom-call(bf16[1728,640]{1,0:T(8,128)(2,1)} %refs_0_.6, bf16[1728,640]{1,0:T(8,128)(2,1)} %collective-permute-done.12.refs_1_, bf16[1728,640]{1,0:T(8,128)(2,1)} %copy-done.10, bf16[1728,640]{1,0:T(8,128)(2,1)} %collective-permute-done.14.refs_3_, bf16[1728,1024]{1,0:T(8,128)(2,1)} %get-tuple-element.87.refs_4_), custom_call_target="tpu_custom_call" | custom-call | tf_op jit(solution)/shard_map/fan_out/pallas_call | solution.py:109
  804.2 11.3 collective-permute-done.48
  830.4 9.8 pull.3
  841.7 11.9 %add_convert_fusion.2 = bf16[640,3456]{1,0:T(8,128)(2,1)} fusion(bf16[640,3456]{1,0:T(8,128)(2,1)} %collective-permute-done.42, bf16[640,1024]{1,0:T(8,128)(2,1)} %bitcast.307, bf16[1728,1024]{1,0:T(8,128)(2,1)S(1)} %copy-done.32, bf16[1728,1024]{1,0:T(8,128)(2,1)S(1)} %copy-done.29), kind=kOutput, calls=%fused_computation.33 | convolution fusion | flops 4555063296 | bytes 17235968 | tf_op jit(solution)/shard_map/dot_general | solution.py:24
  861.1 29.6 %attend_back.1 = (f32[2,4,80,1024]{3,2,1,0:T(8,128)}, f32[2,1024,80]{2,1,0:T(8,128)}, f32[2,1024,80]{2,1,0:T(8,128)}) custom-call(bf16[2,4,80,1024]{3,2,1,0:T(8,128)(2,1)} %bitcast.271, bf16[2,4,80,1024]{3,2,1,0:T(8,128)(2,1)} %copy.234.g_ref, bf16[2,4,1024,80]{3,2,1,0:T(8,128)(2,1)} %bitcast.275, bf16[2,4,1024,80]{3,2,1,0:T(8,128)(2,1)} %get-tuple-element.135.gn_ref, ...), custom_call_target="tpu_custom_call" | custom-call | tf_op jit(solution)/shard_map/attend_back/pallas_call | solution.py:278
  898.4 11.0 collective-permute-done.44
  980.4 32.6 %collective-permute-done.45 = bf16[640,3456]{1,0:T(8,128)(2,1)} collective-permute-done((bf16[640,3456]{1,0:T(8,128)(2,1)}, bf16[640,3456]{1,0:T(8,128)(2,1)}, u32[]{:S(2)}, u32[]{:S(2)}) %collective-permute-start.45) | collective-permute-done | bytes 4423712 | tf_op jit(solution)/shard_map/ppermute | solution.py:355
  1053.5 18.7 %all-reduce.2 = (f32[4,4,160]{2,1,0:T(4,128)S(1)}, f32[4,4,160]{2,1,0:T(4,128)S(1)}) all-reduce(f32[4,4,160]{2,1,0:T(4,128)S(1)} %get-tuple-element.83, f32[4,4,160]{2,1,0:T(4,128)S(1)} %copy-done.78), channel_id=8, replica_groups=mesh['dp'=2,'row'=4,'col'=4] {'col'}, use_global_device_ids=true, to_apply=%region_9.10.clone | all-reduce | flops 5120 | bytes 40960
  1084.5 11.1 collective-permute-done.40
  1103.0 26.9 %collective-permute-done.33 = bf16[160]{0:T(256)(128)(2,1)S(1)} collective-permute-done((bf16[160]{0:T(256)(128)(2,1)S(1)}, bf16[160]{0:T(256)(128)(2,1)S(1)}, u32[]{:S(2)}, u32[]{:S(2)}) %collective-permute-start.33) | collective-permute-done | bytes 352 | tf_op jit(solution)/shard_map/ppermute | solution.py:355
  1156.2 13.3 %collective-permute-done.25 = f32[160,1024]{1,0:T(8,128)} collective-permute-done((f32[160,1024]{1,0:T(8,128)}, f32[160,1024]{1,0:T(8,128)}, u32[]{:S(2)}, u32[]{:S(2)}) %collective-permute-start.25) | collective-permute-done | bytes 655392 | tf_op jit(solution)/shard_map/ppermute | solution.py:29
  (492 shorter events, 370.1 us)
Async XLA Ops:
  7.2 150.5 %all-gather.12.cloned.1.call-start = ((), (), s32[]{:S(2)}) async-start(), calls=%async_computation.10 | async-start | bytes 6553600 | tf_op jit(solution)/shard_map/all_gather | solution.py:343
  57.8 289.5 %reduce-scatter.5.cloned.1.call-start = ((), (), s32[]{:S(2)}) async-start(), calls=%async_computation.4 | async-start | bytes 6553600 | tf_op jit(solution)/shard_map/reduce_scatter | solution.py:347
  62.6 35.2 %collective-permute-start.7 = (bf16[640,1024]{1,0:T(8,128)(2,1)S(1)}, bf16[640,1024]{1,0:T(8,128)(2,1)S(1)}, u32[]{:S(2)}, u32[]{:S(2)}) collective-permute-start(bf16[640,1024]{1,0:T(8,128)(2,1)S(1)} %concatenate.92.refs_0_), channel_id=1, source_target_pairs={{0,8},{4,12},{8,0},{12,4},{1,9},{5,13},{9,1},{13,5},{2,10},{6,14},... | collective-permute-start | bytes 3932168 | tf_op jit(solution)/shard_map/ppermute | solution.py:29
  64.2 102.8 %collective-permute-start.6 = (bf16[640,1024]{1,0:T(8,128)(2,1)S(1)}, bf16[640,1024]{1,0:T(8,128)(2,1)}, u32[]{:S(2)}, u32[]{:S(2)}) collective-permute-start(bf16[640,1024]{1,0:T(8,128)(2,1)S(1)} %concatenate.92.refs_0_), channel_id=1, source_target_pairs={{0,4},{4,0},{8,12},{12,8},{1,5},{5,1},{9,13},{13,9},{2,6},{6,2},{1... | collective-permute-start | bytes 3932168 | tf_op jit(solution)/shard_map/ppermute | solution.py:29
  97.8 69.2 %collective-permute-start.8 = (bf16[640,1024]{1,0:T(8,128)(2,1)S(1)}, bf16[640,1024]{1,0:T(8,128)(2,1)}, u32[]{:S(2)}, u32[]{:S(2)}) collective-permute-start(bf16[640,1024]{1,0:T(8,128)(2,1)S(1)} %collective-permute-done.7.refs_2_), channel_id=1, source_target_pairs={{0,4},{4,0},{8,12},{12,8},{1,5},{5,1},{9,13},{13,9},{2,6},{6,2},{1... | collective-permute-start | bytes 3932168 | tf_op jit(solution)/shard_map/ppermute | solution.py:29
  203.9 36.0 %collective-permute-start.4 = (bf16[640,640]{1,0:T(8,128)(2,1)}, bf16[640,640]{1,0:T(8,128)(2,1)}, u32[]{:S(2)}, u32[]{:S(2)}) collective-permute-start(bf16[640,640]{1,0:T(8,128)(2,1)} %refs_0_.7), channel_id=1, source_target_pairs={{0,8},{4,12},{8,0},{12,4},{1,9},{5,13},{9,1},{13,5},{2,10},{6,14},... | collective-permute-start | bytes 2457608 | tf_op jit(solution)/shard_map/ppermute | solution.py:29
  254.8 245.5 %all-gather.14.cloned.1.call-start = ((), (), s32[]{:S(2)}) async-start(), calls=%async_computation.11 | async-start | bytes 6553600 | tf_op jit(solution)/shard_map/all_gather | solution.py:343
  257.3 288.7 %all-gather.8.cloned.1.call-start = ((), (), s32[]{:S(2)}) async-start(), calls=%async_computation.5 | async-start | bytes 6553600 | tf_op jit(solution)/shard_map/all_gather | solution.py:343
  350.4 372.7 %reduce-scatter.9.cloned.1.call-start = ((), (), s32[]{:S(2)}) async-start(), calls=%async_computation.7 | async-start | bytes 6553600 | tf_op jit(solution)/shard_map/reduce_scatter | solution.py:347
  355.4 98.7 %collective-permute-start.16 = (bf16[640,3456]{1,0:T(8,128)(2,1)}, bf16[640,3456]{1,0:T(8,128)(2,1)}, u32[]{:S(2)}, u32[]{:S(2)}) collective-permute-start(bf16[640,3456]{1,0:T(8,128)(2,1)} %pad_maximum_fusion.1.refs_0_), channel_id=1, source_target_pairs={{0,8},{4,12},{8,0},{12,4},{1,9},{5,13},{9,1},{13,5},{2,10},{6,14},... | collective-permute-start | bytes 13271048 | tf_op jit(solution)/shard_map/ppermute | solution.py:29
  356.9 143.4 %collective-permute-start.13 = (bf16[1728,640]{1,0:T(8,128)(2,1)}, bf16[1728,640]{1,0:T(8,128)(2,1)S(1)}, u32[]{:S(2)}, u32[]{:S(2)}) collective-permute-start(bf16[1728,640]{1,0:T(8,128)(2,1)} %refs_0_.6), channel_id=1, source_target_pairs={{0,8},{4,12},{8,0},{12,4},{1,9},{5,13},{9,1},{13,5},{2,10},{6,14},... | collective-permute-start | bytes 6635528 | tf_op jit(solution)/shard_map/ppermute | solution.py:29
  357.4 197.8 %collective-permute-start.15 = (bf16[640,3456]{1,0:T(8,128)(2,1)}, bf16[640,3456]{1,0:T(8,128)(2,1)}, u32[]{:S(2)}, u32[]{:S(2)}) collective-permute-start(bf16[640,3456]{1,0:T(8,128)(2,1)} %pad_maximum_fusion.1.refs_0_), channel_id=1, source_target_pairs={{0,4},{4,0},{8,12},{12,8},{1,5},{5,1},{9,13},{13,9},{2,6},{6,2},{1... | collective-permute-start | bytes 13271048 | tf_op jit(solution)/shard_map/ppermute | solution.py:29
  454.0 101.1 %collective-permute-start.17 = (bf16[640,3456]{1,0:T(8,128)(2,1)}, bf16[640,3456]{1,0:T(8,128)(2,1)}, u32[]{:S(2)}, u32[]{:S(2)}) collective-permute-start(bf16[640,3456]{1,0:T(8,128)(2,1)} %collective-permute-done.16.refs_2_), channel_id=1, source_target_pairs={{0,4},{4,0},{8,12},{12,8},{1,5},{5,1},{9,13},{13,9},{2,6},{6,2},{1... | collective-permute-start | bytes 13271048 | tf_op jit(solution)/shard_map/ppermute | solution.py:29
  454.0 52.6 %collective-permute-start.12 = (bf16[1728,640]{1,0:T(8,128)(2,1)}, bf16[1728,640]{1,0:T(8,128)(2,1)}, u32[]{:S(2)}, u32[]{:S(2)}) collective-permute-start(bf16[1728,640]{1,0:T(8,128)(2,1)} %refs_0_.6), channel_id=1, source_target_pairs={{0,4},{4,0},{8,12},{12,8},{1,5},{5,1},{9,13},{13,9},{2,6},{6,2},{1... | collective-permute-start | bytes 6635528 | tf_op jit(solution)/shard_map/ppermute | solution.py:29
  630.8 193.9 %all-gather.10.cloned.1.call-start = ((), (), s32[]{:S(2)}) async-start(), calls=%async_computation.8 | async-start | bytes 6553600 | tf_op jit(solution)/shard_map/all_gather | solution.py:343
  726.0 233.2 %reduce-scatter.7.cloned.1.call-start = ((), (), s32[]{:S(2)}) async-start(), calls=%async_computation.6 | async-start | bytes 6553600 | tf_op jit(solution)/shard_map/reduce_scatter | solution.py:347
  736.8 35.0 %collective-permute-start.43 = (bf16[640,3456]{1,0:T(8,128)(2,1)}, bf16[640,3456]{1,0:T(8,128)(2,1)}, u32[]{:S(2)}, u32[]{:S(2)}) collective-permute-start(bf16[640,3456]{1,0:T(8,128)(2,1)} %convolution_convert_fusion), channel_id=1, source_target_pairs={{0,4},{4,0},{8,12},{12,8},{1,5},{5,1},{9,13},{13,9},{2,6},{6,2},{1... | collective-permute-start | bytes 13271048 | tf_op jit(solution)/shard_map/ppermute | solution.py:29
  749.2 55.1 %collective-permute-start.46 = (bf16[1728,640]{1,0:T(8,128)(2,1)}, bf16[1728,640]{1,0:T(8,128)(2,1)}, u32[]{:S(2)}, u32[]{:S(2)}) collective-permute-start(bf16[1728,640]{1,0:T(8,128)(2,1)} %convolution_convert_fusion.6), channel_id=1, source_target_pairs={{0,4},{4,0},{8,12},{12,8},{1,5},{5,1},{9,13},{13,9},{2,6},{6,2},{1... | collective-permute-start | bytes 6635528 | tf_op jit(solution)/shard_map/ppermute | solution.py:29
  758.6 83.1 %collective-permute-start.42 = (bf16[640,3456]{1,0:T(8,128)(2,1)}, bf16[640,3456]{1,0:T(8,128)(2,1)}, u32[]{:S(2)}, u32[]{:S(2)}) collective-permute-start(bf16[640,3456]{1,0:T(8,128)(2,1)} %convolution_convert_fusion.2), channel_id=1, source_target_pairs={{0,4},{4,0},{8,12},{12,8},{1,5},{5,1},{9,13},{13,9},{2,6},{6,2},{1... | collective-permute-start | bytes 13271048 | tf_op jit(solution)/shard_map/ppermute | solution.py:29
  764.3 51.3 %collective-permute-start.48 = (bf16[1728,640]{1,0:T(8,128)(2,1)}, bf16[1728,640]{1,0:T(8,128)(2,1)}, u32[]{:S(2)}, u32[]{:S(2)}) collective-permute-start(bf16[1728,640]{1,0:T(8,128)(2,1)} %add_convert_fusion.4), channel_id=1, source_target_pairs={{0,8},{4,12},{8,0},{12,4},{1,9},{5,13},{9,1},{13,5},{2,10},{6,14},... | collective-permute-start | bytes 6635528 | tf_op jit(solution)/shard_map/ppermute | solution.py:29
  783.7 125.7 %collective-permute-start.44 = (bf16[640,3456]{1,0:T(8,128)(2,1)}, bf16[640,3456]{1,0:T(8,128)(2,1)}, u32[]{:S(2)}, u32[]{:S(2)}) collective-permute-start(bf16[640,3456]{1,0:T(8,128)(2,1)} %add_convert_fusion.1), channel_id=1, source_target_pairs={{0,8},{4,12},{8,0},{12,4},{1,9},{5,13},{9,1},{13,5},{2,10},{6,14},... | collective-permute-start | bytes 13271048 | tf_op jit(solution)/shard_map/ppermute | solution.py:29
  804.2 330.1 %reduce-scatter.11.cloned.1.call-start = ((), (), s32[]{:S(2)}) async-start(), calls=%async_computation.9 | async-start | bytes 6553600 | tf_op jit(solution)/shard_map/reduce_scatter | solution.py:347
  820.0 143.9 %collective-permute-start.49 = (bf16[1728,640]{1,0:T(8,128)(2,1)}, bf16[1728,640]{1,0:T(8,128)(2,1)}, u32[]{:S(2)}, u32[]{:S(2)}) collective-permute-start(bf16[1728,640]{1,0:T(8,128)(2,1)} %add_convert_fusion.3), channel_id=1, source_target_pairs={{0,16},{16,0},{1,17},{17,1},{2,18},{18,2},{3,19},{19,3},{4,20},{20... | collective-permute-start | bytes 6635528 | tf_op jit(solution)/shard_map/ppermute | solution.py:355
  916.2 96.8 %collective-permute-start.45 = (bf16[640,3456]{1,0:T(8,128)(2,1)}, bf16[640,3456]{1,0:T(8,128)(2,1)}, u32[]{:S(2)}, u32[]{:S(2)}) collective-permute-start(bf16[640,3456]{1,0:T(8,128)(2,1)} %add_convert_fusion), channel_id=1, source_target_pairs={{0,16},{16,0},{1,17},{17,1},{2,18},{18,2},{3,19},{19,3},{4,20},{20... | collective-permute-start | bytes 13271048 | tf_op jit(solution)/shard_map/ppermute | solution.py:355
  1043.8 33.3 %collective-permute-start.34 = (bf16[640,1024]{1,0:T(8,128)(2,1)}, bf16[640,1024]{1,0:T(8,128)(2,1)}, u32[]{:S(2)}, u32[]{:S(2)}) collective-permute-start(bf16[640,1024]{1,0:T(8,128)(2,1)} %convolution_convert_fusion.10), channel_id=1, source_target_pairs={{0,4},{4,0},{8,12},{12,8},{1,5},{5,1},{9,13},{13,9},{2,6},{6,2},{1... | collective-permute-start | bytes 3932168 | tf_op jit(solution)/shard_map/ppermute | solution.py:29
  1046.9 31.9 %collective-permute-start.36 = (bf16[640,1024]{1,0:T(8,128)(2,1)}, bf16[640,1024]{1,0:T(8,128)(2,1)}, u32[]{:S(2)}, u32[]{:S(2)}) collective-permute-start(bf16[640,1024]{1,0:T(8,128)(2,1)} %add_convert_fusion.7), channel_id=1, source_target_pairs={{0,8},{4,12},{8,0},{12,4},{1,9},{5,13},{9,1},{13,5},{2,10},{6,14},... | collective-permute-start | bytes 3932168 | tf_op jit(solution)/shard_map/ppermute | solution.py:29
  1050.5 32.4 %collective-permute-start.38 = (bf16[640,640]{1,0:T(8,128)(2,1)}, bf16[640,640]{1,0:T(8,128)(2,1)}, u32[]{:S(2)}, u32[]{:S(2)}) collective-permute-start(bf16[640,640]{1,0:T(8,128)(2,1)} %convolution_convert_fusion.14), channel_id=1, source_target_pairs={{0,4},{4,0},{8,12},{12,8},{1,5},{5,1},{9,13},{13,9},{2,6},{6,2},{1... | collective-permute-start | bytes 2457608 | tf_op jit(solution)/shard_map/ppermute | solution.py:29
  1053.0 42.6 %collective-permute-start.40 = (bf16[640,640]{1,0:T(8,128)(2,1)}, bf16[640,640]{1,0:T(8,128)(2,1)}, u32[]{:S(2)}, u32[]{:S(2)}) collective-permute-start(bf16[640,640]{1,0:T(8,128)(2,1)} %add_convert_fusion.10), channel_id=1, source_target_pairs={{0,8},{4,12},{8,0},{12,4},{1,9},{5,13},{9,1},{13,5},{2,10},{6,14},... | collective-permute-start | bytes 2457608 | tf_op jit(solution)/shard_map/ppermute | solution.py:29
  1082.9 49.4 %collective-permute-start.37 = (bf16[640,1024]{1,0:T(8,128)(2,1)S(1)}, bf16[640,1024]{1,0:T(8,128)(2,1)S(1)}, u32[]{:S(2)}, u32[]{:S(2)}) collective-permute-start(bf16[640,1024]{1,0:T(8,128)(2,1)S(1)} %add_convert_fusion.6), channel_id=1, source_target_pairs={{0,16},{16,0},{1,17},{17,1},{2,18},{18,2},{3,19},{19,3},{4,20},{20... | collective-permute-start | bytes 3932168 | tf_op jit(solution)/shard_map/ppermute | solution.py:355
  1097.3 33.8 %collective-permute-start.41 = (bf16[640,640]{1,0:T(8,128)(2,1)S(1)}, bf16[640,640]{1,0:T(8,128)(2,1)S(1)}, u32[]{:S(2)}, u32[]{:S(2)}) collective-permute-start(bf16[640,640]{1,0:T(8,128)(2,1)S(1)} %add_convert_fusion.9), channel_id=1, source_target_pairs={{0,16},{16,0},{1,17},{17,1},{2,18},{18,2},{3,19},{19,3},{4,20},{20... | collective-permute-start | bytes 2457608 | tf_op jit(solution)/shard_map/ppermute | solution.py:355
  1100.4 29.5 %collective-permute-start.33 = (bf16[160]{0:T(256)(128)(2,1)S(1)}, bf16[160]{0:T(256)(128)(2,1)S(1)}, u32[]{:S(2)}, u32[]{:S(2)}) collective-permute-start(bf16[160]{0:T(256)(128)(2,1)S(1)} %add_convert_fusion.14), channel_id=1, source_target_pairs={{0,16},{16,0},{1,17},{17,1},{2,18},{18,2},{3,19},{19,3},{4,20},{20... | collective-permute-start | bytes 968 | tf_op jit(solution)/shard_map/ppermute | solution.py:355
  1138.8 30.7 %collective-permute-start.25 = (f32[160,1024]{1,0:T(8,128)}, f32[160,1024]{1,0:T(8,128)}, u32[]{:S(2)}, u32[]{:S(2)}) collective-permute-start(f32[160,1024]{1,0:T(8,128)} %get-tuple-element.127), channel_id=1, source_target_pairs={{0,12},{4,8},{8,4},{12,0},{1,13},{5,9},{9,5},{13,1},{2,14},{6,10},... | collective-permute-start | bytes 1966088 | tf_op jit(solution)/shard_map/ppermute | solution.py:29
  (125 other events, 2713.2 us)
Sparse Core Ops, SparseCore 0:
  58.0 99.6 all-gather.11
  254.9 92.3 reduce-scatter.4
  348.9 98.5 all-gather.13
  449.5 96.4 all-gather.7
  630.9 92.1 reduce-scatter.8
  726.2 98.5 all-gather.9
  827.1 92.1 reduce-scatter.6
  954.2 93.3 reduce-scatter.10

commit v2 on v0

v2 whole, which is shorter than its diff:
```python
import functools

import jax
import jax.numpy as jnp
from jax import lax
from jax.experimental import pallas as pl
from jax.experimental.pallas import tpu as pltpu
from jax.sharding import PartitionSpec as P

D = 2560
HEAD = 80
EPS = 1e-05
THETA = 10000.0
NEG = -1e30
LOG2E = 1.4426950408889634
LN2 = 0.6931471805599453
ROOT = HEAD ** (-0.5)
BF = jnp.bfloat16
F32 = jnp.float32
NN = (((1,), (0,)), ((), ()))
TN = (((0,), (0,)), ((), ()))
NT = (((1,), (1,)), ((), ()))


def dot(left, right, dims=NN):
    return lax.dot_general(left, right, dims, preferred_element_type=F32)


def together(*values):
    return lax.optimization_barrier(values)


def swapped(value, axis, mask):
    size = lax.axis_size(axis)
    return lax.ppermute(value, axis, [(i, i ^ mask) for i in range(size)])


def spread(blocks, axis, bits):
    blocks = dict(blocks)
    for bit in bits:
        for k in list(blocks):
            blocks[k | bit] = swapped(blocks[k], axis, bit)
    return blocks


def fold(blocks, axis, bits, low=True):
    held = dict(blocks)
    for bit in bits:
        for k in [k for k in held if k & bit]:
            other = swapped(held.pop(k), axis, bit)
            total = held[k ^ bit].astype(F32) + other.astype(F32)
            held[k ^ bit] = total.astype(BF) if low else total
    return held


def far_bits(size):
    return [1 << i for i in range(1, size.bit_length() - 1)]


def near_bits(size):
    return [1] if size > 1 else []


def exchange_blocks(blocks, axis):
    return [blocks[0]] + [swapped(blocks[k], axis, k) for k in range(1, len(blocks))]


def by_xor(value, index, axis):
    parts = [
        lax.dynamic_index_in_dim(value, index ^ k, axis, keepdims=True)
        for k in range(value.shape[axis])
    ]
    return jnp.concatenate(parts, axis=axis)


def params(mib=58):
    return pltpu.CompilerParams(vmem_limit_bytes=mib * 1024 * 1024)


def shape(dims, dtype):
    return jax.ShapeDtypeStruct(dims, dtype)


SMALL = pl.BlockSpec(memory_space=pltpu.SMEM)
RAW = pl.BlockSpec(memory_space=pl.ANY)


def resident(dims, buffers=None):
    zeros = (0,) * len(dims)
    mode = {} if buffers is None else {"pipeline_mode": pl.Buffered(buffers)}
    return pl.BlockSpec(dims, lambda *_: zeros, **mode)


def normalise(x_ref, gain_ref, out_ref, scale_ref):
    cols, count, piece, _ = x_ref.shape
    total = None
    for c in range(cols):
        for k in range(count):
            value = x_ref[c, k].astype(F32)
            part = jnp.sum(value * value, axis=0, keepdims=True)
            total = part if total is None else total + part
    scale = lax.rsqrt(total / D + EPS)
    scale_ref[...] = scale
    for c in range(cols):
        for k in range(count):
            value = x_ref[c, k].astype(F32) * scale * gain_ref[c, k]
            out_ref[k, c * piece : (c + 1) * piece, :] = value.astype(BF)


def turn(value, cosine, sine):
    half = value.shape[0] // 2
    first, second = value[:half], value[half:]
    return jnp.concatenate([first * cosine - second * sine, second * cosine + first * sine])


def qkv_kernel(count, shared, x_ref, gain_ref, cos_ref, sin_ref, *refs):
    q_w, kv_w = refs[:count], refs[count : 2 * count]
    norm_ref, scale_ref, sets_ref = refs[2 * count :]
    normalise(x_ref, gain_ref, norm_ref, scale_ref)
    query = keyval = None
    for k in range(count):
        normed = norm_ref[k]
        part = dot(q_w[k][...], normed, TN)
        query = part if query is None else query + part
        part = dot(kv_w[k][...], normed)
        keyval = part if keyval is None else keyval + part
    cosine, sine = cos_ref[...], sin_ref[...]
    half = query.shape[0] // 2
    kv_half = keyval.shape[0] // 2
    for h in range(2):
        for at in range(0, half, HEAD):
            value = turn(query[h * half + at : h * half + at + HEAD], cosine, sine)
            sets_ref[h, at : at + HEAD, :] = (value * (ROOT * LOG2E)).astype(BF)
        at = 0 if shared else h * HEAD
        key = turn(keyval[at : at + HEAD], cosine, sine)
        sets_ref[h, half : half + HEAD, :] = key.astype(BF)
        sets_ref[h, half + HEAD : half + 2 * HEAD, :] = keyval[
            kv_half + at : kv_half + at + HEAD
        ].astype(BF)


def qkv_project(x, gain, cosine, sine, q_w, kv_w):
    cols, count, piece, tokens = x.shape
    half = q_w[0].shape[1] // 2
    shared = kv_w[0].shape[0] == 2 * HEAD
    return pl.pallas_call(
        functools.partial(qkv_kernel, count, shared),
        out_shape=(
            shape((count, cols * piece, tokens), BF),
            shape((1, tokens), F32),
            shape((2, half + 2 * HEAD, tokens), BF),
        ),
        compiler_params=params(),
        name="qkv_project",
    )(x, gain, cosine, sine, *q_w, *kv_w)


def pieces_of(half, at, tile, tokens):
    if half == 1:
        return [(0, 0, tokens, False), (1, 0, at + tile, True)]
    head = [(0, 0, at, False)] if at else []
    return head + [(0, at, at + tile, True)]


def seen_of(half, at, begin, end, tile, seg_row, seg_col):
    rows = lax.broadcasted_iota(jnp.int32, (end - begin, tile), 0) + begin
    cols = lax.broadcasted_iota(jnp.int32, (end - begin, tile), 1) + at
    seen = rows <= cols
    if half == 1:
        seen = seen & (seg_col[begin:end] == seg_row[:, at : at + tile])
    return seen


def place(parity, own_ref, other_ref, sets):
    sets[parity] = own_ref[...]
    sets[1 - parity] = other_ref[...]


def attend_kernel(
    tile, parity_ref, own_ref, other_ref, seg_row, seg_col, mine_ref, send_ref, lse_ref, sets, rows
):
    tokens = own_ref.shape[-1]
    heads = pl.num_programs(0)
    head = pl.program_id(0)
    parity = parity_ref[0]
    half_rows = own_ref.shape[0] - 2 * HEAD

    @pl.when(head == 0)
    def _():
        place(parity, own_ref, other_ref, sets)
        for half in range(2):
            keys = sets[half, half_rows : half_rows + HEAD, :]
            rows[half] = keys.astype(F32).T.astype(BF)

    at_head = pl.ds(pl.multiple_of(head * HEAD, 16), HEAD)
    for half in range(2):
        for at in range(0, tokens, tile):
            span = slice(at, at + tile)
            query = sets[half, at_head, span]
            pieces = pieces_of(half, at, tile, tokens)
            scores = []
            for which, begin, end, masked in pieces:
                part = dot(rows[which, begin:end, :], query)
                if masked:
                    part = jnp.where(
                        seen_of(half, at, begin, end, tile, seg_row, seg_col), part, NEG
                    )
                scores.append(part)
            peak = functools.reduce(
                jnp.maximum, [jnp.max(s, axis=0, keepdims=True) for s in scores]
            )
            total = out = None
            for (which, begin, end, _), part in zip(pieces, scores):
                weights = jnp.exp2(part - peak)
                mass = jnp.sum(weights, axis=0, keepdims=True)
                value = dot(sets[which, half_rows + HEAD :, begin:end], weights.astype(BF))
                total = mass if total is None else total + mass
                out = value if out is None else out + value
            out = (out / total).astype(BF)
            lse_ref[half, 0, :, span] = peak + jnp.log2(total)

            @pl.when(parity == half)
            def _():
                mine_ref[at_head, span] = out

            @pl.when(parity != half)
            def _():
                send_ref[at_head, span] = out


def attend(parity, own, other, seg):
    depth, tokens = own.shape
    half_rows = depth - 2 * HEAD
    heads = half_rows // HEAD
    tile = min(256, tokens)
    out = resident((half_rows, tokens))
    return pl.pallas_call(
        functools.partial(attend_kernel, tile),
        out_shape=(
            shape((half_rows, tokens), BF),
            shape((half_rows, tokens), BF),
            shape((2, heads, 1, tokens), F32),
        ),
        grid=(heads,),
        in_specs=[
            SMALL,
            resident((depth, tokens)),
            resident((depth, tokens)),
            resident((1, tokens)),
            resident((tokens, 1)),
        ],
        out_specs=(out, out, pl.BlockSpec((2, 1, 1, tokens), lambda h: (0, h, 0, 0))),
        scratch_shapes=[
            pltpu.VMEM((2, depth, tokens), BF),
            pltpu.VMEM((2, tokens, HEAD), BF),
        ],
        compiler_params=params(),
        name="attend",
    )(parity, own, other, seg[None, :], seg[:, None])


def attend_back_kernel(
    tile,
    parity_ref,
    own_ref,
    other_ref,
    own_out,
    other_out,
    own_grad,
    other_grad,
    lse_ref,
    seg_row,
    seg_col,
    mine_ref,
    send_ref,
    sets,
    outs,
    grads,
    rows,
    key_acc,
    value_acc,
):
    tokens = own_ref.shape[-1]
    heads = pl.num_programs(0)
    head = pl.program_id(0)
    parity = parity_ref[0]
    half_rows = own_ref.shape[0] - 2 * HEAD

    @pl.when(head == 0)
    def _():
        place(parity, own_ref, other_ref, sets)
        place(parity, own_out, other_out, outs)
        place(parity, own_grad, other_grad, grads)
        for half in range(2):
            for i in range(2):
                at = half_rows + i * HEAD
                rows[i, half] = sets[half, at : at + HEAD, :].astype(F32).T.astype(BF)
        key_acc[...] = jnp.zeros_like(key_acc)
        value_acc[...] = jnp.zeros_like(value_acc)

    at_head = pl.ds(pl.multiple_of(head * HEAD, 16), HEAD)
    for half in range(2):
        for at in range(0, tokens, tile):
            span = slice(at, at + tile)
            query = sets[half, at_head, span]
            grad = grads[half, at_head, span]
            lse = lse_ref[half, 0, :, span]
            delta = jnp.sum(
                grad.astype(F32) * outs[half, at_head, span].astype(F32), axis=0, keepdims=True
            )
            total = None
            for which, begin, end, masked in pieces_of(half, at, tile, tokens):
                part = dot(rows[0, which, begin:end, :], query)
                if masked:
                    part = jnp.where(
                        seen_of(half, at, begin, end, tile, seg_row, seg_col), part, NEG
                    )
                weights = jnp.exp2(part - lse)
                dprod = dot(rows[1, which, begin:end, :], grad)
                dscore = (weights * (dprod - delta)).astype(BF)
                value_acc[which, :, begin:end] += dot(grad, weights.astype(BF), NT)
                key_acc[which, :, begin:end] += dot(query, dscore, NT)
                more = dot(sets[which, half_rows : half_rows + HEAD, begin:end], dscore)
                total = more if total is None else total + more
            total = (total * ROOT).astype(BF)

            @pl.when(parity == half)
            def _():
                mine_ref[at_head, span] = total

            @pl.when(parity != half)
            def _():
                send_ref[at_head, span] = total

    @pl.when(head == heads - 1)
    def _():
        for ref, which in ((mine_ref, parity), (send_ref, 1 - parity)):
            ref[half_rows : half_rows + HEAD, :] = (key_acc[which] * LN2).astype(BF)
            ref[half_rows + HEAD :, :] = value_acc[which].astype(BF)


def attend_back(parity, own, other, own_out, other_out, own_grad, other_grad, lse, seg):
    depth, tokens = own.shape
    half_rows = depth - 2 * HEAD
    heads = half_rows // HEAD
    tile = min(256, tokens)
    full, part = resident((depth, tokens)), resident((half_rows, tokens))
    return pl.pallas_call(
        functools.partial(attend_back_kernel, tile),
        out_shape=(shape((depth, tokens), BF), shape((depth, tokens), BF)),
        grid=(heads,),
        in_specs=[
            SMALL,
            full,
            full,
            part,
            part,
            part,
            part,
            pl.BlockSpec((2, 1, 1, tokens), lambda h: (0, h, 0, 0)),
            resident((1, tokens)),
            resident((tokens, 1)),
        ],
        out_specs=(full, full),
        scratch_shapes=[
            pltpu.VMEM((2, depth, tokens), BF),
            pltpu.VMEM((2, half_rows, tokens), BF),
            pltpu.VMEM((2, half_rows, tokens), BF),
            pltpu.VMEM((2, 2, tokens, HEAD), BF),
            pltpu.VMEM((2, HEAD, tokens), F32),
            pltpu.VMEM((2, HEAD, tokens), F32),
        ],
        compiler_params=params(),
        name="attend_back",
    )(
        parity,
        own,
        other,
        own_out,
        other_out,
        own_grad,
        other_grad,
        lse,
        seg[None, :],
        seg[:, None],
    )


def halves_at(parity, half_rows):
    mine = pl.ds(pl.multiple_of(parity * half_rows, 16), half_rows)
    other = pl.ds(pl.multiple_of((1 - parity) * half_rows, 16), half_rows)
    return mine, other


def mix_out_kernel(count, parity_ref, own_ref, other_ref, *refs):
    weights, out_ref = refs[:count], refs[count]
    cols, _, piece, _ = out_ref.shape
    mine, other = halves_at(parity_ref[0], own_ref.shape[0])
    for k in range(count):
        part = dot(weights[k][mine, :], own_ref[...], TN)
        part = part + dot(weights[k][other, :], other_ref[...], TN)
        for c in range(cols):
            out_ref[c, k] = part[c * piece : (c + 1) * piece].astype(BF)


def mix_out(parity, own, other, weights, cols):
    count = len(weights)
    piece = weights[0].shape[1] // cols
    vmem = pl.BlockSpec(memory_space=pltpu.VMEM)
    return pl.pallas_call(
        functools.partial(mix_out_kernel, count),
        out_shape=shape((cols, count, piece, own.shape[1]), BF),
        in_specs=[SMALL] + [vmem] * (2 + count),
        compiler_params=params(),
        name="mix_out",
    )(parity, own, other, *weights)


def mix_back_kernel(count, parity_ref, x_ref, *refs):
    weights = refs[:count]
    rows_ref, own_ref, other_ref = refs[count:]
    cols, _, piece, _ = x_ref.shape
    for c in range(cols):
        for k in range(count):
            rows_ref[k, c * piece : (c + 1) * piece, :] = x_ref[c, k]
    mine, other = halves_at(parity_ref[0], own_ref.shape[0])
    for at, out_ref in ((other, other_ref), (mine, own_ref)):
        total = None
        for k in range(count):
            part = dot(weights[k][at, :], rows_ref[k])
            total = part if total is None else total + part
        out_ref[...] = total.astype(BF)


def mix_back(parity, x, weights):
    cols, count, piece, tokens = x.shape
    half_rows = weights[0].shape[0] // 2
    vmem = pl.BlockSpec(memory_space=pltpu.VMEM)
    return pl.pallas_call(
        functools.partial(mix_back_kernel, count),
        out_shape=(
            shape((count, cols * piece, tokens), BF),
            shape((half_rows, tokens), BF),
            shape((half_rows, tokens), BF),
        ),
        in_specs=[SMALL] + [vmem] * (1 + count),
        compiler_params=params(),
        name="mix_back",
    )(parity, x, *weights)


def fan_kernel(count, x_ref, *refs):
    weights, out_ref = refs[:count], refs[count]
    cols, _, piece, _ = out_ref.shape
    for k in range(count):
        part = dot(weights[k][...], x_ref[...], TN)
        for c in range(cols):
            out_ref[c, k] = part[c * piece : (c + 1) * piece].astype(BF)


def fan_out(weights, x, cols):
    count = len(weights)
    piece = weights[0].shape[1] // cols
    return pl.pallas_call(
        functools.partial(fan_kernel, count),
        out_shape=shape((cols, count, piece, x.shape[1]), BF),
        compiler_params=params(),
        name="fan_out",
    )(x, *weights)


def ff_kernel(count, x_ref, g_ref, gain_ref, *refs):
    gate_w, up_w, down_w = refs[:count], refs[count : 2 * count], refs[2 * count : 3 * count]
    norm_ref, scale_ref, rows_ref, inner_ref, act_ref, dgate_ref, dup_ref = refs[3 * count :]
    cols, _, piece, _ = x_ref.shape

    @pl.when(pl.program_id(0) == 0)
    def _():
        normalise(x_ref, gain_ref, norm_ref, scale_ref)
        for c in range(cols):
            for k in range(count):
                rows_ref[k, c * piece : (c + 1) * piece, :] = g_ref[c, k]
        inner_ref[...] = jnp.zeros_like(inner_ref)

    def summed(weights, ref):
        total = None
        for k in range(count):
            part = dot(weights[k][...], ref[k])
            total = part if total is None else total + part
        return total

    gate = summed(gate_w, norm_ref)
    up = summed(up_w, norm_ref)
    sigma = jax.nn.sigmoid(gate)
    silu = gate * sigma
    act_ref[...] = (silu * up).astype(BF)
    grad = summed(down_w, rows_ref)
    dup = grad * silu
    dgate = grad * up * (sigma + silu * (1.0 - sigma))
    inner_ref[...] += jnp.sum(dgate * gate + dup * up, axis=0, keepdims=True)
    dgate_ref[...] = dgate.astype(BF)
    dup_ref[...] = dup.astype(BF)


def feed_forward(x, g, gain, gate_w, up_w, down_w):
    cols, count, piece, tokens = x.shape
    width, depth = gate_w[0].shape
    tile = 432 if width % 432 == 0 else width
    whole = resident(x.shape, 1)
    rows = (count, cols * piece, tokens)
    w_spec = pl.BlockSpec((tile, depth), lambda n: (n, 0))
    h_spec = pl.BlockSpec((tile, tokens), lambda n: (n, 0))
    hidden = shape((width, tokens), BF)
    return pl.pallas_call(
        functools.partial(ff_kernel, count),
        out_shape=(
            shape(rows, BF),
            shape((1, tokens), F32),
            shape(rows, BF),
            shape((1, tokens), F32),
            hidden,
            hidden,
            hidden,
        ),
        grid=(width // tile,),
        in_specs=[whole, whole, resident(gain.shape, 1)] + [w_spec] * (3 * count),
        out_specs=(
            resident(rows, 1),
            resident((1, tokens)),
            resident(rows, 1),
            resident((1, tokens)),
            h_spec,
            h_spec,
            h_spec,
        ),
        compiler_params=params(60),
        name="feed_forward",
    )(x, g, gain, *gate_w, *up_w, *down_w)


def norm_back(grads, k, x_ref, gain_ref, scale, coef, share_ref, gain_share_ref):
    cols, _, piece, _ = x_ref.shape
    for c in range(cols):
        grad = grads[c * piece : (c + 1) * piece]
        value = x_ref[c, k].astype(F32)
        gain_share_ref[c, k] = jnp.sum(grad * (value * scale), axis=1, keepdims=True)
        share_ref[c, k] = ((grad * gain_ref[c, k]) * scale - value * coef).astype(BF)


def ff_back_kernel(count, x_ref, gain_ref, scale_ref, inner_ref, dgate, dup, *refs):
    gate_w, up_w = refs[:count], refs[count : 2 * count]
    share_ref, gain_share_ref, dgate_buf, dup_buf, gate_buf, up_buf, sems = refs[2 * count :]
    copies = [
        pltpu.make_async_copy(dgate, dgate_buf, sems.at[0]),
        pltpu.make_async_copy(dup, dup_buf, sems.at[1]),
    ]
    for k in range(count):
        copies.append(pltpu.make_async_copy(gate_w[k], gate_buf.at[k], sems.at[2 + 2 * k]))
        copies.append(pltpu.make_async_copy(up_w[k], up_buf.at[k], sems.at[3 + 2 * k]))
    for copy in copies:
        copy.start()
    scale = scale_ref[...]
    coef = scale * scale * inner_ref[...] / D
    copies[0].wait()
    copies[1].wait()
    for k in range(count):
        copies[2 + 2 * k].wait()
        copies[3 + 2 * k].wait()
        grads = dot(gate_buf[k], dgate_buf[...], TN) + dot(up_buf[k], dup_buf[...], TN)
        norm_back(grads, k, x_ref, gain_ref, scale, coef, share_ref, gain_share_ref)


def ff_back(x, gain, scale, inner, dgate, dup, gate_w, up_w):
    count = len(gate_w)
    vmem = pl.BlockSpec(memory_space=pltpu.VMEM)
    width, depth = gate_w[0].shape
    return pl.pallas_call(
        functools.partial(ff_back_kernel, count),
        out_shape=(shape(x.shape, BF), shape(gain.shape, F32)),
        in_specs=[vmem] * 4 + [RAW] * (2 + 2 * count),
        scratch_shapes=[
            pltpu.VMEM(dgate.shape, BF),
            pltpu.VMEM(dup.shape, BF),
            pltpu.VMEM((count, width, depth), BF),
            pltpu.VMEM((count, width, depth), BF),
            pltpu.SemaphoreType.DMA((2 + 2 * count,)),
        ],
        compiler_params=params(60),
        name="ff_back",
    )(x, gain, scale, inner, dgate, dup, *gate_w, *up_w)


def qkv_back_kernel(
    count,
    shared,
    parity_ref,
    x_ref,
    gain_ref,
    scale_ref,
    cos_ref,
    sin_ref,
    sets_ref,
    own_ref,
    other_ref,
    *refs,
):
    q_w, kv_w = refs[:count], refs[count : 2 * count]
    dq_ref, dkv_ref, share_ref, gain_share_ref = refs[2 * count :]
    parity = parity_ref[0]
    half_rows = own_ref.shape[0] - 2 * HEAD
    kv_half = dkv_ref.shape[0] // 2
    cosine, sine = cos_ref[...], -sin_ref[...]
    inner = None
    folded = None
    for grads, which in ((own_ref, parity), (other_ref, 1 - parity)):
        for at in range(0, half_rows + 2 * HEAD, HEAD):
            value = grads[at : at + HEAD, :].astype(F32)
            part = value * sets_ref[which, at : at + HEAD, :].astype(F32)
            part = jnp.sum(part, axis=0, keepdims=True)
            if at < half_rows:
                part = part * (1.0 / (ROOT * LOG2E))
                start = pl.multiple_of(which * half_rows + at, 16)
                dq_ref[pl.ds(start, HEAD), :] = turn(value, cosine, sine).astype(BF)
            else:
                is_key = at == half_rows
                raw = turn(value, cosine, sine) if is_key else value
                base = 0 if is_key else kv_half
                if not shared:
                    start = pl.multiple_of(base + which * HEAD, 16)
                    dkv_ref[pl.ds(start, HEAD), :] = raw.astype(BF)
                elif folded is None or at not in folded:
                    folded = {**(folded or {}), at: raw}
                else:
                    dkv_ref[base : base + HEAD, :] = (folded[at] + raw).astype(BF)
            inner = part if inner is None else inner + part
    scale = scale_ref[...]
    coef = scale * scale * inner / D
    for k in range(count):
        grads = dot(q_w[k][...], dq_ref[...]) + dot(kv_w[k][...], dkv_ref[...], TN)
        norm_back(grads, k, x_ref, gain_ref, scale, coef, share_ref, gain_share_ref)


def qkv_back(parity, x, gain, scale, cosine, sine, sets, own, other, q_w, kv_w):
    cols, count, piece, tokens = x.shape
    shared = kv_w[0].shape[0] == 2 * HEAD
    vmem = pl.BlockSpec(memory_space=pltpu.VMEM)
    return pl.pallas_call(
        functools.partial(qkv_back_kernel, count, shared),
        out_shape=(
            shape((q_w[0].shape[1], tokens), BF),
            shape((kv_w[0].shape[0], tokens), BF),
            shape(x.shape, BF),
            shape(gain.shape, F32),
        ),
        in_specs=[SMALL] + [vmem] * (8 + 2 * count),
        compiler_params=params(),
        name="qkv_back",
    )(parity, x, gain, scale, cosine, sine, sets, own, other, *q_w, *kv_w)


def rope_parts(positions):
    half = HEAD // 2
    freq = THETA ** (-jnp.arange(half, dtype=F32) * 2.0 / HEAD)
    angle = freq[:, None] * positions.astype(F32)[None, :]
    return (jnp.cos(angle), jnp.sin(angle))


def spread_cols(value):
    return lax.all_gather(value, "col", axis=0, tiled=False)


def sum_cols(value):
    return lax.psum_scatter(value, "col", scatter_dimension=0, tiled=False)


def over_dp(value):
    low = value.astype(BF)
    total = low.astype(F32)
    size = lax.axis_size("dp")
    for step in range(1, size):
        other = lax.ppermute(low, "dp", [(i, (i + step) % size) for i in range(size)])
        total = total + other.astype(F32)
    return total


def body(
    layer_input,
    attn_gain,
    mlp_gain,
    query_weight,
    key_weight,
    value_weight,
    mix_weight,
    gate_weight,
    up_weight,
    down_weight,
    output_grad,
    segment_ids,
    position_ids,
):
    rows = segment_ids.shape[0]
    count = lax.axis_size("row")
    cols = lax.axis_size("col")
    piece = layer_input.shape[1]
    row = lax.axis_index("row")
    parity = (row % 2).astype(jnp.int32)
    own_core = parity.reshape(1)
    q_half = query_weight.shape[1] // 2
    near, far = near_bits(count), far_bits(count)

    def row_tokens(value):
        turned = value.T
        outgoing = [
            lax.dynamic_slice(turned, (0, (row ^ k) * rows), (piece, rows)) for k in range(count)
        ]
        return jnp.stack(exchange_blocks(outgoing, "row"))

    def all_tokens(blocks):
        got = exchange_blocks([blocks[k] for k in range(count)], "row")
        result = jnp.zeros((piece, count * rows), blocks.dtype)
        for k in range(count):
            result = lax.dynamic_update_slice(result, got[k], (0, (row ^ k) * rows))
        return result.T

    def listed(blocks):
        return [blocks[k] for k in range(count)]

    source_own = row_tokens(layer_input)
    kv_weight = jnp.concatenate([key_weight.T, value_weight.T])
    q_first = spread({0: query_weight}, "row", far)
    kv_first = spread({0: kv_weight}, "row", far)
    mix_first = spread({0: mix_weight}, "row", far)
    gate_first = spread({0: gate_weight.T}, "row", far)
    up_first = spread({0: up_weight.T}, "row", far)
    down_first = spread({0: down_weight}, "row", far)
    q_blocks = spread(q_first, "row", near)
    kv_blocks = spread(kv_first, "row", near)

    gains = lax.all_gather(jnp.stack([attn_gain, mlp_gain]), ("row", "col"), axis=1, tiled=True)
    gains = gains.reshape(2, count, cols, piece)
    gains = by_xor(gains, row, 1).swapaxes(1, 2)[..., None]
    gain_one, gain_two = gains[0], gains[1]

    cosine, sine = rope_parts(position_ids)
    other_seg = swapped(segment_ids, "row", 1)
    seg = jnp.where(parity == 0, other_seg, segment_ids)

    source = spread_cols(source_own)
    source, q_blocks, kv_blocks, mix_first, gate_first, gain_one, cosine, sine, seg = together(
        source, q_blocks, kv_blocks, mix_first, gate_first, gain_one, cosine, sine, seg
    )
    grad_own = row_tokens(output_grad)
    grad_own, source = together(grad_own, source)
    grad_all = spread_cols(grad_own)
    norm_one, scale_one, sets = qkv_project(
        source, gain_one, cosine, sine, listed(q_blocks), listed(kv_blocks)
    )
    own_set = lax.dynamic_index_in_dim(sets, parity, 0, keepdims=False)
    other_set = swapped(lax.dynamic_index_in_dim(sets, 1 - parity, 0, keepdims=False), "row", 1)
    attn_mine, attn_send, lse = attend(own_core, own_set, other_set, seg)
    attn_other = swapped(attn_send, "row", 1)
    mix_blocks = spread(mix_first, "row", near)
    attn_mine, attn_other, mix_blocks, up_first = together(
        attn_mine, attn_other, mix_blocks, up_first
    )
    attn_part = mix_out(own_core, attn_mine, attn_other, listed(mix_blocks), cols)
    attn_part, grad_all = together(attn_part, grad_all)
    attn_sum = sum_cols(attn_part)
    gate_blocks = spread(gate_first, "row", near)
    up_blocks = spread(up_first, "row", near)
    down_blocks = spread(down_first, "row", near)
    attn_sum, gate_blocks, up_blocks, down_blocks = together(
        attn_sum, gate_blocks, up_blocks, down_blocks
    )
    residual_own = source_own.astype(F32) + attn_sum.astype(F32)

    residual = spread_cols(residual_own.astype(BF))
    norm_two, scale_two, grad_rows, inner, act, dgate, dup = feed_forward(
        residual,
        grad_all,
        gain_two,
        listed(gate_blocks),
        listed(up_blocks),
        listed(down_blocks),
    )
    share, gain_share_two = ff_back(
        residual, gain_two, scale_two, inner, dgate, dup, listed(gate_blocks), listed(up_blocks)
    )
    share_sum = sum_cols(share)
    share, dgate, dup, act, grad_rows, norm_two = together(
        share, dgate, dup, act, grad_rows, norm_two
    )
    down_grads = {k: dot(act, grad_rows[k], NT).astype(BF) for k in range(count)}
    gate_grads = {k: dot(dgate, norm_two[k], NT).astype(BF) for k in range(count)}
    up_grads = {k: dot(dup, norm_two[k], NT).astype(BF) for k in range(count)}
    down_grads = fold(down_grads, "row", near)
    gate_grads = fold(gate_grads, "row", near)
    up_grads = fold(up_grads, "row", near)
    share_sum, down_grads, gate_grads, up_grads = together(
        share_sum, down_grads, gate_grads, up_grads
    )
    residual_grad_own = grad_own.astype(F32) + share_sum.astype(F32)
    down_total = fold(down_grads, "row", far)[0]
    gate_total = fold(gate_grads, "row", far)[0]
    up_total = fold(up_grads, "row", far)[0]

    mix_cols = spread_cols(residual_grad_own.astype(BF))
    ff_part = fan_out(listed(down_blocks), act, cols)
    mix_cols, ff_part = together(mix_cols, ff_part)
    mix_rows, grad_mine, grad_send = mix_back(own_core, mix_cols, listed(mix_blocks))
    ff_sum = sum_cols(ff_part)
    grad_other = swapped(grad_send, "row", 1)
    back_mine, back_send = attend_back(
        own_core, own_set, other_set, attn_mine, attn_send, grad_mine, grad_other, lse, seg
    )
    back_other = swapped(back_send, "row", 1)
    dq, dkv, share, gain_share_one = qkv_back(
        own_core,
        source,
        gain_one,
        scale_one,
        cosine,
        sine,
        sets,
        back_mine,
        back_other,
        listed(q_blocks),
        listed(kv_blocks),
    )
    share, ff_sum = together(share, ff_sum)
    input_sum = sum_cols(share)
    output_own = (residual_own + ff_sum.astype(F32)).astype(BF)
    layer_output = all_tokens(output_own)

    share, dq, dkv, gain_share_one, gain_share_two = together(
        share, dq, dkv, gain_share_one, gain_share_two
    )
    q_grads = {k: dot(norm_one[k], dq, NT).astype(BF) for k in range(count)}
    kv_grads = {k: dot(dkv, norm_one[k], NT).astype(BF) for k in range(count)}
    attn_low = jnp.concatenate(
        [
            jnp.where(parity == 0, attn_mine, attn_other),
            jnp.where(parity == 0, attn_other, attn_mine),
        ]
    )
    mix_grads = {k: dot(attn_low, mix_rows[k], NT).astype(BF) for k in range(count)}
    bits = near + far[::-1]
    q_total = over_dp(fold(q_grads, "row", bits)[0])
    kv_total = over_dp(fold(kv_grads, "row", bits)[0])
    mix_total = over_dp(fold(mix_grads, "row", bits)[0])
    down_total = over_dp(down_total)
    gate_total = over_dp(gate_total)
    up_total = over_dp(up_total)

    shares = jnp.stack([gain_share_one[..., 0], gain_share_two[..., 0]], axis=2)
    shares = by_xor(shares, lax.axis_index("col"), 0)
    shares = {c: shares[c] for c in range(cols)}
    shares = fold(shares, "col", near_bits(cols) + far_bits(cols), low=False)[0]
    shares = fold({k: shares[k] for k in range(count)}, "row", bits, low=False)[0]
    gain_totals = over_dp(shares)

    input_grad = all_tokens((residual_grad_own + input_sum.astype(F32)).astype(BF)).astype(F32)
    kv_rows = kv_total.shape[0] // 2
    return (
        layer_output,
        input_grad,
        gain_totals[0],
        gain_totals[1],
        q_total,
        kv_total[:kv_rows].T,
        kv_total[kv_rows:].T,
        mix_total,
        gate_total.T,
        up_total.T,
        down_total,
    )


def solution(mesh):
    return jax.shard_map(
        body,
        mesh=mesh,
        in_specs=(
            P("dp", ("row", "col")),
            P(("row", "col")),
            P(("row", "col")),
            P("row", "col"),
            P("row", "col"),
            P("row", "col"),
            P("col", "row"),
            P("row", "col"),
            P("row", "col"),
            P("col", "row"),
            P("dp", ("row", "col")),
            P(("dp", "row")),
            P(("dp", "row")),
        ),
        out_specs=(
            P("dp", ("row", "col")),
            P("dp", ("row", "col")),
            P(("row", "col")),
            P(("row", "col")),
            P("row", "col"),
            P("row", "col"),
            P("row", "col"),
            P("col", "row"),
            P("row", "col"),
            P("row", "col"),
            P("col", "row"),
        ),
        check_vma=False,
    )
```

time: 3050 us -> 1060 us (0.35)
  waiting for transfers between devices: 2070 us -> 601 us
  matrix products: 414 us -> 77.1 us
  blocking collectives: 269 us -> 32.7 us
  Pallas kernels: 0 us -> 210 us
  other arithmetic: 160 us -> 44.3 us
  local copies, waits for them, and re-layouts: 106 us -> 23.5 us
  starting transfers between devices: 8.79 us -> 44.5 us
    reduce_scatter x8 -> x4, waiting for transfers between devices: 1370 us -> 63.3 us  [sum_cols(): return lax.psum_scatter(value, 'col', scatter_dimension=0, tiled=False)]
    dot_general x26 -> x24, matrix products: 414 us -> 77.1 us  [dot(): return lax.dot_general(left, right, dims, preferred_element_type=F32)]
    ppermute x4 -> x66, waiting for transfers between devices: 0.54 us -> 324 us  [the longest x59 265 us: swapped(): return lax.ppermute(value, axis, [(i, i ^ mask) for i in range(size)])]
    all_gather x8 -> x4, waiting for transfers between devices: 517 us -> 213 us  [spread_cols(): return lax.all_gather(value, 'col', axis=0, tiled=False)]
    psum x5 -> x0, blocking collectives: 269 us -> none  [the longest x2 134 us: norm_scale(): total = lax.psum(local, ('row', 'col'))]
    pallas_call x0 -> x9, Pallas kernels: none -> 210 us  [the longest x1 47.4 us: feed_forward(): pl.pallas_call(functools.partial(ff_kernel, count), out_shape=(shape(rows...]
    psum x1 -> x0, waiting for transfers between devices: 179 us -> none  [body(): lax.psum(qkv_wgrad.astype(jnp.bfloat16), 'dp').astype(jnp.float32)]
    convert_element_type x11 -> x13, other arithmetic: 73.7 us -> 20 us  [the longest x6 9.31 us: fold(): held[k ^ bit] = total.astype(BF) if low else total]
  transfers between devices with their start and end apart: 21 -> 74, of which waited for: 17 -> 32; matrix products, arithmetic and copies ran while one was open for 15% -> 12% of each run, Pallas kernels for 0% -> 13%
where the time goes in v2:
time: 1060 us; the launch traced here: 1050 us
  waiting for transfers between devices  601 us (57%)
  Pallas kernels  210 us (20%)
  matrix products  77.1 us (7%)
  starting transfers between devices  44.5 us (4%)
  other arithmetic  44.3 us (4%)
  blocking collectives  32.7 us (3%)
  local copies, waits for them, and re-layouts  23.5 us (2%)
  between operations  15.4 us (1%)
    ppermute x59, waiting for transfers between devices, swapped(): return lax.ppermute(value, axis, [(i, i ^ mask) for i in range(size)])  265 us
    all_gather x4, waiting for transfers between devices, spread_cols(): return lax.all_gather(value, 'col', axis=0, tiled=False)  213 us
    dot_general x24, matrix products, dot(): return lax.dot_general(left, right, dims, preferred_element_type=F32)  77.1 us
    reduce_scatter x4, waiting for transfers between devices, sum_cols(): return lax.psum_scatter(value, 'col', scatter_dimension=0, tiled=False)  63.3 us
    ppermute x7, waiting for transfers between devices, over_dp(): lax.ppermute(low, 'dp', [(i, (i + step) % size) for i in range(size)])  59.1 us
    pallas_call x1, Pallas kernels, feed_forward(): pl.pallas_call(functools.partial(ff_kernel, count), out_shape=(shape(rows...  47.4 us
    pallas_call x1, Pallas kernels, attend_back(): pl.pallas_call(functools.partial(attend_back_kernel, tile), out_shape=(sh...  37.6 us
    ppermute x59, starting transfers between devices, swapped(): return lax.ppermute(value, axis, [(i, i ^ mask) for i in range(size)])  34.3 us
  transfers between devices with their start and end apart: 74, of which 32 were waited for; matrix products, arithmetic and copies ran while one was open for 12% of the time, Pallas kernels for 13%

profile of v2, /device:TPU:0, one launch (start us, length us, event | category | flops | bytes accessed | tf_op | source)
XLA Modules:
  0.0 1048.8 jit_solution(9567661520303166126)
XLA Ops:
  11.8 8.5 collective-permute-done.1
  36.6 32.7 %all-gather.4 = f32[16,160,2]{1,2,0:T(2,128)S(1)} all-gather(f32[1,160,2]{1,2,0:T(2,128)S(1)} %maximum_bitcast_fusion.1), channel_id=1, replica_groups=mesh['dp'=2,'row'=4,'col'=4] {'row','col'}, dimensions={0}, use_global_device_ids=true | all-gather | bytes 21760 | tf_op jit(solution)/shard_map/all_gather | solution.py:739
  69.7 35.1 %collective-permute-done.4 = bf16[160,1024]{1,0:T(8,128)(2,1)} collective-permute-done((bf16[160,1024]{1,0:T(8,128)(2,1)}, bf16[160,1024]{1,0:T(8,128)(2,1)}, u32[]{:S(2)}, u32[]{:S(2)}) %collective-permute-start.4) | collective-permute-done | bytes 327712 | tf_op jit(solution)/shard_map/ppermute | solution.py:35
  104.8 14.2 %collective-permute-done.5 = bf16[160,1024]{1,0:T(8,128)(2,1)S(1)} collective-permute-done((bf16[160,1024]{1,0:T(8,128)(2,1)}, bf16[160,1024]{1,0:T(8,128)(2,1)S(1)}, u32[]{:S(2)}, u32[]{:S(2)}) %collective-permute-start.5) | collective-permute-done | bytes 327712 | tf_op jit(solution)/shard_map/ppermute | solution.py:35
  126.8 13.6 %collective-permute-done.12.refs_2_ = bf16[640,640]{1,0:T(8,128)(2,1)} collective-permute-done((bf16[640,640]{1,0:T(8,128)(2,1)}, bf16[640,640]{1,0:T(8,128)(2,1)}, u32[]{:S(2)}, u32[]{:S(2)}) %collective-permute-start.12) | collective-permute-done | bytes 819232 | tf_op jit(solution)/shard_map/ppermute | solution.py:35
  143.9 13.0 %qkv_project.1 = (bf16[4,640,1024]{2,1,0:T(8,128)(2,1)}, f32[1,1024]{1,0:T(1,128)}, bf16[2,480,1024]{2,1,0:T(8,128)(2,1)}) custom-call(bf16[4,4,160,1024]{3,2,1,0:T(8,128)(2,1)} %bitcast.235, f32[4,4,160,1]{3,2,1,0:T(8,128)} %copy.53.gain_ref, f32[40,1024]{1,0:T(8,128)} %get-tuple-element.100.cos_ref, f32[40,1024]{1,0:T(8,128)} %get-tuple-element.101.sin_ref, ...), custom_call_target="tpu_custom_call" | custom-call | tf_op jit(solution)/shard_map/qkv_project/pallas_call | solution.py:146
  164.9 27.7 %attend.1 = (bf16[320,1024]{1,0:T(8,128)(2,1)}, bf16[320,1024]{1,0:T(8,128)(2,1)}, f32[2,4,1,1024]{3,2,1,0:T(1,128)}) custom-call(s32[1]{0:T(128)} %bitcast.8.parity_ref, bf16[480,1024]{1,0:T(8,128)(2,1)} %get-tuple-element.184.own_ref, bf16[480,1024]{1,0:T(8,128)(2,1)} %copy-done.13, s32[1,1024]{1,0:T(1,128)} %bitcast.267, s32[1024,1]{1,0:T(8,128)} %copy.54.seg_col), custom_call_target="tpu_custom_call" | custom-call | tf_op jit(solution)/shard_map/attend/pallas_call | solution.py:237
  195.8 10.2 mix_out.1
  206.0 34.1 %all-gather.12.cloned.1.call-done = bf16[16,160,1024]{2,1,0:T(8,128)(2,1)} async-done(((bf16[4,160,1024]{2,1,0:T(8,128)(2,1)}), bf16[16,160,1024]{2,1,0:T(8,128)(2,1)}) %all-gather.12.cloned.1.call-update) | async-done | bytes 5242896 | tf_op jit(solution)/shard_map/all_gather | solution.py:669
  241.8 48.7 %collective-permute-done.25.refs_10_.refs_2_ = bf16[1728,640]{1,0:T(8,128)(2,1)S(1)} collective-permute-done((bf16[1728,640]{1,0:T(8,128)(2,1)}, bf16[1728,640]{1,0:T(8,128)(2,1)S(1)}, u32[]{:S(2)}, u32[]{:S(2)}) %collective-permute-start.25) | collective-permute-done | bytes 2211872 | tf_op jit(solution)/shard_map/ppermute | solution.py:35
  294.8 9.5 collective-permute-done.20.refs_1_
  309.0 25.6 %reduce-scatter.5.cloned.1.call-done = bf16[1,4,160,1024]{3,2,1,0:T(8,128)(2,1)} async-done(((bf16[4,4,160,1024]{3,2,1,0:T(8,128)(2,1)}), bf16[1,4,160,1024]{3,2,1,0:T(8,128)(2,1)}) %reduce-scatter.5.cloned.1.call-update) | async-done | bytes 1310736 | tf_op jit(solution)/shard_map/reduce_scatter | solution.py:673
  339.2 97.1 %all-gather.14.cloned.1.call-done = bf16[16,160,1024]{2,1,0:T(8,128)(2,1)} async-done(((bf16[4,160,1024]{2,1,0:T(8,128)(2,1)}), bf16[16,160,1024]{2,1,0:T(8,128)(2,1)}) %all-gather.14.cloned.1.call-update) | async-done | bytes 5242896 | tf_op jit(solution)/shard_map/all_gather | solution.py:669
  436.3 47.4 %feed_forward.1 = (bf16[4,640,1024]{2,1,0:T(8,128)(2,1)}, f32[1,1024]{1,0:T(1,128)}, bf16[4,640,1024]{2,1,0:T(8,128)(2,1)}, f32[1,1024]{1,0:T(1,128)}, bf16[1728...) custom-call(bf16[4,4,160,1024]{3,2,1,0:T(8,128)(2,1)} %bitcast.233, ...), custom_call_target="tpu_custom_call" | custom-call | tf_op jit(solution)/shard_map/feed_forward/pallas_call | solution.py:514
  483.7 31.7 %ff_back.1 = (bf16[4,4,160,1024]{3,2,1,0:T(8,128)(2,1)}, f32[4,4,160,1]{3,2,1,0:T(8,128)}) custom-call(bf16[4,4,160,1024]{3,2,1,0:T(8,128)(2,1)} %bitcast.234, f32[4,4,160,1]{3,2,1,0:T(8,128)} %copy.57.gain_ref, f32[1,1024]{1,0:T(1,128)} %get-tuple-element.143.scale_ref, f32[1,1024]{1,0:T(1,128)} %get-tuple-element.144.inner_ref, ...), custom_call_target="tpu_custom_call" | custom-call | tf_op jit(solution)/shard_map/ff_back/pallas_call | solution.py:577
  570.1 37.7 %reduce-scatter.7.cloned.1.call-done = bf16[1,4,160,1024]{3,2,1,0:T(8,128)(2,1)} async-done(((bf16[4,4,160,1024]{3,2,1,0:T(8,128)(2,1)}), bf16[1,4,160,1024]{3,2,1,0:T(8,128)(2,1)}) %reduce-scatter.7.cloned.1.call-update) | async-done | bytes 1310736 | tf_op jit(solution)/shard_map/reduce_scatter | solution.py:673
  610.8 16.6 %fan_out.1 = bf16[4,4,160,1024]{3,2,1,0:T(8,128)(2,1)} custom-call(bf16[1728,1024]{1,0:T(8,128)(2,1)} %get-tuple-element.151.x_ref, bf16[1728,640]{1,0:T(8,128)(2,1)} %refs_0_.2, bf16[1728,640]{1,0:T(8,128)(2,1)} %copy-done.6, bf16[1728,640]{1,0:T(8,128)(2,1)} %copy-done.5, bf16[1728,640]{1,0:T(8,128)(2,1)} %copy-done.7), custom_call_target="tpu_custom_call" | custom-call | tf_op jit(solution)/shard_map/fan_out/pallas_call | solution.py:464
  627.4 82.1 %all-gather.16.cloned.1.call-done = bf16[16,160,1024]{2,1,0:T(8,128)(2,1)} async-done(((bf16[4,160,1024]{2,1,0:T(8,128)(2,1)}), bf16[16,160,1024]{2,1,0:T(8,128)(2,1)}) %all-gather.16.cloned.1.call-update) | async-done | bytes 5242896 | tf_op jit(solution)/shard_map/all_gather | solution.py:669
  711.8 8.6 mix_back.1
  724.0 37.6 %attend_back.1 = (bf16[480,1024]{1,0:T(8,128)(2,1)}, bf16[480,1024]{1,0:T(8,128)(2,1)}) custom-call(s32[1]{0:T(128)} %bitcast.8.parity_ref, bf16[480,1024]{1,0:T(8,128)(2,1)} %get-tuple-element.184.own_ref, bf16[480,1024]{1,0:T(8,128)(2,1)} %copy-done.13, bf16[320,1024]{1,0:T(8,128)(2,1)} %get-tuple-element.116.own_ref.own_out, ...), custom_call_target="tpu_custom_call" | custom-call | tf_op jit(solution)/shard_map/attend_back/pallas_call | solution.py:348
  767.3 41.2 %collective-permute-done.62 = bf16[1728,640]{1,0:T(8,128)(2,1)} collective-permute-done((bf16[1728,640]{1,0:T(8,128)(2,1)}, bf16[1728,640]{1,0:T(8,128)(2,1)}, u32[]{:S(2)}, u32[]{:S(2)}) %collective-permute-start.62) | collective-permute-done | bytes 2211872 | tf_op jit(solution)/shard_map/ppermute | solution.py:35
  815.6 17.3 %qkv_back.1 = (bf16[640,1024]{1,0:T(8,128)(2,1)}, bf16[320,1024]{1,0:T(8,128)(2,1)}, bf16[4,4,160,1024]{3,2,1,0:T(8,128)(2,1)}, f32[4,4,160,1]{3,2,1,0:T(8,128)}) custom-call(s32[1]{0:T(128)} %bitcast.8.parity_ref, bf16[4,4,160,1024]{3,2,1,0:T(8,128)(2,1)} %bitcast.236, f32[4,4,160,1]{3,2,1,0:T(8,128)} %copy.53.gain_ref, ...), custom_call_target="tpu_custom_call" | custom-call | tf_op jit(solution)/shard_map/qkv_back/pallas_call | solution.py:647
  833.0 21.9 %collective-permute-done.60 = bf16[1728,640]{1,0:T(8,128)(2,1)} collective-permute-done((bf16[1728,640]{1,0:T(8,128)(2,1)}, bf16[1728,640]{1,0:T(8,128)(2,1)}, u32[]{:S(2)}, u32[]{:S(2)}) %collective-permute-start.60) | collective-permute-done | bytes 2211872 | tf_op jit(solution)/shard_map/ppermute | solution.py:35
  873.7 11.8 %collective-permute-done.58 = bf16[640,640]{1,0:T(8,128)(2,1)S(1)} collective-permute-done((bf16[640,640]{1,0:T(8,128)(2,1)S(1)}, bf16[640,640]{1,0:T(8,128)(2,1)S(1)}, u32[]{:S(2)}, u32[]{:S(2)}) %collective-permute-start.58) | collective-permute-done | bytes 819232 | tf_op jit(solution)/shard_map/ppermute | solution.py:35
  890.6 21.1 %collective-permute-done.61 = bf16[1728,640]{1,0:T(8,128)(2,1)S(1)} collective-permute-done((bf16[1728,640]{1,0:T(8,128)(2,1)S(1)}, bf16[1728,640]{1,0:T(8,128)(2,1)S(1)}, u32[]{:S(2)}, u32[]{:S(2)}) %collective-permute-start.61) | collective-permute-done | bytes 2211872 | tf_op jit(solution)/shard_map/ppermute | solution.py:681
  914.3 14.1 %collective-permute-done.59 = bf16[640,640]{1,0:T(8,128)(2,1)S(1)} collective-permute-done((bf16[640,640]{1,0:T(8,128)(2,1)S(1)}, bf16[640,640]{1,0:T(8,128)(2,1)S(1)}, u32[]{:S(2)}, u32[]{:S(2)}) %collective-permute-start.59) | collective-permute-done | bytes 819232 | tf_op jit(solution)/shard_map/ppermute | solution.py:681
  963.1 8.2 collective-permute-done.36
  974.9 12.2 %collective-permute-done.54 = bf16[320,640]{1,0:T(8,128)(2,1)S(1)} collective-permute-done((bf16[320,640]{1,0:T(8,128)(2,1)S(1)}, bf16[320,640]{1,0:T(8,128)(2,1)S(1)}, u32[]{:S(2)}, u32[]{:S(2)}) %collective-permute-start.54) | collective-permute-done | bytes 409632 | tf_op jit(solution)/shard_map/ppermute | solution.py:35
  990.1 7.1 collective-permute-done.55
  997.3 6.6 collective-permute-done.50
  1008.8 14.8 %collective-permute-done.51 = bf16[640,640]{1,0:T(8,128)(2,1)} collective-permute-done((bf16[640,640]{1,0:T(8,128)(2,1)S(1)}, bf16[640,640]{1,0:T(8,128)(2,1)}, u32[]{:S(2)}, u32[]{:S(2)}) %collective-permute-start.51) | collective-permute-done | bytes 819232 | tf_op jit(solution)/shard_map/ppermute | solution.py:681
  1027.6 9.2 collective-permute-done.39
  (340 shorter events, 215.9 us)
Async XLA Ops:
  7.2 133.3 %all-gather.10.cloned.1.call-start = ((), (), s32[]{:S(2)}) async-start(), calls=%async_computation.8 | async-start | bytes 6553600 | tf_op jit(solution)/shard_map/all_gather | solution.py:669
  28.9 211.3 %all-gather.12.cloned.1.call-start = ((), (), s32[]{:S(2)}) async-start(), calls=%async_computation.9 | async-start | bytes 6553600 | tf_op jit(solution)/shard_map/all_gather | solution.py:669
  28.9 111.5 %collective-permute-start.13 = (bf16[1728,640]{1,0:T(8,128)(2,1)S(1)}, bf16[1728,640]{1,0:T(8,128)(2,1)}, u32[]{:S(2)}, u32[]{:S(2)}) collective-permute-start(bf16[1728,640]{1,0:T(8,128)(2,1)S(1)} %bitcast.239), channel_id=1, source_target_pairs={{0,8},{4,12},{8,0},{12,4},{1,9},{5,13},{9,1},{13,5},{2,10},{6,14},... | collective-permute-start | bytes 6635528 | tf_op jit(solution)/shard_map/ppermute | solution.py:35
  30.6 91.0 %collective-permute-start.7 = (bf16[640,640]{1,0:T(8,128)(2,1)}, bf16[640,640]{1,0:T(8,128)(2,1)}, u32[]{:S(2)}, u32[]{:S(2)}) collective-permute-start(bf16[640,640]{1,0:T(8,128)(2,1)} %refs_0_.4), channel_id=1, source_target_pairs={{0,8},{4,12},{8,0},{12,4},{1,9},{5,13},{9,1},{13,5},{2,10},{6,14},... | collective-permute-start | bytes 2457608 | tf_op jit(solution)/shard_map/ppermute | solution.py:35
  33.4 36.2 %collective-permute-start.3 = (bf16[160,1024]{1,0:T(8,128)(2,1)}, bf16[160,1024]{1,0:T(8,128)(2,1)}, u32[]{:S(2)}, u32[]{:S(2)}) collective-permute-start(bf16[160,1024]{1,0:T(8,128)(2,1)} %get-tuple-element.198), channel_id=1, source_target_pairs={{0,4},{4,0},{8,12},{12,8},{1,5},{5,1},{9,13},{13,9},{2,6},{6,2},{1... | collective-permute-start | bytes 983048 | tf_op jit(solution)/shard_map/ppermute | solution.py:35
  33.9 70.9 %collective-permute-start.4 = (bf16[160,1024]{1,0:T(8,128)(2,1)}, bf16[160,1024]{1,0:T(8,128)(2,1)}, u32[]{:S(2)}, u32[]{:S(2)}) collective-permute-start(bf16[160,1024]{1,0:T(8,128)(2,1)} %get-tuple-element.200), channel_id=1, source_target_pairs={{0,8},{4,12},{8,0},{12,4},{1,9},{5,13},{9,1},{13,5},{2,10},{6,14},... | collective-permute-start | bytes 983048 | tf_op jit(solution)/shard_map/ppermute | solution.py:35
  35.5 84.3 %collective-permute-start.10 = (bf16[320,640]{1,0:T(8,128)(2,1)S(1)}, bf16[320,640]{1,0:T(8,128)(2,1)S(1)}, u32[]{:S(2)}, u32[]{:S(2)}) collective-permute-start(bf16[320,640]{1,0:T(8,128)(2,1)S(1)} %pad_maximum_fusion.3.refs_4_), channel_id=1, source_target_pairs={{0,8},{4,12},{8,0},{12,4},{1,9},{5,13},{9,1},{13,5},{2,10},{6,14},... | collective-permute-start | bytes 1228808 | tf_op jit(solution)/shard_map/ppermute | solution.py:35
  69.6 49.4 %collective-permute-start.5 = (bf16[160,1024]{1,0:T(8,128)(2,1)}, bf16[160,1024]{1,0:T(8,128)(2,1)S(1)}, u32[]{:S(2)}, u32[]{:S(2)}) collective-permute-start(bf16[160,1024]{1,0:T(8,128)(2,1)} %get-tuple-element.199), channel_id=1, source_target_pairs={{0,12},{4,8},{8,4},{12,0},{1,13},{5,9},{9,5},{13,1},{2,14},{6,10},... | collective-permute-start | bytes 983048 | tf_op jit(solution)/shard_map/ppermute | solution.py:35
  140.5 194.1 %reduce-scatter.5.cloned.1.call-start = ((), (), s32[]{:S(2)}) async-start(), calls=%async_computation.4 | async-start | bytes 6553600 | tf_op jit(solution)/shard_map/reduce_scatter | solution.py:673
  140.5 52.3 %collective-permute-start.19 = (bf16[1728,640]{1,0:T(8,128)(2,1)}, bf16[1728,640]{1,0:T(8,128)(2,1)}, u32[]{:S(2)}, u32[]{:S(2)}) collective-permute-start(bf16[1728,640]{1,0:T(8,128)(2,1)} %bitcast.241), channel_id=1, source_target_pairs={{0,8},{4,12},{8,0},{12,4},{1,9},{5,13},{9,1},{13,5},{2,10},{6,14},... | collective-permute-start | bytes 6635528 | tf_op jit(solution)/shard_map/ppermute | solution.py:35
  159.8 33.0 %collective-permute-start.17 = (bf16[640,640]{1,0:T(8,128)(2,1)}, bf16[640,640]{1,0:T(8,128)(2,1)}, u32[]{:S(2)}, u32[]{:S(2)}) collective-permute-start(bf16[640,640]{1,0:T(8,128)(2,1)} %refs_0_.3), channel_id=1, source_target_pairs={{0,4},{4,0},{8,12},{12,8},{1,5},{5,1},{9,13},{13,9},{2,6},{6,2},{1... | collective-permute-start | bytes 2457608 | tf_op jit(solution)/shard_map/ppermute | solution.py:35
  160.3 32.5 %collective-permute-start.18 = (bf16[640,640]{1,0:T(8,128)(2,1)}, bf16[640,640]{1,0:T(8,128)(2,1)}, u32[]{:S(2)}, u32[]{:S(2)}) collective-permute-start(bf16[640,640]{1,0:T(8,128)(2,1)} %collective-permute-done.12.refs_2_), channel_id=1, source_target_pairs={{0,4},{4,0},{8,12},{12,8},{1,5},{5,1},{9,13},{13,9},{2,6},{6,2},{1... | collective-permute-start | bytes 2457608 | tf_op jit(solution)/shard_map/ppermute | solution.py:35
  240.2 196.1 %all-gather.14.cloned.1.call-start = ((), (), s32[]{:S(2)}) async-start(), calls=%async_computation.10 | async-start | bytes 6553600 | tf_op jit(solution)/shard_map/all_gather | solution.py:669
  240.2 50.3 %collective-permute-start.25 = (bf16[1728,640]{1,0:T(8,128)(2,1)}, bf16[1728,640]{1,0:T(8,128)(2,1)S(1)}, u32[]{:S(2)}, u32[]{:S(2)}) collective-permute-start(bf16[1728,640]{1,0:T(8,128)(2,1)} %refs_0_.2), channel_id=1, source_target_pairs={{0,8},{4,12},{8,0},{12,4},{1,9},{5,13},{9,1},{13,5},{2,10},{6,14},... | collective-permute-start | bytes 6635528 | tf_op jit(solution)/shard_map/ppermute | solution.py:35
  241.8 49.8 %collective-permute-start.24 = (bf16[1728,640]{1,0:T(8,128)(2,1)}, bf16[1728,640]{1,0:T(8,128)(2,1)S(1)}, u32[]{:S(2)}, u32[]{:S(2)}) collective-permute-start(bf16[1728,640]{1,0:T(8,128)(2,1)} %refs_0_.2), channel_id=1, source_target_pairs={{0,4},{4,0},{8,12},{12,8},{1,5},{5,1},{9,13},{13,9},{2,6},{6,2},{1... | collective-permute-start | bytes 6635528 | tf_op jit(solution)/shard_map/ppermute | solution.py:35
  337.6 270.2 %reduce-scatter.7.cloned.1.call-start = ((), (), s32[]{:S(2)}) async-start(), calls=%async_computation.5 | async-start | bytes 6553600 | tf_op jit(solution)/shard_map/reduce_scatter | solution.py:673
  515.5 193.9 %all-gather.16.cloned.1.call-start = ((), (), s32[]{:S(2)}) async-start(), calls=%async_computation.11 | async-start | bytes 6553600 | tf_op jit(solution)/shard_map/all_gather | solution.py:669
  610.7 222.2 %reduce-scatter.9.cloned.1.call-start = ((), (), s32[]{:S(2)}) async-start(), calls=%async_computation.6 | async-start | bytes 6553600 | tf_op jit(solution)/shard_map/reduce_scatter | solution.py:673
  709.5 297.0 %reduce-scatter.11.cloned.1.call-start = ((), (), s32[]{:S(2)}) async-start(), calls=%async_computation.7 | async-start | bytes 6553600 | tf_op jit(solution)/shard_map/reduce_scatter | solution.py:673
  709.7 52.3 %collective-permute-start.64 = (bf16[1728,640]{1,0:T(8,128)(2,1)}, bf16[1728,640]{1,0:T(8,128)(2,1)}, u32[]{:S(2)}, u32[]{:S(2)}) collective-permute-start(bf16[1728,640]{1,0:T(8,128)(2,1)} %add_convert_fusion.7), channel_id=1, source_target_pairs={{0,8},{4,12},{8,0},{12,4},{1,9},{5,13},{9,1},{13,5},{2,10},{6,14},... | collective-permute-start | bytes 6635528 | tf_op jit(solution)/shard_map/ppermute | solution.py:35
  711.3 97.2 %collective-permute-start.62 = (bf16[1728,640]{1,0:T(8,128)(2,1)}, bf16[1728,640]{1,0:T(8,128)(2,1)}, u32[]{:S(2)}, u32[]{:S(2)}) collective-permute-start(bf16[1728,640]{1,0:T(8,128)(2,1)} %add_convert_fusion.3), channel_id=1, source_target_pairs={{0,8},{4,12},{8,0},{12,4},{1,9},{5,13},{9,1},{13,5},{2,10},{6,14},... | collective-permute-start | bytes 6635528 | tf_op jit(solution)/shard_map/ppermute | solution.py:35
  720.5 134.4 %collective-permute-start.60 = (bf16[1728,640]{1,0:T(8,128)(2,1)}, bf16[1728,640]{1,0:T(8,128)(2,1)}, u32[]{:S(2)}, u32[]{:S(2)}) collective-permute-start(bf16[1728,640]{1,0:T(8,128)(2,1)} %add_convert_fusion.5), channel_id=1, source_target_pairs={{0,8},{4,12},{8,0},{12,4},{1,9},{5,13},{9,1},{13,5},{2,10},{6,14},... | collective-permute-start | bytes 6635528 | tf_op jit(solution)/shard_map/ppermute | solution.py:35
  761.6 54.0 %collective-permute-start.34 = (bf16[480,1024]{1,0:T(8,128)(2,1)}, bf16[480,1024]{1,0:T(8,128)(2,1)}, u32[]{:S(2)}, u32[]{:S(2)}) collective-permute-start(bf16[480,1024]{1,0:T(8,128)(2,1)} %get-tuple-element.162), channel_id=1, source_target_pairs={{0,4},{4,0},{8,12},{12,8},{1,5},{5,1},{9,13},{13,9},{2,6},{6,2},{1... | collective-permute-start | bytes 2949128 | tf_op jit(solution)/shard_map/ppermute | solution.py:35
  765.8 100.6 %collective-permute-start.65 = (bf16[1728,640]{1,0:T(8,128)(2,1)}, bf16[1728,640]{1,0:T(8,128)(2,1)}, u32[]{:S(2)}, u32[]{:S(2)}) collective-permute-start(bf16[1728,640]{1,0:T(8,128)(2,1)} %add_convert_fusion), channel_id=1, source_target_pairs={{0,16},{16,0},{1,17},{17,1},{2,18},{18,2},{3,19},{19,3},{4,20},{20... | collective-permute-start | bytes 6635528 | tf_op jit(solution)/shard_map/ppermute | solution.py:681
  810.7 75.8 %collective-permute-start.63 = (bf16[1728,640]{1,0:T(8,128)(2,1)S(1)}, bf16[1728,640]{1,0:T(8,128)(2,1)}, u32[]{:S(2)}, u32[]{:S(2)}) collective-permute-start(bf16[1728,640]{1,0:T(8,128)(2,1)S(1)} %add_convert_fusion.1), channel_id=1, source_target_pairs={{0,16},{16,0},{1,17},{17,1},{2,18},{18,2},{3,19},{19,3},{4,20},{20... | collective-permute-start | bytes 6635528 | tf_op jit(solution)/shard_map/ppermute | solution.py:681
  815.6 46.3 %collective-permute-start.57 = (bf16[640,640]{1,0:T(8,128)(2,1)}, bf16[640,640]{1,0:T(8,128)(2,1)}, u32[]{:S(2)}, u32[]{:S(2)}) collective-permute-start(bf16[640,640]{1,0:T(8,128)(2,1)} %convolution_convert_fusion.12), channel_id=1, source_target_pairs={{0,4},{4,0},{8,12},{12,8},{1,5},{5,1},{9,13},{13,9},{2,6},{6,2},{1... | collective-permute-start | bytes 2457608 | tf_op jit(solution)/shard_map/ppermute | solution.py:35
  857.8 54.0 %collective-permute-start.61 = (bf16[1728,640]{1,0:T(8,128)(2,1)S(1)}, bf16[1728,640]{1,0:T(8,128)(2,1)S(1)}, u32[]{:S(2)}, u32[]{:S(2)}) collective-permute-start(bf16[1728,640]{1,0:T(8,128)(2,1)S(1)} %add_convert_fusion.2), channel_id=1, source_target_pairs={{0,16},{16,0},{1,17},{17,1},{2,18},{18,2},{3,19},{19,3},{4,20},{20... | collective-permute-start | bytes 6635528 | tf_op jit(solution)/shard_map/ppermute | solution.py:681
  885.8 42.6 %collective-permute-start.59 = (bf16[640,640]{1,0:T(8,128)(2,1)S(1)}, bf16[640,640]{1,0:T(8,128)(2,1)S(1)}, u32[]{:S(2)}, u32[]{:S(2)}) collective-permute-start(bf16[640,640]{1,0:T(8,128)(2,1)S(1)} %add_convert_fusion.10), channel_id=1, source_target_pairs={{0,16},{16,0},{1,17},{17,1},{2,18},{18,2},{3,19},{19,3},{4,20},{20... | collective-permute-start | bytes 2457608 | tf_op jit(solution)/shard_map/ppermute | solution.py:681
  942.0 32.9 %collective-permute-start.52 = (bf16[320,640]{1,0:T(8,128)(2,1)S(1)}, bf16[320,640]{1,0:T(8,128)(2,1)S(1)}, u32[]{:S(2)}, u32[]{:S(2)}) collective-permute-start(bf16[320,640]{1,0:T(8,128)(2,1)S(1)} %fusion.45), channel_id=1, source_target_pairs={{0,4},{4,0},{8,12},{12,8},{1,5},{5,1},{9,13},{13,9},{2,6},{6,2},{1... | collective-permute-start | bytes 1228808 | tf_op jit(solution)/shard_map/ppermute | solution.py:35
  942.6 46.2 %collective-permute-start.48 = (bf16[640,640]{1,0:T(8,128)(2,1)S(1)}, bf16[640,640]{1,0:T(8,128)(2,1)S(1)}, u32[]{:S(2)}, u32[]{:S(2)}) collective-permute-start(bf16[640,640]{1,0:T(8,128)(2,1)S(1)} %convolution_convert_fusion.18), channel_id=1, source_target_pairs={{0,4},{4,0},{8,12},{12,8},{1,5},{5,1},{9,13},{13,9},{2,6},{6,2},{1... | collective-permute-start | bytes 2457608 | tf_op jit(solution)/shard_map/ppermute | solution.py:35
  962.0 26.8 %collective-permute-start.37 = (bf16[160,1024]{1,0:T(8,128)(2,1)S(1)}, bf16[160,1024]{1,0:T(8,128)(2,1)S(1)}, u32[]{:S(2)}, u32[]{:S(2)}) collective-permute-start(bf16[160,1024]{1,0:T(8,128)(2,1)S(1)} %get-tuple-element.190), channel_id=1, source_target_pairs={{0,12},{4,8},{8,4},{12,0},{1,13},{5,9},{9,5},{13,1},{2,14},{6,10},... | collective-permute-start | bytes 983048 | tf_op jit(solution)/shard_map/ppermute | solution.py:35
  974.0 29.9 %collective-permute-start.50 = (bf16[640,640]{1,0:T(8,128)(2,1)S(1)}, bf16[640,640]{1,0:T(8,128)(2,1)S(1)}, u32[]{:S(2)}, u32[]{:S(2)}) collective-permute-start(bf16[640,640]{1,0:T(8,128)(2,1)S(1)} %add_convert_fusion.14), channel_id=1, source_target_pairs={{0,8},{4,12},{8,0},{12,4},{1,9},{5,13},{9,1},{13,5},{2,10},{6,14},... | collective-permute-start | bytes 2457608 | tf_op jit(solution)/shard_map/ppermute | solution.py:35
  (99 other events, 1914.9 us)
Sparse Core Ops, SparseCore 0:
  29.0 99.8 all-gather.9
  140.6 99.4 all-gather.11
  242.4 92.1 reduce-scatter.4
  337.7 98.5 all-gather.13
  515.6 92.1 reduce-scatter.6
  610.8 98.5 all-gather.15
  711.7 92.1 reduce-scatter.8
  833.1 91.4 reduce-scatter.10

commit v3 on v2

--- a/solution.py
+++ b/solution.py
@@ -416,13 +416,16 @@
     )(parity, own, other, *weights)
 
 
-def mix_back_kernel(count, parity_ref, x_ref, *refs):
-    weights = refs[:count]
-    rows_ref, own_ref, other_ref = refs[count:]
-    cols, _, piece, _ = x_ref.shape
-    for c in range(cols):
-        for k in range(count):
-            rows_ref[k, c * piece : (c + 1) * piece, :] = x_ref[c, k]
+def mix_back_kernel(count, parts, parity_ref, *refs):
+    x_refs, weights = refs[:parts], refs[parts : parts + count]
+    rows_ref, own_ref, other_ref = refs[parts + count :]
+    for i, x_ref in enumerate(x_refs):
+        cols, _, piece, tokens = x_ref.shape
+        for c in range(cols):
+            for k in range(count):
+                rows_ref[k, c * piece : (c + 1) * piece, i * tokens : (i + 1) * tokens] = x_ref[
+                    c, k
+                ]
     mine, other = halves_at(parity_ref[0], own_ref.shape[0])
     for at, out_ref in ((other, other_ref), (mine, own_ref)):
         total = None
@@ -432,21 +435,23 @@
         out_ref[...] = total.astype(BF)
 
 
-def mix_back(parity, x, weights):
-    cols, count, piece, tokens = x.shape
+def mix_back(parity, x_parts, weights):
+    parts = len(x_parts)
+    cols, count, piece, tokens = x_parts[0].shape
+    tokens = tokens * parts
     half_rows = weights[0].shape[0] // 2
     vmem = pl.BlockSpec(memory_space=pltpu.VMEM)
     return pl.pallas_call(
-        functools.partial(mix_back_kernel, count),
+        functools.partial(mix_back_kernel, count, parts),
         out_shape=(
             shape((count, cols * piece, tokens), BF),
             shape((half_rows, tokens), BF),
             shape((half_rows, tokens), BF),
         ),
-        in_specs=[SMALL] + [vmem] * (1 + count),
+        in_specs=[SMALL] + [vmem] * (parts + count),
         compiler_params=params(),
         name="mix_back",
-    )(parity, x, *weights)
+    )(parity, *x_parts, *weights)
 
 
 def fan_kernel(count, x_ref, *refs):
@@ -469,18 +474,31 @@
     )(x, *weights)
 
 
-def ff_kernel(count, x_ref, g_ref, gain_ref, *refs):
+def norm_back(grads, k, x_ref, gain_ref, scale, coef, share_ref, gain_share_ref):
+    cols, _, piece, _ = x_ref.shape
+    for c in range(cols):
+        grad = grads[c * piece : (c + 1) * piece]
+        value = x_ref[c, k].astype(F32)
+        gain_share_ref[c, k] = jnp.sum(grad * (value * scale), axis=1, keepdims=True)
+        share_ref[c, k] = ((grad * gain_ref[c, k]) * scale - value * coef).astype(BF)
+
+
+def ff_kernel(count, chained, x_ref, g_ref, gain_ref, *refs):
     gate_w, up_w, down_w = refs[:count], refs[count : 2 * count], refs[2 * count : 3 * count]
-    norm_ref, scale_ref, rows_ref, inner_ref, act_ref, dgate_ref, dup_ref = refs[3 * count :]
+    refs = refs[3 * count + (5 if chained else 0) :]
+    norm_ref, rows_ref, act_ref, dgate_ref, dup_ref, share_ref, gain_share_ref = refs[:7]
+    scale_ref, inner_ref, back_ref = refs[7:]
     cols, _, piece, _ = x_ref.shape
-
-    @pl.when(pl.program_id(0) == 0)
+    step = pl.program_id(0)
+
+    @pl.when(step == 0)
     def _():
         normalise(x_ref, gain_ref, norm_ref, scale_ref)
         for c in range(cols):
             for k in range(count):
                 rows_ref[k, c * piece : (c + 1) * piece, :] = g_ref[c, k]
         inner_ref[...] = jnp.zeros_like(inner_ref)
+        back_ref[...] = jnp.zeros_like(back_ref)
 
     def summed(weights, ref):
         total = None
@@ -500,94 +518,64 @@
     inner_ref[...] += jnp.sum(dgate * gate + dup * up, axis=0, keepdims=True)
     dgate_ref[...] = dgate.astype(BF)
     dup_ref[...] = dup.astype(BF)
-
-
-def feed_forward(x, g, gain, gate_w, up_w, down_w):
+    for k in range(count):
+        back_ref[k] += dot(gate_w[k][...], dgate_ref[...], TN) + dot(
+            up_w[k][...], dup_ref[...], TN
+        )
+
+    @pl.when(step == pl.num_programs(0) - 1)
+    def _():
+        scale = scale_ref[...]
+        coef = scale * scale * inner_ref[...] / D
+        for k in range(count):
+            norm_back(back_ref[k], k, x_ref, gain_ref, scale, coef, share_ref, gain_share_ref)
+
+
+def feed_forward(x, g, part, parts, gain, gate_w, up_w, down_w, before):
     cols, count, piece, tokens = x.shape
     width, depth = gate_w[0].shape
     tile = 432 if width % 432 == 0 else width
-    whole = resident(x.shape, 1)
+    g_spec = pl.BlockSpec(x.shape, lambda n: (0, 0, 0, part), pipeline_mode=pl.Buffered(1))
     rows = (count, cols * piece, tokens)
+    rows_spec = pl.BlockSpec(rows, lambda n: (0, 0, part), pipeline_mode=pl.Buffered(1))
     w_spec = pl.BlockSpec((tile, depth), lambda n: (n, 0))
-    h_spec = pl.BlockSpec((tile, tokens), lambda n: (n, 0))
-    hidden = shape((width, tokens), BF)
+    h_spec = pl.BlockSpec((tile, tokens), lambda n: (n, part))
+    rows_all = shape((count, cols * piece, tokens * parts), BF)
+    hidden = shape((width, tokens * parts), BF)
+    first = 3 + 3 * count
     return pl.pallas_call(
-        functools.partial(ff_kernel, count),
+        functools.partial(ff_kernel, count, bool(before)),
         out_shape=(
-            shape(rows, BF),
-            shape((1, tokens), F32),
-            shape(rows, BF),
-            shape((1, tokens), F32),
+            rows_all,
+            rows_all,
             hidden,
             hidden,
             hidden,
+            shape(x.shape, BF),
+            shape(gain.shape, F32),
         ),
         grid=(width // tile,),
-        in_specs=[whole, whole, resident(gain.shape, 1)] + [w_spec] * (3 * count),
+        in_specs=[resident(x.shape, 1), g_spec, resident(gain.shape, 1)]
+        + [w_spec] * (3 * count)
+        + [RAW] * len(before),
         out_specs=(
-            resident(rows, 1),
-            resident((1, tokens)),
-            resident(rows, 1),
-            resident((1, tokens)),
+            rows_spec,
+            rows_spec,
             h_spec,
             h_spec,
             h_spec,
+            resident(x.shape, 1),
+            resident(gain.shape, 1),
         ),
+        scratch_shapes=[
+            pltpu.VMEM((1, tokens), F32),
+            pltpu.VMEM((1, tokens), F32),
+            pltpu.VMEM(rows, F32),
+        ],
+        input_output_aliases={first + i: i for i in range(len(before))},
         compiler_params=params(60),
         name="feed_forward",
-    )(x, g, gain, *gate_w, *up_w, *down_w)
-
-
-def norm_back(grads, k, x_ref, gain_ref, scale, coef, share_ref, gain_share_ref):
-    cols, _, piece, _ = x_ref.shape
-    for c in range(cols):
-        grad = grads[c * piece : (c + 1) * piece]
-        value = x_ref[c, k].astype(F32)
-        gain_share_ref[c, k] = jnp.sum(grad * (value * scale), axis=1, keepdims=True)
-        share_ref[c, k] = ((grad * gain_ref[c, k]) * scale - value * coef).astype(BF)
-
-
-def ff_back_kernel(count, x_ref, gain_ref, scale_ref, inner_ref, dgate, dup, *refs):
-    gate_w, up_w = refs[:count], refs[count : 2 * count]
-    share_ref, gain_share_ref, dgate_buf, dup_buf, gate_buf, up_buf, sems = refs[2 * count :]
-    copies = [
-        pltpu.make_async_copy(dgate, dgate_buf, sems.at[0]),
-        pltpu.make_async_copy(dup, dup_buf, sems.at[1]),
-    ]
-    for k in range(count):
-        copies.append(pltpu.make_async_copy(gate_w[k], gate_buf.at[k], sems.at[2 + 2 * k]))
-        copies.append(pltpu.make_async_copy(up_w[k], up_buf.at[k], sems.at[3 + 2 * k]))
-    for copy in copies:
-        copy.start()
-    scale = scale_ref[...]
-    coef = scale * scale * inner_ref[...] / D
-    copies[0].wait()
-    copies[1].wait()
-    for k in range(count):
-        copies[2 + 2 * k].wait()
-        copies[3 + 2 * k].wait()
-        grads = dot(gate_buf[k], dgate_buf[...], TN) + dot(up_buf[k], dup_buf[...], TN)
-        norm_back(grads, k, x_ref, gain_ref, scale, coef, share_ref, gain_share_ref)
-
-
-def ff_back(x, gain, scale, inner, dgate, dup, gate_w, up_w):
-    count = len(gate_w)
-    vmem = pl.BlockSpec(memory_space=pltpu.VMEM)
-    width, depth = gate_w[0].shape
-    return pl.pallas_call(
-        functools.partial(ff_back_kernel, count),
-        out_shape=(shape(x.shape, BF), shape(gain.shape, F32)),
-        in_specs=[vmem] * 4 + [RAW] * (2 + 2 * count),
-        scratch_shapes=[
-            pltpu.VMEM(dgate.shape, BF),
-            pltpu.VMEM(dup.shape, BF),
-            pltpu.VMEM((count, width, depth), BF),
-            pltpu.VMEM((count, width, depth), BF),
-            pltpu.SemaphoreType.DMA((2 + 2 * count,)),
-        ],
-        compiler_params=params(60),
-        name="ff_back",
-    )(x, gain, scale, inner, dgate, dup, *gate_w, *up_w)
+    )(x, g, gain, *gate_w, *up_w, *down_w, *before)
 
 
 def qkv_back_kernel(
@@ -774,39 +762,53 @@
     )
     residual_own = source_own.astype(F32) + attn_sum.astype(F32)
 
-    residual = spread_cols(residual_own.astype(BF))
-    norm_two, scale_two, grad_rows, inner, act, dgate, dup = feed_forward(
-        residual,
-        grad_all,
-        gain_two,
-        listed(gate_blocks),
-        listed(up_blocks),
-        listed(down_blocks),
-    )
-    share, gain_share_two = ff_back(
-        residual, gain_two, scale_two, inner, dgate, dup, listed(gate_blocks), listed(up_blocks)
-    )
-    share_sum = sum_cols(share)
-    share, dgate, dup, act, grad_rows, norm_two = together(
-        share, dgate, dup, act, grad_rows, norm_two
-    )
+    parts = 2 if rows % 256 == 0 else 1
+    size = rows // parts
+    spans = [slice(i * size, (i + 1) * size) for i in range(parts)]
+    residual_low = residual_own.astype(BF)
+    residual = [spread_cols(residual_low[..., span]) for span in spans]
+    before, shares = (), []
+    gain_share_two = 0.0
+    for i in range(parts):
+        out = feed_forward(
+            residual[i],
+            grad_all,
+            i,
+            parts,
+            gain_two,
+            listed(gate_blocks),
+            listed(up_blocks),
+            listed(down_blocks),
+            before,
+        )
+        before = out[:5]
+        shares.append(out[5])
+        gain_share_two = gain_share_two + out[6]
+    norm_two, grad_rows, act, dgate, dup = before
+    share_sums = [sum_cols(share) for share in shares]
     down_grads = {k: dot(act, grad_rows[k], NT).astype(BF) for k in range(count)}
     gate_grads = {k: dot(dgate, norm_two[k], NT).astype(BF) for k in range(count)}
     up_grads = {k: dot(dup, norm_two[k], NT).astype(BF) for k in range(count)}
     down_grads = fold(down_grads, "row", near)
     gate_grads = fold(gate_grads, "row", near)
     up_grads = fold(up_grads, "row", near)
-    share_sum, down_grads, gate_grads, up_grads = together(
-        share_sum, down_grads, gate_grads, up_grads
-    )
-    residual_grad_own = grad_own.astype(F32) + share_sum.astype(F32)
+    *share_sums, down_grads, gate_grads, up_grads = together(
+        *share_sums, down_grads, gate_grads, up_grads
+    )
+    residual_grad_own = [
+        grad_own[..., span].astype(F32) + total.astype(F32)
+        for span, total in zip(spans, share_sums)
+    ]
     down_total = fold(down_grads, "row", far)[0]
     gate_total = fold(gate_grads, "row", far)[0]
+
+    mix_cols = [spread_cols(value.astype(BF)) for value in residual_grad_own]
+    ff_part = fan_out(listed(down_blocks), act, cols)
+    *mix_cols, ff_part, down_total, gate_total, up_grads = together(
+        *mix_cols, ff_part, down_total, gate_total, up_grads
+    )
     up_total = fold(up_grads, "row", far)[0]
-
-    mix_cols = spread_cols(residual_grad_own.astype(BF))
-    ff_part = fan_out(listed(down_blocks), act, cols)
-    mix_cols, ff_part = together(mix_cols, ff_part)
+    down_total = over_dp(down_total)
     mix_rows, grad_mine, grad_send = mix_back(own_core, mix_cols, listed(mix_blocks))
     ff_sum = sum_cols(ff_part)
     grad_other = swapped(grad_send, "row", 1)
@@ -814,6 +816,10 @@
         own_core, own_set, other_set, attn_mine, attn_send, grad_mine, grad_other, lse, seg
     )
     back_other = swapped(back_send, "row", 1)
+    back_other, up_total, down_total, gate_total = together(
+        back_other, up_total, down_total, gate_total
+    )
+    gate_total = over_dp(gate_total)
     dq, dkv, share, gain_share_one = qkv_back(
         own_core,
         source,
@@ -827,16 +833,6 @@
         listed(q_blocks),
         listed(kv_blocks),
     )
-    share, ff_sum = together(share, ff_sum)
-    input_sum = sum_cols(share)
-    output_own = (residual_own + ff_sum.astype(F32)).astype(BF)
-    layer_output = all_tokens(output_own)
-
-    share, dq, dkv, gain_share_one, gain_share_two = together(
-        share, dq, dkv, gain_share_one, gain_share_two
-    )
-    q_grads = {k: dot(norm_one[k], dq, NT).astype(BF) for k in range(count)}
-    kv_grads = {k: dot(dkv, norm_one[k], NT).astype(BF) for k in range(count)}
     attn_low = jnp.concatenate(
         [
             jnp.where(parity == 0, attn_mine, attn_other),
@@ -844,20 +840,33 @@
         ]
     )
     mix_grads = {k: dot(attn_low, mix_rows[k], NT).astype(BF) for k in range(count)}
+    mix_grads = fold(mix_grads, "row", near)
+    share, ff_sum, mix_grads, gate_total, up_total = together(
+        share, ff_sum, mix_grads, gate_total, up_total
+    )
+    input_sum = sum_cols(share)
+    up_total = over_dp(up_total)
+    mix_total = over_dp(fold(mix_grads, "row", far)[0])
+    output_own = (residual_own + ff_sum.astype(F32)).astype(BF)
+    layer_output = all_tokens(output_own)
+    q_grads = {k: dot(norm_one[k], dq, NT).astype(BF) for k in range(count)}
+    kv_grads = {k: dot(dkv, norm_one[k], NT).astype(BF) for k in range(count)}
     bits = near + far[::-1]
-    q_total = over_dp(fold(q_grads, "row", bits)[0])
-    kv_total = over_dp(fold(kv_grads, "row", bits)[0])
-    mix_total = over_dp(fold(mix_grads, "row", bits)[0])
-    down_total = over_dp(down_total)
-    gate_total = over_dp(gate_total)
-    up_total = over_dp(up_total)
-
-    shares = jnp.stack([gain_share_one[..., 0], gain_share_two[..., 0]], axis=2)
-    shares = by_xor(shares, lax.axis_index("col"), 0)
-    shares = {c: shares[c] for c in range(cols)}
-    shares = fold(shares, "col", near_bits(cols) + far_bits(cols), low=False)[0]
-    shares = fold({k: shares[k] for k in range(count)}, "row", bits, low=False)[0]
-    gain_totals = over_dp(shares)
+    q_total = fold(q_grads, "row", bits)[0]
+    kv_total = fold(kv_grads, "row", bits)[0]
+
+    gain_shares = jnp.stack([gain_share_one[..., 0], gain_share_two[..., 0]], axis=2)
+    gain_shares = by_xor(gain_shares, lax.axis_index("col"), 0)
+    gain_shares = {c: gain_shares[c] for c in range(cols)}
+    gain_shares = fold(gain_shares, "col", near_bits(cols) + far_bits(cols), low=False)[0]
+    gain_shares = fold({k: gain_shares[k] for k in range(count)}, "row", bits, low=False)[0]
+    gain_totals = over_dp(gain_shares)
+    input_sum, q_total, kv_total, mix_total, up_total, gain_totals, layer_output = together(
+        input_sum, q_total, kv_total, mix_total, up_total, gain_totals, layer_output
+    )
+    q_total = over_dp(q_total)
+    kv_total = over_dp(kv_total)
+    residual_grad_own = jnp.concatenate(residual_grad_own, axis=2)
 
     input_grad = all_tokens((residual_grad_own + input_sum.astype(F32)).astype(BF)).astype(F32)
     kv_rows = kv_total.shape[0] // 2

time: 1060 us -> 947 us (0.89)
  waiting for transfers between devices: 601 us -> 483 us
    all_gather x4 -> x6, waiting for transfers between devices: 213 us -> 107 us  [spread_cols(): return lax.all_gather(value, 'col', axis=0, tiled=False)]
    reduce_scatter x4 -> x5, waiting for transfers between devices: 63.3 us -> 35.4 us  [sum_cols(): return lax.psum_scatter(value, 'col', scatter_dimension=0, tiled=False)]
    ppermute x59, waiting for transfers between devices: 265 us -> 290 us  [swapped(): return lax.ppermute(value, axis, [(i, i ^ mask) for i in range(size)])]
    ppermute x7, waiting for transfers between devices: 59.1 us -> 48.5 us  [over_dp(): lax.ppermute(low, 'dp', [(i, (i + step) % size) for i in range(size)])]
  transfers between devices with their start and end apart: 74 -> 77, of which waited for: 32 -> 38; matrix products, arithmetic and copies ran while one was open for 12% -> 14% of each run, Pallas kernels for 13% -> 23%
where the time goes in v3:
time: 947 us; the launch traced here: 939 us
  waiting for transfers between devices  483 us (51%)
  Pallas kernels  216 us (23%)
  matrix products  81.4 us (9%)
  other arithmetic  45 us (5%)
  starting transfers between devices  37.6 us (4%)
  blocking collectives  34.2 us (4%)
  local copies, waits for them, and re-layouts  26.3 us (3%)
  between operations  15.1 us (2%)
    ppermute x59, waiting for transfers between devices, swapped(): return lax.ppermute(value, axis, [(i, i ^ mask) for i in range(size)])  290 us
    all_gather x6, waiting for transfers between devices, spread_cols(): return lax.all_gather(value, 'col', axis=0, tiled=False)  107 us
    pallas_call x2, Pallas kernels, feed_forward(): pl.pallas_call(functools.partial(ff_kernel, count, bool(before)), out_sha...  84 us
    dot_general x24, matrix products, dot(): return lax.dot_general(left, right, dims, preferred_element_type=F32)  81.4 us
    ppermute x7, waiting for transfers between devices, over_dp(): lax.ppermute(low, 'dp', [(i, (i + step) % size) for i in range(size)])  48.5 us
    pallas_call x1, Pallas kernels, attend_back(): pl.pallas_call(functools.partial(attend_back_kernel, tile), out_shape=(sh...  37.4 us
    reduce_scatter x5, waiting for transfers between devices, sum_cols(): return lax.psum_scatter(value, 'col', scatter_dimension=0, tiled=False)  35.4 us
    all_gather x1, blocking collectives, body(): lax.all_gather(jnp.stack([attn_gain, mlp_gain]), ('row', 'col'), axis=1,...  34.2 us
  transfers between devices with their start and end apart: 77, of which 38 were waited for; matrix products, arithmetic and copies ran while one was open for 14% of the time, Pallas kernels for 23%

profile of v3, /device:TPU:0, one launch (start us, length us, event | category | flops | bytes accessed | tf_op | source)
XLA Modules:
  0.0 938.8 jit_solution(7962905184236878970)
XLA Ops:
  11.8 7.4 collective-permute-done.5
  19.2 7.2 collective-permute-done.4
  36.7 34.2 %all-gather.6 = f32[16,160,2]{1,2,0:T(2,128)S(1)} all-gather(f32[1,160,2]{1,2,0:T(2,128)S(1)} %maximum_bitcast_fusion.1), channel_id=1, replica_groups=mesh['dp'=2,'row'=4,'col'=4] {'row','col'}, dimensions={0}, use_global_device_ids=true | all-gather | bytes 21760 | tf_op jit(solution)/shard_map/all_gather | solution.py:727
  71.2 33.1 %collective-permute-done.2 = bf16[160,1024]{1,0:T(8,128)(2,1)} collective-permute-done((bf16[160,1024]{1,0:T(8,128)(2,1)}, bf16[160,1024]{1,0:T(8,128)(2,1)}, u32[]{:S(2)}, u32[]{:S(2)}) %collective-permute-start.2) | collective-permute-done | bytes 327712 | tf_op jit(solution)/shard_map/ppermute | solution.py:35
  104.8 6.4 collective-permute-done.1
  115.0 8.7 collective-permute-done.10.refs_6_
  126.3 13.6 %collective-permute-done.12.refs_2_.refs_4_ = bf16[640,640]{1,0:T(8,128)(2,1)} collective-permute-done((bf16[640,640]{1,0:T(8,128)(2,1)}, bf16[640,640]{1,0:T(8,128)(2,1)}, u32[]{:S(2)}, u32[]{:S(2)}) %collective-permute-start.12) | collective-permute-done | bytes 819232 | tf_op jit(solution)/shard_map/ppermute | solution.py:35
  143.0 13.1 %qkv_project.1 = (bf16[4,640,1024]{2,1,0:T(8,128)(2,1)}, f32[1,1024]{1,0:T(1,128)}, bf16[2,480,1024]{2,1,0:T(8,128)(2,1)}) custom-call(bf16[4,4,160,1024]{3,2,1,0:T(8,128)(2,1)} %bitcast.244, f32[4,4,160,1]{3,2,1,0:T(8,128)} %copy.66.gain_ref, f32[40,1024]{1,0:T(8,128)} %get-tuple-element.117.cos_ref, f32[40,1024]{1,0:T(8,128)} %get-tuple-element.118.sin_ref, ...), custom_call_target="tpu_custom_call" | custom-call | tf_op jit(solution)/shard_map/qkv_project/pallas_call | solution.py:146
  164.1 27.8 %attend.1 = (bf16[320,1024]{1,0:T(8,128)(2,1)}, bf16[320,1024]{1,0:T(8,128)(2,1)}, f32[2,4,1,1024]{3,2,1,0:T(1,128)}) custom-call(s32[1]{0:T(128)} %bitcast.parity_ref, bf16[480,1024]{1,0:T(8,128)(2,1)} %get-tuple-element.222.own_ref, bf16[480,1024]{1,0:T(8,128)(2,1)} %copy-done.17, s32[1,1024]{1,0:T(1,128)} %bitcast.288, s32[1024,1]{1,0:T(8,128)} %copy.61.seg_col), custom_call_target="tpu_custom_call" | custom-call | tf_op jit(solution)/shard_map/attend/pallas_call | solution.py:237
  195.1 10.3 %mix_out.1 = bf16[4,4,160,1024]{3,2,1,0:T(8,128)(2,1)} custom-call(s32[1]{0:T(128)} %bitcast.parity_ref, bf16[320,1024]{1,0:T(8,128)(2,1)} %get-tuple-element.134.own_ref.own_out, bf16[320,1024]{1,0:T(8,128)(2,1)} %copy-done.32, bf16[640,640]{1,0:T(8,128)(2,1)} %refs_2_, bf16[640,640]{1,0:T(8,128)(2,1)} %collective-permute-done.17.refs_1_.refs_3_, ...), custom_call_target="tpu_custom_call" | custom-call | tf_op jit(solution)/shard_map/mix_out/pallas_call | solution.py:410
  205.4 33.8 %all-gather.16.cloned.1.call-done = bf16[16,160,1024]{2,1,0:T(8,128)(2,1)} async-done(((bf16[4,160,1024]{2,1,0:T(8,128)(2,1)}), bf16[16,160,1024]{2,1,0:T(8,128)(2,1)}) %all-gather.16.cloned.1.call-update) | async-done | bytes 5242896 | tf_op jit(solution)/shard_map/all_gather | solution.py:657
  242.3 48.5 %collective-permute-done.25.refs_10_.refs_2_ = bf16[1728,640]{1,0:T(8,128)(2,1)S(1)} collective-permute-done((bf16[1728,640]{1,0:T(8,128)(2,1)S(1)}, bf16[1728,640]{1,0:T(8,128)(2,1)S(1)}, u32[]{:S(2)}, u32[]{:S(2)}) %collective-permute-start.25) | collective-permute-done | bytes 2211872 | tf_op jit(solution)/shard_map/ppermute | solution.py:35
  308.0 25.7 %reduce-scatter.6.cloned.1.call-done = bf16[1,4,160,1024]{3,2,1,0:T(8,128)(2,1)} async-done(((bf16[4,4,160,1024]{3,2,1,0:T(8,128)(2,1)}), bf16[1,4,160,1024]{3,2,1,0:T(8,128)(2,1)}) %reduce-scatter.6.cloned.1.call-update) | async-done | bytes 1310736 | tf_op jit(solution)/shard_map/reduce_scatter | solution.py:661
  338.9 53.3 %all-gather.18.cloned.1.call-done = bf16[16,160,512]{2,1,0:T(8,128)(2,1)} async-done(((bf16[4,160,512]{2,1,0:T(8,128)(2,1)}), bf16[16,160,512]{2,1,0:T(8,128)(2,1)}) %all-gather.18.cloned.1.call-update) | async-done | bytes 2621456 | tf_op jit(solution)/shard_map/all_gather | solution.py:657
  392.2 42.2 %feed_forward.2 = (bf16[4,640,1024]{2,1,0:T(8,128)(2,1)}, bf16[4,640,1024]{2,1,0:T(8,128)(2,1)}, bf16[1728,1024]{1,0:T(8,128)(2,1)}, bf16[1728,1024]{1,0:T(8,128...) custom-call(bf16[4,4,160,512]{3,2,1,0:T(8,128)(2,1)} %bitcast.275, ...), custom_call_target="tpu_custom_call" | custom-call | tf_op jit(solution)/shard_map/feed_forward/pallas_call | solution.py:546
  434.5 12.8 %all-gather.20.cloned.1.call-done = bf16[16,160,512]{2,1,0:T(8,128)(2,1)} async-done(((bf16[4,160,512]{2,1,0:T(8,128)(2,1)}), bf16[16,160,512]{2,1,0:T(8,128)(2,1)}) %all-gather.20.cloned.1.call-update) | async-done | bytes 2621456 | tf_op jit(solution)/shard_map/all_gather | solution.py:657
  447.2 41.8 %feed_forward.3 = (bf16[4,640,1024]{2,1,0:T(8,128)(2,1)}, bf16[4,640,1024]{2,1,0:T(8,128)(2,1)}, bf16[1728,1024]{1,0:T(8,128)(2,1)}, bf16[1728,1024]{1,0:T(8,128...) custom-call(bf16[4,4,160,512]{3,2,1,0:T(8,128)(2,1)} %bitcast.278, ...), custom_call_target="tpu_custom_call", output_to_operand_aliasing={{0}: (15, {}), {1}: (16, {}), {2}: (17, {}), {3}: (18, {}),... | custom-call | tf_op jit(solution)/shard_map/feed_forward/pallas_call | solution.py:546
  489.1 6.9 convolution_convert_fusion.10
  552.7 9.7 %reduce-scatter.10.cloned.1.call-done = bf16[1,4,160,512]{3,2,1,0:T(8,128)(2,1)} async-done(((bf16[4,4,160,512]{3,2,1,0:T(8,128)(2,1)}), bf16[1,4,160,512]{3,2,1,0:T(8,128)(2,1)}) %reduce-scatter.10.cloned.1.call-update) | async-done | bytes 655376 | tf_op jit(solution)/shard_map/reduce_scatter | solution.py:661
  568.7 16.9 %fan_out.1 = bf16[4,4,160,1024]{3,2,1,0:T(8,128)(2,1)} custom-call(bf16[1728,1024]{1,0:T(8,128)(2,1)} %get-tuple-element.167.x_ref, bf16[1728,640]{1,0:T(8,128)(2,1)} %refs_0_.2, bf16[1728,640]{1,0:T(8,128)(2,1)} %copy-done.2, bf16[1728,640]{1,0:T(8,128)(2,1)} %copy-done.1, bf16[1728,640]{1,0:T(8,128)(2,1)} %copy-done.3), custom_call_target="tpu_custom_call" | custom-call | tf_op jit(solution)/shard_map/fan_out/pallas_call | solution.py:469
  585.7 32.3 %collective-permute-done.33 = bf16[1728,640]{1,0:T(8,128)(2,1)} collective-permute-done((bf16[1728,640]{1,0:T(8,128)(2,1)}, bf16[1728,640]{1,0:T(8,128)(2,1)}, u32[]{:S(2)}, u32[]{:S(2)}) %collective-permute-start.33) | collective-permute-done | bytes 2211872 | tf_op jit(solution)/shard_map/ppermute | solution.py:35
  621.6 42.5 %collective-permute-done.34 = bf16[1728,640]{1,0:T(8,128)(2,1)} collective-permute-done((bf16[1728,640]{1,0:T(8,128)(2,1)}, bf16[1728,640]{1,0:T(8,128)(2,1)}, u32[]{:S(2)}, u32[]{:S(2)}) %collective-permute-start.34) | collective-permute-done | bytes 2211872 | tf_op jit(solution)/shard_map/ppermute | solution.py:35
  667.7 7.7 all-gather.24.cloned.1.call-done
  678.6 8.7 mix_back.1
  690.4 37.4 %attend_back.1 = (bf16[480,1024]{1,0:T(8,128)(2,1)}, bf16[480,1024]{1,0:T(8,128)(2,1)}) custom-call(s32[1]{0:T(128)} %bitcast.parity_ref, bf16[480,1024]{1,0:T(8,128)(2,1)} %get-tuple-element.222.own_ref, bf16[480,1024]{1,0:T(8,128)(2,1)} %copy-done.17, bf16[320,1024]{1,0:T(8,128)(2,1)} %get-tuple-element.134.own_ref.own_out, ...), custom_call_target="tpu_custom_call" | custom-call | tf_op jit(solution)/shard_map/attend_back/pallas_call | solution.py:348
  744.2 18.0 %qkv_back.1 = (bf16[640,1024]{1,0:T(8,128)(2,1)}, bf16[320,1024]{1,0:T(8,128)(2,1)}, bf16[4,4,160,1024]{3,2,1,0:T(8,128)(2,1)}, f32[4,4,160,1]{3,2,1,0:T(8,128)}) custom-call(s32[1]{0:T(128)} %bitcast.parity_ref, bf16[4,4,160,1024]{3,2,1,0:T(8,128)(2,1)} %bitcast.245, f32[4,4,160,1]{3,2,1,0:T(8,128)} %copy.66.gain_ref, ...), custom_call_target="tpu_custom_call" | custom-call | tf_op jit(solution)/shard_map/qkv_back/pallas_call | solution.py:635
  762.1 23.9 %collective-permute-done.41 = bf16[1728,640]{1,0:T(8,128)(2,1)} collective-permute-done((bf16[1728,640]{1,0:T(8,128)(2,1)S(1)}, bf16[1728,640]{1,0:T(8,128)(2,1)}, u32[]{:S(2)}, u32[]{:S(2)}) %collective-permute-start.41) | collective-permute-done | bytes 2211872 | tf_op jit(solution)/shard_map/ppermute | solution.py:669
  825.2 7.0 collective-permute-done.47
  834.8 30.4 %collective-permute-done.48 = bf16[640,640]{1,0:T(8,128)(2,1)S(1)} collective-permute-done((bf16[640,640]{1,0:T(8,128)(2,1)S(1)}, bf16[640,640]{1,0:T(8,128)(2,1)S(1)}, u32[]{:S(2)}, u32[]{:S(2)}) %collective-permute-start.48) | collective-permute-done | bytes 819232 | tf_op jit(solution)/shard_map/ppermute | solution.py:35
  871.2 7.1 collective-permute-done.59
  882.3 9.3 collective-permute-done.49
  916.6 13.1 %collective-permute-done.65 = bf16[320,640]{1,0:T(8,128)(2,1)S(1)} collective-permute-done((bf16[320,640]{1,0:T(8,128)(2,1)S(1)}, bf16[320,640]{1,0:T(8,128)(2,1)S(1)}, u32[]{:S(2)}, u32[]{:S(2)}) %collective-permute-start.65) | collective-permute-done | bytes 409632 | tf_op jit(solution)/shard_map/ppermute | solution.py:669
  (365 shorter events, 233.0 us)
Async XLA Ops:
  7.2 132.7 %all-gather.14.cloned.1.call-start = ((), (), s32[]{:S(2)}) async-start(), calls=%async_computation.10 | async-start | bytes 6553600 | tf_op jit(solution)/shard_map/all_gather | solution.py:657
  28.5 210.7 %all-gather.16.cloned.1.call-start = ((), (), s32[]{:S(2)}) async-start(), calls=%async_computation.11 | async-start | bytes 6553600 | tf_op jit(solution)/shard_map/all_gather | solution.py:657
  28.6 111.2 %collective-permute-start.13 = (bf16[1728,640]{1,0:T(8,128)(2,1)S(1)}, bf16[1728,640]{1,0:T(8,128)(2,1)}, u32[]{:S(2)}, u32[]{:S(2)}) collective-permute-start(bf16[1728,640]{1,0:T(8,128)(2,1)S(1)} %bitcast.251), channel_id=1, source_target_pairs={{0,8},{4,12},{8,0},{12,4},{1,9},{5,13},{9,1},{13,5},{2,10},{6,14},... | collective-permute-start | bytes 6635528 | tf_op jit(solution)/shard_map/ppermute | solution.py:35
  31.0 82.5 %collective-permute-start.7 = (bf16[640,640]{1,0:T(8,128)(2,1)}, bf16[640,640]{1,0:T(8,128)(2,1)}, u32[]{:S(2)}, u32[]{:S(2)}) collective-permute-start(bf16[640,640]{1,0:T(8,128)(2,1)} %refs_0_.3), channel_id=1, source_target_pairs={{0,8},{4,12},{8,0},{12,4},{1,9},{5,13},{9,1},{13,5},{2,10},{6,14},... | collective-permute-start | bytes 2457608 | tf_op jit(solution)/shard_map/ppermute | solution.py:35
  33.4 70.9 %collective-permute-start.2 = (bf16[160,1024]{1,0:T(8,128)(2,1)}, bf16[160,1024]{1,0:T(8,128)(2,1)}, u32[]{:S(2)}, u32[]{:S(2)}) collective-permute-start(bf16[160,1024]{1,0:T(8,128)(2,1)} %get-tuple-element.241), channel_id=1, source_target_pairs={{0,12},{4,8},{8,4},{12,0},{1,13},{5,9},{9,5},{13,1},{2,14},{6,10},... | collective-permute-start | bytes 983048 | tf_op jit(solution)/shard_map/ppermute | solution.py:35
  34.5 76.7 %collective-permute-start.1 = (bf16[160,1024]{1,0:T(8,128)(2,1)}, bf16[160,1024]{1,0:T(8,128)(2,1)}, u32[]{:S(2)}, u32[]{:S(2)}) collective-permute-start(bf16[160,1024]{1,0:T(8,128)(2,1)} %get-tuple-element.242), channel_id=1, source_target_pairs={{0,8},{4,12},{8,0},{12,4},{1,9},{5,13},{9,1},{13,5},{2,10},{6,14},... | collective-permute-start | bytes 983048 | tf_op jit(solution)/shard_map/ppermute | solution.py:35
  36.5 76.5 %collective-permute-start.9 = (bf16[320,640]{1,0:T(8,128)(2,1)S(1)}, bf16[320,640]{1,0:T(8,128)(2,1)S(1)}, u32[]{:S(2)}, u32[]{:S(2)}) collective-permute-start(bf16[320,640]{1,0:T(8,128)(2,1)S(1)} %pad_maximum_fusion.3.refs_4_), channel_id=1, source_target_pairs={{0,4},{4,0},{8,12},{12,8},{1,5},{5,1},{9,13},{13,9},{2,6},{6,2},{1... | collective-permute-start | bytes 1228808 | tf_op jit(solution)/shard_map/ppermute | solution.py:35
  139.9 193.8 %reduce-scatter.6.cloned.1.call-start = ((), (), s32[]{:S(2)}) async-start(), calls=%async_computation.5 | async-start | bytes 6553600 | tf_op jit(solution)/shard_map/reduce_scatter | solution.py:661
  139.9 52.3 %collective-permute-start.19 = (bf16[1728,640]{1,0:T(8,128)(2,1)}, bf16[1728,640]{1,0:T(8,128)(2,1)S(1)}, u32[]{:S(2)}, u32[]{:S(2)}) collective-permute-start(bf16[1728,640]{1,0:T(8,128)(2,1)} %bitcast.252), channel_id=1, source_target_pairs={{0,8},{4,12},{8,0},{12,4},{1,9},{5,13},{9,1},{13,5},{2,10},{6,14},... | collective-permute-start | bytes 6635528 | tf_op jit(solution)/shard_map/ppermute | solution.py:35
  159.1 33.1 %collective-permute-start.17 = (bf16[640,640]{1,0:T(8,128)(2,1)}, bf16[640,640]{1,0:T(8,128)(2,1)}, u32[]{:S(2)}, u32[]{:S(2)}) collective-permute-start(bf16[640,640]{1,0:T(8,128)(2,1)} %refs_2_), channel_id=1, source_target_pairs={{0,4},{4,0},{8,12},{12,8},{1,5},{5,1},{9,13},{13,9},{2,6},{6,2},{1... | collective-permute-start | bytes 2457608 | tf_op jit(solution)/shard_map/ppermute | solution.py:35
  159.6 32.6 %collective-permute-start.18 = (bf16[640,640]{1,0:T(8,128)(2,1)}, bf16[640,640]{1,0:T(8,128)(2,1)}, u32[]{:S(2)}, u32[]{:S(2)}) collective-permute-start(bf16[640,640]{1,0:T(8,128)(2,1)} %collective-permute-done.12.refs_2_.refs_4_), channel_id=1, source_target_pairs={{0,4},{4,0},{8,12},{12,8},{1,5},{5,1},{9,13},{13,9},{2,6},{6,2},{1... | collective-permute-start | bytes 2457608 | tf_op jit(solution)/shard_map/ppermute | solution.py:35
  239.2 153.0 %all-gather.18.cloned.1.call-start = ((), (), s32[]{:S(2)}) async-start(), calls=%async_computation.12 | async-start | bytes 3276800 | tf_op jit(solution)/shard_map/all_gather | solution.py:657
  240.8 50.0 %collective-permute-start.25 = (bf16[1728,640]{1,0:T(8,128)(2,1)S(1)}, bf16[1728,640]{1,0:T(8,128)(2,1)S(1)}, u32[]{:S(2)}, u32[]{:S(2)}) collective-permute-start(bf16[1728,640]{1,0:T(8,128)(2,1)S(1)} %copy-done), channel_id=1, source_target_pairs={{0,8},{4,12},{8,0},{12,4},{1,9},{5,13},{9,1},{13,5},{2,10},{6,14},... | collective-permute-start | bytes 6635528 | tf_op jit(solution)/shard_map/ppermute | solution.py:35
  242.3 49.5 %collective-permute-start.24 = (bf16[1728,640]{1,0:T(8,128)(2,1)S(1)}, bf16[1728,640]{1,0:T(8,128)(2,1)S(1)}, u32[]{:S(2)}, u32[]{:S(2)}) collective-permute-start(bf16[1728,640]{1,0:T(8,128)(2,1)S(1)} %copy-done), channel_id=1, source_target_pairs={{0,4},{4,0},{8,12},{12,8},{1,5},{5,1},{9,13},{13,9},{2,6},{6,2},{1... | collective-permute-start | bytes 6635528 | tf_op jit(solution)/shard_map/ppermute | solution.py:35
  336.7 110.5 %all-gather.20.cloned.1.call-start = ((), (), s32[]{:S(2)}) async-start(), calls=%async_computation.13 | async-start | bytes 3276800 | tf_op jit(solution)/shard_map/all_gather | solution.py:657
  337.3 215.3 %reduce-scatter.8.cloned.1.call-start = ((), (), s32[]{:S(2)}) async-start(), calls=%async_computation.6 | async-start | bytes 3276800 | tf_op jit(solution)/shard_map/reduce_scatter | solution.py:661
  434.4 127.9 %reduce-scatter.10.cloned.1.call-start = ((), (), s32[]{:S(2)}) async-start(), calls=%async_computation.7 | async-start | bytes 3276800 | tf_op jit(solution)/shard_map/reduce_scatter | solution.py:661
  511.6 156.1 %all-gather.22.cloned.1.call-start = ((), (), s32[]{:S(2)}) async-start(), calls=%async_computation.14 | async-start | bytes 3276800 | tf_op jit(solution)/shard_map/all_gather | solution.py:657
  565.5 109.9 %all-gather.24.cloned.1.call-start = ((), (), s32[]{:S(2)}) async-start(), calls=%async_computation.15 | async-start | bytes 3276800 | tf_op jit(solution)/shard_map/all_gather | solution.py:657
  566.2 224.0 %reduce-scatter.12.cloned.1.call-start = ((), (), s32[]{:S(2)}) async-start(), calls=%async_computation.8 | async-start | bytes 6553600 | tf_op jit(solution)/shard_map/reduce_scatter | solution.py:661
  566.7 51.4 %collective-permute-start.33 = (bf16[1728,640]{1,0:T(8,128)(2,1)}, bf16[1728,640]{1,0:T(8,128)(2,1)}, u32[]{:S(2)}, u32[]{:S(2)}) collective-permute-start(bf16[1728,640]{1,0:T(8,128)(2,1)} %add_convert_fusion.7), channel_id=1, source_target_pairs={{0,8},{4,12},{8,0},{12,4},{1,9},{5,13},{9,1},{13,5},{2,10},{6,14},... | collective-permute-start | bytes 6635528 | tf_op jit(solution)/shard_map/ppermute | solution.py:35
  568.2 95.9 %collective-permute-start.34 = (bf16[1728,640]{1,0:T(8,128)(2,1)}, bf16[1728,640]{1,0:T(8,128)(2,1)}, u32[]{:S(2)}, u32[]{:S(2)}) collective-permute-start(bf16[1728,640]{1,0:T(8,128)(2,1)} %add_convert_fusion.5), channel_id=1, source_target_pairs={{0,8},{4,12},{8,0},{12,4},{1,9},{5,13},{9,1},{13,5},{2,10},{6,14},... | collective-permute-start | bytes 6635528 | tf_op jit(solution)/shard_map/ppermute | solution.py:35
  675.3 220.1 %reduce-scatter.14.cloned.1.call-start = ((), (), s32[]{:S(2)}) async-start(), calls=%async_computation.9 | async-start | bytes 6553600 | tf_op jit(solution)/shard_map/reduce_scatter | solution.py:661
  675.6 52.6 %collective-permute-start.37 = (bf16[1728,640]{1,0:T(8,128)(2,1)}, bf16[1728,640]{1,0:T(8,128)(2,1)}, u32[]{:S(2)}, u32[]{:S(2)}) collective-permute-start(bf16[1728,640]{1,0:T(8,128)(2,1)} %add_convert_fusion.3), channel_id=1, source_target_pairs={{0,8},{4,12},{8,0},{12,4},{1,9},{5,13},{9,1},{13,5},{2,10},{6,14},... | collective-permute-start | bytes 6635528 | tf_op jit(solution)/shard_map/ppermute | solution.py:35
  677.1 53.5 %collective-permute-start.38 = (bf16[1728,640]{1,0:T(8,128)(2,1)}, bf16[1728,640]{1,0:T(8,128)(2,1)}, u32[]{:S(2)}, u32[]{:S(2)}) collective-permute-start(bf16[1728,640]{1,0:T(8,128)(2,1)} %add_convert_fusion.2), channel_id=1, source_target_pairs={{0,16},{16,0},{1,17},{17,1},{2,18},{18,2},{3,19},{19,3},{4,20},{20... | collective-permute-start | bytes 6635528 | tf_op jit(solution)/shard_map/ppermute | solution.py:669
  735.6 50.4 %collective-permute-start.41 = (bf16[1728,640]{1,0:T(8,128)(2,1)S(1)}, bf16[1728,640]{1,0:T(8,128)(2,1)}, u32[]{:S(2)}, u32[]{:S(2)}) collective-permute-start(bf16[1728,640]{1,0:T(8,128)(2,1)S(1)} %copy-done.6), channel_id=1, source_target_pairs={{0,16},{16,0},{1,17},{17,1},{2,18},{18,2},{3,19},{19,3},{4,20},{20... | collective-permute-start | bytes 6635528 | tf_op jit(solution)/shard_map/ppermute | solution.py:669
  821.7 44.7 %collective-permute-start.44 = (bf16[640,640]{1,0:T(8,128)(2,1)S(1)}, bf16[640,640]{1,0:T(8,128)(2,1)S(1)}, u32[]{:S(2)}, u32[]{:S(2)}) collective-permute-start(bf16[640,640]{1,0:T(8,128)(2,1)S(1)} %add_convert_fusion.12), channel_id=1, source_target_pairs={{0,8},{4,12},{8,0},{12,4},{1,9},{5,13},{9,1},{13,5},{2,10},{6,14},... | collective-permute-start | bytes 2457608 | tf_op jit(solution)/shard_map/ppermute | solution.py:35
  824.4 40.7 %collective-permute-start.48 = (bf16[640,640]{1,0:T(8,128)(2,1)S(1)}, bf16[640,640]{1,0:T(8,128)(2,1)S(1)}, u32[]{:S(2)}, u32[]{:S(2)}) collective-permute-start(bf16[640,640]{1,0:T(8,128)(2,1)S(1)} %copy-done.52), channel_id=1, source_target_pairs={{0,8},{4,12},{8,0},{12,4},{1,9},{5,13},{9,1},{13,5},{2,10},{6,14},... | collective-permute-start | bytes 2457608 | tf_op jit(solution)/shard_map/ppermute | solution.py:35
  825.2 67.7 %collective-permute-start.50 = (bf16[1728,640]{1,0:T(8,128)(2,1)S(1)}, bf16[1728,640]{1,0:T(8,128)(2,1)S(1)}, u32[]{:S(2)}, u32[]{:S(2)}) collective-permute-start(bf16[1728,640]{1,0:T(8,128)(2,1)S(1)} %add_convert_fusion), channel_id=1, source_target_pairs={{0,16},{16,0},{1,17},{17,1},{2,18},{18,2},{3,19},{19,3},{4,20},{20... | collective-permute-start | bytes 6635528 | tf_op jit(solution)/shard_map/ppermute | solution.py:669
  834.7 35.8 %collective-permute-start.58 = (bf16[160,1024]{1,0:T(8,128)(2,1)S(1)}, bf16[160,1024]{1,0:T(8,128)(2,1)S(1)}, u32[]{:S(2)}, u32[]{:S(2)}) collective-permute-start(bf16[160,1024]{1,0:T(8,128)(2,1)S(1)} %get-tuple-element.230), channel_id=1, source_target_pairs={{0,4},{4,0},{8,12},{12,8},{1,5},{5,1},{9,13},{13,9},{2,6},{6,2},{1... | collective-permute-start | bytes 983048 | tf_op jit(solution)/shard_map/ppermute | solution.py:35
  900.5 30.3 %collective-permute-start.64 = (bf16[640,640]{1,0:T(8,128)(2,1)S(1)}, bf16[640,640]{1,0:T(8,128)(2,1)S(1)}, u32[]{:S(2)}, u32[]{:S(2)}) collective-permute-start(bf16[640,640]{1,0:T(8,128)(2,1)S(1)} %copy-done.22), channel_id=1, source_target_pairs={{0,16},{16,0},{1,17},{17,1},{2,18},{18,2},{3,19},{19,3},{4,20},{20... | collective-permute-start | bytes 2457608 | tf_op jit(solution)/shard_map/ppermute | solution.py:669
  900.7 28.9 %collective-permute-start.65 = (bf16[320,640]{1,0:T(8,128)(2,1)S(1)}, bf16[320,640]{1,0:T(8,128)(2,1)S(1)}, u32[]{:S(2)}, u32[]{:S(2)}) collective-permute-start(bf16[320,640]{1,0:T(8,128)(2,1)S(1)} %copy-done.42), channel_id=1, source_target_pairs={{0,16},{16,0},{1,17},{17,1},{2,18},{18,2},{3,19},{19,3},{4,20},{20... | collective-permute-start | bytes 1228808 | tf_op jit(solution)/shard_map/ppermute | solution.py:669
  (109 other events, 1902.6 us)
Sparse Core Ops, SparseCore 0:
  28.7 100.5 all-gather.13
  140.0 99.1 all-gather.15
  241.5 92.1 reduce-scatter.5
  336.9 55.3 all-gather.17
  393.6 53.5 all-gather.19
  450.0 50.8 reduce-scatter.7
  511.7 50.6 reduce-scatter.9
  565.6 54.4 all-gather.21
  621.7 53.5 all-gather.23
  677.5 92.5 reduce-scatter.11
  790.3 91.1 reduce-scatter.13

commit v4 on v3

--- a/solution.py
+++ b/solution.py
@@ -795,31 +795,27 @@
     *share_sums, down_grads, gate_grads, up_grads = together(
         *share_sums, down_grads, gate_grads, up_grads
     )
-    residual_grad_own = [
-        grad_own[..., span].astype(F32) + total.astype(F32)
-        for span, total in zip(spans, share_sums)
-    ]
+    residual_grad_own = grad_own.astype(F32) + jnp.concatenate(share_sums, axis=2).astype(F32)
     down_total = fold(down_grads, "row", far)[0]
     gate_total = fold(gate_grads, "row", far)[0]
-
-    mix_cols = [spread_cols(value.astype(BF)) for value in residual_grad_own]
+    down_total_all = over_dp(down_total)
+
+    mix_cols = spread_cols(residual_grad_own.astype(BF))
     ff_part = fan_out(listed(down_blocks), act, cols)
-    *mix_cols, ff_part, down_total, gate_total, up_grads = together(
-        *mix_cols, ff_part, down_total, gate_total, up_grads
+    mix_cols, ff_part, down_total, gate_total, up_grads = together(
+        mix_cols, ff_part, down_total_all, gate_total, up_grads
     )
     up_total = fold(up_grads, "row", far)[0]
-    down_total = over_dp(down_total)
-    mix_rows, grad_mine, grad_send = mix_back(own_core, mix_cols, listed(mix_blocks))
+    gate_total = over_dp(gate_total)
+    mix_rows, grad_mine, grad_send = mix_back(own_core, [mix_cols], listed(mix_blocks))
     ff_sum = sum_cols(ff_part)
     grad_other = swapped(grad_send, "row", 1)
     back_mine, back_send = attend_back(
         own_core, own_set, other_set, attn_mine, attn_send, grad_mine, grad_other, lse, seg
     )
     back_other = swapped(back_send, "row", 1)
-    back_other, up_total, down_total, gate_total = together(
-        back_other, up_total, down_total, gate_total
-    )
-    gate_total = over_dp(gate_total)
+    back_other, up_total, gate_total = together(back_other, up_total, gate_total)
+    up_total = over_dp(up_total)
     dq, dkv, share, gain_share_one = qkv_back(
         own_core,
         source,
@@ -833,6 +829,15 @@
         listed(q_blocks),
         listed(kv_blocks),
     )
+    share, ff_sum = together(share, ff_sum)
+    input_sum = sum_cols(share)
+    output_own = (residual_own + ff_sum.astype(F32)).astype(BF)
+    layer_output = all_tokens(output_own)
+
+    share, dq, dkv, mix_rows = together(share, dq, dkv, mix_rows)
+    bits = near + far[::-1]
+    q_grads = {k: dot(norm_one[k], dq, NT).astype(BF) for k in range(count)}
+    kv_grads = {k: dot(dkv, norm_one[k], NT).astype(BF) for k in range(count)}
     attn_low = jnp.concatenate(
         [
             jnp.where(parity == 0, attn_mine, attn_other),
@@ -840,20 +845,9 @@
         ]
     )
     mix_grads = {k: dot(attn_low, mix_rows[k], NT).astype(BF) for k in range(count)}
-    mix_grads = fold(mix_grads, "row", near)
-    share, ff_sum, mix_grads, gate_total, up_total = together(
-        share, ff_sum, mix_grads, gate_total, up_total
-    )
-    input_sum = sum_cols(share)
-    up_total = over_dp(up_total)
-    mix_total = over_dp(fold(mix_grads, "row", far)[0])
-    output_own = (residual_own + ff_sum.astype(F32)).astype(BF)
-    layer_output = all_tokens(output_own)
-    q_grads = {k: dot(norm_one[k], dq, NT).astype(BF) for k in range(count)}
-    kv_grads = {k: dot(dkv, norm_one[k], NT).astype(BF) for k in range(count)}
-    bits = near + far[::-1]
-    q_total = fold(q_grads, "row", bits)[0]
-    kv_total = fold(kv_grads, "row", bits)[0]
+    q_total = over_dp(fold(q_grads, "row", bits)[0])
+    kv_total = over_dp(fold(kv_grads, "row", bits)[0])
+    mix_total = over_dp(fold(mix_grads, "row", bits)[0])
 
     gain_shares = jnp.stack([gain_share_one[..., 0], gain_share_two[..., 0]], axis=2)
     gain_shares = by_xor(gain_shares, lax.axis_index("col"), 0)
@@ -864,9 +858,6 @@
     input_sum, q_total, kv_total, mix_total, up_total, gain_totals, layer_output = together(
         input_sum, q_total, kv_total, mix_total, up_total, gain_totals, layer_output
     )
-    q_total = over_dp(q_total)
-    kv_total = over_dp(kv_total)
-    residual_grad_own = jnp.concatenate(residual_grad_own, axis=2)
 
     input_grad = all_tokens((residual_grad_own + input_sum.astype(F32)).astype(BF)).astype(F32)
     kv_rows = kv_total.shape[0] // 2

time: 947 us -> 964 us (1.018)
  waiting for transfers between devices: 483 us -> 498 us
    reduce_scatter x5, waiting for transfers between devices: 35.4 us -> 51.2 us  [sum_cols(): return lax.psum_scatter(value, 'col', scatter_dimension=0, tiled=False)]
    all_gather x6 -> x5, waiting for transfers between devices: 107 us -> 100 us  [spread_cols(): return lax.all_gather(value, 'col', axis=0, tiled=False)]
  transfers between devices with their start and end apart: 77 -> 76, of which waited for: 38 -> 37; matrix products, arithmetic and copies ran while one was open for 14% -> 13% of each run, Pallas kernels for 23% -> 23%
where the time goes in v4:
time: 964 us; the launch traced here: 956 us
  waiting for transfers between devices  498 us (52%)
  Pallas kernels  216 us (22%)
  matrix products  75.8 us (8%)
  starting transfers between devices  47.1 us (5%)
  other arithmetic  46.1 us (5%)
  blocking collectives  34.2 us (4%)
  local copies, waits for them, and re-layouts  22.6 us (2%)
  between operations  15.7 us (2%)
    ppermute x59, waiting for transfers between devices, swapped(): return lax.ppermute(value, axis, [(i, i ^ mask) for i in range(size)])  291 us
    all_gather x5, waiting for transfers between devices, spread_cols(): return lax.all_gather(value, 'col', axis=0, tiled=False)  100 us
    pallas_call x2, Pallas kernels, feed_forward(): pl.pallas_call(functools.partial(ff_kernel, count, bool(before)), out_sha...  83.9 us
    dot_general x24, matrix products, dot(): return lax.dot_general(left, right, dims, preferred_element_type=F32)  75.8 us
    ppermute x7, waiting for transfers between devices, over_dp(): lax.ppermute(low, 'dp', [(i, (i + step) % size) for i in range(size)])  55.3 us
    reduce_scatter x5, waiting for transfers between devices, sum_cols(): return lax.psum_scatter(value, 'col', scatter_dimension=0, tiled=False)  51.2 us
    pallas_call x1, Pallas kernels, attend_back(): pl.pallas_call(functools.partial(attend_back_kernel, tile), out_shape=(sh...  37.6 us
    ppermute x59, starting transfers between devices, swapped(): return lax.ppermute(value, axis, [(i, i ^ mask) for i in range(size)])  36.9 us
  transfers between devices with their start and end apart: 76, of which 37 were waited for; matrix products, arithmetic and copies ran while one was open for 13% of the time, Pallas kernels for 23%

profile of v4, /device:TPU:0, one launch (start us, length us, event | category | flops | bytes accessed | tf_op | source)
XLA Modules:
  0.0 955.7 jit_solution(6755184377737900862)
XLA Ops:
  11.9 7.4 collective-permute-done.5
  19.3 7.2 collective-permute-done.4
  36.8 34.2 %all-gather.5 = f32[16,160,2]{1,2,0:T(2,128)S(1)} all-gather(f32[1,160,2]{1,2,0:T(2,128)S(1)} %maximum_bitcast_fusion.1), channel_id=1, replica_groups=mesh['dp'=2,'row'=4,'col'=4] {'row','col'}, dimensions={0}, use_global_device_ids=true | all-gather | bytes 21760 | tf_op jit(solution)/shard_map/all_gather | solution.py:727
  71.3 33.1 %collective-permute-done.2 = bf16[160,1024]{1,0:T(8,128)(2,1)} collective-permute-done((bf16[160,1024]{1,0:T(8,128)(2,1)}, bf16[160,1024]{1,0:T(8,128)(2,1)}, u32[]{:S(2)}, u32[]{:S(2)}) %collective-permute-start.2) | collective-permute-done | bytes 327712 | tf_op jit(solution)/shard_map/ppermute | solution.py:35
  115.1 8.7 collective-permute-done.10.refs_6_
  126.3 13.6 %collective-permute-done.12.refs_2_.refs_3_ = bf16[640,640]{1,0:T(8,128)(2,1)} collective-permute-done((bf16[640,640]{1,0:T(8,128)(2,1)}, bf16[640,640]{1,0:T(8,128)(2,1)}, u32[]{:S(2)}, u32[]{:S(2)}) %collective-permute-start.12) | collective-permute-done | bytes 819232 | tf_op jit(solution)/shard_map/ppermute | solution.py:35
  143.0 13.0 %qkv_project.1 = (bf16[4,640,1024]{2,1,0:T(8,128)(2,1)}, f32[1,1024]{1,0:T(1,128)}, bf16[2,480,1024]{2,1,0:T(8,128)(2,1)}) custom-call(bf16[4,4,160,1024]{3,2,1,0:T(8,128)(2,1)} %bitcast.231, f32[4,4,160,1]{3,2,1,0:T(8,128)} %copy.66.gain_ref, f32[40,1024]{1,0:T(8,128)} %get-tuple-element.114.cos_ref, f32[40,1024]{1,0:T(8,128)} %get-tuple-element.115.sin_ref, ...), custom_call_target="tpu_custom_call" | custom-call | tf_op jit(solution)/shard_map/qkv_project/pallas_call | solution.py:146
  164.2 27.7 %attend.1 = (bf16[320,1024]{1,0:T(8,128)(2,1)}, bf16[320,1024]{1,0:T(8,128)(2,1)}, f32[2,4,1,1024]{3,2,1,0:T(1,128)}) custom-call(s32[1]{0:T(128)} %bitcast.parity_ref, bf16[480,1024]{1,0:T(8,128)(2,1)} %get-tuple-element.212.own_ref, bf16[480,1024]{1,0:T(8,128)(2,1)} %copy-done.15, s32[1,1024]{1,0:T(1,128)} %bitcast.277, s32[1024,1]{1,0:T(8,128)} %copy.61.seg_col), custom_call_target="tpu_custom_call" | custom-call | tf_op jit(solution)/shard_map/attend/pallas_call | solution.py:237
  195.0 10.2 %mix_out.1 = bf16[4,4,160,1024]{3,2,1,0:T(8,128)(2,1)} custom-call(s32[1]{0:T(128)} %bitcast.parity_ref, bf16[320,1024]{1,0:T(8,128)(2,1)} %get-tuple-element.131.own_ref.own_out, bf16[320,1024]{1,0:T(8,128)(2,1)} %copy-done.29, bf16[640,640]{1,0:T(8,128)(2,1)} %refs_1_, bf16[640,640]{1,0:T(8,128)(2,1)} %collective-permute-done.17.refs_1_.refs_2_, ...), custom_call_target="tpu_custom_call" | custom-call | tf_op jit(solution)/shard_map/mix_out/pallas_call | solution.py:410
  205.3 34.0 %all-gather.14.cloned.1.call-done = bf16[16,160,1024]{2,1,0:T(8,128)(2,1)} async-done(((bf16[4,160,1024]{2,1,0:T(8,128)(2,1)}), bf16[16,160,1024]{2,1,0:T(8,128)(2,1)}) %all-gather.14.cloned.1.call-update) | async-done | bytes 5242896 | tf_op jit(solution)/shard_map/all_gather | solution.py:657
  242.4 48.5 %collective-permute-done.25.refs_10_.refs_2_ = bf16[1728,640]{1,0:T(8,128)(2,1)S(1)} collective-permute-done((bf16[1728,640]{1,0:T(8,128)(2,1)S(1)}, bf16[1728,640]{1,0:T(8,128)(2,1)S(1)}, u32[]{:S(2)}, u32[]{:S(2)}) %collective-permute-start.25) | collective-permute-done | bytes 2211872 | tf_op jit(solution)/shard_map/ppermute | solution.py:35
  308.1 25.7 %reduce-scatter.6.cloned.1.call-done = bf16[1,4,160,1024]{3,2,1,0:T(8,128)(2,1)} async-done(((bf16[4,4,160,1024]{3,2,1,0:T(8,128)(2,1)}), bf16[1,4,160,1024]{3,2,1,0:T(8,128)(2,1)}) %reduce-scatter.6.cloned.1.call-update) | async-done | bytes 1310736 | tf_op jit(solution)/shard_map/reduce_scatter | solution.py:661
  339.0 53.3 %all-gather.16.cloned.1.call-done = bf16[16,160,512]{2,1,0:T(8,128)(2,1)} async-done(((bf16[4,160,512]{2,1,0:T(8,128)(2,1)}), bf16[16,160,512]{2,1,0:T(8,128)(2,1)}) %all-gather.16.cloned.1.call-update) | async-done | bytes 2621456 | tf_op jit(solution)/shard_map/all_gather | solution.py:657
  392.3 42.1 %feed_forward.2 = (bf16[4,640,1024]{2,1,0:T(8,128)(2,1)}, bf16[4,640,1024]{2,1,0:T(8,128)(2,1)}, bf16[1728,1024]{1,0:T(8,128)(2,1)}, bf16[1728,1024]{1,0:T(8,128...) custom-call(bf16[4,4,160,512]{3,2,1,0:T(8,128)(2,1)} %bitcast.263, ...), custom_call_target="tpu_custom_call" | custom-call | tf_op jit(solution)/shard_map/feed_forward/pallas_call | solution.py:546
  434.5 12.8 %all-gather.18.cloned.1.call-done = bf16[16,160,512]{2,1,0:T(8,128)(2,1)} async-done(((bf16[4,160,512]{2,1,0:T(8,128)(2,1)}), bf16[16,160,512]{2,1,0:T(8,128)(2,1)}) %all-gather.18.cloned.1.call-update) | async-done | bytes 2621456 | tf_op jit(solution)/shard_map/all_gather | solution.py:657
  447.3 41.8 %feed_forward.3 = (bf16[4,640,1024]{2,1,0:T(8,128)(2,1)}, bf16[4,640,1024]{2,1,0:T(8,128)(2,1)}, bf16[1728,1024]{1,0:T(8,128)(2,1)}, bf16[1728,1024]{1,0:T(8,128...) custom-call(bf16[4,4,160,512]{3,2,1,0:T(8,128)(2,1)} %bitcast.268, ...), custom_call_target="tpu_custom_call", output_to_operand_aliasing={{0}: (15, {}), {1}: (16, {}), {2}: (17, {}), {3}: (18, {}),... | custom-call | tf_op jit(solution)/shard_map/feed_forward/pallas_call | solution.py:546
  489.1 6.9 convolution_convert_fusion.10
  552.7 9.8 %reduce-scatter.10.cloned.1.call-done = bf16[1,4,160,512]{3,2,1,0:T(8,128)(2,1)} async-done(((bf16[4,4,160,512]{3,2,1,0:T(8,128)(2,1)}), bf16[1,4,160,512]{3,2,1,0:T(8,128)(2,1)}) %reduce-scatter.10.cloned.1.call-update) | async-done | bytes 655376 | tf_op jit(solution)/shard_map/reduce_scatter | solution.py:661
  568.0 49.0 %collective-permute-done.33 = bf16[1728,640]{1,0:T(8,128)(2,1)S(1)} collective-permute-done((bf16[1728,640]{1,0:T(8,128)(2,1)S(1)}, bf16[1728,640]{1,0:T(8,128)(2,1)S(1)}, u32[]{:S(2)}, u32[]{:S(2)}) %collective-permute-start.33) | collective-permute-done | bytes 2211872 | tf_op jit(solution)/shard_map/ppermute | solution.py:35
  620.7 16.6 %fan_out.1 = bf16[4,4,160,1024]{3,2,1,0:T(8,128)(2,1)} custom-call(bf16[1728,1024]{1,0:T(8,128)(2,1)} %get-tuple-element.164.x_ref, bf16[1728,640]{1,0:T(8,128)(2,1)} %refs_0_.2, bf16[1728,640]{1,0:T(8,128)(2,1)} %copy-done.3, bf16[1728,640]{1,0:T(8,128)(2,1)} %copy-done.2, bf16[1728,640]{1,0:T(8,128)(2,1)} %copy-done.4), custom_call_target="tpu_custom_call" | custom-call | tf_op jit(solution)/shard_map/fan_out/pallas_call | solution.py:469
  637.3 25.8 %collective-permute-done.35 = bf16[1728,640]{1,0:T(8,128)(2,1)} collective-permute-done((bf16[1728,640]{1,0:T(8,128)(2,1)}, bf16[1728,640]{1,0:T(8,128)(2,1)}, u32[]{:S(2)}, u32[]{:S(2)}) %collective-permute-start.35) | collective-permute-done | bytes 2211872 | tf_op jit(solution)/shard_map/ppermute | solution.py:35
  674.7 9.3 mix_back.1
  687.2 37.6 %attend_back.1 = (bf16[480,1024]{1,0:T(8,128)(2,1)}, bf16[480,1024]{1,0:T(8,128)(2,1)}) custom-call(s32[1]{0:T(128)} %bitcast.parity_ref, bf16[480,1024]{1,0:T(8,128)(2,1)} %get-tuple-element.212.own_ref, bf16[480,1024]{1,0:T(8,128)(2,1)} %copy-done.15, bf16[320,1024]{1,0:T(8,128)(2,1)} %get-tuple-element.131.own_ref.own_out, ...), custom_call_target="tpu_custom_call" | custom-call | tf_op jit(solution)/shard_map/attend_back/pallas_call | solution.py:348
  732.0 17.5 %qkv_back.1 = (bf16[640,1024]{1,0:T(8,128)(2,1)}, bf16[320,1024]{1,0:T(8,128)(2,1)}, bf16[4,4,160,1024]{3,2,1,0:T(8,128)(2,1)}, f32[4,4,160,1]{3,2,1,0:T(8,128)}) custom-call(s32[1]{0:T(128)} %bitcast.parity_ref, bf16[4,4,160,1024]{3,2,1,0:T(8,128)(2,1)} %bitcast.232, f32[4,4,160,1]{3,2,1,0:T(8,128)} %copy.66.gain_ref, ...), custom_call_target="tpu_custom_call" | custom-call | tf_op jit(solution)/shard_map/qkv_back/pallas_call | solution.py:635
  749.6 15.7 %reduce-scatter.12.cloned.1.call-done = bf16[1,4,160,1024]{3,2,1,0:T(8,128)(2,1)} async-done(((bf16[4,4,160,1024]{3,2,1,0:T(8,128)(2,1)}), bf16[1,4,160,1024]{3,2,1,0:T(8,128)(2,1)}) %reduce-scatter.12.cloned.1.call-update) | async-done | bytes 1310736 | tf_op jit(solution)/shard_map/reduce_scatter | solution.py:661
  789.4 26.0 %collective-permute-done.59 = bf16[2,160]{1,0:T(2,128)(2,1)S(1)} collective-permute-done((bf16[2,160]{1,0:T(2,128)(2,1)S(1)}, bf16[2,160]{1,0:T(2,128)(2,1)S(1)}, u32[]{:S(2)}, u32[]{:S(2)}) %collective-permute-start.59) | collective-permute-done | bytes 672 | tf_op jit(solution)/shard_map/ppermute | solution.py:669
  833.6 9.9 %collective-permute-done.46 = bf16[320,640]{1,0:T(8,128)(2,1)S(1)} collective-permute-done((bf16[320,640]{1,0:T(8,128)(2,1)S(1)}, bf16[320,640]{1,0:T(8,128)(2,1)S(1)}, u32[]{:S(2)}, u32[]{:S(2)}) %collective-permute-start.46) | collective-permute-done | bytes 409632 | tf_op jit(solution)/shard_map/ppermute | solution.py:35
  852.4 19.4 %collective-permute-done.42 = bf16[640,640]{1,0:T(8,128)(2,1)S(1)} collective-permute-done((bf16[640,640]{1,0:T(8,128)(2,1)S(1)}, bf16[640,640]{1,0:T(8,128)(2,1)S(1)}, u32[]{:S(2)}, u32[]{:S(2)}) %collective-permute-start.42) | collective-permute-done | bytes 819232 | tf_op jit(solution)/shard_map/ppermute | solution.py:35
  873.7 15.6 %collective-permute-done.50 = bf16[640,640]{1,0:T(8,128)(2,1)S(1)} collective-permute-done((bf16[640,640]{1,0:T(8,128)(2,1)S(1)}, bf16[640,640]{1,0:T(8,128)(2,1)S(1)}, u32[]{:S(2)}, u32[]{:S(2)}) %collective-permute-start.50) | collective-permute-done | bytes 819232 | tf_op jit(solution)/shard_map/ppermute | solution.py:35
  895.7 14.8 %collective-permute-done.43 = bf16[640,640]{1,0:T(8,128)(2,1)S(1)} collective-permute-done((bf16[640,640]{1,0:T(8,128)(2,1)S(1)}, bf16[640,640]{1,0:T(8,128)(2,1)S(1)}, u32[]{:S(2)}, u32[]{:S(2)}) %collective-permute-start.43) | collective-permute-done | bytes 819232 | tf_op jit(solution)/shard_map/ppermute | solution.py:669
  911.8 14.5 %collective-permute-done.51 = bf16[640,640]{1,0:T(8,128)(2,1)S(1)} collective-permute-done((bf16[640,640]{1,0:T(8,128)(2,1)S(1)}, bf16[640,640]{1,0:T(8,128)(2,1)S(1)}, u32[]{:S(2)}, u32[]{:S(2)}) %collective-permute-start.51) | collective-permute-done | bytes 819232 | tf_op jit(solution)/shard_map/ppermute | solution.py:669
  933.4 7.0 collective-permute-done.64
  (351 shorter events, 231.4 us)
Async XLA Ops:
  7.2 132.7 %all-gather.12.cloned.1.call-start = ((), (), s32[]{:S(2)}) async-start(), calls=%async_computation.10 | async-start | bytes 6553600 | tf_op jit(solution)/shard_map/all_gather | solution.py:657
  28.6 210.7 %all-gather.14.cloned.1.call-start = ((), (), s32[]{:S(2)}) async-start(), calls=%async_computation.11 | async-start | bytes 6553600 | tf_op jit(solution)/shard_map/all_gather | solution.py:657
  28.7 111.2 %collective-permute-start.13 = (bf16[1728,640]{1,0:T(8,128)(2,1)S(1)}, bf16[1728,640]{1,0:T(8,128)(2,1)}, u32[]{:S(2)}, u32[]{:S(2)}) collective-permute-start(bf16[1728,640]{1,0:T(8,128)(2,1)S(1)} %bitcast.238), channel_id=1, source_target_pairs={{0,8},{4,12},{8,0},{12,4},{1,9},{5,13},{9,1},{13,5},{2,10},{6,14},... | collective-permute-start | bytes 6635528 | tf_op jit(solution)/shard_map/ppermute | solution.py:35
  31.0 82.5 %collective-permute-start.7 = (bf16[640,640]{1,0:T(8,128)(2,1)}, bf16[640,640]{1,0:T(8,128)(2,1)}, u32[]{:S(2)}, u32[]{:S(2)}) collective-permute-start(bf16[640,640]{1,0:T(8,128)(2,1)} %refs_0_.3), channel_id=1, source_target_pairs={{0,8},{4,12},{8,0},{12,4},{1,9},{5,13},{9,1},{13,5},{2,10},{6,14},... | collective-permute-start | bytes 2457608 | tf_op jit(solution)/shard_map/ppermute | solution.py:35
  33.4 70.9 %collective-permute-start.2 = (bf16[160,1024]{1,0:T(8,128)(2,1)}, bf16[160,1024]{1,0:T(8,128)(2,1)}, u32[]{:S(2)}, u32[]{:S(2)}) collective-permute-start(bf16[160,1024]{1,0:T(8,128)(2,1)} %get-tuple-element.229), channel_id=1, source_target_pairs={{0,12},{4,8},{8,4},{12,0},{1,13},{5,9},{9,5},{13,1},{2,14},{6,10},... | collective-permute-start | bytes 983048 | tf_op jit(solution)/shard_map/ppermute | solution.py:35
  34.5 76.7 %collective-permute-start.1 = (bf16[160,1024]{1,0:T(8,128)(2,1)}, bf16[160,1024]{1,0:T(8,128)(2,1)}, u32[]{:S(2)}, u32[]{:S(2)}) collective-permute-start(bf16[160,1024]{1,0:T(8,128)(2,1)} %get-tuple-element.230), channel_id=1, source_target_pairs={{0,8},{4,12},{8,0},{12,4},{1,9},{5,13},{9,1},{13,5},{2,10},{6,14},... | collective-permute-start | bytes 983048 | tf_op jit(solution)/shard_map/ppermute | solution.py:35
  36.6 76.5 %collective-permute-start.9 = (bf16[320,640]{1,0:T(8,128)(2,1)S(1)}, bf16[320,640]{1,0:T(8,128)(2,1)S(1)}, u32[]{:S(2)}, u32[]{:S(2)}) collective-permute-start(bf16[320,640]{1,0:T(8,128)(2,1)S(1)} %pad_maximum_fusion.4.refs_4_), channel_id=1, source_target_pairs={{0,4},{4,0},{8,12},{12,8},{1,5},{5,1},{9,13},{13,9},{2,6},{6,2},{1... | collective-permute-start | bytes 1228808 | tf_op jit(solution)/shard_map/ppermute | solution.py:35
  139.9 193.8 %reduce-scatter.6.cloned.1.call-start = ((), (), s32[]{:S(2)}) async-start(), calls=%async_computation.5 | async-start | bytes 6553600 | tf_op jit(solution)/shard_map/reduce_scatter | solution.py:661
  140.0 52.1 %collective-permute-start.19 = (bf16[1728,640]{1,0:T(8,128)(2,1)}, bf16[1728,640]{1,0:T(8,128)(2,1)S(1)}, u32[]{:S(2)}, u32[]{:S(2)}) collective-permute-start(bf16[1728,640]{1,0:T(8,128)(2,1)} %bitcast.239), channel_id=1, source_target_pairs={{0,8},{4,12},{8,0},{12,4},{1,9},{5,13},{9,1},{13,5},{2,10},{6,14},... | collective-permute-start | bytes 6635528 | tf_op jit(solution)/shard_map/ppermute | solution.py:35
  159.0 33.0 %collective-permute-start.17 = (bf16[640,640]{1,0:T(8,128)(2,1)}, bf16[640,640]{1,0:T(8,128)(2,1)}, u32[]{:S(2)}, u32[]{:S(2)}) collective-permute-start(bf16[640,640]{1,0:T(8,128)(2,1)} %refs_1_), channel_id=1, source_target_pairs={{0,4},{4,0},{8,12},{12,8},{1,5},{5,1},{9,13},{13,9},{2,6},{6,2},{1... | collective-permute-start | bytes 2457608 | tf_op jit(solution)/shard_map/ppermute | solution.py:35
  159.5 32.5 %collective-permute-start.18 = (bf16[640,640]{1,0:T(8,128)(2,1)}, bf16[640,640]{1,0:T(8,128)(2,1)}, u32[]{:S(2)}, u32[]{:S(2)}) collective-permute-start(bf16[640,640]{1,0:T(8,128)(2,1)} %collective-permute-done.12.refs_2_.refs_3_), channel_id=1, source_target_pairs={{0,4},{4,0},{8,12},{12,8},{1,5},{5,1},{9,13},{13,9},{2,6},{6,2},{1... | collective-permute-start | bytes 2457608 | tf_op jit(solution)/shard_map/ppermute | solution.py:35
  239.3 153.0 %all-gather.16.cloned.1.call-start = ((), (), s32[]{:S(2)}) async-start(), calls=%async_computation.12 | async-start | bytes 3276800 | tf_op jit(solution)/shard_map/all_gather | solution.py:657
  240.9 50.0 %collective-permute-start.25 = (bf16[1728,640]{1,0:T(8,128)(2,1)S(1)}, bf16[1728,640]{1,0:T(8,128)(2,1)S(1)}, u32[]{:S(2)}, u32[]{:S(2)}) collective-permute-start(bf16[1728,640]{1,0:T(8,128)(2,1)S(1)} %copy-done.1), channel_id=1, source_target_pairs={{0,8},{4,12},{8,0},{12,4},{1,9},{5,13},{9,1},{13,5},{2,10},{6,14},... | collective-permute-start | bytes 6635528 | tf_op jit(solution)/shard_map/ppermute | solution.py:35
  242.4 49.5 %collective-permute-start.24 = (bf16[1728,640]{1,0:T(8,128)(2,1)S(1)}, bf16[1728,640]{1,0:T(8,128)(2,1)S(1)}, u32[]{:S(2)}, u32[]{:S(2)}) collective-permute-start(bf16[1728,640]{1,0:T(8,128)(2,1)S(1)} %copy-done.1), channel_id=1, source_target_pairs={{0,4},{4,0},{8,12},{12,8},{1,5},{5,1},{9,13},{13,9},{2,6},{6,2},{1... | collective-permute-start | bytes 6635528 | tf_op jit(solution)/shard_map/ppermute | solution.py:35
  336.8 110.5 %all-gather.18.cloned.1.call-start = ((), (), s32[]{:S(2)}) async-start(), calls=%async_computation.13 | async-start | bytes 3276800 | tf_op jit(solution)/shard_map/all_gather | solution.py:657
  337.4 215.3 %reduce-scatter.8.cloned.1.call-start = ((), (), s32[]{:S(2)}) async-start(), calls=%async_computation.6 | async-start | bytes 3276800 | tf_op jit(solution)/shard_map/reduce_scatter | solution.py:661
  434.4 128.0 %reduce-scatter.10.cloned.1.call-start = ((), (), s32[]{:S(2)}) async-start(), calls=%async_computation.7 | async-start | bytes 3276800 | tf_op jit(solution)/shard_map/reduce_scatter | solution.py:661
  511.5 159.9 %all-gather.20.cloned.1.call-start = ((), (), s32[]{:S(2)}) async-start(), calls=%async_computation.14 | async-start | bytes 6553600 | tf_op jit(solution)/shard_map/all_gather | solution.py:657
  565.4 199.9 %reduce-scatter.12.cloned.1.call-start = ((), (), s32[]{:S(2)}) async-start(), calls=%async_computation.8 | async-start | bytes 6553600 | tf_op jit(solution)/shard_map/reduce_scatter | solution.py:661
  565.9 51.1 %collective-permute-start.33 = (bf16[1728,640]{1,0:T(8,128)(2,1)S(1)}, bf16[1728,640]{1,0:T(8,128)(2,1)S(1)}, u32[]{:S(2)}, u32[]{:S(2)}) collective-permute-start(bf16[1728,640]{1,0:T(8,128)(2,1)S(1)} %copy-done.45), channel_id=1, source_target_pairs={{0,8},{4,12},{8,0},{12,4},{1,9},{5,13},{9,1},{13,5},{2,10},{6,14},... | collective-permute-start | bytes 6635528 | tf_op jit(solution)/shard_map/ppermute | solution.py:35
  567.4 95.7 %collective-permute-start.35 = (bf16[1728,640]{1,0:T(8,128)(2,1)}, bf16[1728,640]{1,0:T(8,128)(2,1)}, u32[]{:S(2)}, u32[]{:S(2)}) collective-permute-start(bf16[1728,640]{1,0:T(8,128)(2,1)} %add_convert_fusion.5), channel_id=1, source_target_pairs={{0,8},{4,12},{8,0},{12,4},{1,9},{5,13},{9,1},{13,5},{2,10},{6,14},... | collective-permute-start | bytes 6635528 | tf_op jit(solution)/shard_map/ppermute | solution.py:35
  619.2 48.1 %collective-permute-start.34 = (bf16[1728,640]{1,0:T(8,128)(2,1)S(1)}, bf16[1728,640]{1,0:T(8,128)(2,1)}, u32[]{:S(2)}, u32[]{:S(2)}) collective-permute-start(bf16[1728,640]{1,0:T(8,128)(2,1)S(1)} %add_convert_fusion.2), channel_id=1, source_target_pairs={{0,16},{16,0},{1,17},{17,1},{2,18},{18,2},{3,19},{19,3},{4,20},{20... | collective-permute-start | bytes 6635528 | tf_op jit(solution)/shard_map/ppermute | solution.py:669
  671.5 256.2 %reduce-scatter.14.cloned.1.call-start = ((), (), s32[]{:S(2)}) async-start(), calls=%async_computation.9 | async-start | bytes 6553600 | tf_op jit(solution)/shard_map/reduce_scatter | solution.py:661
  671.7 53.3 %collective-permute-start.38 = (bf16[1728,640]{1,0:T(8,128)(2,1)}, bf16[1728,640]{1,0:T(8,128)(2,1)}, u32[]{:S(2)}, u32[]{:S(2)}) collective-permute-start(bf16[1728,640]{1,0:T(8,128)(2,1)} %add_convert_fusion.3), channel_id=1, source_target_pairs={{0,8},{4,12},{8,0},{12,4},{1,9},{5,13},{9,1},{13,5},{2,10},{6,14},... | collective-permute-start | bytes 6635528 | tf_op jit(solution)/shard_map/ppermute | solution.py:35
  673.2 53.9 %collective-permute-start.39 = (bf16[1728,640]{1,0:T(8,128)(2,1)}, bf16[1728,640]{1,0:T(8,128)(2,1)}, u32[]{:S(2)}, u32[]{:S(2)}) collective-permute-start(bf16[1728,640]{1,0:T(8,128)(2,1)} %add_convert_fusion.1), channel_id=1, source_target_pairs={{0,16},{16,0},{1,17},{17,1},{2,18},{18,2},{3,19},{19,3},{4,20},{20... | collective-permute-start | bytes 6635528 | tf_op jit(solution)/shard_map/ppermute | solution.py:669
  765.3 50.1 %collective-permute-start.52 = (bf16[1728,640]{1,0:T(8,128)(2,1)S(1)}, bf16[1728,640]{1,0:T(8,128)(2,1)}, u32[]{:S(2)}, u32[]{:S(2)}) collective-permute-start(bf16[1728,640]{1,0:T(8,128)(2,1)S(1)} %add_convert_fusion), channel_id=1, source_target_pairs={{0,16},{16,0},{1,17},{17,1},{2,18},{18,2},{3,19},{19,3},{4,20},{20... | collective-permute-start | bytes 6635528 | tf_op jit(solution)/shard_map/ppermute | solution.py:669
  786.7 28.7 %collective-permute-start.59 = (bf16[2,160]{1,0:T(2,128)(2,1)S(1)}, bf16[2,160]{1,0:T(2,128)(2,1)S(1)}, u32[]{:S(2)}, u32[]{:S(2)}) collective-permute-start(bf16[2,160]{1,0:T(2,128)(2,1)S(1)} %fusion.90), channel_id=1, source_target_pairs={{0,16},{16,0},{1,17},{17,1},{2,18},{18,2},{3,19},{19,3},{4,20},{20... | collective-permute-start | bytes 1928 | tf_op jit(solution)/shard_map/ppermute | solution.py:669
  843.5 47.5 %collective-permute-start.60 = (bf16[160,1024]{1,0:T(8,128)(2,1)S(1)}, bf16[160,1024]{1,0:T(8,128)(2,1)S(1)}, u32[]{:S(2)}, u32[]{:S(2)}) collective-permute-start(bf16[160,1024]{1,0:T(8,128)(2,1)S(1)} %get-tuple-element.218), channel_id=1, source_target_pairs={{0,4},{4,0},{8,12},{12,8},{1,5},{5,1},{9,13},{13,9},{2,6},{6,2},{1... | collective-permute-start | bytes 983048 | tf_op jit(solution)/shard_map/ppermute | solution.py:35
  843.6 48.0 %collective-permute-start.61 = (bf16[160,1024]{1,0:T(8,128)(2,1)S(1)}, bf16[160,1024]{1,0:T(8,128)(2,1)S(1)}, u32[]{:S(2)}, u32[]{:S(2)}) collective-permute-start(bf16[160,1024]{1,0:T(8,128)(2,1)S(1)} %get-tuple-element.217), channel_id=1, source_target_pairs={{0,8},{4,12},{8,0},{12,4},{1,9},{5,13},{9,1},{13,5},{2,10},{6,14},... | collective-permute-start | bytes 983048 | tf_op jit(solution)/shard_map/ppermute | solution.py:35
  848.3 41.0 %collective-permute-start.50 = (bf16[640,640]{1,0:T(8,128)(2,1)S(1)}, bf16[640,640]{1,0:T(8,128)(2,1)S(1)}, u32[]{:S(2)}, u32[]{:S(2)}) collective-permute-start(bf16[640,640]{1,0:T(8,128)(2,1)S(1)} %add_convert_fusion.12), channel_id=1, source_target_pairs={{0,8},{4,12},{8,0},{12,4},{1,9},{5,13},{9,1},{13,5},{2,10},{6,14},... | collective-permute-start | bytes 2457608 | tf_op jit(solution)/shard_map/ppermute | solution.py:35
  851.0 44.5 %collective-permute-start.62 = (bf16[160,1024]{1,0:T(8,128)(2,1)S(1)}, bf16[160,1024]{1,0:T(8,128)(2,1)S(1)}, u32[]{:S(2)}, u32[]{:S(2)}) collective-permute-start(bf16[160,1024]{1,0:T(8,128)(2,1)S(1)} %get-tuple-element.216), channel_id=1, source_target_pairs={{0,12},{4,8},{8,4},{12,0},{1,13},{5,9},{9,5},{13,1},{2,14},{6,10},... | collective-permute-start | bytes 983048 | tf_op jit(solution)/shard_map/ppermute | solution.py:35
  891.0 35.4 %collective-permute-start.51 = (bf16[640,640]{1,0:T(8,128)(2,1)S(1)}, bf16[640,640]{1,0:T(8,128)(2,1)S(1)}, u32[]{:S(2)}, u32[]{:S(2)}) collective-permute-start(bf16[640,640]{1,0:T(8,128)(2,1)S(1)} %add_convert_fusion.11), channel_id=1, source_target_pairs={{0,16},{16,0},{1,17},{17,1},{2,18},{18,2},{3,19},{19,3},{4,20},{20... | collective-permute-start | bytes 2457608 | tf_op jit(solution)/shard_map/ppermute | solution.py:669
  (102 other events, 1781.8 us)
Sparse Core Ops, SparseCore 0:
  28.7 100.5 all-gather.11
  140.0 99.1 all-gather.13
  241.6 92.1 reduce-scatter.5
  336.9 55.3 all-gather.15
  393.7 53.5 all-gather.17
  450.0 50.8 reduce-scatter.7
  511.6 50.7 reduce-scatter.9
  565.6 97.7 all-gather.19
  671.6 93.6 reduce-scatter.11
  767.5 94.4 reduce-scatter.13

commit v5 on v4

--- a/solution.py
+++ b/solution.py
@@ -786,27 +786,26 @@
         gain_share_two = gain_share_two + out[6]
     norm_two, grad_rows, act, dgate, dup = before
     share_sums = [sum_cols(share) for share in shares]
-    down_grads = {k: dot(act, grad_rows[k], NT).astype(BF) for k in range(count)}
-    gate_grads = {k: dot(dgate, norm_two[k], NT).astype(BF) for k in range(count)}
-    up_grads = {k: dot(dup, norm_two[k], NT).astype(BF) for k in range(count)}
-    down_grads = fold(down_grads, "row", near)
-    gate_grads = fold(gate_grads, "row", near)
-    up_grads = fold(up_grads, "row", near)
-    *share_sums, down_grads, gate_grads, up_grads = together(
-        *share_sums, down_grads, gate_grads, up_grads
-    )
+    down_near = fold({k: dot(act, grad_rows[k], NT).astype(BF) for k in range(count)}, "row", near)
+    dgate, dup, norm_two, down_near = together(dgate, dup, norm_two, down_near)
+    down_far = fold(down_near, "row", far)[0]
+    gate_near = {k: dot(dgate, norm_two[k], NT).astype(BF) for k in range(count)}
+    gate_near = fold(gate_near, "row", near)
+    up_near = {k: dot(dup, norm_two[k], NT).astype(BF) for k in range(count)}
+    up_near = fold(up_near, "row", near)
+    *share_sums, gate_near, up_near, down_far = together(
+        *share_sums, gate_near, up_near, down_far
+    )
+    gate_far = fold(gate_near, "row", far)[0]
+    up_near, gate_far = together(up_near, gate_far)
+    up_far = fold(up_near, "row", far)[0]
+    down_total = over_dp(down_far)
+    gate_total = over_dp(gate_far)
     residual_grad_own = grad_own.astype(F32) + jnp.concatenate(share_sums, axis=2).astype(F32)
-    down_total = fold(down_grads, "row", far)[0]
-    gate_total = fold(gate_grads, "row", far)[0]
-    down_total_all = over_dp(down_total)
 
     mix_cols = spread_cols(residual_grad_own.astype(BF))
     ff_part = fan_out(listed(down_blocks), act, cols)
-    mix_cols, ff_part, down_total, gate_total, up_grads = together(
-        mix_cols, ff_part, down_total_all, gate_total, up_grads
-    )
-    up_total = fold(up_grads, "row", far)[0]
-    gate_total = over_dp(gate_total)
+    mix_cols, ff_part, down_total = together(mix_cols, ff_part, down_total)
     mix_rows, grad_mine, grad_send = mix_back(own_core, [mix_cols], listed(mix_blocks))
     ff_sum = sum_cols(ff_part)
     grad_other = swapped(grad_send, "row", 1)
@@ -814,8 +813,8 @@
         own_core, own_set, other_set, attn_mine, attn_send, grad_mine, grad_other, lse, seg
     )
     back_other = swapped(back_send, "row", 1)
-    back_other, up_total, gate_total = together(back_other, up_total, gate_total)
-    up_total = over_dp(up_total)
+    back_other, gate_total = together(back_other, gate_total)
+    up_total = over_dp(up_far)
     dq, dkv, share, gain_share_one = qkv_back(
         own_core,
         source,
@@ -829,34 +828,37 @@
         listed(q_blocks),
         listed(kv_blocks),
     )
-    share, ff_sum = together(share, ff_sum)
-    input_sum = sum_cols(share)
-    output_own = (residual_own + ff_sum.astype(F32)).astype(BF)
-    layer_output = all_tokens(output_own)
-
-    share, dq, dkv, mix_rows = together(share, dq, dkv, mix_rows)
-    bits = near + far[::-1]
-    q_grads = {k: dot(norm_one[k], dq, NT).astype(BF) for k in range(count)}
-    kv_grads = {k: dot(dkv, norm_one[k], NT).astype(BF) for k in range(count)}
+    share, attn_mine, mix_rows = together(share, attn_mine, mix_rows)
     attn_low = jnp.concatenate(
         [
             jnp.where(parity == 0, attn_mine, attn_other),
             jnp.where(parity == 0, attn_other, attn_mine),
         ]
     )
-    mix_grads = {k: dot(attn_low, mix_rows[k], NT).astype(BF) for k in range(count)}
-    q_total = over_dp(fold(q_grads, "row", bits)[0])
-    kv_total = over_dp(fold(kv_grads, "row", bits)[0])
-    mix_total = over_dp(fold(mix_grads, "row", bits)[0])
-
+    mix_near = {k: dot(attn_low, mix_rows[k], NT).astype(BF) for k in range(count)}
+    mix_near = fold(mix_near, "row", near)
+    share, ff_sum, mix_near, up_total = together(share, ff_sum, mix_near, up_total)
+    input_sum = sum_cols(share)
+
+    share, dq, dkv = together(share, dq, dkv)
+    mix_total = over_dp(fold(mix_near, "row", far)[0])
+    q_near = fold({k: dot(norm_one[k], dq, NT).astype(BF) for k in range(count)}, "row", near)
+    kv_near = fold({k: dot(dkv, norm_one[k], NT).astype(BF) for k in range(count)}, "row", near)
+    ff_sum, gain_share_one, q_near, kv_near = together(ff_sum, gain_share_one, q_near, kv_near)
+    q_total = over_dp(fold(q_near, "row", far)[0])
+    kv_total = over_dp(fold(kv_near, "row", far)[0])
+    output_own = (residual_own + ff_sum.astype(F32)).astype(BF)
+    layer_output = all_tokens(output_own)
+
+    bits = near + far[::-1]
     gain_shares = jnp.stack([gain_share_one[..., 0], gain_share_two[..., 0]], axis=2)
     gain_shares = by_xor(gain_shares, lax.axis_index("col"), 0)
     gain_shares = {c: gain_shares[c] for c in range(cols)}
     gain_shares = fold(gain_shares, "col", near_bits(cols) + far_bits(cols), low=False)[0]
     gain_shares = fold({k: gain_shares[k] for k in range(count)}, "row", bits, low=False)[0]
     gain_totals = over_dp(gain_shares)
-    input_sum, q_total, kv_total, mix_total, up_total, gain_totals, layer_output = together(
-        input_sum, q_total, kv_total, mix_total, up_total, gain_totals, layer_output
+    input_sum, q_total, kv_total, mix_total, gain_totals, layer_output = together(
+        input_sum, q_total, kv_total, mix_total, gain_totals, layer_output
     )
 
     input_grad = all_tokens((residual_grad_own + input_sum.astype(F32)).astype(BF)).astype(F32)

time: 964 us -> 992 us (1.029)
  waiting for transfers between devices: 498 us -> 533 us
    all_gather x5, waiting for transfers between devices: 100 us -> 144 us  [spread_cols(): return lax.all_gather(value, 'col', axis=0, tiled=False)]
    reduce_scatter x5, waiting for transfers between devices: 51.2 us -> 25.7 us  [sum_cols(): return lax.psum_scatter(value, 'col', scatter_dimension=0, tiled=False)]
    ppermute x59, waiting for transfers between devices: 291 us -> 314 us  [swapped(): return lax.ppermute(value, axis, [(i, i ^ mask) for i in range(size)])]
  transfers between devices with their start and end apart: 76 -> 76, of which waited for: 37 -> 32; matrix products, arithmetic and copies ran while one was open for 13% -> 12% of each run, Pallas kernels for 23% -> 22%
where the time goes in v5:
time: 992 us; the launch traced here: 984 us
  waiting for transfers between devices  533 us (54%)
  Pallas kernels  215 us (22%)
  matrix products  78.9 us (8%)
  starting transfers between devices  43.4 us (4%)
  other arithmetic  41.3 us (4%)
  blocking collectives  34.2 us (3%)
  local copies, waits for them, and re-layouts  22.9 us (2%)
  between operations  15.4 us (2%)
    ppermute x59, waiting for transfers between devices, swapped(): return lax.ppermute(value, axis, [(i, i ^ mask) for i in range(size)])  314 us
    all_gather x5, waiting for transfers between devices, spread_cols(): return lax.all_gather(value, 'col', axis=0, tiled=False)  144 us
    pallas_call x2, Pallas kernels, feed_forward(): pl.pallas_call(functools.partial(ff_kernel, count, bool(before)), out_sha...  83.7 us
    dot_general x24, matrix products, dot(): return lax.dot_general(left, right, dims, preferred_element_type=F32)  78.9 us
    ppermute x7, waiting for transfers between devices, over_dp(): lax.ppermute(low, 'dp', [(i, (i + step) % size) for i in range(size)])  48.8 us
    pallas_call x1, Pallas kernels, attend_back(): pl.pallas_call(functools.partial(attend_back_kernel, tile), out_shape=(sh...  37.6 us
    ppermute x59, starting transfers between devices, swapped(): return lax.ppermute(value, axis, [(i, i ^ mask) for i in range(size)])  35.4 us
    all_gather x1, blocking collectives, body(): lax.all_gather(jnp.stack([attn_gain, mlp_gain]), ('row', 'col'), axis=1,...  34.2 us
  transfers between devices with their start and end apart: 76, of which 32 were waited for; matrix products, arithmetic and copies ran while one was open for 12% of the time, Pallas kernels for 22%

profile of v5, /device:TPU:0, one launch (start us, length us, event | category | flops | bytes accessed | tf_op | source)
XLA Modules:
  0.0 984.2 jit_solution(10333792359622952102)
XLA Ops:
  11.9 7.4 collective-permute-done.5
  19.3 7.2 collective-permute-done.4
  36.8 34.2 %all-gather.5 = f32[16,160,2]{1,2,0:T(2,128)S(1)} all-gather(f32[1,160,2]{1,2,0:T(2,128)S(1)} %maximum_bitcast_fusion.1), channel_id=1, replica_groups=mesh['dp'=2,'row'=4,'col'=4] {'row','col'}, dimensions={0}, use_global_device_ids=true | all-gather | bytes 21760 | tf_op jit(solution)/shard_map/all_gather | solution.py:727
  71.3 33.1 %collective-permute-done.2 = bf16[160,1024]{1,0:T(8,128)(2,1)} collective-permute-done((bf16[160,1024]{1,0:T(8,128)(2,1)}, bf16[160,1024]{1,0:T(8,128)(2,1)}, u32[]{:S(2)}, u32[]{:S(2)}) %collective-permute-start.2) | collective-permute-done | bytes 327712 | tf_op jit(solution)/shard_map/ppermute | solution.py:35
  104.9 6.4 collective-permute-done.1
  115.1 8.7 collective-permute-done.10.refs_6_
  126.3 13.6 %collective-permute-done.12.refs_2_.refs_3_ = bf16[640,640]{1,0:T(8,128)(2,1)} collective-permute-done((bf16[640,640]{1,0:T(8,128)(2,1)}, bf16[640,640]{1,0:T(8,128)(2,1)}, u32[]{:S(2)}, u32[]{:S(2)}) %collective-permute-start.12) | collective-permute-done | bytes 819232 | tf_op jit(solution)/shard_map/ppermute | solution.py:35
  143.0 13.1 %qkv_project.1 = (bf16[4,640,1024]{2,1,0:T(8,128)(2,1)}, f32[1,1024]{1,0:T(1,128)}, bf16[2,480,1024]{2,1,0:T(8,128)(2,1)}) custom-call(bf16[4,4,160,1024]{3,2,1,0:T(8,128)(2,1)} %bitcast.233, f32[4,4,160,1]{3,2,1,0:T(8,128)} %copy.66.gain_ref, f32[40,1024]{1,0:T(8,128)} %get-tuple-element.127.cos_ref, f32[40,1024]{1,0:T(8,128)} %get-tuple-element.128.sin_ref, ...), custom_call_target="tpu_custom_call" | custom-call | tf_op jit(solution)/shard_map/qkv_project/pallas_call | solution.py:146
  164.2 28.0 %attend.1 = (bf16[320,1024]{1,0:T(8,128)(2,1)}, bf16[320,1024]{1,0:T(8,128)(2,1)}, f32[2,4,1,1024]{3,2,1,0:T(1,128)}) custom-call(s32[1]{0:T(128)} %bitcast.parity_ref, bf16[480,1024]{1,0:T(8,128)(2,1)} %get-tuple-element.238.own_ref, bf16[480,1024]{1,0:T(8,128)(2,1)} %copy-done.15, s32[1,1024]{1,0:T(1,128)} %bitcast.275, s32[1024,1]{1,0:T(8,128)} %copy.61.seg_col), custom_call_target="tpu_custom_call" | custom-call | tf_op jit(solution)/shard_map/attend/pallas_call | solution.py:237
  195.3 10.2 %mix_out.1 = bf16[4,4,160,1024]{3,2,1,0:T(8,128)(2,1)} custom-call(s32[1]{0:T(128)} %bitcast.parity_ref, bf16[320,1024]{1,0:T(8,128)(2,1)} %get-tuple-element.206.own_ref.own_out, bf16[320,1024]{1,0:T(8,128)(2,1)} %copy-done.28, bf16[640,640]{1,0:T(8,128)(2,1)} %refs_1_, bf16[640,640]{1,0:T(8,128)(2,1)} %collective-permute-done.17.refs_1_.refs_2_, ...), custom_call_target="tpu_custom_call" | custom-call | tf_op jit(solution)/shard_map/mix_out/pallas_call | solution.py:410
  205.6 33.7 %all-gather.14.cloned.1.call-done = bf16[16,160,1024]{2,1,0:T(8,128)(2,1)} async-done(((bf16[4,160,1024]{2,1,0:T(8,128)(2,1)}), bf16[16,160,1024]{2,1,0:T(8,128)(2,1)}) %all-gather.14.cloned.1.call-update) | async-done | bytes 5242896 | tf_op jit(solution)/shard_map/all_gather | solution.py:657
  242.4 48.5 %collective-permute-done.25.refs_10_.refs_2_ = bf16[1728,640]{1,0:T(8,128)(2,1)S(1)} collective-permute-done((bf16[1728,640]{1,0:T(8,128)(2,1)S(1)}, bf16[1728,640]{1,0:T(8,128)(2,1)S(1)}, u32[]{:S(2)}, u32[]{:S(2)}) %collective-permute-start.25) | collective-permute-done | bytes 2211872 | tf_op jit(solution)/shard_map/ppermute | solution.py:35
  292.2 6.1 collective-permute-done.26.refs_11_.refs_3_
  308.1 25.7 %reduce-scatter.6.cloned.1.call-done = bf16[1,4,160,1024]{3,2,1,0:T(8,128)(2,1)} async-done(((bf16[4,4,160,1024]{3,2,1,0:T(8,128)(2,1)}), bf16[1,4,160,1024]{3,2,1,0:T(8,128)(2,1)}) %reduce-scatter.6.cloned.1.call-update) | async-done | bytes 1310736 | tf_op jit(solution)/shard_map/reduce_scatter | solution.py:661
  339.0 53.3 %all-gather.16.cloned.1.call-done = bf16[16,160,512]{2,1,0:T(8,128)(2,1)} async-done(((bf16[4,160,512]{2,1,0:T(8,128)(2,1)}), bf16[16,160,512]{2,1,0:T(8,128)(2,1)}) %all-gather.16.cloned.1.call-update) | async-done | bytes 2621456 | tf_op jit(solution)/shard_map/all_gather | solution.py:657
  392.3 41.8 %feed_forward.2 = (bf16[4,640,1024]{2,1,0:T(8,128)(2,1)}, bf16[4,640,1024]{2,1,0:T(8,128)(2,1)}, bf16[1728,1024]{1,0:T(8,128)(2,1)}, bf16[1728,1024]{1,0:T(8,128...) custom-call(bf16[4,4,160,512]{3,2,1,0:T(8,128)(2,1)} %bitcast.261, ...), custom_call_target="tpu_custom_call" | custom-call | tf_op jit(solution)/shard_map/feed_forward/pallas_call | solution.py:546
  434.2 13.1 %all-gather.18.cloned.1.call-done = bf16[16,160,512]{2,1,0:T(8,128)(2,1)} async-done(((bf16[4,160,512]{2,1,0:T(8,128)(2,1)}), bf16[16,160,512]{2,1,0:T(8,128)(2,1)}) %all-gather.18.cloned.1.call-update) | async-done | bytes 2621456 | tf_op jit(solution)/shard_map/all_gather | solution.py:657
  447.3 41.8 %feed_forward.3 = (bf16[4,640,1024]{2,1,0:T(8,128)(2,1)}, bf16[4,640,1024]{2,1,0:T(8,128)(2,1)}, bf16[1728,1024]{1,0:T(8,128)(2,1)}, bf16[1728,1024]{1,0:T(8,128...) custom-call(bf16[4,4,160,512]{3,2,1,0:T(8,128)(2,1)} %bitcast.266, ...), custom_call_target="tpu_custom_call", output_to_operand_aliasing={{0}: (15, {}), {1}: (16, {}), {2}: (17, {}), {3}: (18, {}),... | custom-call | tf_op jit(solution)/shard_map/feed_forward/pallas_call | solution.py:546
  489.1 6.9 convolution_convert_fusion.10
  529.3 33.7 %collective-permute-done.33 = bf16[1728,640]{1,0:T(8,128)(2,1)S(1)} collective-permute-done((bf16[1728,640]{1,0:T(8,128)(2,1)S(1)}, bf16[1728,640]{1,0:T(8,128)(2,1)S(1)}, u32[]{:S(2)}, u32[]{:S(2)}) %collective-permute-start.33) | collective-permute-done | bytes 2211872 | tf_op jit(solution)/shard_map/ppermute | solution.py:35
  584.7 16.9 %fan_out.1 = bf16[4,4,160,1024]{3,2,1,0:T(8,128)(2,1)} custom-call(bf16[1728,1024]{1,0:T(8,128)(2,1)} %get-tuple-element.180.x_ref, bf16[1728,640]{1,0:T(8,128)(2,1)} %refs_0_.2, bf16[1728,640]{1,0:T(8,128)(2,1)} %copy-done.3, bf16[1728,640]{1,0:T(8,128)(2,1)} %copy-done.2, bf16[1728,640]{1,0:T(8,128)(2,1)} %copy-done.4), custom_call_target="tpu_custom_call" | custom-call | tf_op jit(solution)/shard_map/fan_out/pallas_call | solution.py:469
  601.6 30.8 %collective-permute-done.34 = bf16[1728,640]{1,0:T(8,128)(2,1)} collective-permute-done((bf16[1728,640]{1,0:T(8,128)(2,1)S(1)}, bf16[1728,640]{1,0:T(8,128)(2,1)}, u32[]{:S(2)}, u32[]{:S(2)}) %collective-permute-start.34) | collective-permute-done | bytes 2211872 | tf_op jit(solution)/shard_map/ppermute | solution.py:669
  636.6 43.4 %all-gather.20.cloned.1.call-done = bf16[16,160,1024]{2,1,0:T(8,128)(2,1)} async-done(((bf16[4,160,1024]{2,1,0:T(8,128)(2,1)}), bf16[16,160,1024]{2,1,0:T(8,128)(2,1)}) %all-gather.20.cloned.1.call-update) | async-done | bytes 5242896 | tf_op jit(solution)/shard_map/all_gather | solution.py:657
  681.8 48.7 %collective-permute-done.37 = bf16[1728,640]{1,0:T(8,128)(2,1)S(1)} collective-permute-done((bf16[1728,640]{1,0:T(8,128)(2,1)}, bf16[1728,640]{1,0:T(8,128)(2,1)S(1)}, u32[]{:S(2)}, u32[]{:S(2)}) %collective-permute-start.37) | collective-permute-done | bytes 2211872 | tf_op jit(solution)/shard_map/ppermute | solution.py:35
  734.1 8.7 mix_back.1
  742.8 37.9 %collective-permute-done.41 = bf16[1728,640]{1,0:T(8,128)(2,1)} collective-permute-done((bf16[1728,640]{1,0:T(8,128)(2,1)}, bf16[1728,640]{1,0:T(8,128)(2,1)}, u32[]{:S(2)}, u32[]{:S(2)}) %collective-permute-start.41) | collective-permute-done | bytes 2211872 | tf_op jit(solution)/shard_map/ppermute | solution.py:35
  785.1 37.6 %attend_back.1 = (bf16[480,1024]{1,0:T(8,128)(2,1)}, bf16[480,1024]{1,0:T(8,128)(2,1)}) custom-call(s32[1]{0:T(128)} %bitcast.parity_ref, bf16[480,1024]{1,0:T(8,128)(2,1)} %get-tuple-element.238.own_ref, bf16[480,1024]{1,0:T(8,128)(2,1)} %copy-done.15, bf16[320,1024]{1,0:T(8,128)(2,1)} %get-tuple-element.206.own_ref.own_out, ...), custom_call_target="tpu_custom_call" | custom-call | tf_op jit(solution)/shard_map/attend_back/pallas_call | solution.py:348
  826.9 17.4 %qkv_back.1 = (bf16[640,1024]{1,0:T(8,128)(2,1)}, bf16[320,1024]{1,0:T(8,128)(2,1)}, bf16[4,4,160,1024]{3,2,1,0:T(8,128)(2,1)}, f32[4,4,160,1]{3,2,1,0:T(8,128)}) custom-call(s32[1]{0:T(128)} %bitcast.parity_ref, bf16[4,4,160,1024]{3,2,1,0:T(8,128)(2,1)} %bitcast.234, f32[4,4,160,1]{3,2,1,0:T(8,128)} %copy.66.gain_ref, ...), custom_call_target="tpu_custom_call" | custom-call | tf_op jit(solution)/shard_map/qkv_back/pallas_call | solution.py:635
  899.9 20.5 %collective-permute-done.58 = f32[2,160]{1,0:T(2,128)S(1)} collective-permute-done((f32[2,160]{1,0:T(2,128)S(1)}, f32[2,160]{1,0:T(2,128)S(1)}, u32[]{:S(2)}, u32[]{:S(2)}) %collective-permute-start.58) | collective-permute-done | bytes 1312 | tf_op jit(solution)/shard_map/ppermute | solution.py:35
  928.0 6.6 collective-permute-done.61
  940.1 15.1 %collective-permute-done.48 = bf16[640,640]{1,0:T(8,128)(2,1)S(1)} collective-permute-done((bf16[640,640]{1,0:T(8,128)(2,1)S(1)}, bf16[640,640]{1,0:T(8,128)(2,1)S(1)}, u32[]{:S(2)}, u32[]{:S(2)}) %collective-permute-start.48) | collective-permute-done | bytes 819232 | tf_op jit(solution)/shard_map/ppermute | solution.py:669
  962.3 7.0 collective-permute-done.64
  (341 shorter events, 212.0 us)
Async XLA Ops:
  7.2 132.7 %all-gather.12.cloned.1.call-start = ((), (), s32[]{:S(2)}) async-start(), calls=%async_computation.10 | async-start | bytes 6553600 | tf_op jit(solution)/shard_map/all_gather | solution.py:657
  28.6 210.7 %all-gather.14.cloned.1.call-start = ((), (), s32[]{:S(2)}) async-start(), calls=%async_computation.11 | async-start | bytes 6553600 | tf_op jit(solution)/shard_map/all_gather | solution.py:657
  28.7 111.2 %collective-permute-start.13 = (bf16[1728,640]{1,0:T(8,128)(2,1)S(1)}, bf16[1728,640]{1,0:T(8,128)(2,1)}, u32[]{:S(2)}, u32[]{:S(2)}) collective-permute-start(bf16[1728,640]{1,0:T(8,128)(2,1)S(1)} %bitcast.240), channel_id=1, source_target_pairs={{0,8},{4,12},{8,0},{12,4},{1,9},{5,13},{9,1},{13,5},{2,10},{6,14},... | collective-permute-start | bytes 6635528 | tf_op jit(solution)/shard_map/ppermute | solution.py:35
  31.0 82.5 %collective-permute-start.7 = (bf16[640,640]{1,0:T(8,128)(2,1)}, bf16[640,640]{1,0:T(8,128)(2,1)}, u32[]{:S(2)}, u32[]{:S(2)}) collective-permute-start(bf16[640,640]{1,0:T(8,128)(2,1)} %refs_0_.3), channel_id=1, source_target_pairs={{0,8},{4,12},{8,0},{12,4},{1,9},{5,13},{9,1},{13,5},{2,10},{6,14},... | collective-permute-start | bytes 2457608 | tf_op jit(solution)/shard_map/ppermute | solution.py:35
  33.5 70.9 %collective-permute-start.2 = (bf16[160,1024]{1,0:T(8,128)(2,1)}, bf16[160,1024]{1,0:T(8,128)(2,1)}, u32[]{:S(2)}, u32[]{:S(2)}) collective-permute-start(bf16[160,1024]{1,0:T(8,128)(2,1)} %get-tuple-element.255), channel_id=1, source_target_pairs={{0,12},{4,8},{8,4},{12,0},{1,13},{5,9},{9,5},{13,1},{2,14},{6,10},... | collective-permute-start | bytes 983048 | tf_op jit(solution)/shard_map/ppermute | solution.py:35
  34.5 76.7 %collective-permute-start.1 = (bf16[160,1024]{1,0:T(8,128)(2,1)}, bf16[160,1024]{1,0:T(8,128)(2,1)}, u32[]{:S(2)}, u32[]{:S(2)}) collective-permute-start(bf16[160,1024]{1,0:T(8,128)(2,1)} %get-tuple-element.256), channel_id=1, source_target_pairs={{0,8},{4,12},{8,0},{12,4},{1,9},{5,13},{9,1},{13,5},{2,10},{6,14},... | collective-permute-start | bytes 983048 | tf_op jit(solution)/shard_map/ppermute | solution.py:35
  36.6 76.5 %collective-permute-start.9 = (bf16[320,640]{1,0:T(8,128)(2,1)S(1)}, bf16[320,640]{1,0:T(8,128)(2,1)S(1)}, u32[]{:S(2)}, u32[]{:S(2)}) collective-permute-start(bf16[320,640]{1,0:T(8,128)(2,1)S(1)} %pad_maximum_fusion.4.refs_4_), channel_id=1, source_target_pairs={{0,4},{4,0},{8,12},{12,8},{1,5},{5,1},{9,13},{13,9},{2,6},{6,2},{1... | collective-permute-start | bytes 1228808 | tf_op jit(solution)/shard_map/ppermute | solution.py:35
  139.9 193.8 %reduce-scatter.6.cloned.1.call-start = ((), (), s32[]{:S(2)}) async-start(), calls=%async_computation.5 | async-start | bytes 6553600 | tf_op jit(solution)/shard_map/reduce_scatter | solution.py:661
  140.0 52.4 %collective-permute-start.19 = (bf16[1728,640]{1,0:T(8,128)(2,1)}, bf16[1728,640]{1,0:T(8,128)(2,1)S(1)}, u32[]{:S(2)}, u32[]{:S(2)}) collective-permute-start(bf16[1728,640]{1,0:T(8,128)(2,1)} %bitcast.241), channel_id=1, source_target_pairs={{0,8},{4,12},{8,0},{12,4},{1,9},{5,13},{9,1},{13,5},{2,10},{6,14},... | collective-permute-start | bytes 6635528 | tf_op jit(solution)/shard_map/ppermute | solution.py:35
  239.3 153.0 %all-gather.16.cloned.1.call-start = ((), (), s32[]{:S(2)}) async-start(), calls=%async_computation.12 | async-start | bytes 3276800 | tf_op jit(solution)/shard_map/all_gather | solution.py:657
  240.9 50.0 %collective-permute-start.25 = (bf16[1728,640]{1,0:T(8,128)(2,1)S(1)}, bf16[1728,640]{1,0:T(8,128)(2,1)S(1)}, u32[]{:S(2)}, u32[]{:S(2)}) collective-permute-start(bf16[1728,640]{1,0:T(8,128)(2,1)S(1)} %copy-done.1), channel_id=1, source_target_pairs={{0,8},{4,12},{8,0},{12,4},{1,9},{5,13},{9,1},{13,5},{2,10},{6,14},... | collective-permute-start | bytes 6635528 | tf_op jit(solution)/shard_map/ppermute | solution.py:35
  242.4 49.5 %collective-permute-start.24 = (bf16[1728,640]{1,0:T(8,128)(2,1)S(1)}, bf16[1728,640]{1,0:T(8,128)(2,1)S(1)}, u32[]{:S(2)}, u32[]{:S(2)}) collective-permute-start(bf16[1728,640]{1,0:T(8,128)(2,1)S(1)} %copy-done.1), channel_id=1, source_target_pairs={{0,4},{4,0},{8,12},{12,8},{1,5},{5,1},{9,13},{13,9},{2,6},{6,2},{1... | collective-permute-start | bytes 6635528 | tf_op jit(solution)/shard_map/ppermute | solution.py:35
  336.8 110.5 %all-gather.18.cloned.1.call-start = ((), (), s32[]{:S(2)}) async-start(), calls=%async_computation.13 | async-start | bytes 3276800 | tf_op jit(solution)/shard_map/all_gather | solution.py:657
  337.4 243.0 %reduce-scatter.8.cloned.1.call-start = ((), (), s32[]{:S(2)}) async-start(), calls=%async_computation.6 | async-start | bytes 3276800 | tf_op jit(solution)/shard_map/reduce_scatter | solution.py:661
  434.2 146.3 %reduce-scatter.10.cloned.1.call-start = ((), (), s32[]{:S(2)}) async-start(), calls=%async_computation.7 | async-start | bytes 3276800 | tf_op jit(solution)/shard_map/reduce_scatter | solution.py:661
  502.1 177.9 %all-gather.20.cloned.1.call-start = ((), (), s32[]{:S(2)}) async-start(), calls=%async_computation.14 | async-start | bytes 6553600 | tf_op jit(solution)/shard_map/all_gather | solution.py:657
  513.1 49.8 %collective-permute-start.33 = (bf16[1728,640]{1,0:T(8,128)(2,1)S(1)}, bf16[1728,640]{1,0:T(8,128)(2,1)S(1)}, u32[]{:S(2)}, u32[]{:S(2)}) collective-permute-start(bf16[1728,640]{1,0:T(8,128)(2,1)S(1)} %add_convert_fusion.7), channel_id=1, source_target_pairs={{0,8},{4,12},{8,0},{12,4},{1,9},{5,13},{9,1},{13,5},{2,10},{6,14},... | collective-permute-start | bytes 6635528 | tf_op jit(solution)/shard_map/ppermute | solution.py:35
  518.6 45.0 %collective-permute-start.29 = (bf16[1728,640]{1,0:T(8,128)(2,1)}, bf16[1728,640]{1,0:T(8,128)(2,1)S(1)}, u32[]{:S(2)}, u32[]{:S(2)}) collective-permute-start(bf16[1728,640]{1,0:T(8,128)(2,1)} %convolution_convert_fusion.6), channel_id=1, source_target_pairs={{0,4},{4,0},{8,12},{12,8},{1,5},{5,1},{9,13},{13,9},{2,6},{6,2},{1... | collective-permute-start | bytes 6635528 | tf_op jit(solution)/shard_map/ppermute | solution.py:35
  521.7 46.0 %collective-permute-start.30 = (bf16[1728,640]{1,0:T(8,128)(2,1)S(1)}, bf16[1728,640]{1,0:T(8,128)(2,1)S(1)}, u32[]{:S(2)}, u32[]{:S(2)}) collective-permute-start(bf16[1728,640]{1,0:T(8,128)(2,1)S(1)} %convolution_convert_fusion.4), channel_id=1, source_target_pairs={{0,4},{4,0},{8,12},{12,8},{1,5},{5,1},{9,13},{13,9},{2,6},{6,2},{1... | collective-permute-start | bytes 6635528 | tf_op jit(solution)/shard_map/ppermute | solution.py:35
  525.5 46.4 %collective-permute-start.31 = (bf16[1728,640]{1,0:T(8,128)(2,1)S(1)}, bf16[1728,640]{1,0:T(8,128)(2,1)S(1)}, u32[]{:S(2)}, u32[]{:S(2)}) collective-permute-start(bf16[1728,640]{1,0:T(8,128)(2,1)S(1)} %convolution_convert_fusion.2), channel_id=1, source_target_pairs={{0,4},{4,0},{8,12},{12,8},{1,5},{5,1},{9,13},{13,9},{2,6},{6,2},{1... | collective-permute-start | bytes 6635528 | tf_op jit(solution)/shard_map/ppermute | solution.py:35
  528.8 47.5 %collective-permute-start.32 = (bf16[1728,640]{1,0:T(8,128)(2,1)S(1)}, bf16[1728,640]{1,0:T(8,128)(2,1)S(1)}, u32[]{:S(2)}, u32[]{:S(2)}) collective-permute-start(bf16[1728,640]{1,0:T(8,128)(2,1)S(1)} %convolution_convert_fusion), channel_id=1, source_target_pairs={{0,4},{4,0},{8,12},{12,8},{1,5},{5,1},{9,13},{13,9},{2,6},{6,2},{1... | collective-permute-start | bytes 6635528 | tf_op jit(solution)/shard_map/ppermute | solution.py:35
  583.3 276.9 %reduce-scatter.12.cloned.1.call-start = ((), (), s32[]{:S(2)}) async-start(), calls=%async_computation.8 | async-start | bytes 6553600 | tf_op jit(solution)/shard_map/reduce_scatter | solution.py:661
  583.3 49.1 %collective-permute-start.34 = (bf16[1728,640]{1,0:T(8,128)(2,1)S(1)}, bf16[1728,640]{1,0:T(8,128)(2,1)}, u32[]{:S(2)}, u32[]{:S(2)}) collective-permute-start(bf16[1728,640]{1,0:T(8,128)(2,1)S(1)} %add_convert_fusion.2), channel_id=1, source_target_pairs={{0,16},{16,0},{1,17},{17,1},{2,18},{18,2},{3,19},{19,3},{4,20},{20... | collective-permute-start | bytes 6635528 | tf_op jit(solution)/shard_map/ppermute | solution.py:669
  680.0 276.5 %reduce-scatter.14.cloned.1.call-start = ((), (), s32[]{:S(2)}) async-start(), calls=%async_computation.9 | async-start | bytes 6553600 | tf_op jit(solution)/shard_map/reduce_scatter | solution.py:661
  680.3 50.3 %collective-permute-start.37 = (bf16[1728,640]{1,0:T(8,128)(2,1)}, bf16[1728,640]{1,0:T(8,128)(2,1)S(1)}, u32[]{:S(2)}, u32[]{:S(2)}) collective-permute-start(bf16[1728,640]{1,0:T(8,128)(2,1)} %add_convert_fusion.5), channel_id=1, source_target_pairs={{0,8},{4,12},{8,0},{12,4},{1,9},{5,13},{9,1},{13,5},{2,10},{6,14},... | collective-permute-start | bytes 6635528 | tf_op jit(solution)/shard_map/ppermute | solution.py:35
  731.1 49.6 %collective-permute-start.41 = (bf16[1728,640]{1,0:T(8,128)(2,1)}, bf16[1728,640]{1,0:T(8,128)(2,1)}, u32[]{:S(2)}, u32[]{:S(2)}) collective-permute-start(bf16[1728,640]{1,0:T(8,128)(2,1)} %add_convert_fusion.3), channel_id=1, source_target_pairs={{0,8},{4,12},{8,0},{12,4},{1,9},{5,13},{9,1},{13,5},{2,10},{6,14},... | collective-permute-start | bytes 6635528 | tf_op jit(solution)/shard_map/ppermute | solution.py:35
  732.7 90.1 %collective-permute-start.38 = (bf16[1728,640]{1,0:T(8,128)(2,1)S(1)}, bf16[1728,640]{1,0:T(8,128)(2,1)}, u32[]{:S(2)}, u32[]{:S(2)}) collective-permute-start(bf16[1728,640]{1,0:T(8,128)(2,1)S(1)} %add_convert_fusion.1), channel_id=1, source_target_pairs={{0,16},{16,0},{1,17},{17,1},{2,18},{18,2},{3,19},{19,3},{4,20},{20... | collective-permute-start | bytes 6635528 | tf_op jit(solution)/shard_map/ppermute | solution.py:669
  742.8 42.3 %collective-permute-start.35 = (bf16[320,1024]{1,0:T(8,128)(2,1)}, bf16[320,1024]{1,0:T(8,128)(2,1)}, u32[]{:S(2)}, u32[]{:S(2)}) collective-permute-start(bf16[320,1024]{1,0:T(8,128)(2,1)} %get-tuple-element.192), channel_id=1, source_target_pairs={{0,4},{4,0},{8,12},{12,8},{1,5},{5,1},{9,13},{13,9},{2,6},{6,2},{1... | collective-permute-start | bytes 1966088 | tf_op jit(solution)/shard_map/ppermute | solution.py:35
  783.6 68.0 %collective-permute-start.42 = (bf16[1728,640]{1,0:T(8,128)(2,1)S(1)}, bf16[1728,640]{1,0:T(8,128)(2,1)}, u32[]{:S(2)}, u32[]{:S(2)}) collective-permute-start(bf16[1728,640]{1,0:T(8,128)(2,1)S(1)} %add_convert_fusion), channel_id=1, source_target_pairs={{0,16},{16,0},{1,17},{17,1},{2,18},{18,2},{3,19},{19,3},{4,20},{20... | collective-permute-start | bytes 6635528 | tf_op jit(solution)/shard_map/ppermute | solution.py:669
  884.2 41.3 %collective-permute-start.47 = (bf16[640,640]{1,0:T(8,128)(2,1)}, bf16[640,640]{1,0:T(8,128)(2,1)S(1)}, u32[]{:S(2)}, u32[]{:S(2)}) collective-permute-start(bf16[640,640]{1,0:T(8,128)(2,1)} %add_convert_fusion.13), channel_id=1, source_target_pairs={{0,8},{4,12},{8,0},{12,4},{1,9},{5,13},{9,1},{13,5},{2,10},{6,14},... | collective-permute-start | bytes 2457608 | tf_op jit(solution)/shard_map/ppermute | solution.py:35
  884.9 40.6 %collective-permute-start.49 = (bf16[320,640]{1,0:T(8,128)(2,1)}, bf16[320,640]{1,0:T(8,128)(2,1)S(1)}, u32[]{:S(2)}, u32[]{:S(2)}) collective-permute-start(bf16[320,640]{1,0:T(8,128)(2,1)} %add_convert_fusion.18), channel_id=1, source_target_pairs={{0,8},{4,12},{8,0},{12,4},{1,9},{5,13},{9,1},{13,5},{2,10},{6,14},... | collective-permute-start | bytes 1228808 | tf_op jit(solution)/shard_map/ppermute | solution.py:35
  896.3 42.4 %collective-permute-start.52 = (bf16[640,640]{1,0:T(8,128)(2,1)S(1)}, bf16[640,640]{1,0:T(8,128)(2,1)S(1)}, u32[]{:S(2)}, u32[]{:S(2)}) collective-permute-start(bf16[640,640]{1,0:T(8,128)(2,1)S(1)} %add_convert_fusion.11), channel_id=1, source_target_pairs={{0,16},{16,0},{1,17},{17,1},{2,18},{18,2},{3,19},{19,3},{4,20},{20... | collective-permute-start | bytes 2457608 | tf_op jit(solution)/shard_map/ppermute | solution.py:669
  (98 other events, 1746.5 us)
Sparse Core Ops, SparseCore 0:
  28.7 100.5 all-gather.11
  140.0 99.1 all-gather.13
  241.6 92.1 reduce-scatter.5
  336.9 55.3 all-gather.15
  393.7 53.5 all-gather.17
  450.0 50.8 reduce-scatter.7
  503.3 51.7 reduce-scatter.9
  583.4 96.5 all-gather.19
  682.3 92.1 reduce-scatter.11
  860.4 91.8 reduce-scatter.13

commit v6 on v5

--- a/solution.py
+++ b/solution.py
@@ -53,6 +53,13 @@
     return held
 
 
+def fold_landed(held, moved, bit):
+    return {
+        k ^ bit: (held[k ^ bit].astype(F32) + other.astype(F32)).astype(BF)
+        for k, other in moved.items()
+    }
+
+
 def far_bits(size):
     return [1 << i for i in range(1, size.bit_length() - 1)]
 
@@ -75,6 +82,10 @@
 
 def params(mib=58):
     return pltpu.CompilerParams(vmem_limit_bytes=mib * 1024 * 1024)
+
+
+def takes(micros):
+    return pl.CostEstimate(flops=int(micros * 1.0e9), transcendentals=0, bytes_accessed=0)
 
 
 def shape(dims, dtype):
@@ -152,6 +163,7 @@
         ),
         compiler_params=params(),
         name="qkv_project",
+        cost_estimate=takes(12),
     )(x, gain, cosine, sine, *q_w, *kv_w)
 
 
@@ -256,6 +268,7 @@
         ],
         compiler_params=params(),
         name="attend",
+        cost_estimate=takes(27),
     )(parity, own, other, seg[None, :], seg[:, None])
 
 
@@ -372,6 +385,7 @@
         ],
         compiler_params=params(),
         name="attend_back",
+        cost_estimate=takes(37),
     )(
         parity,
         own,
@@ -413,6 +427,7 @@
         in_specs=[SMALL] + [vmem] * (2 + count),
         compiler_params=params(),
         name="mix_out",
+        cost_estimate=takes(10),
     )(parity, own, other, *weights)
 
 
@@ -451,6 +466,7 @@
         in_specs=[SMALL] + [vmem] * (parts + count),
         compiler_params=params(),
         name="mix_back",
+        cost_estimate=takes(9),
     )(parity, *x_parts, *weights)
 
 
@@ -471,6 +487,7 @@
         out_shape=shape((cols, count, piece, x.shape[1]), BF),
         compiler_params=params(),
         name="fan_out",
+        cost_estimate=takes(17),
     )(x, *weights)
 
 
@@ -575,6 +592,7 @@
         input_output_aliases={first + i: i for i in range(len(before))},
         compiler_params=params(60),
         name="feed_forward",
+        cost_estimate=takes(42),
     )(x, g, gain, *gate_w, *up_w, *down_w, *before)
 
 
@@ -643,6 +661,7 @@
         in_specs=[SMALL] + [vmem] * (8 + 2 * count),
         compiler_params=params(),
         name="qkv_back",
+        cost_estimate=takes(17),
     )(parity, x, gain, scale, cosine, sine, sets, own, other, *q_w, *kv_w)
 
 
@@ -695,6 +714,7 @@
     own_core = parity.reshape(1)
     q_half = query_weight.shape[1] // 2
     near, far = near_bits(count), far_bits(count)
+    far_mask = far[-1]
 
     def row_tokens(value):
         turned = value.T
@@ -788,33 +808,43 @@
     share_sums = [sum_cols(share) for share in shares]
     down_near = fold({k: dot(act, grad_rows[k], NT).astype(BF) for k in range(count)}, "row", near)
     dgate, dup, norm_two, down_near = together(dgate, dup, norm_two, down_near)
-    down_far = fold(down_near, "row", far)[0]
     gate_near = {k: dot(dgate, norm_two[k], NT).astype(BF) for k in range(count)}
     gate_near = fold(gate_near, "row", near)
     up_near = {k: dot(dup, norm_two[k], NT).astype(BF) for k in range(count)}
     up_near = fold(up_near, "row", near)
-    *share_sums, gate_near, up_near, down_far = together(
-        *share_sums, gate_near, up_near, down_far
-    )
+    cut = act.shape[0] // 2
+    down_head = {k: v[:cut] for k, v in down_near.items()}
+    down_tail = {k: v[cut:] for k, v in down_near.items()}
+    head_moved = {k: swapped(down_head[k], "row", far_mask) for k in down_head if k & far_mask}
+    *share_sums, gate_near, up_near, down_head, down_tail, head_moved = together(
+        *share_sums, gate_near, up_near, down_head, down_tail, head_moved
+    )
+    down_head = fold_landed(down_head, head_moved, far_mask)
+    down_head = fold(down_head, "row", far[::-1][1:])[0]
+    down_tail = fold(down_tail, "row", far[::-1])[0]
+    down_tail, up_near = together(down_tail, up_near)
+    down_far = jnp.concatenate([down_head, down_tail])
+    residual_grad_own = grad_own.astype(F32) + jnp.concatenate(share_sums, axis=2).astype(F32)
     gate_far = fold(gate_near, "row", far)[0]
-    up_near, gate_far = together(up_near, gate_far)
-    up_far = fold(up_near, "row", far)[0]
+    up_moved = {k: swapped(up_near[k], "row", far_mask) for k in up_near if k & far_mask}
     down_total = over_dp(down_far)
-    gate_total = over_dp(gate_far)
-    residual_grad_own = grad_own.astype(F32) + jnp.concatenate(share_sums, axis=2).astype(F32)
 
     mix_cols = spread_cols(residual_grad_own.astype(BF))
     ff_part = fan_out(listed(down_blocks), act, cols)
     mix_cols, ff_part, down_total = together(mix_cols, ff_part, down_total)
+    gate_total = over_dp(gate_far)
     mix_rows, grad_mine, grad_send = mix_back(own_core, [mix_cols], listed(mix_blocks))
     ff_sum = sum_cols(ff_part)
     grad_other = swapped(grad_send, "row", 1)
+    grad_mine, up_moved, up_near = together(grad_mine, up_moved, up_near)
+    up_far = fold_landed(up_near, up_moved, far_mask)
+    grad_other, gate_total, up_far = together(grad_other, gate_total, up_far)
+    up_total = over_dp(fold(up_far, "row", far[::-1][1:])[0])
     back_mine, back_send = attend_back(
         own_core, own_set, other_set, attn_mine, attn_send, grad_mine, grad_other, lse, seg
     )
     back_other = swapped(back_send, "row", 1)
-    back_other, gate_total = together(back_other, gate_total)
-    up_total = over_dp(up_far)
+    back_other, up_total = together(back_other, up_total)
     dq, dkv, share, gain_share_one = qkv_back(
         own_core,
         source,
@@ -837,7 +867,7 @@
     )
     mix_near = {k: dot(attn_low, mix_rows[k], NT).astype(BF) for k in range(count)}
     mix_near = fold(mix_near, "row", near)
-    share, ff_sum, mix_near, up_total = together(share, ff_sum, mix_near, up_total)
+    share, ff_sum, mix_near = together(share, ff_sum, mix_near)
     input_sum = sum_cols(share)
 
     share, dq, dkv = together(share, dq, dkv)

time: 992 us -> 949 us (0.957)
  waiting for transfers between devices: 533 us -> 485 us
    all_gather x5, waiting for transfers between devices: 144 us -> 86.4 us  [spread_cols(): return lax.all_gather(value, 'col', axis=0, tiled=False)]
    ppermute x7, waiting for transfers between devices: 48.8 us -> 85.7 us  [over_dp(): lax.ppermute(low, 'dp', [(i, (i + step) % size) for i in range(size)])]
    ppermute x59 -> x60, waiting for transfers between devices: 314 us -> 288 us  [swapped(): return lax.ppermute(value, axis, [(i, i ^ mask) for i in range(size)])]
    ppermute x59 -> x60, starting transfers between devices: 35.4 us -> 38 us  [swapped(): return lax.ppermute(value, axis, [(i, i ^ mask) for i in range(size)])]
  transfers between devices with their start and end apart: 76 -> 77, of which waited for: 32 -> 30; matrix products, arithmetic and copies ran while one was open for 12% -> 13% of each run, Pallas kernels for 22% -> 23%
where the time goes in v6:
time: 949 us; the launch traced here: 941 us
  waiting for transfers between devices  485 us (51%)
  Pallas kernels  215 us (23%)
  matrix products  78 us (8%)
  starting transfers between devices  48.5 us (5%)
  other arithmetic  43.6 us (5%)
  blocking collectives  34 us (4%)
  local copies, waits for them, and re-layouts  21.5 us (2%)
  between operations  15.4 us (2%)
    ppermute x60, waiting for transfers between devices, swapped(): return lax.ppermute(value, axis, [(i, i ^ mask) for i in range(size)])  288 us
    all_gather x5, waiting for transfers between devices, spread_cols(): return lax.all_gather(value, 'col', axis=0, tiled=False)  86.4 us
    ppermute x7, waiting for transfers between devices, over_dp(): lax.ppermute(low, 'dp', [(i, (i + step) % size) for i in range(size)])  85.7 us
    pallas_call x2, Pallas kernels, feed_forward(): pl.pallas_call(functools.partial(ff_kernel, count, bool(before)), out_sha...  83.7 us
    dot_general x24, matrix products, dot(): return lax.dot_general(left, right, dims, preferred_element_type=F32)  78 us
    ppermute x60, starting transfers between devices, swapped(): return lax.ppermute(value, axis, [(i, i ^ mask) for i in range(size)])  38 us
    pallas_call x1, Pallas kernels, attend_back(): pl.pallas_call(functools.partial(attend_back_kernel, tile), out_shape=(sh...  37.5 us
    all_gather x1, blocking collectives, body(): lax.all_gather(jnp.stack([attn_gain, mlp_gain]), ('row', 'col'), axis=1,...  34 us
  transfers between devices with their start and end apart: 77, of which 30 were waited for; matrix products, arithmetic and copies ran while one was open for 13% of the time, Pallas kernels for 23%

profile of v6, /device:TPU:0, one launch (start us, length us, event | category | flops | bytes accessed | tf_op | source)
XLA Modules:
  0.0 941.1 jit_solution(4350278627452023859)
XLA Ops:
  11.8 7.4 collective-permute-done.5
  19.2 7.2 collective-permute-done.4
  34.9 34.0 %all-gather.5 = f32[16,160,2]{1,2,0:T(2,128)S(1)} all-gather(f32[1,160,2]{1,2,0:T(2,128)S(1)} %maximum_bitcast_fusion.1), channel_id=1, replica_groups=mesh['dp'=2,'row'=4,'col'=4] {'row','col'}, dimensions={0}, use_global_device_ids=true | all-gather | bytes 21760 | tf_op jit(solution)/shard_map/all_gather | solution.py:747
  69.1 34.5 %collective-permute-done.2 = bf16[160,1024]{1,0:T(8,128)(2,1)S(1)} collective-permute-done((bf16[160,1024]{1,0:T(8,128)(2,1)}, bf16[160,1024]{1,0:T(8,128)(2,1)S(1)}, u32[]{:S(2)}, u32[]{:S(2)}) %collective-permute-start.2) | collective-permute-done | bytes 327712 | tf_op jit(solution)/shard_map/ppermute | solution.py:35
  114.3 8.7 collective-permute-done.10.refs_6_
  125.1 14.1 %collective-permute-done.12.refs_2_.refs_3_ = bf16[640,640]{1,0:T(8,128)(2,1)} collective-permute-done((bf16[640,640]{1,0:T(8,128)(2,1)}, bf16[640,640]{1,0:T(8,128)(2,1)}, u32[]{:S(2)}, u32[]{:S(2)}) %collective-permute-start.12) | collective-permute-done | bytes 819232 | tf_op jit(solution)/shard_map/ppermute | solution.py:35
  140.9 13.2 %qkv_project.1 = (bf16[4,640,1024]{2,1,0:T(8,128)(2,1)}, f32[1,1024]{1,0:T(1,128)}, bf16[2,480,1024]{2,1,0:T(8,128)(2,1)}) custom-call(bf16[4,4,160,1024]{3,2,1,0:T(8,128)(2,1)} %bitcast.272, f32[4,4,160,1]{3,2,1,0:T(8,128)} %copy.66.gain_ref, f32[40,1024]{1,0:T(8,128)} %get-tuple-element.135.cos_ref, f32[40,1024]{1,0:T(8,128)} %get-tuple-element.136.sin_ref, ...), custom_call_target="tpu_custom_call" | custom-call | flops 12000000000 | tf_op jit(solution)/shard_map/qkv_project/pallas_call | solution.py:157
  159.7 28.0 %attend.1 = (bf16[320,1024]{1,0:T(8,128)(2,1)}, bf16[320,1024]{1,0:T(8,128)(2,1)}, f32[2,4,1,1024]{3,2,1,0:T(1,128)}) custom-call(s32[1]{0:T(128)} %bitcast.parity_ref, bf16[480,1024]{1,0:T(8,128)(2,1)} %get-tuple-element.258.own_ref, bf16[480,1024]{1,0:T(8,128)(2,1)} %collective-permute-done.15.other_ref, s32[1,1024]{1,0:T(1,128)} %bitcast.264, ...), custom_call_target="tpu_custom_call" | custom-call | flops 27000000512 | tf_op jit(solution)/shard_map/attend/pallas_call | solution.py:249
  187.9 19.6 %collective-permute-done.19.refs_6_ = bf16[1728,640]{1,0:T(8,128)(2,1)} collective-permute-done((bf16[1728,640]{1,0:T(8,128)(2,1)}, bf16[1728,640]{1,0:T(8,128)(2,1)}, u32[]{:S(2)}, u32[]{:S(2)}) %collective-permute-start.19) | collective-permute-done | bytes 2211872 | tf_op jit(solution)/shard_map/ppermute | solution.py:35
  208.9 10.2 %mix_out.1 = bf16[4,4,160,1024]{3,2,1,0:T(8,128)(2,1)} custom-call(s32[1]{0:T(128)} %bitcast.parity_ref, bf16[320,1024]{1,0:T(8,128)(2,1)} %get-tuple-element.224.own_ref.own_out, bf16[320,1024]{1,0:T(8,128)(2,1)} %copy-done.20, bf16[640,640]{1,0:T(8,128)(2,1)} %refs_1_, bf16[640,640]{1,0:T(8,128)(2,1)} %copy-done.36, ...), custom_call_target="tpu_custom_call" | custom-call | flops 10000000000 | tf_op jit(solution)/shard_map/mix_out/pallas_call | solution.py:424
  219.1 19.5 %all-gather.14.cloned.1.call-done = bf16[16,160,1024]{2,1,0:T(8,128)(2,1)} async-done(((bf16[4,160,1024]{2,1,0:T(8,128)(2,1)}), bf16[16,160,1024]{2,1,0:T(8,128)(2,1)}) %all-gather.14.cloned.1.call-update) | async-done | bytes 5242896 | tf_op jit(solution)/shard_map/all_gather | solution.py:676
  240.2 48.7 %collective-permute-done.25.refs_10_.refs_2_ = bf16[1728,640]{1,0:T(8,128)(2,1)S(1)} collective-permute-done((bf16[1728,640]{1,0:T(8,128)(2,1)}, bf16[1728,640]{1,0:T(8,128)(2,1)S(1)}, u32[]{:S(2)}, u32[]{:S(2)}) %collective-permute-start.25) | collective-permute-done | bytes 2211872 | tf_op jit(solution)/shard_map/ppermute | solution.py:35
  291.4 6.4 collective-permute-done.26.refs_11_.refs_3_
  308.8 24.2 %reduce-scatter.6.cloned.1.call-done = bf16[1,4,160,1024]{3,2,1,0:T(8,128)(2,1)} async-done(((bf16[4,4,160,1024]{3,2,1,0:T(8,128)(2,1)}), bf16[1,4,160,1024]{3,2,1,0:T(8,128)(2,1)}) %reduce-scatter.6.cloned.1.call-update) | async-done | bytes 1310736 | tf_op jit(solution)/shard_map/reduce_scatter | solution.py:680
  337.8 53.8 %all-gather.16.cloned.1.call-done = bf16[16,160,512]{2,1,0:T(8,128)(2,1)} async-done(((bf16[4,160,512]{2,1,0:T(8,128)(2,1)}), bf16[16,160,512]{2,1,0:T(8,128)(2,1)}) %all-gather.16.cloned.1.call-update) | async-done | bytes 2621456 | tf_op jit(solution)/shard_map/all_gather | solution.py:676
  391.6 41.9 %feed_forward.2 = (bf16[4,640,1024]{2,1,0:T(8,128)(2,1)}, bf16[4,640,1024]{2,1,0:T(8,128)(2,1)}, bf16[1728,1024]{1,0:T(8,128)(2,1)}, bf16[1728,1024]{1,0:T(8,128...) custom-call(bf16[4,4,160,512]{3,2,1,0:T(8,128)(2,1)} %bitcast.278, ...), custom_call_target="tpu_custom_call" | custom-call | flops 41999998976 | tf_op jit(solution)/shard_map/feed_forward/pallas_call | solution.py:563
  433.5 13.1 %all-gather.18.cloned.1.call-done = bf16[16,160,512]{2,1,0:T(8,128)(2,1)} async-done(((bf16[4,160,512]{2,1,0:T(8,128)(2,1)}), bf16[16,160,512]{2,1,0:T(8,128)(2,1)}) %all-gather.18.cloned.1.call-update) | async-done | bytes 2621456 | tf_op jit(solution)/shard_map/all_gather | solution.py:676
  446.6 41.8 %feed_forward.3 = (bf16[4,640,1024]{2,1,0:T(8,128)(2,1)}, bf16[4,640,1024]{2,1,0:T(8,128)(2,1)}, bf16[1728,1024]{1,0:T(8,128)(2,1)}, bf16[1728,1024]{1,0:T(8,128...) custom-call(bf16[4,4,160,512]{3,2,1,0:T(8,128)(2,1)} %bitcast.277, ...), custom_call_target="tpu_custom_call", output_to_operand_aliasing={{0}: (15, {}), {1}: (16, {}), {2}: (17, {}), {3}: (18, {}),... | custom-call | flops 41999998976 | tf_op jit(solution)/shard_map/feed_forward/pallas_call | solution.py:563
  488.5 6.9 convolution_convert_fusion.10
  547.9 8.0 collective-permute-done.33
  562.4 69.6 %collective-permute-done.34 = bf16[864,640]{1,0:T(8,128)(2,1)S(1)} collective-permute-done((bf16[864,640]{1,0:T(8,128)(2,1)}, bf16[864,640]{1,0:T(8,128)(2,1)S(1)}, u32[]{:S(2)}, u32[]{:S(2)}) %collective-permute-start.34) | collective-permute-done | bytes 1105952 | tf_op jit(solution)/shard_map/ppermute | solution.py:35
  639.4 16.5 %fan_out.1 = bf16[4,4,160,1024]{3,2,1,0:T(8,128)(2,1)} custom-call(bf16[1728,1024]{1,0:T(8,128)(2,1)} %get-tuple-element.188.x_ref, bf16[1728,640]{1,0:T(8,128)(2,1)} %refs_0_.2, bf16[1728,640]{1,0:T(8,128)(2,1)} %copy-done.30, bf16[1728,640]{1,0:T(8,128)(2,1)} %copy-done.29, bf16[1728,640]{1,0:T(8,128)(2,1)} %copy-done.31), custom_call_target="tpu_custom_call" | custom-call | flops 16999999488 | tf_op jit(solution)/shard_map/fan_out/pallas_call | solution.py:485
  657.4 29.0 %collective-permute-done.35 = bf16[1728,640]{1,0:T(8,128)(2,1)} collective-permute-done((bf16[1728,640]{1,0:T(8,128)(2,1)}, bf16[1728,640]{1,0:T(8,128)(2,1)}, u32[]{:S(2)}, u32[]{:S(2)}) %collective-permute-start.35) | collective-permute-done | bytes 2211872 | tf_op jit(solution)/shard_map/ppermute | solution.py:688
  690.9 8.6 mix_back.1
  699.5 31.8 %collective-permute-done.39 = bf16[1728,640]{1,0:T(8,128)(2,1)} collective-permute-done((bf16[1728,640]{1,0:T(8,128)(2,1)}, bf16[1728,640]{1,0:T(8,128)(2,1)}, u32[]{:S(2)}, u32[]{:S(2)}) %collective-permute-start.39) | collective-permute-done | bytes 2211872 | tf_op jit(solution)/shard_map/ppermute | solution.py:688
  740.0 37.5 %attend_back.1 = (bf16[480,1024]{1,0:T(8,128)(2,1)}, bf16[480,1024]{1,0:T(8,128)(2,1)}) custom-call(s32[1]{0:T(128)} %bitcast.parity_ref, bf16[480,1024]{1,0:T(8,128)(2,1)} %get-tuple-element.258.own_ref, bf16[480,1024]{1,0:T(8,128)(2,1)} %collective-permute-done.15.other_ref, bf16[320,1024]{1,0:T(8,128)(2,1)} %get-tuple-element.224.own_ref.own_out, ...), custom_call_target="tpu_custom_call" | custom-call | flops 36999999488 | tf_op jit(solution)/shard_map/attend_back/pallas_call | solution.py:361
  777.5 8.3 collective-permute-done.41
  789.4 17.5 %qkv_back.1 = (bf16[640,1024]{1,0:T(8,128)(2,1)}, bf16[320,1024]{1,0:T(8,128)(2,1)}, bf16[4,4,160,1024]{3,2,1,0:T(8,128)(2,1)}, f32[4,4,160,1]{3,2,1,0:T(8,128)}) custom-call(s32[1]{0:T(128)} %bitcast.parity_ref, bf16[4,4,160,1024]{3,2,1,0:T(8,128)(2,1)} %bitcast.273, f32[4,4,160,1]{3,2,1,0:T(8,128)} %copy.66.gain_ref, ...), custom_call_target="tpu_custom_call" | custom-call | flops 16999999488 | tf_op jit(solution)/shard_map/qkv_back/pallas_call | solution.py:653
  858.0 19.2 %collective-permute-done.59 = f32[2,160]{1,0:T(2,128)S(1)} collective-permute-done((f32[2,160]{1,0:T(2,128)S(1)}, f32[2,160]{1,0:T(2,128)S(1)}, u32[]{:S(2)}, u32[]{:S(2)}) %collective-permute-start.59) | collective-permute-done | bytes 1312 | tf_op jit(solution)/shard_map/ppermute | solution.py:35
  885.0 6.4 collective-permute-done.62
  897.2 14.9 %collective-permute-done.49 = bf16[640,640]{1,0:T(8,128)(2,1)S(1)} collective-permute-done((bf16[640,640]{1,0:T(8,128)(2,1)S(1)}, bf16[640,640]{1,0:T(8,128)(2,1)S(1)}, u32[]{:S(2)}, u32[]{:S(2)}) %collective-permute-start.49) | collective-permute-done | bytes 819232 | tf_op jit(solution)/shard_map/ppermute | solution.py:688
  919.2 7.0 collective-permute-done.65
  (341 shorter events, 218.1 us)
Async XLA Ops:
  7.2 132.0 %all-gather.12.cloned.1.call-start = ((), (), s32[]{:S(2)}) async-start(), calls=%async_computation.10 | async-start | bytes 6553600 | tf_op jit(solution)/shard_map/all_gather | solution.py:676
  27.7 210.9 %all-gather.14.cloned.1.call-start = ((), (), s32[]{:S(2)}) async-start(), calls=%async_computation.11 | async-start | bytes 6553600 | tf_op jit(solution)/shard_map/all_gather | solution.py:676
  27.8 111.4 %collective-permute-start.13 = (bf16[1728,640]{1,0:T(8,128)(2,1)}, bf16[1728,640]{1,0:T(8,128)(2,1)}, u32[]{:S(2)}, u32[]{:S(2)}) collective-permute-start(bf16[1728,640]{1,0:T(8,128)(2,1)} %bitcast.279), channel_id=1, source_target_pairs={{0,8},{4,12},{8,0},{12,4},{1,9},{5,13},{9,1},{13,5},{2,10},{6,14},... | collective-permute-start | bytes 6635528 | tf_op jit(solution)/shard_map/ppermute | solution.py:35
  30.1 82.6 %collective-permute-start.7 = (bf16[640,640]{1,0:T(8,128)(2,1)}, bf16[640,640]{1,0:T(8,128)(2,1)}, u32[]{:S(2)}, u32[]{:S(2)}) collective-permute-start(bf16[640,640]{1,0:T(8,128)(2,1)} %refs_0_.3), channel_id=1, source_target_pairs={{0,8},{4,12},{8,0},{12,4},{1,9},{5,13},{9,1},{13,5},{2,10},{6,14},... | collective-permute-start | bytes 2457608 | tf_op jit(solution)/shard_map/ppermute | solution.py:35
  31.2 72.5 %collective-permute-start.2 = (bf16[160,1024]{1,0:T(8,128)(2,1)}, bf16[160,1024]{1,0:T(8,128)(2,1)S(1)}, u32[]{:S(2)}, u32[]{:S(2)}) collective-permute-start(bf16[160,1024]{1,0:T(8,128)(2,1)} %get-tuple-element.275), channel_id=1, source_target_pairs={{0,12},{4,8},{8,4},{12,0},{1,13},{5,9},{9,5},{13,1},{2,14},{6,10},... | collective-permute-start | bytes 983048 | tf_op jit(solution)/shard_map/ppermute | solution.py:35
  32.3 78.2 %collective-permute-start.1 = (bf16[160,1024]{1,0:T(8,128)(2,1)}, bf16[160,1024]{1,0:T(8,128)(2,1)S(1)}, u32[]{:S(2)}, u32[]{:S(2)}) collective-permute-start(bf16[160,1024]{1,0:T(8,128)(2,1)} %get-tuple-element.276), channel_id=1, source_target_pairs={{0,8},{4,12},{8,0},{12,4},{1,9},{5,13},{9,1},{13,5},{2,10},{6,14},... | collective-permute-start | bytes 983048 | tf_op jit(solution)/shard_map/ppermute | solution.py:35
  34.4 78.0 %collective-permute-start.9 = (bf16[320,640]{1,0:T(8,128)(2,1)S(1)}, bf16[320,640]{1,0:T(8,128)(2,1)}, u32[]{:S(2)}, u32[]{:S(2)}) collective-permute-start(bf16[320,640]{1,0:T(8,128)(2,1)S(1)} %pad_maximum_fusion.5.refs_4_), channel_id=1, source_target_pairs={{0,4},{4,0},{8,12},{12,8},{1,5},{5,1},{9,13},{13,9},{2,6},{6,2},{1... | collective-permute-start | bytes 1228808 | tf_op jit(solution)/shard_map/ppermute | solution.py:35
  112.4 26.9 %collective-permute-start.12 = (bf16[640,640]{1,0:T(8,128)(2,1)}, bf16[640,640]{1,0:T(8,128)(2,1)}, u32[]{:S(2)}, u32[]{:S(2)}) collective-permute-start(bf16[640,640]{1,0:T(8,128)(2,1)} %refs_1_), channel_id=1, source_target_pairs={{0,8},{4,12},{8,0},{12,4},{1,9},{5,13},{9,1},{13,5},{2,10},{6,14},... | collective-permute-start | bytes 2457608 | tf_op jit(solution)/shard_map/ppermute | solution.py:35
  139.3 193.8 %reduce-scatter.6.cloned.1.call-start = ((), (), s32[]{:S(2)}) async-start(), calls=%async_computation.5 | async-start | bytes 6553600 | tf_op jit(solution)/shard_map/reduce_scatter | solution.py:680
  156.7 50.8 %collective-permute-start.19 = (bf16[1728,640]{1,0:T(8,128)(2,1)}, bf16[1728,640]{1,0:T(8,128)(2,1)}, u32[]{:S(2)}, u32[]{:S(2)}) collective-permute-start(bf16[1728,640]{1,0:T(8,128)(2,1)} %bitcast.32.refs_4_), channel_id=1, source_target_pairs={{0,8},{4,12},{8,0},{12,4},{1,9},{5,13},{9,1},{13,5},{2,10},{6,14},... | collective-permute-start | bytes 6635528 | tf_op jit(solution)/shard_map/ppermute | solution.py:35
  159.2 48.4 %collective-permute-start.17 = (bf16[640,640]{1,0:T(8,128)(2,1)}, bf16[640,640]{1,0:T(8,128)(2,1)S(1)}, u32[]{:S(2)}, u32[]{:S(2)}) collective-permute-start(bf16[640,640]{1,0:T(8,128)(2,1)} %refs_1_), channel_id=1, source_target_pairs={{0,4},{4,0},{8,12},{12,8},{1,5},{5,1},{9,13},{13,9},{2,6},{6,2},{1... | collective-permute-start | bytes 2457608 | tf_op jit(solution)/shard_map/ppermute | solution.py:35
  159.4 48.1 %collective-permute-start.18 = (bf16[640,640]{1,0:T(8,128)(2,1)}, bf16[640,640]{1,0:T(8,128)(2,1)S(1)}, u32[]{:S(2)}, u32[]{:S(2)}) collective-permute-start(bf16[640,640]{1,0:T(8,128)(2,1)} %collective-permute-done.12.refs_2_.refs_3_), channel_id=1, source_target_pairs={{0,4},{4,0},{8,12},{12,8},{1,5},{5,1},{9,13},{13,9},{2,6},{6,2},{1... | collective-permute-start | bytes 2457608 | tf_op jit(solution)/shard_map/ppermute | solution.py:35
  238.6 153.0 %all-gather.16.cloned.1.call-start = ((), (), s32[]{:S(2)}) async-start(), calls=%async_computation.12 | async-start | bytes 3276800 | tf_op jit(solution)/shard_map/all_gather | solution.py:676
  238.7 50.3 %collective-permute-start.25 = (bf16[1728,640]{1,0:T(8,128)(2,1)}, bf16[1728,640]{1,0:T(8,128)(2,1)S(1)}, u32[]{:S(2)}, u32[]{:S(2)}) collective-permute-start(bf16[1728,640]{1,0:T(8,128)(2,1)} %refs_0_.2), channel_id=1, source_target_pairs={{0,8},{4,12},{8,0},{12,4},{1,9},{5,13},{9,1},{13,5},{2,10},{6,14},... | collective-permute-start | bytes 6635528 | tf_op jit(solution)/shard_map/ppermute | solution.py:35
  240.2 51.1 %collective-permute-start.24 = (bf16[1728,640]{1,0:T(8,128)(2,1)}, bf16[1728,640]{1,0:T(8,128)(2,1)S(1)}, u32[]{:S(2)}, u32[]{:S(2)}) collective-permute-start(bf16[1728,640]{1,0:T(8,128)(2,1)} %refs_0_.2), channel_id=1, source_target_pairs={{0,4},{4,0},{8,12},{12,8},{1,5},{5,1},{9,13},{13,9},{2,6},{6,2},{1... | collective-permute-start | bytes 6635528 | tf_op jit(solution)/shard_map/ppermute | solution.py:35
  336.1 110.5 %all-gather.18.cloned.1.call-start = ((), (), s32[]{:S(2)}) async-start(), calls=%async_computation.13 | async-start | bytes 3276800 | tf_op jit(solution)/shard_map/all_gather | solution.py:676
  337.8 218.1 %reduce-scatter.8.cloned.1.call-start = ((), (), s32[]{:S(2)}) async-start(), calls=%async_computation.6 | async-start | bytes 3276800 | tf_op jit(solution)/shard_map/reduce_scatter | solution.py:680
  433.5 122.4 %reduce-scatter.10.cloned.1.call-start = ((), (), s32[]{:S(2)}) async-start(), calls=%async_computation.7 | async-start | bytes 3276800 | tf_op jit(solution)/shard_map/reduce_scatter | solution.py:680
  501.4 189.2 %all-gather.20.cloned.1.call-start = ((), (), s32[]{:S(2)}) async-start(), calls=%async_computation.14 | async-start | bytes 6553600 | tf_op jit(solution)/shard_map/all_gather | solution.py:676
  558.7 258.6 %reduce-scatter.12.cloned.1.call-start = ((), (), s32[]{:S(2)}) async-start(), calls=%async_computation.8 | async-start | bytes 6553600 | tf_op jit(solution)/shard_map/reduce_scatter | solution.py:680
  558.8 77.9 %collective-permute-start.38 = (bf16[1728,640]{1,0:T(8,128)(2,1)}, bf16[1728,640]{1,0:T(8,128)(2,1)S(1)}, u32[]{:S(2)}, u32[]{:S(2)}) collective-permute-start(bf16[1728,640]{1,0:T(8,128)(2,1)} %add_convert_fusion.4), channel_id=1, source_target_pairs={{0,8},{4,12},{8,0},{12,4},{1,9},{5,13},{9,1},{13,5},{2,10},{6,14},... | collective-permute-start | bytes 6635528 | tf_op jit(solution)/shard_map/ppermute | solution.py:35
  560.4 71.6 %collective-permute-start.34 = (bf16[864,640]{1,0:T(8,128)(2,1)}, bf16[864,640]{1,0:T(8,128)(2,1)S(1)}, u32[]{:S(2)}, u32[]{:S(2)}) collective-permute-start(bf16[864,640]{1,0:T(8,128)(2,1)} %get-tuple-element.200), channel_id=1, source_target_pairs={{0,8},{4,12},{8,0},{12,4},{1,9},{5,13},{9,1},{13,5},{2,10},{6,14},... | collective-permute-start | bytes 3317768 | tf_op jit(solution)/shard_map/ppermute | solution.py:35
  635.1 51.3 %collective-permute-start.35 = (bf16[1728,640]{1,0:T(8,128)(2,1)}, bf16[1728,640]{1,0:T(8,128)(2,1)}, u32[]{:S(2)}, u32[]{:S(2)}) collective-permute-start(bf16[1728,640]{1,0:T(8,128)(2,1)} %pad_maximum_fusion), channel_id=1, source_target_pairs={{0,16},{16,0},{1,17},{17,1},{2,18},{18,2},{3,19},{19,3},{4,20},{20... | collective-permute-start | bytes 6635528 | tf_op jit(solution)/shard_map/ppermute | solution.py:688
  638.6 92.7 %collective-permute-start.39 = (bf16[1728,640]{1,0:T(8,128)(2,1)}, bf16[1728,640]{1,0:T(8,128)(2,1)}, u32[]{:S(2)}, u32[]{:S(2)}) collective-permute-start(bf16[1728,640]{1,0:T(8,128)(2,1)} %add_convert_fusion.1), channel_id=1, source_target_pairs={{0,16},{16,0},{1,17},{17,1},{2,18},{18,2},{3,19},{19,3},{4,20},{20... | collective-permute-start | bytes 6635528 | tf_op jit(solution)/shard_map/ppermute | solution.py:688
  656.0 80.2 %collective-permute-start.36 = (bf16[1728,640]{1,0:T(8,128)(2,1)}, bf16[1728,640]{1,0:T(8,128)(2,1)}, u32[]{:S(2)}, u32[]{:S(2)}) collective-permute-start(bf16[1728,640]{1,0:T(8,128)(2,1)} %add_convert_fusion.2), channel_id=1, source_target_pairs={{0,8},{4,12},{8,0},{12,4},{1,9},{5,13},{9,1},{13,5},{2,10},{6,14},... | collective-permute-start | bytes 6635528 | tf_op jit(solution)/shard_map/ppermute | solution.py:35
  690.6 222.8 %reduce-scatter.14.cloned.1.call-start = ((), (), s32[]{:S(2)}) async-start(), calls=%async_computation.9 | async-start | bytes 6553600 | tf_op jit(solution)/shard_map/reduce_scatter | solution.py:680
  699.5 38.8 %collective-permute-start.37 = (bf16[320,1024]{1,0:T(8,128)(2,1)}, bf16[320,1024]{1,0:T(8,128)(2,1)}, u32[]{:S(2)}, u32[]{:S(2)}) collective-permute-start(bf16[320,1024]{1,0:T(8,128)(2,1)} %get-tuple-element.209), channel_id=1, source_target_pairs={{0,4},{4,0},{8,12},{12,8},{1,5},{5,1},{9,13},{13,9},{2,6},{6,2},{1... | collective-permute-start | bytes 1966088 | tf_op jit(solution)/shard_map/ppermute | solution.py:35
  738.3 47.5 %collective-permute-start.41 = (bf16[1728,640]{1,0:T(8,128)(2,1)S(1)}, bf16[1728,640]{1,0:T(8,128)(2,1)S(1)}, u32[]{:S(2)}, u32[]{:S(2)}) collective-permute-start(bf16[1728,640]{1,0:T(8,128)(2,1)S(1)} %add_convert_fusion), channel_id=1, source_target_pairs={{0,16},{16,0},{1,17},{17,1},{2,18},{18,2},{3,19},{19,3},{4,20},{20... | collective-permute-start | bytes 6635528 | tf_op jit(solution)/shard_map/ppermute | solution.py:688
  841.2 41.4 %collective-permute-start.48 = (bf16[640,640]{1,0:T(8,128)(2,1)}, bf16[640,640]{1,0:T(8,128)(2,1)S(1)}, u32[]{:S(2)}, u32[]{:S(2)}) collective-permute-start(bf16[640,640]{1,0:T(8,128)(2,1)} %add_convert_fusion.14), channel_id=1, source_target_pairs={{0,8},{4,12},{8,0},{12,4},{1,9},{5,13},{9,1},{13,5},{2,10},{6,14},... | collective-permute-start | bytes 2457608 | tf_op jit(solution)/shard_map/ppermute | solution.py:35
  841.7 40.8 %collective-permute-start.50 = (bf16[320,640]{1,0:T(8,128)(2,1)}, bf16[320,640]{1,0:T(8,128)(2,1)S(1)}, u32[]{:S(2)}, u32[]{:S(2)}) collective-permute-start(bf16[320,640]{1,0:T(8,128)(2,1)} %add_convert_fusion.19), channel_id=1, source_target_pairs={{0,8},{4,12},{8,0},{12,4},{1,9},{5,13},{9,1},{13,5},{2,10},{6,14},... | collective-permute-start | bytes 1228808 | tf_op jit(solution)/shard_map/ppermute | solution.py:35
  853.2 42.5 %collective-permute-start.53 = (bf16[640,640]{1,0:T(8,128)(2,1)S(1)}, bf16[640,640]{1,0:T(8,128)(2,1)S(1)}, u32[]{:S(2)}, u32[]{:S(2)}) collective-permute-start(bf16[640,640]{1,0:T(8,128)(2,1)S(1)} %add_convert_fusion.12), channel_id=1, source_target_pairs={{0,16},{16,0},{1,17},{17,1},{2,18},{18,2},{3,19},{19,3},{4,20},{20... | collective-permute-start | bytes 2457608 | tf_op jit(solution)/shard_map/ppermute | solution.py:688
  884.4 27.7 %collective-permute-start.49 = (bf16[640,640]{1,0:T(8,128)(2,1)S(1)}, bf16[640,640]{1,0:T(8,128)(2,1)S(1)}, u32[]{:S(2)}, u32[]{:S(2)}) collective-permute-start(bf16[640,640]{1,0:T(8,128)(2,1)S(1)} %add_convert_fusion.13), channel_id=1, source_target_pairs={{0,16},{16,0},{1,17},{17,1},{2,18},{18,2},{3,19},{19,3},{4,20},{20... | collective-permute-start | bytes 2457608 | tf_op jit(solution)/shard_map/ppermute | solution.py:688
  (96 other events, 2329.1 us)
Sparse Core Ops, SparseCore 0:
  27.9 100.4 all-gather.11
  139.4 99.1 all-gather.13
  240.9 92.1 reduce-scatter.5
  336.3 55.3 all-gather.15
  393.0 53.5 all-gather.17
  449.4 50.8 reduce-scatter.7
  502.6 51.7 reduce-scatter.9
  558.9 96.6 all-gather.19
  690.8 92.5 reduce-scatter.11
  817.5 93.5 reduce-scatter.13

commit v7 on v4

--- a/solution.py
+++ b/solution.py
@@ -75,6 +75,10 @@
 
 def params(mib=58):
     return pltpu.CompilerParams(vmem_limit_bytes=mib * 1024 * 1024)
+
+
+def takes(micros):
+    return pl.CostEstimate(flops=int(micros * 0.1e9), transcendentals=0, bytes_accessed=0)
 
 
 def shape(dims, dtype):
@@ -152,6 +156,7 @@
         ),
         compiler_params=params(),
         name="qkv_project",
+        cost_estimate=takes(12),
     )(x, gain, cosine, sine, *q_w, *kv_w)
 
 
@@ -256,6 +261,7 @@
         ],
         compiler_params=params(),
         name="attend",
+        cost_estimate=takes(27),
     )(parity, own, other, seg[None, :], seg[:, None])
 
 
@@ -372,6 +378,7 @@
         ],
         compiler_params=params(),
         name="attend_back",
+        cost_estimate=takes(37),
     )(
         parity,
         own,
@@ -413,6 +420,7 @@
         in_specs=[SMALL] + [vmem] * (2 + count),
         compiler_params=params(),
         name="mix_out",
+        cost_estimate=takes(10),
     )(parity, own, other, *weights)
 
 
@@ -451,6 +459,7 @@
         in_specs=[SMALL] + [vmem] * (parts + count),
         compiler_params=params(),
         name="mix_back",
+        cost_estimate=takes(9),
     )(parity, *x_parts, *weights)
 
 
@@ -471,6 +480,7 @@
         out_shape=shape((cols, count, piece, x.shape[1]), BF),
         compiler_params=params(),
         name="fan_out",
+        cost_estimate=takes(17),
     )(x, *weights)
 
 
@@ -575,6 +585,7 @@
         input_output_aliases={first + i: i for i in range(len(before))},
         compiler_params=params(60),
         name="feed_forward",
+        cost_estimate=takes(42),
     )(x, g, gain, *gate_w, *up_w, *down_w, *before)
 
 
@@ -643,6 +654,7 @@
         in_specs=[SMALL] + [vmem] * (8 + 2 * count),
         compiler_params=params(),
         name="qkv_back",
+        cost_estimate=takes(17),
     )(parity, x, gain, scale, cosine, sine, sets, own, other, *q_w, *kv_w)
 
 
@@ -798,12 +810,12 @@
     residual_grad_own = grad_own.astype(F32) + jnp.concatenate(share_sums, axis=2).astype(F32)
     down_total = fold(down_grads, "row", far)[0]
     gate_total = fold(gate_grads, "row", far)[0]
-    down_total_all = over_dp(down_total)
 
     mix_cols = spread_cols(residual_grad_own.astype(BF))
     ff_part = fan_out(listed(down_blocks), act, cols)
+    down_total = over_dp(down_total)
     mix_cols, ff_part, down_total, gate_total, up_grads = together(
-        mix_cols, ff_part, down_total_all, gate_total, up_grads
+        mix_cols, ff_part, down_total, gate_total, up_grads
     )
     up_total = fold(up_grads, "row", far)[0]
     gate_total = over_dp(gate_total)
@@ -814,8 +826,11 @@
         own_core, own_set, other_set, attn_mine, attn_send, grad_mine, grad_other, lse, seg
     )
     back_other = swapped(back_send, "row", 1)
-    back_other, up_total, gate_total = together(back_other, up_total, gate_total)
-    up_total = over_dp(up_total)
+    back_other, up_total, gate_total, down_total = together(
+        back_other, up_total, gate_total, down_total
+    )
+    cut = up_total.shape[0] * 5 // 9 // 16 * 16
+    up_head, up_tail = over_dp(up_total[:cut]), over_dp(up_total[cut:])
     dq, dkv, share, gain_share_one = qkv_back(
         own_core,
         source,
@@ -829,35 +844,39 @@
         listed(q_blocks),
         listed(kv_blocks),
     )
-    share, ff_sum = together(share, ff_sum)
-    input_sum = sum_cols(share)
-    output_own = (residual_own + ff_sum.astype(F32)).astype(BF)
-    layer_output = all_tokens(output_own)
-
-    share, dq, dkv, mix_rows = together(share, dq, dkv, mix_rows)
-    bits = near + far[::-1]
-    q_grads = {k: dot(norm_one[k], dq, NT).astype(BF) for k in range(count)}
-    kv_grads = {k: dot(dkv, norm_one[k], NT).astype(BF) for k in range(count)}
+    share, attn_mine, mix_rows, up_head = together(share, attn_mine, mix_rows, up_head)
     attn_low = jnp.concatenate(
         [
             jnp.where(parity == 0, attn_mine, attn_other),
             jnp.where(parity == 0, attn_other, attn_mine),
         ]
     )
-    mix_grads = {k: dot(attn_low, mix_rows[k], NT).astype(BF) for k in range(count)}
-    q_total = over_dp(fold(q_grads, "row", bits)[0])
-    kv_total = over_dp(fold(kv_grads, "row", bits)[0])
-    mix_total = over_dp(fold(mix_grads, "row", bits)[0])
-
+    mix_near = {k: dot(attn_low, mix_rows[k], NT).astype(BF) for k in range(count)}
+    mix_near = fold(mix_near, "row", near)
+    share, ff_sum, mix_near = together(share, ff_sum, mix_near)
+    input_sum = sum_cols(share)
+
+    share, dq, dkv = together(share, dq, dkv)
+    mix_total = over_dp(fold(mix_near, "row", far)[0])
+    q_near = fold({k: dot(norm_one[k], dq, NT).astype(BF) for k in range(count)}, "row", near)
+    kv_near = fold({k: dot(dkv, norm_one[k], NT).astype(BF) for k in range(count)}, "row", near)
+    ff_sum, gain_share_one, q_near, kv_near = together(ff_sum, gain_share_one, q_near, kv_near)
+    q_total = over_dp(fold(q_near, "row", far)[0])
+    kv_total = over_dp(fold(kv_near, "row", far)[0])
+    output_own = (residual_own + ff_sum.astype(F32)).astype(BF)
+    layer_output = all_tokens(output_own)
+
+    bits = near + far[::-1]
     gain_shares = jnp.stack([gain_share_one[..., 0], gain_share_two[..., 0]], axis=2)
     gain_shares = by_xor(gain_shares, lax.axis_index("col"), 0)
     gain_shares = {c: gain_shares[c] for c in range(cols)}
     gain_shares = fold(gain_shares, "col", near_bits(cols) + far_bits(cols), low=False)[0]
     gain_shares = fold({k: gain_shares[k] for k in range(count)}, "row", bits, low=False)[0]
     gain_totals = over_dp(gain_shares)
-    input_sum, q_total, kv_total, mix_total, up_total, gain_totals, layer_output = together(
-        input_sum, q_total, kv_total, mix_total, up_total, gain_totals, layer_output
-    )
+    input_sum, q_total, kv_total, mix_total, gain_totals, layer_output, up_tail = together(
+        input_sum, q_total, kv_total, mix_total, gain_totals, layer_output, up_tail
+    )
+    up_total = jnp.concatenate([up_head, up_tail])
 
     input_grad = all_tokens((residual_grad_own + input_sum.astype(F32)).astype(BF)).astype(F32)
     kv_rows = kv_total.shape[0] // 2

time: 964 us -> 908 us (0.942)
  waiting for transfers between devices: 498 us -> 431 us
  matrix products: 75.8 us -> 87.3 us
    ppermute x59, waiting for transfers between devices: 291 us -> 261 us  [swapped(): return lax.ppermute(value, axis, [(i, i ^ mask) for i in range(size)])]
    ppermute x7 -> x8, waiting for transfers between devices: 55.3 us -> 31.3 us  [over_dp(): lax.ppermute(low, 'dp', [(i, (i + step) % size) for i in range(size)])]
    reduce_scatter x5, waiting for transfers between devices: 51.2 us -> 35.5 us  [sum_cols(): return lax.psum_scatter(value, 'col', scatter_dimension=0, tiled=False)]
    dot_general x24, matrix products: 75.8 us -> 87.3 us  [dot(): return lax.dot_general(left, right, dims, preferred_element_type=F32)]
  transfers between devices with their start and end apart: 76 -> 77, of which waited for: 37 -> 35; matrix products, arithmetic and copies ran while one was open for 13% -> 16% of each run, Pallas kernels for 23% -> 24%
where the time goes in v7:
time: 908 us; the launch traced here: 900 us
  waiting for transfers between devices  431 us (47%)
  Pallas kernels  216 us (24%)
  matrix products  87.3 us (10%)
  other arithmetic  49.9 us (5%)
  starting transfers between devices  41.4 us (5%)
  blocking collectives  34.2 us (4%)
  local copies, waits for them, and re-layouts  24.7 us (3%)
  between operations  15.4 us (2%)
    ppermute x59, waiting for transfers between devices, swapped(): return lax.ppermute(value, axis, [(i, i ^ mask) for i in range(size)])  261 us
    all_gather x5, waiting for transfers between devices, spread_cols(): return lax.all_gather(value, 'col', axis=0, tiled=False)  102 us
    dot_general x24, matrix products, dot(): return lax.dot_general(left, right, dims, preferred_element_type=F32)  87.3 us
    pallas_call x2, Pallas kernels, feed_forward(): pl.pallas_call(functools.partial(ff_kernel, count, bool(before)), out_sha...  84 us
    pallas_call x1, Pallas kernels, attend_back(): pl.pallas_call(functools.partial(attend_back_kernel, tile), out_shape=(sh...  37.4 us
    reduce_scatter x5, waiting for transfers between devices, sum_cols(): return lax.psum_scatter(value, 'col', scatter_dimension=0, tiled=False)  35.5 us
    all_gather x1, blocking collectives, body(): lax.all_gather(jnp.stack([attn_gain, mlp_gain]), ('row', 'col'), axis=1,...  34.2 us
    ppermute x8, waiting for transfers between devices, over_dp(): lax.ppermute(low, 'dp', [(i, (i + step) % size) for i in range(size)])  31.3 us
  transfers between devices with their start and end apart: 77, of which 35 were waited for; matrix products, arithmetic and copies ran while one was open for 16% of the time, Pallas kernels for 24%

profile of v7, /device:TPU:0, one launch (start us, length us, event | category | flops | bytes accessed | tf_op | source)
XLA Modules:
  0.0 899.8 jit_solution(4700201170231616722)
XLA Ops:
  11.8 7.4 collective-permute-done.5
  19.2 7.2 collective-permute-done.4
  36.7 34.2 %all-gather.5 = f32[16,160,2]{1,2,0:T(2,128)S(1)} all-gather(f32[1,160,2]{1,2,0:T(2,128)S(1)} %maximum_bitcast_fusion.2), channel_id=1, replica_groups=mesh['dp'=2,'row'=4,'col'=4] {'row','col'}, dimensions={0}, use_global_device_ids=true | all-gather | bytes 21760 | tf_op jit(solution)/shard_map/all_gather | solution.py:739
  71.2 33.1 %collective-permute-done.2 = bf16[160,1024]{1,0:T(8,128)(2,1)} collective-permute-done((bf16[160,1024]{1,0:T(8,128)(2,1)}, bf16[160,1024]{1,0:T(8,128)(2,1)}, u32[]{:S(2)}, u32[]{:S(2)}) %collective-permute-start.2) | collective-permute-done | bytes 327712 | tf_op jit(solution)/shard_map/ppermute | solution.py:35
  104.8 6.4 collective-permute-done.1
  115.0 8.6 collective-permute-done.10.refs_6_
  126.2 13.6 %collective-permute-done.12.refs_2_.refs_3_ = bf16[640,640]{1,0:T(8,128)(2,1)} collective-permute-done((bf16[640,640]{1,0:T(8,128)(2,1)}, bf16[640,640]{1,0:T(8,128)(2,1)}, u32[]{:S(2)}, u32[]{:S(2)}) %collective-permute-start.12) | collective-permute-done | bytes 819232 | tf_op jit(solution)/shard_map/ppermute | solution.py:35
  143.0 13.0 %qkv_project.1 = (bf16[4,640,1024]{2,1,0:T(8,128)(2,1)}, f32[1,1024]{1,0:T(1,128)}, bf16[2,480,1024]{2,1,0:T(8,128)(2,1)}) custom-call(bf16[4,4,160,1024]{3,2,1,0:T(8,128)(2,1)} %bitcast.234, f32[4,4,160,1]{3,2,1,0:T(8,128)} %copy.66.gain_ref, f32[40,1024]{1,0:T(8,128)} %get-tuple-element.126.cos_ref, f32[40,1024]{1,0:T(8,128)} %get-tuple-element.127.sin_ref, ...), custom_call_target="tpu_custom_call" | custom-call | flops 1200000000 | tf_op jit(solution)/shard_map/qkv_project/pallas_call | solution.py:150
  162.0 27.8 %attend.1 = (bf16[320,1024]{1,0:T(8,128)(2,1)}, bf16[320,1024]{1,0:T(8,128)(2,1)}, f32[2,4,1,1024]{3,2,1,0:T(1,128)}) custom-call(s32[1]{0:T(128)} %bitcast.parity_ref, bf16[480,1024]{1,0:T(8,128)(2,1)} %get-tuple-element.236.own_ref, bf16[480,1024]{1,0:T(8,128)(2,1)} %collective-permute-done.15.other_ref, s32[1,1024]{1,0:T(1,128)} %bitcast.283, ...), custom_call_target="tpu_custom_call" | custom-call | flops 2700000000 | tf_op jit(solution)/shard_map/attend/pallas_call | solution.py:242
  193.0 10.3 %mix_out.1 = bf16[4,4,160,1024]{3,2,1,0:T(8,128)(2,1)} custom-call(s32[1]{0:T(128)} %bitcast.parity_ref, bf16[320,1024]{1,0:T(8,128)(2,1)} %get-tuple-element.205.own_ref.own_out, bf16[320,1024]{1,0:T(8,128)(2,1)} %copy-done.33, bf16[640,640]{1,0:T(8,128)(2,1)} %refs_1_, bf16[640,640]{1,0:T(8,128)(2,1)} %copy-done.22, ...), custom_call_target="tpu_custom_call" | custom-call | flops 1000000000 | tf_op jit(solution)/shard_map/mix_out/pallas_call | solution.py:417
  203.3 35.9 %all-gather.14.cloned.1.call-done = bf16[16,160,1024]{2,1,0:T(8,128)(2,1)} async-done(((bf16[4,160,1024]{2,1,0:T(8,128)(2,1)}), bf16[16,160,1024]{2,1,0:T(8,128)(2,1)}) %all-gather.14.cloned.1.call-update) | async-done | bytes 5242896 | tf_op jit(solution)/shard_map/all_gather | solution.py:669
  242.3 48.5 %collective-permute-done.25.refs_10_.refs_2_ = bf16[1728,640]{1,0:T(8,128)(2,1)S(1)} collective-permute-done((bf16[1728,640]{1,0:T(8,128)(2,1)S(1)}, bf16[1728,640]{1,0:T(8,128)(2,1)S(1)}, u32[]{:S(2)}, u32[]{:S(2)}) %collective-permute-start.25) | collective-permute-done | bytes 2211872 | tf_op jit(solution)/shard_map/ppermute | solution.py:35
  292.2 6.0 collective-permute-done.26.refs_11_.refs_3_
  308.0 25.7 %reduce-scatter.6.cloned.1.call-done = bf16[1,4,160,1024]{3,2,1,0:T(8,128)(2,1)} async-done(((bf16[4,4,160,1024]{3,2,1,0:T(8,128)(2,1)}), bf16[1,4,160,1024]{3,2,1,0:T(8,128)(2,1)}) %reduce-scatter.6.cloned.1.call-update) | async-done | bytes 1310736 | tf_op jit(solution)/shard_map/reduce_scatter | solution.py:673
  338.9 53.3 %all-gather.16.cloned.1.call-done = bf16[16,160,512]{2,1,0:T(8,128)(2,1)} async-done(((bf16[4,160,512]{2,1,0:T(8,128)(2,1)}), bf16[16,160,512]{2,1,0:T(8,128)(2,1)}) %all-gather.16.cloned.1.call-update) | async-done | bytes 2621456 | tf_op jit(solution)/shard_map/all_gather | solution.py:669
  392.2 42.2 %feed_forward.2 = (bf16[4,640,1024]{2,1,0:T(8,128)(2,1)}, bf16[4,640,1024]{2,1,0:T(8,128)(2,1)}, bf16[1728,1024]{1,0:T(8,128)(2,1)}, bf16[1728,1024]{1,0:T(8,128...) custom-call(bf16[4,4,160,512]{3,2,1,0:T(8,128)(2,1)} %bitcast.265, ...), custom_call_target="tpu_custom_call" | custom-call | flops 4200000000 | tf_op jit(solution)/shard_map/feed_forward/pallas_call | solution.py:556
  434.5 12.7 %all-gather.18.cloned.1.call-done = bf16[16,160,512]{2,1,0:T(8,128)(2,1)} async-done(((bf16[4,160,512]{2,1,0:T(8,128)(2,1)}), bf16[16,160,512]{2,1,0:T(8,128)(2,1)}) %all-gather.18.cloned.1.call-update) | async-done | bytes 2621456 | tf_op jit(solution)/shard_map/all_gather | solution.py:669
  447.2 41.8 %feed_forward.3 = (bf16[4,640,1024]{2,1,0:T(8,128)(2,1)}, bf16[4,640,1024]{2,1,0:T(8,128)(2,1)}, bf16[1728,1024]{1,0:T(8,128)(2,1)}, bf16[1728,1024]{1,0:T(8,128...) custom-call(bf16[4,4,160,512]{3,2,1,0:T(8,128)(2,1)} %bitcast.270, ...), custom_call_target="tpu_custom_call", output_to_operand_aliasing={{0}: (15, {}), {1}: (16, {}), {2}: (17, {}), {3}: (18, {}),... | custom-call | flops 4200000000 | tf_op jit(solution)/shard_map/feed_forward/pallas_call | solution.py:556
  489.1 6.9 convolution_convert_fusion.10
  496.0 5.6 convolution_convert_fusion.8
  527.8 5.6 add_convert_fusion.7
  552.6 9.8 %reduce-scatter.10.cloned.1.call-done = bf16[1,4,160,512]{3,2,1,0:T(8,128)(2,1)} async-done(((bf16[4,4,160,512]{3,2,1,0:T(8,128)(2,1)}), bf16[1,4,160,512]{3,2,1,0:T(8,128)(2,1)}) %reduce-scatter.10.cloned.1.call-update) | async-done | bytes 655376 | tf_op jit(solution)/shard_map/reduce_scatter | solution.py:673
  568.0 49.0 %collective-permute-done.33 = bf16[1728,640]{1,0:T(8,128)(2,1)S(1)} collective-permute-done((bf16[1728,640]{1,0:T(8,128)(2,1)S(1)}, bf16[1728,640]{1,0:T(8,128)(2,1)S(1)}, u32[]{:S(2)}, u32[]{:S(2)}) %collective-permute-start.33) | collective-permute-done | bytes 2211872 | tf_op jit(solution)/shard_map/ppermute | solution.py:35
  620.7 16.6 %fan_out.1 = bf16[4,4,160,1024]{3,2,1,0:T(8,128)(2,1)} custom-call(bf16[1728,1024]{1,0:T(8,128)(2,1)} %get-tuple-element.176.x_ref, bf16[1728,640]{1,0:T(8,128)(2,1)} %refs_0_.2, bf16[1728,640]{1,0:T(8,128)(2,1)} %copy-done.3, bf16[1728,640]{1,0:T(8,128)(2,1)} %copy-done.2, bf16[1728,640]{1,0:T(8,128)(2,1)} %copy-done.4), custom_call_target="tpu_custom_call" | custom-call | flops 1700000000 | tf_op jit(solution)/shard_map/fan_out/pallas_call | solution.py:478
  637.4 25.8 %collective-permute-done.35 = bf16[1728,640]{1,0:T(8,128)(2,1)} collective-permute-done((bf16[1728,640]{1,0:T(8,128)(2,1)}, bf16[1728,640]{1,0:T(8,128)(2,1)}, u32[]{:S(2)}, u32[]{:S(2)}) %collective-permute-start.35) | collective-permute-done | bytes 2211872 | tf_op jit(solution)/shard_map/ppermute | solution.py:35
  676.1 9.6 %mix_back.1 = (bf16[4,640,1024]{2,1,0:T(8,128)(2,1)}, bf16[320,1024]{1,0:T(8,128)(2,1)}, bf16[320,1024]{1,0:T(8,128)(2,1)}) custom-call(s32[1]{0:T(128)} %bitcast.parity_ref, bf16[4,4,160,1024]{3,2,1,0:T(8,128)(2,1)} %bitcast.246, bf16[640,640]{1,0:T(8,128)(2,1)} %refs_1_, bf16[640,640]{1,0:T(8,128)(2,1)} %copy-done.22, ...), custom_call_target="tpu_custom_call" | custom-call | flops 900000000 | tf_op jit(solution)/shard_map/mix_back/pallas_call | solution.py:452
  688.8 37.4 %attend_back.1 = (bf16[480,1024]{1,0:T(8,128)(2,1)}, bf16[480,1024]{1,0:T(8,128)(2,1)}) custom-call(s32[1]{0:T(128)} %bitcast.parity_ref, bf16[480,1024]{1,0:T(8,128)(2,1)} %get-tuple-element.236.own_ref, bf16[480,1024]{1,0:T(8,128)(2,1)} %collective-permute-done.15.other_ref, bf16[320,1024]{1,0:T(8,128)(2,1)} %get-tuple-element.205.own_ref.own_out, ...), custom_call_target="tpu_custom_call" | custom-call | flops 3700000000 | tf_op jit(solution)/shard_map/attend_back/pallas_call | solution.py:354
  734.5 17.5 %qkv_back.1 = (bf16[640,1024]{1,0:T(8,128)(2,1)}, bf16[320,1024]{1,0:T(8,128)(2,1)}, bf16[4,4,160,1024]{3,2,1,0:T(8,128)(2,1)}, f32[4,4,160,1]{3,2,1,0:T(8,128)}) custom-call(s32[1]{0:T(128)} %bitcast.parity_ref, bf16[4,4,160,1024]{3,2,1,0:T(8,128)(2,1)} %bitcast.235, f32[4,4,160,1]{3,2,1,0:T(8,128)} %copy.66.gain_ref, ...), custom_call_target="tpu_custom_call" | custom-call | flops 1700000000 | tf_op jit(solution)/shard_map/qkv_back/pallas_call | solution.py:646
  752.1 10.9 %collective-permute-done.40 = bf16[960,640]{1,0:T(8,128)(2,1)S(1)} collective-permute-done((bf16[960,640]{1,0:T(8,128)(2,1)S(1)}, bf16[960,640]{1,0:T(8,128)(2,1)S(1)}, u32[]{:S(2)}, u32[]{:S(2)}) %collective-permute-start.40) | collective-permute-done | bytes 1228832 | tf_op jit(solution)/shard_map/ppermute | solution.py:681
  820.1 17.4 %collective-permute-done.58 = f32[2,160]{1,0:T(2,128)S(1)} collective-permute-done((f32[2,160]{1,0:T(2,128)S(1)}, f32[2,160]{1,0:T(2,128)S(1)}, u32[]{:S(2)}, u32[]{:S(2)}) %collective-permute-start.58) | collective-permute-done | bytes 1312 | tf_op jit(solution)/shard_map/ppermute | solution.py:35
  843.9 7.8 collective-permute-done.61
  856.1 14.5 %collective-permute-done.48 = bf16[640,640]{1,0:T(8,128)(2,1)S(1)} collective-permute-done((bf16[640,640]{1,0:T(8,128)(2,1)S(1)}, bf16[640,640]{1,0:T(8,128)(2,1)S(1)}, u32[]{:S(2)}, u32[]{:S(2)}) %collective-permute-start.48) | collective-permute-done | bytes 819232 | tf_op jit(solution)/shard_map/ppermute | solution.py:681
  (379 shorter events, 222.2 us)
Async XLA Ops:
  7.2 132.7 %all-gather.12.cloned.1.call-start = ((), (), s32[]{:S(2)}) async-start(), calls=%async_computation.10 | async-start | bytes 6553600 | tf_op jit(solution)/shard_map/all_gather | solution.py:669
  28.5 210.7 %all-gather.14.cloned.1.call-start = ((), (), s32[]{:S(2)}) async-start(), calls=%async_computation.11 | async-start | bytes 6553600 | tf_op jit(solution)/shard_map/all_gather | solution.py:669
  28.6 111.2 %collective-permute-start.13 = (bf16[1728,640]{1,0:T(8,128)(2,1)S(1)}, bf16[1728,640]{1,0:T(8,128)(2,1)}, u32[]{:S(2)}, u32[]{:S(2)}) collective-permute-start(bf16[1728,640]{1,0:T(8,128)(2,1)S(1)} %bitcast.241), channel_id=1, source_target_pairs={{0,8},{4,12},{8,0},{12,4},{1,9},{5,13},{9,1},{13,5},{2,10},{6,14},... | collective-permute-start | bytes 6635528 | tf_op jit(solution)/shard_map/ppermute | solution.py:35
  31.0 82.5 %collective-permute-start.7 = (bf16[640,640]{1,0:T(8,128)(2,1)}, bf16[640,640]{1,0:T(8,128)(2,1)}, u32[]{:S(2)}, u32[]{:S(2)}) collective-permute-start(bf16[640,640]{1,0:T(8,128)(2,1)} %refs_0_.3), channel_id=1, source_target_pairs={{0,8},{4,12},{8,0},{12,4},{1,9},{5,13},{9,1},{13,5},{2,10},{6,14},... | collective-permute-start | bytes 2457608 | tf_op jit(solution)/shard_map/ppermute | solution.py:35
  33.4 70.9 %collective-permute-start.2 = (bf16[160,1024]{1,0:T(8,128)(2,1)}, bf16[160,1024]{1,0:T(8,128)(2,1)}, u32[]{:S(2)}, u32[]{:S(2)}) collective-permute-start(bf16[160,1024]{1,0:T(8,128)(2,1)} %get-tuple-element.253), channel_id=1, source_target_pairs={{0,12},{4,8},{8,4},{12,0},{1,13},{5,9},{9,5},{13,1},{2,14},{6,10},... | collective-permute-start | bytes 983048 | tf_op jit(solution)/shard_map/ppermute | solution.py:35
  34.5 76.7 %collective-permute-start.1 = (bf16[160,1024]{1,0:T(8,128)(2,1)}, bf16[160,1024]{1,0:T(8,128)(2,1)}, u32[]{:S(2)}, u32[]{:S(2)}) collective-permute-start(bf16[160,1024]{1,0:T(8,128)(2,1)} %get-tuple-element.254), channel_id=1, source_target_pairs={{0,8},{4,12},{8,0},{12,4},{1,9},{5,13},{9,1},{13,5},{2,10},{6,14},... | collective-permute-start | bytes 983048 | tf_op jit(solution)/shard_map/ppermute | solution.py:35
  36.5 76.5 %collective-permute-start.9 = (bf16[320,640]{1,0:T(8,128)(2,1)S(1)}, bf16[320,640]{1,0:T(8,128)(2,1)S(1)}, u32[]{:S(2)}, u32[]{:S(2)}) collective-permute-start(bf16[320,640]{1,0:T(8,128)(2,1)S(1)} %pad_maximum_fusion.4.refs_4_), channel_id=1, source_target_pairs={{0,4},{4,0},{8,12},{12,8},{1,5},{5,1},{9,13},{13,9},{2,6},{6,2},{1... | collective-permute-start | bytes 1228808 | tf_op jit(solution)/shard_map/ppermute | solution.py:35
  113.1 26.7 %collective-permute-start.12 = (bf16[640,640]{1,0:T(8,128)(2,1)}, bf16[640,640]{1,0:T(8,128)(2,1)}, u32[]{:S(2)}, u32[]{:S(2)}) collective-permute-start(bf16[640,640]{1,0:T(8,128)(2,1)} %refs_1_), channel_id=1, source_target_pairs={{0,8},{4,12},{8,0},{12,4},{1,9},{5,13},{9,1},{13,5},{2,10},{6,14},... | collective-permute-start | bytes 2457608 | tf_op jit(solution)/shard_map/ppermute | solution.py:35
  139.9 193.8 %reduce-scatter.6.cloned.1.call-start = ((), (), s32[]{:S(2)}) async-start(), calls=%async_computation.5 | async-start | bytes 6553600 | tf_op jit(solution)/shard_map/reduce_scatter | solution.py:673
  139.9 50.1 %collective-permute-start.19 = (bf16[1728,640]{1,0:T(8,128)(2,1)}, bf16[1728,640]{1,0:T(8,128)(2,1)S(1)}, u32[]{:S(2)}, u32[]{:S(2)}) collective-permute-start(bf16[1728,640]{1,0:T(8,128)(2,1)} %bitcast.242), channel_id=1, source_target_pairs={{0,8},{4,12},{8,0},{12,4},{1,9},{5,13},{9,1},{13,5},{2,10},{6,14},... | collective-permute-start | bytes 6635528 | tf_op jit(solution)/shard_map/ppermute | solution.py:35
  160.1 29.9 %collective-permute-start.17 = (bf16[640,640]{1,0:T(8,128)(2,1)S(1)}, bf16[640,640]{1,0:T(8,128)(2,1)S(1)}, u32[]{:S(2)}, u32[]{:S(2)}) collective-permute-start(bf16[640,640]{1,0:T(8,128)(2,1)S(1)} %copy-done.21), channel_id=1, source_target_pairs={{0,4},{4,0},{8,12},{12,8},{1,5},{5,1},{9,13},{13,9},{2,6},{6,2},{1... | collective-permute-start | bytes 2457608 | tf_op jit(solution)/shard_map/ppermute | solution.py:35
  160.6 29.4 %collective-permute-start.18 = (bf16[640,640]{1,0:T(8,128)(2,1)}, bf16[640,640]{1,0:T(8,128)(2,1)S(1)}, u32[]{:S(2)}, u32[]{:S(2)}) collective-permute-start(bf16[640,640]{1,0:T(8,128)(2,1)} %collective-permute-done.12.refs_2_.refs_3_), channel_id=1, source_target_pairs={{0,4},{4,0},{8,12},{12,8},{1,5},{5,1},{9,13},{13,9},{2,6},{6,2},{1... | collective-permute-start | bytes 2457608 | tf_op jit(solution)/shard_map/ppermute | solution.py:35
  239.2 153.0 %all-gather.16.cloned.1.call-start = ((), (), s32[]{:S(2)}) async-start(), calls=%async_computation.12 | async-start | bytes 3276800 | tf_op jit(solution)/shard_map/all_gather | solution.py:669
  240.8 50.0 %collective-permute-start.25 = (bf16[1728,640]{1,0:T(8,128)(2,1)S(1)}, bf16[1728,640]{1,0:T(8,128)(2,1)S(1)}, u32[]{:S(2)}, u32[]{:S(2)}) collective-permute-start(bf16[1728,640]{1,0:T(8,128)(2,1)S(1)} %copy-done.1), channel_id=1, source_target_pairs={{0,8},{4,12},{8,0},{12,4},{1,9},{5,13},{9,1},{13,5},{2,10},{6,14},... | collective-permute-start | bytes 6635528 | tf_op jit(solution)/shard_map/ppermute | solution.py:35
  242.3 49.5 %collective-permute-start.24 = (bf16[1728,640]{1,0:T(8,128)(2,1)S(1)}, bf16[1728,640]{1,0:T(8,128)(2,1)S(1)}, u32[]{:S(2)}, u32[]{:S(2)}) collective-permute-start(bf16[1728,640]{1,0:T(8,128)(2,1)S(1)} %copy-done.1), channel_id=1, source_target_pairs={{0,4},{4,0},{8,12},{12,8},{1,5},{5,1},{9,13},{13,9},{2,6},{6,2},{1... | collective-permute-start | bytes 6635528 | tf_op jit(solution)/shard_map/ppermute | solution.py:35
  336.7 110.5 %all-gather.18.cloned.1.call-start = ((), (), s32[]{:S(2)}) async-start(), calls=%async_computation.13 | async-start | bytes 3276800 | tf_op jit(solution)/shard_map/all_gather | solution.py:669
  337.3 215.3 %reduce-scatter.8.cloned.1.call-start = ((), (), s32[]{:S(2)}) async-start(), calls=%async_computation.6 | async-start | bytes 3276800 | tf_op jit(solution)/shard_map/reduce_scatter | solution.py:673
  434.5 128.0 %reduce-scatter.10.cloned.1.call-start = ((), (), s32[]{:S(2)}) async-start(), calls=%async_computation.7 | async-start | bytes 3276800 | tf_op jit(solution)/shard_map/reduce_scatter | solution.py:673
  510.9 27.9 %collective-permute-start.30 = (bf16[1728,640]{1,0:T(8,128)(2,1)}, bf16[1728,640]{1,0:T(8,128)(2,1)}, u32[]{:S(2)}, u32[]{:S(2)}) collective-permute-start(bf16[1728,640]{1,0:T(8,128)(2,1)} %convolution_convert_fusion.4), channel_id=1, source_target_pairs={{0,4},{4,0},{8,12},{12,8},{1,5},{5,1},{9,13},{13,9},{2,6},{6,2},{1... | collective-permute-start | bytes 6635528 | tf_op jit(solution)/shard_map/ppermute | solution.py:35
  511.5 160.0 %all-gather.20.cloned.1.call-start = ((), (), s32[]{:S(2)}) async-start(), calls=%async_computation.14 | async-start | bytes 6553600 | tf_op jit(solution)/shard_map/all_gather | solution.py:669
  565.4 211.4 %reduce-scatter.12.cloned.1.call-start = ((), (), s32[]{:S(2)}) async-start(), calls=%async_computation.8 | async-start | bytes 6553600 | tf_op jit(solution)/shard_map/reduce_scatter | solution.py:673
  565.9 51.1 %collective-permute-start.33 = (bf16[1728,640]{1,0:T(8,128)(2,1)S(1)}, bf16[1728,640]{1,0:T(8,128)(2,1)S(1)}, u32[]{:S(2)}, u32[]{:S(2)}) collective-permute-start(bf16[1728,640]{1,0:T(8,128)(2,1)S(1)} %copy-done.53), channel_id=1, source_target_pairs={{0,8},{4,12},{8,0},{12,4},{1,9},{5,13},{9,1},{13,5},{2,10},{6,14},... | collective-permute-start | bytes 6635528 | tf_op jit(solution)/shard_map/ppermute | solution.py:35
  567.4 95.7 %collective-permute-start.35 = (bf16[1728,640]{1,0:T(8,128)(2,1)}, bf16[1728,640]{1,0:T(8,128)(2,1)}, u32[]{:S(2)}, u32[]{:S(2)}) collective-permute-start(bf16[1728,640]{1,0:T(8,128)(2,1)} %add_convert_fusion.5), channel_id=1, source_target_pairs={{0,8},{4,12},{8,0},{12,4},{1,9},{5,13},{9,1},{13,5},{2,10},{6,14},... | collective-permute-start | bytes 6635528 | tf_op jit(solution)/shard_map/ppermute | solution.py:35
  619.2 48.2 %collective-permute-start.34 = (bf16[1728,640]{1,0:T(8,128)(2,1)S(1)}, bf16[1728,640]{1,0:T(8,128)(2,1)}, u32[]{:S(2)}, u32[]{:S(2)}) collective-permute-start(bf16[1728,640]{1,0:T(8,128)(2,1)S(1)} %add_convert_fusion.2), channel_id=1, source_target_pairs={{0,16},{16,0},{1,17},{17,1},{2,18},{18,2},{3,19},{19,3},{4,20},{20... | collective-permute-start | bytes 6635528 | tf_op jit(solution)/shard_map/ppermute | solution.py:681
  671.5 200.4 %reduce-scatter.14.cloned.1.call-start = ((), (), s32[]{:S(2)}) async-start(), calls=%async_computation.9 | async-start | bytes 6553600 | tf_op jit(solution)/shard_map/reduce_scatter | solution.py:673
  673.1 53.4 %collective-permute-start.38 = (bf16[1728,640]{1,0:T(8,128)(2,1)S(1)}, bf16[1728,640]{1,0:T(8,128)(2,1)}, u32[]{:S(2)}, u32[]{:S(2)}) collective-permute-start(bf16[1728,640]{1,0:T(8,128)(2,1)S(1)} %copy-done.52), channel_id=1, source_target_pairs={{0,8},{4,12},{8,0},{12,4},{1,9},{5,13},{9,1},{13,5},{2,10},{6,14},... | collective-permute-start | bytes 6635528 | tf_op jit(solution)/shard_map/ppermute | solution.py:35
  674.6 54.2 %collective-permute-start.39 = (bf16[1728,640]{1,0:T(8,128)(2,1)}, bf16[1728,640]{1,0:T(8,128)(2,1)}, u32[]{:S(2)}, u32[]{:S(2)}) collective-permute-start(bf16[1728,640]{1,0:T(8,128)(2,1)} %add_convert_fusion.1), channel_id=1, source_target_pairs={{0,16},{16,0},{1,17},{17,1},{2,18},{18,2},{3,19},{19,3},{4,20},{20... | collective-permute-start | bytes 6635528 | tf_op jit(solution)/shard_map/ppermute | solution.py:681
  733.7 29.3 %collective-permute-start.40 = (bf16[960,640]{1,0:T(8,128)(2,1)S(1)}, bf16[960,640]{1,0:T(8,128)(2,1)S(1)}, u32[]{:S(2)}, u32[]{:S(2)}) collective-permute-start(bf16[960,640]{1,0:T(8,128)(2,1)S(1)} %slice.136), channel_id=1, source_target_pairs={{0,16},{16,0},{1,17},{17,1},{2,18},{18,2},{3,19},{19,3},{4,20},{20... | collective-permute-start | bytes 3686408 | tf_op jit(solution)/shard_map/ppermute | solution.py:681
  807.2 34.2 %collective-permute-start.47 = (bf16[640,640]{1,0:T(8,128)(2,1)S(1)}, bf16[640,640]{1,0:T(8,128)(2,1)S(1)}, u32[]{:S(2)}, u32[]{:S(2)}) collective-permute-start(bf16[640,640]{1,0:T(8,128)(2,1)S(1)} %copy-done.55), channel_id=1, source_target_pairs={{0,8},{4,12},{8,0},{12,4},{1,9},{5,13},{9,1},{13,5},{2,10},{6,14},... | collective-permute-start | bytes 2457608 | tf_op jit(solution)/shard_map/ppermute | solution.py:35
  807.6 33.7 %collective-permute-start.49 = (bf16[320,640]{1,0:T(8,128)(2,1)S(1)}, bf16[320,640]{1,0:T(8,128)(2,1)S(1)}, u32[]{:S(2)}, u32[]{:S(2)}) collective-permute-start(bf16[320,640]{1,0:T(8,128)(2,1)S(1)} %copy-done.58), channel_id=1, source_target_pairs={{0,8},{4,12},{8,0},{12,4},{1,9},{5,13},{9,1},{13,5},{2,10},{6,14},... | collective-permute-start | bytes 1228808 | tf_op jit(solution)/shard_map/ppermute | solution.py:35
  813.4 41.3 %collective-permute-start.52 = (bf16[640,640]{1,0:T(8,128)(2,1)S(1)}, bf16[640,640]{1,0:T(8,128)(2,1)S(1)}, u32[]{:S(2)}, u32[]{:S(2)}) collective-permute-start(bf16[640,640]{1,0:T(8,128)(2,1)S(1)} %add_convert_fusion.11), channel_id=1, source_target_pairs={{0,16},{16,0},{1,17},{17,1},{2,18},{18,2},{3,19},{19,3},{4,20},{20... | collective-permute-start | bytes 2457608 | tf_op jit(solution)/shard_map/ppermute | solution.py:681
  843.5 27.1 %collective-permute-start.48 = (bf16[640,640]{1,0:T(8,128)(2,1)S(1)}, bf16[640,640]{1,0:T(8,128)(2,1)S(1)}, u32[]{:S(2)}, u32[]{:S(2)}) collective-permute-start(bf16[640,640]{1,0:T(8,128)(2,1)S(1)} %add_convert_fusion.12), channel_id=1, source_target_pairs={{0,16},{16,0},{1,17},{17,1},{2,18},{18,2},{3,19},{19,3},{4,20},{20... | collective-permute-start | bytes 2457608 | tf_op jit(solution)/shard_map/ppermute | solution.py:681
  (114 other events, 1814.3 us)
Sparse Core Ops, SparseCore 0:
  28.7 100.5 all-gather.11
  140.0 99.1 all-gather.13
  241.5 92.1 reduce-scatter.5
  336.9 55.3 all-gather.15
  393.6 53.5 all-gather.17
  450.0 50.8 reduce-scatter.7
  511.6 50.7 reduce-scatter.9
  565.6 97.7 all-gather.19
  671.6 93.6 reduce-scatter.11
  777.0 92.4 reduce-scatter.13

commit v8 on v7

--- a/solution.py
+++ b/solution.py
@@ -673,14 +673,25 @@
     return lax.psum_scatter(value, "col", scatter_dimension=0, tiled=False)
 
 
-def over_dp(value):
+def sent_over_dp(value):
     low = value.astype(BF)
-    total = low.astype(F32)
     size = lax.axis_size("dp")
-    for step in range(1, size):
-        other = lax.ppermute(low, "dp", [(i, (i + step) % size) for i in range(size)])
+    others = [
+        lax.ppermute(low, "dp", [(i, (i + step) % size) for i in range(size)])
+        for step in range(1, size)
+    ]
+    return [low] + others
+
+
+def summed_up(parts):
+    total = parts[0].astype(F32)
+    for other in parts[1:]:
         total = total + other.astype(F32)
     return total
+
+
+def over_dp(value):
+    return summed_up(sent_over_dp(value))
 
 
 def body(
@@ -830,7 +841,7 @@
         back_other, up_total, gate_total, down_total
     )
     cut = up_total.shape[0] * 5 // 9 // 16 * 16
-    up_head, up_tail = over_dp(up_total[:cut]), over_dp(up_total[cut:])
+    up_head, up_tail = over_dp(up_total[:cut]), sent_over_dp(up_total[cut:])
     dq, dkv, share, gain_share_one = qkv_back(
         own_core,
         source,
@@ -844,39 +855,43 @@
         listed(q_blocks),
         listed(kv_blocks),
     )
-    share, attn_mine, mix_rows, up_head = together(share, attn_mine, mix_rows, up_head)
+    share, attn_mine, mix_rows = together(share, attn_mine, mix_rows)
     attn_low = jnp.concatenate(
         [
             jnp.where(parity == 0, attn_mine, attn_other),
             jnp.where(parity == 0, attn_other, attn_mine),
         ]
     )
-    mix_near = {k: dot(attn_low, mix_rows[k], NT).astype(BF) for k in range(count)}
-    mix_near = fold(mix_near, "row", near)
-    share, ff_sum, mix_near = together(share, ff_sum, mix_near)
+    mix_odd = {k: dot(attn_low, mix_rows[k], NT).astype(BF) for k in range(1, count, 2)}
+    share, ff_sum, mix_odd, up_head = together(share, ff_sum, mix_odd, up_head)
     input_sum = sum_cols(share)
 
-    share, dq, dkv = together(share, dq, dkv)
-    mix_total = over_dp(fold(mix_near, "row", far)[0])
+    gain_shares = jnp.stack([gain_share_one[..., 0], gain_share_two[..., 0]], axis=2)
+    bits = near + far[::-1]
+    gain_shares = fold({k: gain_shares[:, k] for k in range(count)}, "row", bits, low=False)[0]
+    share, dq, dkv, attn_low, mix_rows = together(share, dq, dkv, attn_low, mix_rows)
+    mix_even = {k: dot(attn_low, mix_rows[k], NT).astype(BF) for k in range(0, count, 2)}
+    mix_near = fold({**mix_even, **mix_odd}, "row", near)
     q_near = fold({k: dot(norm_one[k], dq, NT).astype(BF) for k in range(count)}, "row", near)
     kv_near = fold({k: dot(dkv, norm_one[k], NT).astype(BF) for k in range(count)}, "row", near)
-    ff_sum, gain_share_one, q_near, kv_near = together(ff_sum, gain_share_one, q_near, kv_near)
-    q_total = over_dp(fold(q_near, "row", far)[0])
-    kv_total = over_dp(fold(kv_near, "row", far)[0])
+    mix_total = over_dp(fold(mix_near, "row", far)[0])
+    ff_sum, gain_shares, q_near, kv_near, up_tail = together(
+        ff_sum, gain_shares, q_near, kv_near, up_tail
+    )
+    q_far = fold(q_near, "row", far)[0]
+    kv_far = fold(kv_near, "row", far)[0]
+    q_total, kv_total = over_dp(q_far), over_dp(kv_far)
     output_own = (residual_own + ff_sum.astype(F32)).astype(BF)
     layer_output = all_tokens(output_own)
 
-    bits = near + far[::-1]
-    gain_shares = jnp.stack([gain_share_one[..., 0], gain_share_two[..., 0]], axis=2)
     gain_shares = by_xor(gain_shares, lax.axis_index("col"), 0)
     gain_shares = {c: gain_shares[c] for c in range(cols)}
     gain_shares = fold(gain_shares, "col", near_bits(cols) + far_bits(cols), low=False)[0]
-    gain_shares = fold({k: gain_shares[k] for k in range(count)}, "row", bits, low=False)[0]
     gain_totals = over_dp(gain_shares)
-    input_sum, q_total, kv_total, mix_total, gain_totals, layer_output, up_tail = together(
-        input_sum, q_total, kv_total, mix_total, gain_totals, layer_output, up_tail
-    )
-    up_total = jnp.concatenate([up_head, up_tail])
+    up_total = jnp.concatenate([up_head, summed_up(up_tail)])
+    input_sum, q_total, kv_total, mix_total, gain_totals, layer_output, up_total = together(
+        input_sum, q_total, kv_total, mix_total, gain_totals, layer_output, up_total
+    )
 
     input_grad = all_tokens((residual_grad_own + input_sum.astype(F32)).astype(BF)).astype(F32)
     kv_rows = kv_total.shape[0] // 2

time: 908 us -> 921 us (1.014)
  transfers between devices with their start and end apart: 77 -> 77, of which waited for: 35 -> 36; matrix products, arithmetic and copies ran while one was open for 16% -> 15% of each run, Pallas kernels for 24% -> 24%
where the time goes in v8:
time: 921 us; the launch traced here: 913 us
  waiting for transfers between devices  437 us (47%)
  Pallas kernels  217 us (24%)
  matrix products  84.7 us (9%)
  other arithmetic  54 us (6%)
  starting transfers between devices  44.8 us (5%)
  blocking collectives  34.2 us (4%)
  local copies, waits for them, and re-layouts  26.7 us (3%)
  between operations  15.4 us (2%)
    ppermute x59, waiting for transfers between devices, swapped(): return lax.ppermute(value, axis, [(i, i ^ mask) for i in range(size)])  269 us
    all_gather x5, waiting for transfers between devices, spread_cols(): return lax.all_gather(value, 'col', axis=0, tiled=False)  102 us
    dot_general x24, matrix products, dot(): return lax.dot_general(left, right, dims, preferred_element_type=F32)  84.7 us
    pallas_call x2, Pallas kernels, feed_forward(): pl.pallas_call(functools.partial(ff_kernel, count, bool(before)), out_sha...  84.1 us
    pallas_call x1, Pallas kernels, attend_back(): pl.pallas_call(functools.partial(attend_back_kernel, tile), out_shape=(sh...  37.4 us
    ppermute x59, starting transfers between devices, swapped(): return lax.ppermute(value, axis, [(i, i ^ mask) for i in range(size)])  35.5 us
    reduce_scatter x5, waiting for transfers between devices, sum_cols(): return lax.psum_scatter(value, 'col', scatter_dimension=0, tiled=False)  35.4 us
    all_gather x1, blocking collectives, body(): lax.all_gather(jnp.stack([attn_gain, mlp_gain]), ('row', 'col'), axis=1,...  34.2 us
  transfers between devices with their start and end apart: 77, of which 36 were waited for; matrix products, arithmetic and copies ran while one was open for 15% of the time, Pallas kernels for 24%

profile of v8, /device:TPU:0, one launch (start us, length us, event | category | flops | bytes accessed | tf_op | source)
XLA Modules:
  0.0 912.9 jit_solution(18168897228900962545)
XLA Ops:
  12.5 7.4 collective-permute-done.5
  19.9 7.2 collective-permute-done.4
  38.7 34.2 %all-gather.5 = f32[16,160,2]{1,2,0:T(2,128)S(1)} all-gather(f32[1,160,2]{1,2,0:T(2,128)S(1)} %maximum_bitcast_fusion.1), channel_id=1, replica_groups=mesh['dp'=2,'row'=4,'col'=4] {'row','col'}, dimensions={0}, use_global_device_ids=true | all-gather | bytes 21760 | tf_op jit(solution)/shard_map/all_gather | solution.py:750
  73.1 32.8 %collective-permute-done.2 = bf16[160,1024]{1,0:T(8,128)(2,1)} collective-permute-done((bf16[160,1024]{1,0:T(8,128)(2,1)}, bf16[160,1024]{1,0:T(8,128)(2,1)}, u32[]{:S(2)}, u32[]{:S(2)}) %collective-permute-start.2) | collective-permute-done | bytes 327712 | tf_op jit(solution)/shard_map/ppermute | solution.py:35
  106.5 6.4 collective-permute-done.1
  116.7 8.7 collective-permute-done.10.refs_6_
  127.9 13.6 %collective-permute-done.12.refs_2_.refs_3_ = bf16[640,640]{1,0:T(8,128)(2,1)} collective-permute-done((bf16[640,640]{1,0:T(8,128)(2,1)S(1)}, bf16[640,640]{1,0:T(8,128)(2,1)}, u32[]{:S(2)}, u32[]{:S(2)}) %collective-permute-start.12) | collective-permute-done | bytes 819232 | tf_op jit(solution)/shard_map/ppermute | solution.py:35
  144.6 13.1 %qkv_project.1 = (bf16[4,640,1024]{2,1,0:T(8,128)(2,1)}, f32[1,1024]{1,0:T(1,128)}, bf16[2,480,1024]{2,1,0:T(8,128)(2,1)}) custom-call(bf16[4,4,160,1024]{3,2,1,0:T(8,128)(2,1)} %bitcast.233, f32[4,4,160,1]{3,2,1,0:T(8,128)} %copy.66.gain_ref, f32[40,1024]{1,0:T(8,128)} %get-tuple-element.130.cos_ref, f32[40,1024]{1,0:T(8,128)} %get-tuple-element.131.sin_ref, ...), custom_call_target="tpu_custom_call" | custom-call | flops 1200000000 | tf_op jit(solution)/shard_map/qkv_project/pallas_call | solution.py:150
  163.6 27.8 %attend.1 = (bf16[320,1024]{1,0:T(8,128)(2,1)}, bf16[320,1024]{1,0:T(8,128)(2,1)}, f32[2,4,1,1024]{3,2,1,0:T(1,128)}) custom-call(s32[1]{0:T(128)} %bitcast.parity_ref, bf16[480,1024]{1,0:T(8,128)(2,1)} %get-tuple-element.244.own_ref, bf16[480,1024]{1,0:T(8,128)(2,1)} %collective-permute-done.15.other_ref, s32[1,1024]{1,0:T(1,128)} %bitcast.283, ...), custom_call_target="tpu_custom_call" | custom-call | flops 2700000000 | tf_op jit(solution)/shard_map/attend/pallas_call | solution.py:242
  194.6 10.2 %mix_out.1 = bf16[4,4,160,1024]{3,2,1,0:T(8,128)(2,1)} custom-call(s32[1]{0:T(128)} %bitcast.parity_ref, bf16[320,1024]{1,0:T(8,128)(2,1)} %get-tuple-element.208.own_ref.own_out, bf16[320,1024]{1,0:T(8,128)(2,1)} %copy-done.27, bf16[640,640]{1,0:T(8,128)(2,1)} %refs_1_, bf16[640,640]{1,0:T(8,128)(2,1)} %copy-done.19, ...), custom_call_target="tpu_custom_call" | custom-call | flops 1000000000 | tf_op jit(solution)/shard_map/mix_out/pallas_call | solution.py:417
  204.9 36.0 %all-gather.14.cloned.1.call-done = bf16[16,160,1024]{2,1,0:T(8,128)(2,1)} async-done(((bf16[4,160,1024]{2,1,0:T(8,128)(2,1)}), bf16[16,160,1024]{2,1,0:T(8,128)(2,1)}) %all-gather.14.cloned.1.call-update) | async-done | bytes 5242896 | tf_op jit(solution)/shard_map/all_gather | solution.py:669
  244.0 48.5 %collective-permute-done.25.refs_10_.refs_2_ = bf16[1728,640]{1,0:T(8,128)(2,1)S(1)} collective-permute-done((bf16[1728,640]{1,0:T(8,128)(2,1)S(1)}, bf16[1728,640]{1,0:T(8,128)(2,1)S(1)}, u32[]{:S(2)}, u32[]{:S(2)}) %collective-permute-start.25) | collective-permute-done | bytes 2211872 | tf_op jit(solution)/shard_map/ppermute | solution.py:35
  293.9 6.0 collective-permute-done.26.refs_11_.refs_3_
  309.7 25.7 %reduce-scatter.6.cloned.1.call-done = bf16[1,4,160,1024]{3,2,1,0:T(8,128)(2,1)} async-done(((bf16[4,4,160,1024]{3,2,1,0:T(8,128)(2,1)}), bf16[1,4,160,1024]{3,2,1,0:T(8,128)(2,1)}) %reduce-scatter.6.cloned.1.call-update) | async-done | bytes 1310736 | tf_op jit(solution)/shard_map/reduce_scatter | solution.py:673
  340.9 53.3 %all-gather.16.cloned.1.call-done = bf16[16,160,512]{2,1,0:T(8,128)(2,1)} async-done(((bf16[4,160,512]{2,1,0:T(8,128)(2,1)}), bf16[16,160,512]{2,1,0:T(8,128)(2,1)}) %all-gather.16.cloned.1.call-update) | async-done | bytes 2621456 | tf_op jit(solution)/shard_map/all_gather | solution.py:669
  394.2 42.2 %feed_forward.2 = (bf16[4,640,1024]{2,1,0:T(8,128)(2,1)}, bf16[4,640,1024]{2,1,0:T(8,128)(2,1)}, bf16[1728,1024]{1,0:T(8,128)(2,1)}, bf16[1728,1024]{1,0:T(8,128...) custom-call(bf16[4,4,160,512]{3,2,1,0:T(8,128)(2,1)} %bitcast.265, ...), custom_call_target="tpu_custom_call" | custom-call | flops 4200000000 | tf_op jit(solution)/shard_map/feed_forward/pallas_call | solution.py:556
  436.5 12.7 %all-gather.18.cloned.1.call-done = bf16[16,160,512]{2,1,0:T(8,128)(2,1)} async-done(((bf16[4,160,512]{2,1,0:T(8,128)(2,1)}), bf16[16,160,512]{2,1,0:T(8,128)(2,1)}) %all-gather.18.cloned.1.call-update) | async-done | bytes 2621456 | tf_op jit(solution)/shard_map/all_gather | solution.py:669
  449.2 41.8 %feed_forward.3 = (bf16[4,640,1024]{2,1,0:T(8,128)(2,1)}, bf16[4,640,1024]{2,1,0:T(8,128)(2,1)}, bf16[1728,1024]{1,0:T(8,128)(2,1)}, bf16[1728,1024]{1,0:T(8,128...) custom-call(bf16[4,4,160,512]{3,2,1,0:T(8,128)(2,1)} %bitcast.270, ...), custom_call_target="tpu_custom_call", output_to_operand_aliasing={{0}: (15, {}), {1}: (16, {}), {2}: (17, {}), {3}: (18, {}),... | custom-call | flops 4200000000 | tf_op jit(solution)/shard_map/feed_forward/pallas_call | solution.py:556
  491.1 6.9 convolution_convert_fusion.10
  554.6 9.7 %reduce-scatter.10.cloned.1.call-done = bf16[1,4,160,512]{3,2,1,0:T(8,128)(2,1)} async-done(((bf16[4,4,160,512]{3,2,1,0:T(8,128)(2,1)}), bf16[1,4,160,512]{3,2,1,0:T(8,128)(2,1)}) %reduce-scatter.10.cloned.1.call-update) | async-done | bytes 655376 | tf_op jit(solution)/shard_map/reduce_scatter | solution.py:673
  569.9 49.0 %collective-permute-done.33 = bf16[1728,640]{1,0:T(8,128)(2,1)S(1)} collective-permute-done((bf16[1728,640]{1,0:T(8,128)(2,1)S(1)}, bf16[1728,640]{1,0:T(8,128)(2,1)S(1)}, u32[]{:S(2)}, u32[]{:S(2)}) %collective-permute-start.33) | collective-permute-done | bytes 2211872 | tf_op jit(solution)/shard_map/ppermute | solution.py:35
  622.6 16.6 %fan_out.1 = bf16[4,4,160,1024]{3,2,1,0:T(8,128)(2,1)} custom-call(bf16[1728,1024]{1,0:T(8,128)(2,1)} %get-tuple-element.180.x_ref, bf16[1728,640]{1,0:T(8,128)(2,1)} %refs_0_.2, bf16[1728,640]{1,0:T(8,128)(2,1)} %copy-done.3, bf16[1728,640]{1,0:T(8,128)(2,1)} %copy-done.2, bf16[1728,640]{1,0:T(8,128)(2,1)} %copy-done.4), custom_call_target="tpu_custom_call" | custom-call | flops 1700000000 | tf_op jit(solution)/shard_map/fan_out/pallas_call | solution.py:478
  639.3 25.8 %collective-permute-done.35 = bf16[1728,640]{1,0:T(8,128)(2,1)} collective-permute-done((bf16[1728,640]{1,0:T(8,128)(2,1)}, bf16[1728,640]{1,0:T(8,128)(2,1)}, u32[]{:S(2)}, u32[]{:S(2)}) %collective-permute-start.35) | collective-permute-done | bytes 2211872 | tf_op jit(solution)/shard_map/ppermute | solution.py:35
  678.0 9.6 %mix_back.1 = (bf16[4,640,1024]{2,1,0:T(8,128)(2,1)}, bf16[320,1024]{1,0:T(8,128)(2,1)}, bf16[320,1024]{1,0:T(8,128)(2,1)}) custom-call(s32[1]{0:T(128)} %bitcast.parity_ref, bf16[4,4,160,1024]{3,2,1,0:T(8,128)(2,1)} %bitcast.245, bf16[640,640]{1,0:T(8,128)(2,1)} %refs_1_, bf16[640,640]{1,0:T(8,128)(2,1)} %copy-done.19, ...), custom_call_target="tpu_custom_call" | custom-call | flops 900000000 | tf_op jit(solution)/shard_map/mix_back/pallas_call | solution.py:452
  690.7 37.4 %attend_back.1 = (bf16[480,1024]{1,0:T(8,128)(2,1)}, bf16[480,1024]{1,0:T(8,128)(2,1)}) custom-call(s32[1]{0:T(128)} %bitcast.parity_ref, bf16[480,1024]{1,0:T(8,128)(2,1)} %get-tuple-element.244.own_ref, bf16[480,1024]{1,0:T(8,128)(2,1)} %collective-permute-done.15.other_ref, bf16[320,1024]{1,0:T(8,128)(2,1)} %get-tuple-element.208.own_ref.own_out, ...), custom_call_target="tpu_custom_call" | custom-call | flops 3700000000 | tf_op jit(solution)/shard_map/attend_back/pallas_call | solution.py:354
  737.0 17.6 %qkv_back.1 = (bf16[640,1024]{1,0:T(8,128)(2,1)}, bf16[320,1024]{1,0:T(8,128)(2,1)}, bf16[4,4,160,1024]{3,2,1,0:T(8,128)(2,1)}, f32[4,4,160,1]{3,2,1,0:T(8,128)}) custom-call(s32[1]{0:T(128)} %bitcast.parity_ref, bf16[4,4,160,1024]{3,2,1,0:T(8,128)(2,1)} %bitcast.234, f32[4,4,160,1]{3,2,1,0:T(8,128)} %copy.66.gain_ref, ...), custom_call_target="tpu_custom_call" | custom-call | flops 1700000000 | tf_op jit(solution)/shard_map/qkv_back/pallas_call | solution.py:646
  822.6 9.6 %collective-permute-done.51 = bf16[320,640]{1,0:T(8,128)(2,1)S(1)} collective-permute-done((bf16[320,640]{1,0:T(8,128)(2,1)S(1)}, bf16[320,640]{1,0:T(8,128)(2,1)S(1)}, u32[]{:S(2)}, u32[]{:S(2)}) %collective-permute-start.51) | collective-permute-done | bytes 409632 | tf_op jit(solution)/shard_map/ppermute | solution.py:35
  834.7 15.0 %collective-permute-done.55 = bf16[640,640]{1,0:T(8,128)(2,1)S(1)} collective-permute-done((bf16[640,640]{1,0:T(8,128)(2,1)S(1)}, bf16[640,640]{1,0:T(8,128)(2,1)S(1)}, u32[]{:S(2)}, u32[]{:S(2)}) %collective-permute-start.55) | collective-permute-done | bytes 819232 | tf_op jit(solution)/shard_map/ppermute | solution.py:35
  861.2 9.7 %collective-permute-done.50 = bf16[640,640]{1,0:T(8,128)(2,1)S(1)} collective-permute-done((bf16[640,640]{1,0:T(8,128)(2,1)S(1)}, bf16[640,640]{1,0:T(8,128)(2,1)S(1)}, u32[]{:S(2)}, u32[]{:S(2)}) %collective-permute-start.50) | collective-permute-done | bytes 819232 | tf_op jit(solution)/shard_map/ppermute | solution.py:680
  872.2 11.7 %collective-permute-done.56 = bf16[640,640]{1,0:T(8,128)(2,1)S(1)} collective-permute-done((bf16[640,640]{1,0:T(8,128)(2,1)S(1)}, bf16[640,640]{1,0:T(8,128)(2,1)S(1)}, u32[]{:S(2)}, u32[]{:S(2)}) %collective-permute-start.56) | collective-permute-done | bytes 819232 | tf_op jit(solution)/shard_map/ppermute | solution.py:680
  891.0 7.0 collective-permute-done.65
  898.0 6.1 collective-permute-done.66
  (363 shorter events, 238.3 us)
Async XLA Ops:
  7.2 134.3 %all-gather.12.cloned.1.call-start = ((), (), s32[]{:S(2)}) async-start(), calls=%async_computation.10 | async-start | bytes 6553600 | tf_op jit(solution)/shard_map/all_gather | solution.py:669
  30.2 210.7 %all-gather.14.cloned.1.call-start = ((), (), s32[]{:S(2)}) async-start(), calls=%async_computation.11 | async-start | bytes 6553600 | tf_op jit(solution)/shard_map/all_gather | solution.py:669
  30.3 111.2 %collective-permute-start.13 = (bf16[1728,640]{1,0:T(8,128)(2,1)S(1)}, bf16[1728,640]{1,0:T(8,128)(2,1)}, u32[]{:S(2)}, u32[]{:S(2)}) collective-permute-start(bf16[1728,640]{1,0:T(8,128)(2,1)S(1)} %bitcast.240), channel_id=1, source_target_pairs={{0,8},{4,12},{8,0},{12,4},{1,9},{5,13},{9,1},{13,5},{2,10},{6,14},... | collective-permute-start | bytes 6635528 | tf_op jit(solution)/shard_map/ppermute | solution.py:35
  32.6 82.5 %collective-permute-start.7 = (bf16[640,640]{1,0:T(8,128)(2,1)}, bf16[640,640]{1,0:T(8,128)(2,1)}, u32[]{:S(2)}, u32[]{:S(2)}) collective-permute-start(bf16[640,640]{1,0:T(8,128)(2,1)} %refs_0_.3), channel_id=1, source_target_pairs={{0,8},{4,12},{8,0},{12,4},{1,9},{5,13},{9,1},{13,5},{2,10},{6,14},... | collective-permute-start | bytes 2457608 | tf_op jit(solution)/shard_map/ppermute | solution.py:35
  35.0 70.9 %collective-permute-start.2 = (bf16[160,1024]{1,0:T(8,128)(2,1)}, bf16[160,1024]{1,0:T(8,128)(2,1)}, u32[]{:S(2)}, u32[]{:S(2)}) collective-permute-start(bf16[160,1024]{1,0:T(8,128)(2,1)} %get-tuple-element.261), channel_id=1, source_target_pairs={{0,12},{4,8},{8,4},{12,0},{1,13},{5,9},{9,5},{13,1},{2,14},{6,10},... | collective-permute-start | bytes 983048 | tf_op jit(solution)/shard_map/ppermute | solution.py:35
  36.1 76.7 %collective-permute-start.1 = (bf16[160,1024]{1,0:T(8,128)(2,1)}, bf16[160,1024]{1,0:T(8,128)(2,1)}, u32[]{:S(2)}, u32[]{:S(2)}) collective-permute-start(bf16[160,1024]{1,0:T(8,128)(2,1)} %get-tuple-element.262), channel_id=1, source_target_pairs={{0,8},{4,12},{8,0},{12,4},{1,9},{5,13},{9,1},{13,5},{2,10},{6,14},... | collective-permute-start | bytes 983048 | tf_op jit(solution)/shard_map/ppermute | solution.py:35
  38.2 76.5 %collective-permute-start.9 = (bf16[320,640]{1,0:T(8,128)(2,1)S(1)}, bf16[320,640]{1,0:T(8,128)(2,1)}, u32[]{:S(2)}, u32[]{:S(2)}) collective-permute-start(bf16[320,640]{1,0:T(8,128)(2,1)S(1)} %pad_maximum_fusion.5.refs_4_), channel_id=1, source_target_pairs={{0,4},{4,0},{8,12},{12,8},{1,5},{5,1},{9,13},{13,9},{2,6},{6,2},{1... | collective-permute-start | bytes 1228808 | tf_op jit(solution)/shard_map/ppermute | solution.py:35
  141.5 193.8 %reduce-scatter.6.cloned.1.call-start = ((), (), s32[]{:S(2)}) async-start(), calls=%async_computation.5 | async-start | bytes 6553600 | tf_op jit(solution)/shard_map/reduce_scatter | solution.py:673
  141.6 50.1 %collective-permute-start.19 = (bf16[1728,640]{1,0:T(8,128)(2,1)}, bf16[1728,640]{1,0:T(8,128)(2,1)S(1)}, u32[]{:S(2)}, u32[]{:S(2)}) collective-permute-start(bf16[1728,640]{1,0:T(8,128)(2,1)} %bitcast.241), channel_id=1, source_target_pairs={{0,8},{4,12},{8,0},{12,4},{1,9},{5,13},{9,1},{13,5},{2,10},{6,14},... | collective-permute-start | bytes 6635528 | tf_op jit(solution)/shard_map/ppermute | solution.py:35
  161.7 29.9 %collective-permute-start.17 = (bf16[640,640]{1,0:T(8,128)(2,1)S(1)}, bf16[640,640]{1,0:T(8,128)(2,1)S(1)}, u32[]{:S(2)}, u32[]{:S(2)}) collective-permute-start(bf16[640,640]{1,0:T(8,128)(2,1)S(1)} %copy-done.18), channel_id=1, source_target_pairs={{0,4},{4,0},{8,12},{12,8},{1,5},{5,1},{9,13},{13,9},{2,6},{6,2},{1... | collective-permute-start | bytes 2457608 | tf_op jit(solution)/shard_map/ppermute | solution.py:35
  162.2 29.4 %collective-permute-start.18 = (bf16[640,640]{1,0:T(8,128)(2,1)}, bf16[640,640]{1,0:T(8,128)(2,1)S(1)}, u32[]{:S(2)}, u32[]{:S(2)}) collective-permute-start(bf16[640,640]{1,0:T(8,128)(2,1)} %collective-permute-done.12.refs_2_.refs_3_), channel_id=1, source_target_pairs={{0,4},{4,0},{8,12},{12,8},{1,5},{5,1},{9,13},{13,9},{2,6},{6,2},{1... | collective-permute-start | bytes 2457608 | tf_op jit(solution)/shard_map/ppermute | solution.py:35
  240.9 153.3 %all-gather.16.cloned.1.call-start = ((), (), s32[]{:S(2)}) async-start(), calls=%async_computation.12 | async-start | bytes 3276800 | tf_op jit(solution)/shard_map/all_gather | solution.py:669
  242.5 50.0 %collective-permute-start.25 = (bf16[1728,640]{1,0:T(8,128)(2,1)S(1)}, bf16[1728,640]{1,0:T(8,128)(2,1)S(1)}, u32[]{:S(2)}, u32[]{:S(2)}) collective-permute-start(bf16[1728,640]{1,0:T(8,128)(2,1)S(1)} %copy-done.1), channel_id=1, source_target_pairs={{0,8},{4,12},{8,0},{12,4},{1,9},{5,13},{9,1},{13,5},{2,10},{6,14},... | collective-permute-start | bytes 6635528 | tf_op jit(solution)/shard_map/ppermute | solution.py:35
  244.0 49.5 %collective-permute-start.24 = (bf16[1728,640]{1,0:T(8,128)(2,1)S(1)}, bf16[1728,640]{1,0:T(8,128)(2,1)S(1)}, u32[]{:S(2)}, u32[]{:S(2)}) collective-permute-start(bf16[1728,640]{1,0:T(8,128)(2,1)S(1)} %copy-done.1), channel_id=1, source_target_pairs={{0,4},{4,0},{8,12},{12,8},{1,5},{5,1},{9,13},{13,9},{2,6},{6,2},{1... | collective-permute-start | bytes 6635528 | tf_op jit(solution)/shard_map/ppermute | solution.py:35
  338.7 110.5 %all-gather.18.cloned.1.call-start = ((), (), s32[]{:S(2)}) async-start(), calls=%async_computation.13 | async-start | bytes 3276800 | tf_op jit(solution)/shard_map/all_gather | solution.py:669
  339.3 215.3 %reduce-scatter.8.cloned.1.call-start = ((), (), s32[]{:S(2)}) async-start(), calls=%async_computation.6 | async-start | bytes 3276800 | tf_op jit(solution)/shard_map/reduce_scatter | solution.py:673
  436.5 127.9 %reduce-scatter.10.cloned.1.call-start = ((), (), s32[]{:S(2)}) async-start(), calls=%async_computation.7 | async-start | bytes 3276800 | tf_op jit(solution)/shard_map/reduce_scatter | solution.py:673
  513.5 159.9 %all-gather.20.cloned.1.call-start = ((), (), s32[]{:S(2)}) async-start(), calls=%async_computation.14 | async-start | bytes 6553600 | tf_op jit(solution)/shard_map/all_gather | solution.py:669
  567.4 201.9 %reduce-scatter.12.cloned.1.call-start = ((), (), s32[]{:S(2)}) async-start(), calls=%async_computation.8 | async-start | bytes 6553600 | tf_op jit(solution)/shard_map/reduce_scatter | solution.py:673
  567.8 51.1 %collective-permute-start.33 = (bf16[1728,640]{1,0:T(8,128)(2,1)S(1)}, bf16[1728,640]{1,0:T(8,128)(2,1)S(1)}, u32[]{:S(2)}, u32[]{:S(2)}) collective-permute-start(bf16[1728,640]{1,0:T(8,128)(2,1)S(1)} %copy-done.43), channel_id=1, source_target_pairs={{0,8},{4,12},{8,0},{12,4},{1,9},{5,13},{9,1},{13,5},{2,10},{6,14},... | collective-permute-start | bytes 6635528 | tf_op jit(solution)/shard_map/ppermute | solution.py:35
  569.4 95.7 %collective-permute-start.35 = (bf16[1728,640]{1,0:T(8,128)(2,1)}, bf16[1728,640]{1,0:T(8,128)(2,1)}, u32[]{:S(2)}, u32[]{:S(2)}) collective-permute-start(bf16[1728,640]{1,0:T(8,128)(2,1)} %add_convert_fusion.5), channel_id=1, source_target_pairs={{0,8},{4,12},{8,0},{12,4},{1,9},{5,13},{9,1},{13,5},{2,10},{6,14},... | collective-permute-start | bytes 6635528 | tf_op jit(solution)/shard_map/ppermute | solution.py:35
  621.1 48.1 %collective-permute-start.34 = (bf16[1728,640]{1,0:T(8,128)(2,1)S(1)}, bf16[1728,640]{1,0:T(8,128)(2,1)}, u32[]{:S(2)}, u32[]{:S(2)}) collective-permute-start(bf16[1728,640]{1,0:T(8,128)(2,1)S(1)} %add_convert_fusion.2), channel_id=1, source_target_pairs={{0,16},{16,0},{1,17},{17,1},{2,18},{18,2},{3,19},{19,3},{4,20},{20... | collective-permute-start | bytes 6635528 | tf_op jit(solution)/shard_map/ppermute | solution.py:680
  673.4 211.8 %reduce-scatter.14.cloned.1.call-start = ((), (), s32[]{:S(2)}) async-start(), calls=%async_computation.9 | async-start | bytes 6553600 | tf_op jit(solution)/shard_map/reduce_scatter | solution.py:673
  675.0 53.4 %collective-permute-start.38 = (bf16[1728,640]{1,0:T(8,128)(2,1)S(1)}, bf16[1728,640]{1,0:T(8,128)(2,1)}, u32[]{:S(2)}, u32[]{:S(2)}) collective-permute-start(bf16[1728,640]{1,0:T(8,128)(2,1)S(1)} %copy-done.42), channel_id=1, source_target_pairs={{0,8},{4,12},{8,0},{12,4},{1,9},{5,13},{9,1},{13,5},{2,10},{6,14},... | collective-permute-start | bytes 6635528 | tf_op jit(solution)/shard_map/ppermute | solution.py:35
  676.5 54.2 %collective-permute-start.39 = (bf16[1728,640]{1,0:T(8,128)(2,1)}, bf16[1728,640]{1,0:T(8,128)(2,1)}, u32[]{:S(2)}, u32[]{:S(2)}) collective-permute-start(bf16[1728,640]{1,0:T(8,128)(2,1)} %add_convert_fusion.1), channel_id=1, source_target_pairs={{0,16},{16,0},{1,17},{17,1},{2,18},{18,2},{3,19},{19,3},{4,20},{20... | collective-permute-start | bytes 6635528 | tf_op jit(solution)/shard_map/ppermute | solution.py:680
  736.7 29.6 %collective-permute-start.40 = (bf16[960,640]{1,0:T(8,128)(2,1)}, bf16[960,640]{1,0:T(8,128)(2,1)}, u32[]{:S(2)}, u32[]{:S(2)}) collective-permute-start(bf16[960,640]{1,0:T(8,128)(2,1)} %slice.138), channel_id=1, source_target_pairs={{0,16},{16,0},{1,17},{17,1},{2,18},{18,2},{3,19},{19,3},{4,20},{20... | collective-permute-start | bytes 3686408 | tf_op jit(solution)/shard_map/ppermute | solution.py:680
  794.5 39.7 %collective-permute-start.53 = (bf16[640,640]{1,0:T(8,128)(2,1)S(1)}, bf16[640,640]{1,0:T(8,128)(2,1)S(1)}, u32[]{:S(2)}, u32[]{:S(2)}) collective-permute-start(bf16[640,640]{1,0:T(8,128)(2,1)S(1)} %copy-done.45), channel_id=1, source_target_pairs={{0,4},{4,0},{8,12},{12,8},{1,5},{5,1},{9,13},{13,9},{2,6},{6,2},{1... | collective-permute-start | bytes 2457608 | tf_op jit(solution)/shard_map/ppermute | solution.py:35
  802.2 31.7 %collective-permute-start.49 = (bf16[640,640]{1,0:T(8,128)(2,1)S(1)}, bf16[640,640]{1,0:T(8,128)(2,1)S(1)}, u32[]{:S(2)}, u32[]{:S(2)}) collective-permute-start(bf16[640,640]{1,0:T(8,128)(2,1)S(1)} %add_convert_fusion.15), channel_id=1, source_target_pairs={{0,8},{4,12},{8,0},{12,4},{1,9},{5,13},{9,1},{13,5},{2,10},{6,14},... | collective-permute-start | bytes 2457608 | tf_op jit(solution)/shard_map/ppermute | solution.py:35
  803.8 28.3 %collective-permute-start.51 = (bf16[320,640]{1,0:T(8,128)(2,1)S(1)}, bf16[320,640]{1,0:T(8,128)(2,1)S(1)}, u32[]{:S(2)}, u32[]{:S(2)}) collective-permute-start(bf16[320,640]{1,0:T(8,128)(2,1)S(1)} %add_convert_fusion.18), channel_id=1, source_target_pairs={{0,8},{4,12},{8,0},{12,4},{1,9},{5,13},{9,1},{13,5},{2,10},{6,14},... | collective-permute-start | bytes 1228808 | tf_op jit(solution)/shard_map/ppermute | solution.py:35
  815.3 34.5 %collective-permute-start.55 = (bf16[640,640]{1,0:T(8,128)(2,1)S(1)}, bf16[640,640]{1,0:T(8,128)(2,1)S(1)}, u32[]{:S(2)}, u32[]{:S(2)}) collective-permute-start(bf16[640,640]{1,0:T(8,128)(2,1)S(1)} %add_convert_fusion.12), channel_id=1, source_target_pairs={{0,8},{4,12},{8,0},{12,4},{1,9},{5,13},{9,1},{13,5},{2,10},{6,14},... | collective-permute-start | bytes 2457608 | tf_op jit(solution)/shard_map/ppermute | solution.py:35
  822.6 28.5 %collective-permute-start.61 = (bf16[160,1024]{1,0:T(8,128)(2,1)S(1)}, bf16[160,1024]{1,0:T(8,128)(2,1)S(1)}, u32[]{:S(2)}, u32[]{:S(2)}) collective-permute-start(bf16[160,1024]{1,0:T(8,128)(2,1)S(1)} %get-tuple-element.250), channel_id=1, source_target_pairs={{0,4},{4,0},{8,12},{12,8},{1,5},{5,1},{9,13},{13,9},{2,6},{6,2},{1... | collective-permute-start | bytes 983048 | tf_op jit(solution)/shard_map/ppermute | solution.py:35
  851.1 32.8 %collective-permute-start.56 = (bf16[640,640]{1,0:T(8,128)(2,1)S(1)}, bf16[640,640]{1,0:T(8,128)(2,1)S(1)}, u32[]{:S(2)}, u32[]{:S(2)}) collective-permute-start(bf16[640,640]{1,0:T(8,128)(2,1)S(1)} %add_convert_fusion.11), channel_id=1, source_target_pairs={{0,16},{16,0},{1,17},{17,1},{2,18},{18,2},{3,19},{19,3},{4,20},{20... | collective-permute-start | bytes 2457608 | tf_op jit(solution)/shard_map/ppermute | solution.py:680
  (104 other events, 1253.5 us)
Sparse Core Ops, SparseCore 0:
  30.3 100.5 all-gather.11
  141.6 99.1 all-gather.13
  243.2 92.1 reduce-scatter.5
  338.9 55.3 all-gather.15
  395.6 53.5 all-gather.17
  452.0 50.8 reduce-scatter.7
  513.6 50.6 reduce-scatter.9
  567.5 97.7 all-gather.19
  673.6 93.6 reduce-scatter.11
  769.4 94.3 reduce-scatter.13

commit v9 on v8

--- a/solution.py
+++ b/solution.py
@@ -51,6 +51,13 @@
             total = held[k ^ bit].astype(F32) + other.astype(F32)
             held[k ^ bit] = total.astype(BF) if low else total
     return held
+
+
+def fold_landed(held, moved, bit):
+    return {
+        k ^ bit: (held[k ^ bit].astype(F32) + other.astype(F32)).astype(BF)
+        for k, other in moved.items()
+    }
 
 
 def far_bits(size):
@@ -718,6 +725,7 @@
     own_core = parity.reshape(1)
     q_half = query_weight.shape[1] // 2
     near, far = near_bits(count), far_bits(count)
+    far_mask = far[-1]
 
     def row_tokens(value):
         turned = value.T
@@ -863,21 +871,26 @@
         ]
     )
     mix_odd = {k: dot(attn_low, mix_rows[k], NT).astype(BF) for k in range(1, count, 2)}
-    share, ff_sum, mix_odd, up_head = together(share, ff_sum, mix_odd, up_head)
+    gain_shares = jnp.stack([gain_share_one[..., 0], gain_share_two[..., 0]], axis=2)
+    share, ff_sum, mix_odd, up_head, gain_shares = together(
+        share, ff_sum, mix_odd, up_head, gain_shares
+    )
     input_sum = sum_cols(share)
 
-    gain_shares = jnp.stack([gain_share_one[..., 0], gain_share_two[..., 0]], axis=2)
     bits = near + far[::-1]
     gain_shares = fold({k: gain_shares[:, k] for k in range(count)}, "row", bits, low=False)[0]
     share, dq, dkv, attn_low, mix_rows = together(share, dq, dkv, attn_low, mix_rows)
     mix_even = {k: dot(attn_low, mix_rows[k], NT).astype(BF) for k in range(0, count, 2)}
     mix_near = fold({**mix_even, **mix_odd}, "row", near)
+    dq, dkv, mix_near = together(dq, dkv, mix_near)
+    mix_moved = {k: swapped(mix_near[k], "row", far_mask) for k in mix_near if k & far_mask}
     q_near = fold({k: dot(norm_one[k], dq, NT).astype(BF) for k in range(count)}, "row", near)
     kv_near = fold({k: dot(dkv, norm_one[k], NT).astype(BF) for k in range(count)}, "row", near)
-    mix_total = over_dp(fold(mix_near, "row", far)[0])
-    ff_sum, gain_shares, q_near, kv_near, up_tail = together(
-        ff_sum, gain_shares, q_near, kv_near, up_tail
-    )
+    ff_sum, gain_shares, q_near, kv_near, up_tail, mix_near, mix_moved = together(
+        ff_sum, gain_shares, q_near, kv_near, up_tail, mix_near, mix_moved
+    )
+    mix_far = fold_landed(mix_near, mix_moved, far_mask)
+    mix_total = over_dp(fold(mix_far, "row", far[::-1][1:])[0])
     q_far = fold(q_near, "row", far)[0]
     kv_far = fold(kv_near, "row", far)[0]
     q_total, kv_total = over_dp(q_far), over_dp(kv_far)

time: 921 us -> 905 us (0.983)
  waiting for transfers between devices: 437 us -> 427 us
  transfers between devices with their start and end apart: 77 -> 77, of which waited for: 36 -> 34; matrix products, arithmetic and copies ran while one was open for 15% -> 15% of each run, Pallas kernels for 24% -> 24%
where the time goes in v9:
time: 905 us; the launch traced here: 896 us
  waiting for transfers between devices  427 us (47%)
  Pallas kernels  216 us (24%)
  matrix products  82.4 us (9%)
  other arithmetic  51.3 us (6%)
  starting transfers between devices  43.9 us (5%)
  blocking collectives  34.2 us (4%)
  local copies, waits for them, and re-layouts  26.2 us (3%)
  between operations  15.5 us (2%)
    ppermute x59, waiting for transfers between devices, swapped(): return lax.ppermute(value, axis, [(i, i ^ mask) for i in range(size)])  262 us
    all_gather x5, waiting for transfers between devices, spread_cols(): return lax.all_gather(value, 'col', axis=0, tiled=False)  102 us
    pallas_call x2, Pallas kernels, feed_forward(): pl.pallas_call(functools.partial(ff_kernel, count, bool(before)), out_sha...  84 us
    dot_general x24, matrix products, dot(): return lax.dot_general(left, right, dims, preferred_element_type=F32)  82.4 us
    pallas_call x1, Pallas kernels, attend_back(): pl.pallas_call(functools.partial(attend_back_kernel, tile), out_shape=(sh...  37.4 us
    reduce_scatter x5, waiting for transfers between devices, sum_cols(): return lax.psum_scatter(value, 'col', scatter_dimension=0, tiled=False)  35.5 us
    ppermute x59, starting transfers between devices, swapped(): return lax.ppermute(value, axis, [(i, i ^ mask) for i in range(size)])  34.2 us
    all_gather x1, blocking collectives, body(): lax.all_gather(jnp.stack([attn_gain, mlp_gain]), ('row', 'col'), axis=1,...  34.2 us
  transfers between devices with their start and end apart: 77, of which 34 were waited for; matrix products, arithmetic and copies ran while one was open for 15% of the time, Pallas kernels for 24%

profile of v9, /device:TPU:0, one launch (start us, length us, event | category | flops | bytes accessed | tf_op | source)
XLA Modules:
  0.0 896.4 jit_solution(5895513218171939442)
XLA Ops:
  12.5 7.4 collective-permute-done.5
  19.9 7.2 collective-permute-done.4
  38.7 34.2 %all-gather.5 = f32[16,160,2]{1,2,0:T(2,128)S(1)} all-gather(f32[1,160,2]{1,2,0:T(2,128)S(1)} %maximum_bitcast_fusion.1), channel_id=1, replica_groups=mesh['dp'=2,'row'=4,'col'=4] {'row','col'}, dimensions={0}, use_global_device_ids=true | all-gather | bytes 21760 | tf_op jit(solution)/shard_map/all_gather | solution.py:758
  73.1 32.8 %collective-permute-done.2 = bf16[160,1024]{1,0:T(8,128)(2,1)} collective-permute-done((bf16[160,1024]{1,0:T(8,128)(2,1)}, bf16[160,1024]{1,0:T(8,128)(2,1)}, u32[]{:S(2)}, u32[]{:S(2)}) %collective-permute-start.2) | collective-permute-done | bytes 327712 | tf_op jit(solution)/shard_map/ppermute | solution.py:35
  106.5 6.4 collective-permute-done.1
  116.7 8.7 collective-permute-done.10.refs_6_
  127.9 13.6 %collective-permute-done.12.refs_2_.refs_3_ = bf16[640,640]{1,0:T(8,128)(2,1)} collective-permute-done((bf16[640,640]{1,0:T(8,128)(2,1)S(1)}, bf16[640,640]{1,0:T(8,128)(2,1)}, u32[]{:S(2)}, u32[]{:S(2)}) %collective-permute-start.12) | collective-permute-done | bytes 819232 | tf_op jit(solution)/shard_map/ppermute | solution.py:35
  144.6 13.1 %qkv_project.1 = (bf16[4,640,1024]{2,1,0:T(8,128)(2,1)}, f32[1,1024]{1,0:T(1,128)}, bf16[2,480,1024]{2,1,0:T(8,128)(2,1)}) custom-call(bf16[4,4,160,1024]{3,2,1,0:T(8,128)(2,1)} %bitcast.236, f32[4,4,160,1]{3,2,1,0:T(8,128)} %copy.66.gain_ref, f32[40,1024]{1,0:T(8,128)} %get-tuple-element.137.cos_ref, f32[40,1024]{1,0:T(8,128)} %get-tuple-element.138.sin_ref, ...), custom_call_target="tpu_custom_call" | custom-call | flops 1200000000 | tf_op jit(solution)/shard_map/qkv_project/pallas_call | solution.py:157
  163.6 27.8 %attend.1 = (bf16[320,1024]{1,0:T(8,128)(2,1)}, bf16[320,1024]{1,0:T(8,128)(2,1)}, f32[2,4,1,1024]{3,2,1,0:T(1,128)}) custom-call(s32[1]{0:T(128)} %bitcast.parity_ref, bf16[480,1024]{1,0:T(8,128)(2,1)} %get-tuple-element.258.own_ref, bf16[480,1024]{1,0:T(8,128)(2,1)} %collective-permute-done.15.other_ref, s32[1,1024]{1,0:T(1,128)} %bitcast.286, ...), custom_call_target="tpu_custom_call" | custom-call | flops 2700000000 | tf_op jit(solution)/shard_map/attend/pallas_call | solution.py:249
  194.6 10.2 %mix_out.1 = bf16[4,4,160,1024]{3,2,1,0:T(8,128)(2,1)} custom-call(s32[1]{0:T(128)} %bitcast.parity_ref, bf16[320,1024]{1,0:T(8,128)(2,1)} %get-tuple-element.215.own_ref.own_out, bf16[320,1024]{1,0:T(8,128)(2,1)} %copy-done.27, bf16[640,640]{1,0:T(8,128)(2,1)} %refs_1_, bf16[640,640]{1,0:T(8,128)(2,1)} %copy-done.19, ...), custom_call_target="tpu_custom_call" | custom-call | flops 1000000000 | tf_op jit(solution)/shard_map/mix_out/pallas_call | solution.py:424
  204.8 36.0 %all-gather.14.cloned.1.call-done = bf16[16,160,1024]{2,1,0:T(8,128)(2,1)} async-done(((bf16[4,160,1024]{2,1,0:T(8,128)(2,1)}), bf16[16,160,1024]{2,1,0:T(8,128)(2,1)}) %all-gather.14.cloned.1.call-update) | async-done | bytes 5242896 | tf_op jit(solution)/shard_map/all_gather | solution.py:676
  244.0 48.5 %collective-permute-done.25.refs_10_.refs_2_ = bf16[1728,640]{1,0:T(8,128)(2,1)S(1)} collective-permute-done((bf16[1728,640]{1,0:T(8,128)(2,1)S(1)}, bf16[1728,640]{1,0:T(8,128)(2,1)S(1)}, u32[]{:S(2)}, u32[]{:S(2)}) %collective-permute-start.25) | collective-permute-done | bytes 2211872 | tf_op jit(solution)/shard_map/ppermute | solution.py:35
  293.9 6.0 collective-permute-done.26.refs_11_.refs_3_
  309.7 25.7 %reduce-scatter.6.cloned.1.call-done = bf16[1,4,160,1024]{3,2,1,0:T(8,128)(2,1)} async-done(((bf16[4,4,160,1024]{3,2,1,0:T(8,128)(2,1)}), bf16[1,4,160,1024]{3,2,1,0:T(8,128)(2,1)}) %reduce-scatter.6.cloned.1.call-update) | async-done | bytes 1310736 | tf_op jit(solution)/shard_map/reduce_scatter | solution.py:680
  340.9 53.3 %all-gather.16.cloned.1.call-done = bf16[16,160,512]{2,1,0:T(8,128)(2,1)} async-done(((bf16[4,160,512]{2,1,0:T(8,128)(2,1)}), bf16[16,160,512]{2,1,0:T(8,128)(2,1)}) %all-gather.16.cloned.1.call-update) | async-done | bytes 2621456 | tf_op jit(solution)/shard_map/all_gather | solution.py:676
  394.2 42.2 %feed_forward.2 = (bf16[4,640,1024]{2,1,0:T(8,128)(2,1)}, bf16[4,640,1024]{2,1,0:T(8,128)(2,1)}, bf16[1728,1024]{1,0:T(8,128)(2,1)}, bf16[1728,1024]{1,0:T(8,128...) custom-call(bf16[4,4,160,512]{3,2,1,0:T(8,128)(2,1)} %bitcast.268, ...), custom_call_target="tpu_custom_call" | custom-call | flops 4200000000 | tf_op jit(solution)/shard_map/feed_forward/pallas_call | solution.py:563
  436.5 12.7 %all-gather.18.cloned.1.call-done = bf16[16,160,512]{2,1,0:T(8,128)(2,1)} async-done(((bf16[4,160,512]{2,1,0:T(8,128)(2,1)}), bf16[16,160,512]{2,1,0:T(8,128)(2,1)}) %all-gather.18.cloned.1.call-update) | async-done | bytes 2621456 | tf_op jit(solution)/shard_map/all_gather | solution.py:676
  449.2 41.8 %feed_forward.3 = (bf16[4,640,1024]{2,1,0:T(8,128)(2,1)}, bf16[4,640,1024]{2,1,0:T(8,128)(2,1)}, bf16[1728,1024]{1,0:T(8,128)(2,1)}, bf16[1728,1024]{1,0:T(8,128...) custom-call(bf16[4,4,160,512]{3,2,1,0:T(8,128)(2,1)} %bitcast.273, ...), custom_call_target="tpu_custom_call", output_to_operand_aliasing={{0}: (15, {}), {1}: (16, {}), {2}: (17, {}), {3}: (18, {}),... | custom-call | flops 4200000000 | tf_op jit(solution)/shard_map/feed_forward/pallas_call | solution.py:563
  491.0 6.9 convolution_convert_fusion.10
  497.9 5.6 convolution_convert_fusion.8
  554.6 9.8 %reduce-scatter.10.cloned.1.call-done = bf16[1,4,160,512]{3,2,1,0:T(8,128)(2,1)} async-done(((bf16[4,4,160,512]{3,2,1,0:T(8,128)(2,1)}), bf16[1,4,160,512]{3,2,1,0:T(8,128)(2,1)}) %reduce-scatter.10.cloned.1.call-update) | async-done | bytes 655376 | tf_op jit(solution)/shard_map/reduce_scatter | solution.py:680
  569.9 49.0 %collective-permute-done.33 = bf16[1728,640]{1,0:T(8,128)(2,1)S(1)} collective-permute-done((bf16[1728,640]{1,0:T(8,128)(2,1)S(1)}, bf16[1728,640]{1,0:T(8,128)(2,1)S(1)}, u32[]{:S(2)}, u32[]{:S(2)}) %collective-permute-start.33) | collective-permute-done | bytes 2211872 | tf_op jit(solution)/shard_map/ppermute | solution.py:35
  622.6 16.6 %fan_out.1 = bf16[4,4,160,1024]{3,2,1,0:T(8,128)(2,1)} custom-call(bf16[1728,1024]{1,0:T(8,128)(2,1)} %get-tuple-element.187.x_ref, bf16[1728,640]{1,0:T(8,128)(2,1)} %refs_0_.2, bf16[1728,640]{1,0:T(8,128)(2,1)} %copy-done.3, bf16[1728,640]{1,0:T(8,128)(2,1)} %copy-done.2, bf16[1728,640]{1,0:T(8,128)(2,1)} %copy-done.4), custom_call_target="tpu_custom_call" | custom-call | flops 1700000000 | tf_op jit(solution)/shard_map/fan_out/pallas_call | solution.py:485
  639.3 25.8 %collective-permute-done.35 = bf16[1728,640]{1,0:T(8,128)(2,1)} collective-permute-done((bf16[1728,640]{1,0:T(8,128)(2,1)}, bf16[1728,640]{1,0:T(8,128)(2,1)}, u32[]{:S(2)}, u32[]{:S(2)}) %collective-permute-start.35) | collective-permute-done | bytes 2211872 | tf_op jit(solution)/shard_map/ppermute | solution.py:35
  678.0 9.6 %mix_back.1 = (bf16[4,640,1024]{2,1,0:T(8,128)(2,1)}, bf16[320,1024]{1,0:T(8,128)(2,1)}, bf16[320,1024]{1,0:T(8,128)(2,1)}) custom-call(s32[1]{0:T(128)} %bitcast.parity_ref, bf16[4,4,160,1024]{3,2,1,0:T(8,128)(2,1)} %bitcast.248, bf16[640,640]{1,0:T(8,128)(2,1)} %refs_1_, bf16[640,640]{1,0:T(8,128)(2,1)} %copy-done.19, ...), custom_call_target="tpu_custom_call" | custom-call | flops 900000000 | tf_op jit(solution)/shard_map/mix_back/pallas_call | solution.py:459
  690.7 37.4 %attend_back.1 = (bf16[480,1024]{1,0:T(8,128)(2,1)}, bf16[480,1024]{1,0:T(8,128)(2,1)}) custom-call(s32[1]{0:T(128)} %bitcast.parity_ref, bf16[480,1024]{1,0:T(8,128)(2,1)} %get-tuple-element.258.own_ref, bf16[480,1024]{1,0:T(8,128)(2,1)} %collective-permute-done.15.other_ref, bf16[320,1024]{1,0:T(8,128)(2,1)} %get-tuple-element.215.own_ref.own_out, ...), custom_call_target="tpu_custom_call" | custom-call | flops 3700000000 | tf_op jit(solution)/shard_map/attend_back/pallas_call | solution.py:361
  739.0 17.6 %qkv_back.1 = (bf16[640,1024]{1,0:T(8,128)(2,1)}, bf16[320,1024]{1,0:T(8,128)(2,1)}, bf16[4,4,160,1024]{3,2,1,0:T(8,128)(2,1)}, f32[4,4,160,1]{3,2,1,0:T(8,128)}) custom-call(s32[1]{0:T(128)} %bitcast.parity_ref, bf16[4,4,160,1024]{3,2,1,0:T(8,128)(2,1)} %bitcast.237, f32[4,4,160,1]{3,2,1,0:T(8,128)} %copy.66.gain_ref, ...), custom_call_target="tpu_custom_call" | custom-call | flops 1700000000 | tf_op jit(solution)/shard_map/qkv_back/pallas_call | solution.py:653
  796.2 11.3 %collective-permute-done.51 = bf16[640,640]{1,0:T(8,128)(2,1)S(1)} collective-permute-done((bf16[640,640]{1,0:T(8,128)(2,1)S(1)}, bf16[640,640]{1,0:T(8,128)(2,1)S(1)}, u32[]{:S(2)}, u32[]{:S(2)}) %collective-permute-start.51) | collective-permute-done | bytes 819232 | tf_op jit(solution)/shard_map/ppermute | solution.py:35
  829.9 7.6 collective-permute-done.54
  851.3 16.1 %collective-permute-done.53 = bf16[640,640]{1,0:T(8,128)(2,1)S(1)} collective-permute-done((bf16[640,640]{1,0:T(8,128)(2,1)S(1)}, bf16[640,640]{1,0:T(8,128)(2,1)S(1)}, u32[]{:S(2)}, u32[]{:S(2)}) %collective-permute-start.53) | collective-permute-done | bytes 819232 | tf_op jit(solution)/shard_map/ppermute | solution.py:687
  874.5 7.1 collective-permute-done.65
  881.7 5.9 collective-permute-done.66
  (369 shorter events, 227.0 us)
Async XLA Ops:
  7.2 134.3 %all-gather.12.cloned.1.call-start = ((), (), s32[]{:S(2)}) async-start(), calls=%async_computation.10 | async-start | bytes 6553600 | tf_op jit(solution)/shard_map/all_gather | solution.py:676
  30.2 210.7 %all-gather.14.cloned.1.call-start = ((), (), s32[]{:S(2)}) async-start(), calls=%async_computation.11 | async-start | bytes 6553600 | tf_op jit(solution)/shard_map/all_gather | solution.py:676
  30.2 111.2 %collective-permute-start.13 = (bf16[1728,640]{1,0:T(8,128)(2,1)S(1)}, bf16[1728,640]{1,0:T(8,128)(2,1)}, u32[]{:S(2)}, u32[]{:S(2)}) collective-permute-start(bf16[1728,640]{1,0:T(8,128)(2,1)S(1)} %bitcast.243), channel_id=1, source_target_pairs={{0,8},{4,12},{8,0},{12,4},{1,9},{5,13},{9,1},{13,5},{2,10},{6,14},... | collective-permute-start | bytes 6635528 | tf_op jit(solution)/shard_map/ppermute | solution.py:35
  32.6 82.5 %collective-permute-start.7 = (bf16[640,640]{1,0:T(8,128)(2,1)}, bf16[640,640]{1,0:T(8,128)(2,1)}, u32[]{:S(2)}, u32[]{:S(2)}) collective-permute-start(bf16[640,640]{1,0:T(8,128)(2,1)} %refs_0_.3), channel_id=1, source_target_pairs={{0,8},{4,12},{8,0},{12,4},{1,9},{5,13},{9,1},{13,5},{2,10},{6,14},... | collective-permute-start | bytes 2457608 | tf_op jit(solution)/shard_map/ppermute | solution.py:35
  35.0 70.9 %collective-permute-start.2 = (bf16[160,1024]{1,0:T(8,128)(2,1)}, bf16[160,1024]{1,0:T(8,128)(2,1)}, u32[]{:S(2)}, u32[]{:S(2)}) collective-permute-start(bf16[160,1024]{1,0:T(8,128)(2,1)} %get-tuple-element.275), channel_id=1, source_target_pairs={{0,12},{4,8},{8,4},{12,0},{1,13},{5,9},{9,5},{13,1},{2,14},{6,10},... | collective-permute-start | bytes 983048 | tf_op jit(solution)/shard_map/ppermute | solution.py:35
  36.1 76.7 %collective-permute-start.1 = (bf16[160,1024]{1,0:T(8,128)(2,1)}, bf16[160,1024]{1,0:T(8,128)(2,1)}, u32[]{:S(2)}, u32[]{:S(2)}) collective-permute-start(bf16[160,1024]{1,0:T(8,128)(2,1)} %get-tuple-element.276), channel_id=1, source_target_pairs={{0,8},{4,12},{8,0},{12,4},{1,9},{5,13},{9,1},{13,5},{2,10},{6,14},... | collective-permute-start | bytes 983048 | tf_op jit(solution)/shard_map/ppermute | solution.py:35
  38.2 76.5 %collective-permute-start.9 = (bf16[320,640]{1,0:T(8,128)(2,1)S(1)}, bf16[320,640]{1,0:T(8,128)(2,1)}, u32[]{:S(2)}, u32[]{:S(2)}) collective-permute-start(bf16[320,640]{1,0:T(8,128)(2,1)S(1)} %pad_maximum_fusion.5.refs_4_), channel_id=1, source_target_pairs={{0,4},{4,0},{8,12},{12,8},{1,5},{5,1},{9,13},{13,9},{2,6},{6,2},{1... | collective-permute-start | bytes 1228808 | tf_op jit(solution)/shard_map/ppermute | solution.py:35
  114.7 26.7 %collective-permute-start.12 = (bf16[640,640]{1,0:T(8,128)(2,1)S(1)}, bf16[640,640]{1,0:T(8,128)(2,1)}, u32[]{:S(2)}, u32[]{:S(2)}) collective-permute-start(bf16[640,640]{1,0:T(8,128)(2,1)S(1)} %copy-done.18), channel_id=1, source_target_pairs={{0,8},{4,12},{8,0},{12,4},{1,9},{5,13},{9,1},{13,5},{2,10},{6,14},... | collective-permute-start | bytes 2457608 | tf_op jit(solution)/shard_map/ppermute | solution.py:35
  141.5 193.8 %reduce-scatter.6.cloned.1.call-start = ((), (), s32[]{:S(2)}) async-start(), calls=%async_computation.5 | async-start | bytes 6553600 | tf_op jit(solution)/shard_map/reduce_scatter | solution.py:680
  141.6 50.0 %collective-permute-start.19 = (bf16[1728,640]{1,0:T(8,128)(2,1)}, bf16[1728,640]{1,0:T(8,128)(2,1)S(1)}, u32[]{:S(2)}, u32[]{:S(2)}) collective-permute-start(bf16[1728,640]{1,0:T(8,128)(2,1)} %bitcast.244), channel_id=1, source_target_pairs={{0,8},{4,12},{8,0},{12,4},{1,9},{5,13},{9,1},{13,5},{2,10},{6,14},... | collective-permute-start | bytes 6635528 | tf_op jit(solution)/shard_map/ppermute | solution.py:35
  161.8 29.9 %collective-permute-start.17 = (bf16[640,640]{1,0:T(8,128)(2,1)S(1)}, bf16[640,640]{1,0:T(8,128)(2,1)S(1)}, u32[]{:S(2)}, u32[]{:S(2)}) collective-permute-start(bf16[640,640]{1,0:T(8,128)(2,1)S(1)} %copy-done.18), channel_id=1, source_target_pairs={{0,4},{4,0},{8,12},{12,8},{1,5},{5,1},{9,13},{13,9},{2,6},{6,2},{1... | collective-permute-start | bytes 2457608 | tf_op jit(solution)/shard_map/ppermute | solution.py:35
  162.3 29.4 %collective-permute-start.18 = (bf16[640,640]{1,0:T(8,128)(2,1)}, bf16[640,640]{1,0:T(8,128)(2,1)S(1)}, u32[]{:S(2)}, u32[]{:S(2)}) collective-permute-start(bf16[640,640]{1,0:T(8,128)(2,1)} %collective-permute-done.12.refs_2_.refs_3_), channel_id=1, source_target_pairs={{0,4},{4,0},{8,12},{12,8},{1,5},{5,1},{9,13},{13,9},{2,6},{6,2},{1... | collective-permute-start | bytes 2457608 | tf_op jit(solution)/shard_map/ppermute | solution.py:35
  240.9 153.3 %all-gather.16.cloned.1.call-start = ((), (), s32[]{:S(2)}) async-start(), calls=%async_computation.12 | async-start | bytes 3276800 | tf_op jit(solution)/shard_map/all_gather | solution.py:676
  242.5 50.0 %collective-permute-start.25 = (bf16[1728,640]{1,0:T(8,128)(2,1)S(1)}, bf16[1728,640]{1,0:T(8,128)(2,1)S(1)}, u32[]{:S(2)}, u32[]{:S(2)}) collective-permute-start(bf16[1728,640]{1,0:T(8,128)(2,1)S(1)} %copy-done.1), channel_id=1, source_target_pairs={{0,8},{4,12},{8,0},{12,4},{1,9},{5,13},{9,1},{13,5},{2,10},{6,14},... | collective-permute-start | bytes 6635528 | tf_op jit(solution)/shard_map/ppermute | solution.py:35
  244.0 49.5 %collective-permute-start.24 = (bf16[1728,640]{1,0:T(8,128)(2,1)S(1)}, bf16[1728,640]{1,0:T(8,128)(2,1)S(1)}, u32[]{:S(2)}, u32[]{:S(2)}) collective-permute-start(bf16[1728,640]{1,0:T(8,128)(2,1)S(1)} %copy-done.1), channel_id=1, source_target_pairs={{0,4},{4,0},{8,12},{12,8},{1,5},{5,1},{9,13},{13,9},{2,6},{6,2},{1... | collective-permute-start | bytes 6635528 | tf_op jit(solution)/shard_map/ppermute | solution.py:35
  338.7 110.5 %all-gather.18.cloned.1.call-start = ((), (), s32[]{:S(2)}) async-start(), calls=%async_computation.13 | async-start | bytes 3276800 | tf_op jit(solution)/shard_map/all_gather | solution.py:676
  339.3 215.2 %reduce-scatter.8.cloned.1.call-start = ((), (), s32[]{:S(2)}) async-start(), calls=%async_computation.6 | async-start | bytes 3276800 | tf_op jit(solution)/shard_map/reduce_scatter | solution.py:680
  436.5 127.9 %reduce-scatter.10.cloned.1.call-start = ((), (), s32[]{:S(2)}) async-start(), calls=%async_computation.7 | async-start | bytes 3276800 | tf_op jit(solution)/shard_map/reduce_scatter | solution.py:680
  512.9 27.9 %collective-permute-start.30 = (bf16[1728,640]{1,0:T(8,128)(2,1)}, bf16[1728,640]{1,0:T(8,128)(2,1)}, u32[]{:S(2)}, u32[]{:S(2)}) collective-permute-start(bf16[1728,640]{1,0:T(8,128)(2,1)} %convolution_convert_fusion.4), channel_id=1, source_target_pairs={{0,4},{4,0},{8,12},{12,8},{1,5},{5,1},{9,13},{13,9},{2,6},{6,2},{1... | collective-permute-start | bytes 6635528 | tf_op jit(solution)/shard_map/ppermute | solution.py:35
  513.4 160.0 %all-gather.20.cloned.1.call-start = ((), (), s32[]{:S(2)}) async-start(), calls=%async_computation.14 | async-start | bytes 6553600 | tf_op jit(solution)/shard_map/all_gather | solution.py:676
  567.4 204.7 %reduce-scatter.12.cloned.1.call-start = ((), (), s32[]{:S(2)}) async-start(), calls=%async_computation.8 | async-start | bytes 6553600 | tf_op jit(solution)/shard_map/reduce_scatter | solution.py:680
  567.8 51.1 %collective-permute-start.33 = (bf16[1728,640]{1,0:T(8,128)(2,1)S(1)}, bf16[1728,640]{1,0:T(8,128)(2,1)S(1)}, u32[]{:S(2)}, u32[]{:S(2)}) collective-permute-start(bf16[1728,640]{1,0:T(8,128)(2,1)S(1)} %copy-done.47), channel_id=1, source_target_pairs={{0,8},{4,12},{8,0},{12,4},{1,9},{5,13},{9,1},{13,5},{2,10},{6,14},... | collective-permute-start | bytes 6635528 | tf_op jit(solution)/shard_map/ppermute | solution.py:35
  569.4 95.7 %collective-permute-start.35 = (bf16[1728,640]{1,0:T(8,128)(2,1)}, bf16[1728,640]{1,0:T(8,128)(2,1)}, u32[]{:S(2)}, u32[]{:S(2)}) collective-permute-start(bf16[1728,640]{1,0:T(8,128)(2,1)} %add_convert_fusion.5), channel_id=1, source_target_pairs={{0,8},{4,12},{8,0},{12,4},{1,9},{5,13},{9,1},{13,5},{2,10},{6,14},... | collective-permute-start | bytes 6635528 | tf_op jit(solution)/shard_map/ppermute | solution.py:35
  621.1 48.1 %collective-permute-start.34 = (bf16[1728,640]{1,0:T(8,128)(2,1)S(1)}, bf16[1728,640]{1,0:T(8,128)(2,1)}, u32[]{:S(2)}, u32[]{:S(2)}) collective-permute-start(bf16[1728,640]{1,0:T(8,128)(2,1)S(1)} %add_convert_fusion.2), channel_id=1, source_target_pairs={{0,16},{16,0},{1,17},{17,1},{2,18},{18,2},{3,19},{19,3},{4,20},{20... | collective-permute-start | bytes 6635528 | tf_op jit(solution)/shard_map/ppermute | solution.py:687
  673.4 195.4 %reduce-scatter.14.cloned.1.call-start = ((), (), s32[]{:S(2)}) async-start(), calls=%async_computation.9 | async-start | bytes 6553600 | tf_op jit(solution)/shard_map/reduce_scatter | solution.py:680
  675.0 53.5 %collective-permute-start.38 = (bf16[1728,640]{1,0:T(8,128)(2,1)S(1)}, bf16[1728,640]{1,0:T(8,128)(2,1)}, u32[]{:S(2)}, u32[]{:S(2)}) collective-permute-start(bf16[1728,640]{1,0:T(8,128)(2,1)S(1)} %copy-done.46), channel_id=1, source_target_pairs={{0,8},{4,12},{8,0},{12,4},{1,9},{5,13},{9,1},{13,5},{2,10},{6,14},... | collective-permute-start | bytes 6635528 | tf_op jit(solution)/shard_map/ppermute | solution.py:35
  676.5 54.2 %collective-permute-start.39 = (bf16[1728,640]{1,0:T(8,128)(2,1)}, bf16[1728,640]{1,0:T(8,128)(2,1)}, u32[]{:S(2)}, u32[]{:S(2)}) collective-permute-start(bf16[1728,640]{1,0:T(8,128)(2,1)} %add_convert_fusion.1), channel_id=1, source_target_pairs={{0,16},{16,0},{1,17},{17,1},{2,18},{18,2},{3,19},{19,3},{4,20},{20... | collective-permute-start | bytes 6635528 | tf_op jit(solution)/shard_map/ppermute | solution.py:687
  736.8 32.3 %collective-permute-start.40 = (bf16[960,640]{1,0:T(8,128)(2,1)}, bf16[960,640]{1,0:T(8,128)(2,1)}, u32[]{:S(2)}, u32[]{:S(2)}) collective-permute-start(bf16[960,640]{1,0:T(8,128)(2,1)} %slice.138), channel_id=1, source_target_pairs={{0,16},{16,0},{1,17},{17,1},{2,18},{18,2},{3,19},{19,3},{4,20},{20... | collective-permute-start | bytes 3686408 | tf_op jit(solution)/shard_map/ppermute | solution.py:687
  807.5 30.1 %collective-permute-start.52 = (bf16[640,640]{1,0:T(8,128)(2,1)S(1)}, bf16[640,640]{1,0:T(8,128)(2,1)S(1)}, u32[]{:S(2)}, u32[]{:S(2)}) collective-permute-start(bf16[640,640]{1,0:T(8,128)(2,1)S(1)} %add_convert_fusion.13), channel_id=1, source_target_pairs={{0,8},{4,12},{8,0},{12,4},{1,9},{5,13},{9,1},{13,5},{2,10},{6,14},... | collective-permute-start | bytes 2457608 | tf_op jit(solution)/shard_map/ppermute | solution.py:35
  808.5 29.0 %collective-permute-start.54 = (bf16[320,640]{1,0:T(8,128)(2,1)S(1)}, bf16[320,640]{1,0:T(8,128)(2,1)S(1)}, u32[]{:S(2)}, u32[]{:S(2)}) collective-permute-start(bf16[320,640]{1,0:T(8,128)(2,1)S(1)} %fusion.62), channel_id=1, source_target_pairs={{0,8},{4,12},{8,0},{12,4},{1,9},{5,13},{9,1},{13,5},{2,10},{6,14},... | collective-permute-start | bytes 1228808 | tf_op jit(solution)/shard_map/ppermute | solution.py:35
  809.8 40.2 %collective-permute-start.56 = (bf16[640,640]{1,0:T(8,128)(2,1)S(1)}, bf16[640,640]{1,0:T(8,128)(2,1)S(1)}, u32[]{:S(2)}, u32[]{:S(2)}) collective-permute-start(bf16[640,640]{1,0:T(8,128)(2,1)S(1)} %add_convert_fusion.11), channel_id=1, source_target_pairs={{0,16},{16,0},{1,17},{17,1},{2,18},{18,2},{3,19},{19,3},{4,20},{20... | collective-permute-start | bytes 2457608 | tf_op jit(solution)/shard_map/ppermute | solution.py:687
  839.0 28.5 %collective-permute-start.53 = (bf16[640,640]{1,0:T(8,128)(2,1)S(1)}, bf16[640,640]{1,0:T(8,128)(2,1)S(1)}, u32[]{:S(2)}, u32[]{:S(2)}) collective-permute-start(bf16[640,640]{1,0:T(8,128)(2,1)S(1)} %add_convert_fusion.12), channel_id=1, source_target_pairs={{0,16},{16,0},{1,17},{17,1},{2,18},{18,2},{3,19},{19,3},{4,20},{20... | collective-permute-start | bytes 2457608 | tf_op jit(solution)/shard_map/ppermute | solution.py:687
  (106 other events, 1164.5 us)
Sparse Core Ops, SparseCore 0:
  30.3 100.5 all-gather.11
  141.6 99.1 all-gather.13
  243.2 92.1 reduce-scatter.5
  338.9 55.3 all-gather.15
  395.6 53.5 all-gather.17
  452.0 50.8 reduce-scatter.7
  513.5 50.7 reduce-scatter.9
  567.5 97.7 all-gather.19
  673.5 93.6 reduce-scatter.11
  772.2 92.3 reduce-scatter.13

commit v10 on v9

--- a/solution.py
+++ b/solution.py
@@ -745,10 +745,17 @@
         return [blocks[k] for k in range(count)]
 
     source_own = row_tokens(layer_input)
+    source_own, output_grad = together(source_own, output_grad)
+    grad_own = row_tokens(output_grad)
     kv_weight = jnp.concatenate([key_weight.T, value_weight.T])
+    grad_own, query_weight, kv_weight = together(grad_own, query_weight, kv_weight)
     q_first = spread({0: query_weight}, "row", far)
     kv_first = spread({0: kv_weight}, "row", far)
+    q_first, kv_first, mix_weight, gate_weight, attn_gain = together(
+        q_first, kv_first, mix_weight, gate_weight, attn_gain
+    )
     mix_first = spread({0: mix_weight}, "row", far)
+    mix_first, up_weight = together(mix_first, up_weight)
     gate_first = spread({0: gate_weight.T}, "row", far)
     up_first = spread({0: up_weight.T}, "row", far)
     down_first = spread({0: down_weight}, "row", far)
@@ -765,10 +772,9 @@
     seg = jnp.where(parity == 0, other_seg, segment_ids)
 
     source = spread_cols(source_own)
-    source, q_blocks, kv_blocks, mix_first, gate_first, gain_one, cosine, sine, seg = together(
-        source, q_blocks, kv_blocks, mix_first, gate_first, gain_one, cosine, sine, seg
-    )
-    grad_own = row_tokens(output_grad)
+    source, q_blocks, kv_blocks, gate_first, gain_one, cosine, sine, seg = together(
+        source, q_blocks, kv_blocks, gate_first, gain_one, cosine, sine, seg
+    )
     grad_own, source = together(grad_own, source)
     grad_all = spread_cols(grad_own)
     norm_one, scale_one, sets = qkv_project(

time: 905 us -> 891 us (0.985)
    all_gather x5, waiting for transfers between devices: 102 us -> 82.6 us  [spread_cols(): return lax.all_gather(value, 'col', axis=0, tiled=False)]
    ppermute x59, waiting for transfers between devices: 262 us -> 273 us  [swapped(): return lax.ppermute(value, axis, [(i, i ^ mask) for i in range(size)])]
  transfers between devices with their start and end apart: 77 -> 77, of which waited for: 34 -> 36; matrix products, arithmetic and copies ran while one was open for 15% -> 15% of each run, Pallas kernels for 24% -> 24%
where the time goes in v10:
time: 891 us; the launch traced here: 882 us
  waiting for transfers between devices  419 us (47%)
  Pallas kernels  216 us (24%)
  matrix products  82.5 us (9%)
  other arithmetic  46.5 us (5%)
  starting transfers between devices  45.3 us (5%)
  blocking collectives  34 us (4%)
  local copies, waits for them, and re-layouts  23.2 us (3%)
  between operations  15.4 us (2%)
    ppermute x59, waiting for transfers between devices, swapped(): return lax.ppermute(value, axis, [(i, i ^ mask) for i in range(size)])  273 us
    pallas_call x2, Pallas kernels, feed_forward(): pl.pallas_call(functools.partial(ff_kernel, count, bool(before)), out_sha...  84 us
    all_gather x5, waiting for transfers between devices, spread_cols(): return lax.all_gather(value, 'col', axis=0, tiled=False)  82.6 us
    dot_general x24, matrix products, dot(): return lax.dot_general(left, right, dims, preferred_element_type=F32)  82.5 us
    pallas_call x1, Pallas kernels, attend_back(): pl.pallas_call(functools.partial(attend_back_kernel, tile), out_shape=(sh...  37.4 us
    ppermute x59, starting transfers between devices, swapped(): return lax.ppermute(value, axis, [(i, i ^ mask) for i in range(size)])  35.6 us
    reduce_scatter x5, waiting for transfers between devices, sum_cols(): return lax.psum_scatter(value, 'col', scatter_dimension=0, tiled=False)  35.4 us
    all_gather x1, blocking collectives, body(): lax.all_gather(jnp.stack([attn_gain, mlp_gain]), ('row', 'col'), axis=1,...  34 us
  transfers between devices with their start and end apart: 77, of which 36 were waited for; matrix products, arithmetic and copies ran while one was open for 15% of the time, Pallas kernels for 24%

profile of v10, /device:TPU:0, one launch (start us, length us, event | category | flops | bytes accessed | tf_op | source)
XLA Modules:
  0.0 882.2 jit_solution(15874102477736293222)
XLA Ops:
  11.8 7.4 collective-permute-done.2
  19.2 7.2 collective-permute-done.1
  30.5 7.6 collective-permute-done.5
  38.1 7.2 collective-permute-done.4
  48.6 27.3 %collective-permute-done.7.refs_6_ = bf16[320,640]{1,0:T(8,128)(2,1)S(1)} collective-permute-done((bf16[320,640]{1,0:T(8,128)(2,1)S(1)}, bf16[320,640]{1,0:T(8,128)(2,1)S(1)}, u32[]{:S(2)}, u32[]{:S(2)}) %collective-permute-start.7) | collective-permute-done | bytes 409632 | tf_op jit(solution)/shard_map/ppermute | solution.py:35
  80.4 34.0 %all-gather.5 = f32[16,160,2]{1,2,0:T(2,128)S(1)} all-gather(f32[1,160,2]{1,2,0:T(2,128)S(1)} %maximum_bitcast_fusion.1), channel_id=1, replica_groups=mesh['dp'=2,'row'=4,'col'=4] {'row','col'}, dimensions={0}, use_global_device_ids=true | all-gather | bytes 21760 | tf_op jit(solution)/shard_map/all_gather | solution.py:765
  114.7 11.0 %collective-permute-done.12.refs_2_ = bf16[1728,640]{1,0:T(8,128)(2,1)} collective-permute-done((bf16[1728,640]{1,0:T(8,128)(2,1)S(1)}, bf16[1728,640]{1,0:T(8,128)(2,1)}, u32[]{:S(2)}, u32[]{:S(2)}) %collective-permute-start.12) | collective-permute-done | bytes 2211872 | tf_op jit(solution)/shard_map/ppermute | solution.py:35
  130.1 18.7 %collective-permute-done.16.refs_2_.refs_3_ = bf16[640,640]{1,0:T(8,128)(2,1)} collective-permute-done((bf16[640,640]{1,0:T(8,128)(2,1)S(1)}, bf16[640,640]{1,0:T(8,128)(2,1)}, u32[]{:S(2)}, u32[]{:S(2)}) %collective-permute-start.16) | collective-permute-done | bytes 819232 | tf_op jit(solution)/shard_map/ppermute | solution.py:35
  151.9 13.1 %qkv_project.1 = (bf16[4,640,1024]{2,1,0:T(8,128)(2,1)}, f32[1,1024]{1,0:T(1,128)}, bf16[2,480,1024]{2,1,0:T(8,128)(2,1)}) custom-call(bf16[4,4,160,1024]{3,2,1,0:T(8,128)(2,1)} %bitcast.236, f32[4,4,160,1]{3,2,1,0:T(8,128)} %copy.66.gain_ref, f32[40,1024]{1,0:T(8,128)} %get-tuple-element.161.cos_ref, f32[40,1024]{1,0:T(8,128)} %get-tuple-element.162.sin_ref, ...), custom_call_target="tpu_custom_call" | custom-call | flops 1200000000 | tf_op jit(solution)/shard_map/qkv_project/pallas_call | solution.py:157
  172.0 27.8 %attend.1 = (bf16[320,1024]{1,0:T(8,128)(2,1)}, bf16[320,1024]{1,0:T(8,128)(2,1)}, f32[2,4,1,1024]{3,2,1,0:T(1,128)}) custom-call(s32[1]{0:T(128)} %bitcast.parity_ref, bf16[480,1024]{1,0:T(8,128)(2,1)} %get-tuple-element.284.own_ref, bf16[480,1024]{1,0:T(8,128)(2,1)} %collective-permute-done.14.other_ref, s32[1,1024]{1,0:T(1,128)} %bitcast.282, ...), custom_call_target="tpu_custom_call" | custom-call | flops 2700000000 | tf_op jit(solution)/shard_map/attend/pallas_call | solution.py:249
  202.9 10.2 %mix_out.1 = bf16[4,4,160,1024]{3,2,1,0:T(8,128)(2,1)} custom-call(s32[1]{0:T(128)} %bitcast.parity_ref, bf16[320,1024]{1,0:T(8,128)(2,1)} %get-tuple-element.241.own_ref.own_out, bf16[320,1024]{1,0:T(8,128)(2,1)} %copy-done.21, bf16[640,640]{1,0:T(8,128)(2,1)} %refs_1_, bf16[640,640]{1,0:T(8,128)(2,1)} %collective-permute-done.17.refs_1_.refs_2_, ...), custom_call_target="tpu_custom_call" | custom-call | flops 1000000000 | tf_op jit(solution)/shard_map/mix_out/pallas_call | solution.py:424
  213.1 14.0 %all-gather.14.cloned.1.call-done = bf16[16,160,1024]{2,1,0:T(8,128)(2,1)} async-done(((bf16[4,160,1024]{2,1,0:T(8,128)(2,1)}), bf16[16,160,1024]{2,1,0:T(8,128)(2,1)}) %all-gather.14.cloned.1.call-update) | async-done | bytes 5242896 | tf_op jit(solution)/shard_map/all_gather | solution.py:676
  230.2 48.5 %collective-permute-done.25.refs_10_.refs_2_ = bf16[1728,640]{1,0:T(8,128)(2,1)S(1)} collective-permute-done((bf16[1728,640]{1,0:T(8,128)(2,1)S(1)}, bf16[1728,640]{1,0:T(8,128)(2,1)S(1)}, u32[]{:S(2)}, u32[]{:S(2)}) %collective-permute-start.25) | collective-permute-done | bytes 2211872 | tf_op jit(solution)/shard_map/ppermute | solution.py:35
  280.1 6.1 collective-permute-done.26.refs_11_.refs_3_
  295.9 25.7 %reduce-scatter.6.cloned.1.call-done = bf16[1,4,160,1024]{3,2,1,0:T(8,128)(2,1)} async-done(((bf16[4,4,160,1024]{3,2,1,0:T(8,128)(2,1)}), bf16[1,4,160,1024]{3,2,1,0:T(8,128)(2,1)}) %reduce-scatter.6.cloned.1.call-update) | async-done | bytes 1310736 | tf_op jit(solution)/shard_map/reduce_scatter | solution.py:680
  326.9 53.2 %all-gather.16.cloned.1.call-done = bf16[16,160,512]{2,1,0:T(8,128)(2,1)} async-done(((bf16[4,160,512]{2,1,0:T(8,128)(2,1)}), bf16[16,160,512]{2,1,0:T(8,128)(2,1)}) %all-gather.16.cloned.1.call-update) | async-done | bytes 2621456 | tf_op jit(solution)/shard_map/all_gather | solution.py:676
  380.1 42.2 %feed_forward.2 = (bf16[4,640,1024]{2,1,0:T(8,128)(2,1)}, bf16[4,640,1024]{2,1,0:T(8,128)(2,1)}, bf16[1728,1024]{1,0:T(8,128)(2,1)}, bf16[1728,1024]{1,0:T(8,128...) custom-call(bf16[4,4,160,512]{3,2,1,0:T(8,128)(2,1)} %bitcast.259, ...), custom_call_target="tpu_custom_call" | custom-call | flops 4200000000 | tf_op jit(solution)/shard_map/feed_forward/pallas_call | solution.py:563
  422.4 12.7 %all-gather.18.cloned.1.call-done = bf16[16,160,512]{2,1,0:T(8,128)(2,1)} async-done(((bf16[4,160,512]{2,1,0:T(8,128)(2,1)}), bf16[16,160,512]{2,1,0:T(8,128)(2,1)}) %all-gather.18.cloned.1.call-update) | async-done | bytes 2621456 | tf_op jit(solution)/shard_map/all_gather | solution.py:676
  435.1 41.8 %feed_forward.3 = (bf16[4,640,1024]{2,1,0:T(8,128)(2,1)}, bf16[4,640,1024]{2,1,0:T(8,128)(2,1)}, bf16[1728,1024]{1,0:T(8,128)(2,1)}, bf16[1728,1024]{1,0:T(8,128...) custom-call(bf16[4,4,160,512]{3,2,1,0:T(8,128)(2,1)} %bitcast.264, ...), custom_call_target="tpu_custom_call", output_to_operand_aliasing={{0}: (15, {}), {1}: (16, {}), {2}: (17, {}), {3}: (18, {}),... | custom-call | flops 4200000000 | tf_op jit(solution)/shard_map/feed_forward/pallas_call | solution.py:563
  477.0 6.9 convolution_convert_fusion.10
  540.5 9.8 %reduce-scatter.10.cloned.1.call-done = bf16[1,4,160,512]{3,2,1,0:T(8,128)(2,1)} async-done(((bf16[4,4,160,512]{3,2,1,0:T(8,128)(2,1)}), bf16[1,4,160,512]{3,2,1,0:T(8,128)(2,1)}) %reduce-scatter.10.cloned.1.call-update) | async-done | bytes 655376 | tf_op jit(solution)/shard_map/reduce_scatter | solution.py:680
  555.9 49.0 %collective-permute-done.33 = bf16[1728,640]{1,0:T(8,128)(2,1)S(1)} collective-permute-done((bf16[1728,640]{1,0:T(8,128)(2,1)S(1)}, bf16[1728,640]{1,0:T(8,128)(2,1)S(1)}, u32[]{:S(2)}, u32[]{:S(2)}) %collective-permute-start.33) | collective-permute-done | bytes 2211872 | tf_op jit(solution)/shard_map/ppermute | solution.py:35
  608.6 16.6 %fan_out.1 = bf16[4,4,160,1024]{3,2,1,0:T(8,128)(2,1)} custom-call(bf16[1728,1024]{1,0:T(8,128)(2,1)} %get-tuple-element.213.x_ref, bf16[1728,640]{1,0:T(8,128)(2,1)} %refs_0_.2, bf16[1728,640]{1,0:T(8,128)(2,1)} %copy-done.5, bf16[1728,640]{1,0:T(8,128)(2,1)} %copy-done.4, bf16[1728,640]{1,0:T(8,128)(2,1)} %copy-done.6), custom_call_target="tpu_custom_call" | custom-call | flops 1700000000 | tf_op jit(solution)/shard_map/fan_out/pallas_call | solution.py:485
  625.2 25.8 %collective-permute-done.35 = bf16[1728,640]{1,0:T(8,128)(2,1)} collective-permute-done((bf16[1728,640]{1,0:T(8,128)(2,1)}, bf16[1728,640]{1,0:T(8,128)(2,1)}, u32[]{:S(2)}, u32[]{:S(2)}) %collective-permute-start.35) | collective-permute-done | bytes 2211872 | tf_op jit(solution)/shard_map/ppermute | solution.py:35
  664.0 9.6 %mix_back.1 = (bf16[4,640,1024]{2,1,0:T(8,128)(2,1)}, bf16[320,1024]{1,0:T(8,128)(2,1)}, bf16[320,1024]{1,0:T(8,128)(2,1)}) custom-call(s32[1]{0:T(128)} %bitcast.parity_ref, bf16[4,4,160,1024]{3,2,1,0:T(8,128)(2,1)} %bitcast.248, bf16[640,640]{1,0:T(8,128)(2,1)} %refs_1_, bf16[640,640]{1,0:T(8,128)(2,1)} %collective-permute-done.17.refs_1_.refs_2_, ...), custom_call_target="tpu_custom_call" | custom-call | flops 900000000 | tf_op jit(solution)/shard_map/mix_back/pallas_call | solution.py:459
  676.7 37.4 %attend_back.1 = (bf16[480,1024]{1,0:T(8,128)(2,1)}, bf16[480,1024]{1,0:T(8,128)(2,1)}) custom-call(s32[1]{0:T(128)} %bitcast.parity_ref, bf16[480,1024]{1,0:T(8,128)(2,1)} %get-tuple-element.284.own_ref, bf16[480,1024]{1,0:T(8,128)(2,1)} %collective-permute-done.14.other_ref, bf16[320,1024]{1,0:T(8,128)(2,1)} %get-tuple-element.241.own_ref.own_out, ...), custom_call_target="tpu_custom_call" | custom-call | flops 3700000000 | tf_op jit(solution)/shard_map/attend_back/pallas_call | solution.py:361
  725.0 17.3 %qkv_back.1 = (bf16[640,1024]{1,0:T(8,128)(2,1)}, bf16[320,1024]{1,0:T(8,128)(2,1)}, bf16[4,4,160,1024]{3,2,1,0:T(8,128)(2,1)}, f32[4,4,160,1]{3,2,1,0:T(8,128)}) custom-call(s32[1]{0:T(128)} %bitcast.parity_ref, bf16[4,4,160,1024]{3,2,1,0:T(8,128)(2,1)} %bitcast.237, f32[4,4,160,1]{3,2,1,0:T(8,128)} %copy.66.gain_ref, ...), custom_call_target="tpu_custom_call" | custom-call | flops 1700000000 | tf_op jit(solution)/shard_map/qkv_back/pallas_call | solution.py:653
  782.0 11.3 %collective-permute-done.51 = bf16[640,640]{1,0:T(8,128)(2,1)S(1)} collective-permute-done((bf16[640,640]{1,0:T(8,128)(2,1)S(1)}, bf16[640,640]{1,0:T(8,128)(2,1)S(1)}, u32[]{:S(2)}, u32[]{:S(2)}) %collective-permute-start.51) | collective-permute-done | bytes 819232 | tf_op jit(solution)/shard_map/ppermute | solution.py:35
  815.7 7.6 collective-permute-done.54
  837.2 16.1 %collective-permute-done.53 = bf16[640,640]{1,0:T(8,128)(2,1)S(1)} collective-permute-done((bf16[640,640]{1,0:T(8,128)(2,1)S(1)}, bf16[640,640]{1,0:T(8,128)(2,1)S(1)}, u32[]{:S(2)}, u32[]{:S(2)}) %collective-permute-start.53) | collective-permute-done | bytes 819232 | tf_op jit(solution)/shard_map/ppermute | solution.py:687
  860.4 7.1 collective-permute-done.65
  867.5 5.9 collective-permute-done.66
  (363 shorter events, 230.5 us)
Async XLA Ops:
  7.2 121.3 %all-gather.12.cloned.1.call-start = ((), (), s32[]{:S(2)}) async-start(), calls=%async_computation.10 | async-start | bytes 6553600 | tf_op jit(solution)/shard_map/all_gather | solution.py:676
  27.7 199.4 %all-gather.14.cloned.1.call-start = ((), (), s32[]{:S(2)}) async-start(), calls=%async_computation.11 | async-start | bytes 6553600 | tf_op jit(solution)/shard_map/all_gather | solution.py:676
  46.5 29.4 %collective-permute-start.6 = (bf16[640,640]{1,0:T(8,128)(2,1)}, bf16[640,640]{1,0:T(8,128)(2,1)}, u32[]{:S(2)}, u32[]{:S(2)}) collective-permute-start(bf16[640,640]{1,0:T(8,128)(2,1)} %refs_0_.3), channel_id=1, source_target_pairs={{0,8},{4,12},{8,0},{12,4},{1,9},{5,13},{9,1},{13,5},{2,10},{6,14},... | collective-permute-start | bytes 2457608 | tf_op jit(solution)/shard_map/ppermute | solution.py:35
  75.9 49.8 %collective-permute-start.12 = (bf16[1728,640]{1,0:T(8,128)(2,1)S(1)}, bf16[1728,640]{1,0:T(8,128)(2,1)}, u32[]{:S(2)}, u32[]{:S(2)}) collective-permute-start(bf16[1728,640]{1,0:T(8,128)(2,1)S(1)} %bitcast.243), channel_id=1, source_target_pairs={{0,8},{4,12},{8,0},{12,4},{1,9},{5,13},{9,1},{13,5},{2,10},{6,14},... | collective-permute-start | bytes 6635528 | tf_op jit(solution)/shard_map/ppermute | solution.py:35
  77.8 36.9 %collective-permute-start.8 = (bf16[640,640]{1,0:T(8,128)(2,1)}, bf16[640,640]{1,0:T(8,128)(2,1)}, u32[]{:S(2)}, u32[]{:S(2)}) collective-permute-start(bf16[640,640]{1,0:T(8,128)(2,1)} %refs_0_.3), channel_id=1, source_target_pairs={{0,4},{4,0},{8,12},{12,8},{1,5},{5,1},{9,13},{13,9},{2,6},{6,2},{1... | collective-permute-start | bytes 2457608 | tf_op jit(solution)/shard_map/ppermute | solution.py:35
  78.3 36.4 %collective-permute-start.9 = (bf16[640,640]{1,0:T(8,128)(2,1)}, bf16[640,640]{1,0:T(8,128)(2,1)}, u32[]{:S(2)}, u32[]{:S(2)}) collective-permute-start(bf16[640,640]{1,0:T(8,128)(2,1)} %collective-permute-done.6.refs_2_), channel_id=1, source_target_pairs={{0,4},{4,0},{8,12},{12,8},{1,5},{5,1},{9,13},{13,9},{2,6},{6,2},{1... | collective-permute-start | bytes 2457608 | tf_op jit(solution)/shard_map/ppermute | solution.py:35
  79.8 34.9 %collective-permute-start.10 = (bf16[320,640]{1,0:T(8,128)(2,1)S(1)}, bf16[320,640]{1,0:T(8,128)(2,1)}, u32[]{:S(2)}, u32[]{:S(2)}) collective-permute-start(bf16[320,640]{1,0:T(8,128)(2,1)S(1)} %pad_maximum_fusion.5.refs_4_), channel_id=1, source_target_pairs={{0,4},{4,0},{8,12},{12,8},{1,5},{5,1},{9,13},{13,9},{2,6},{6,2},{1... | collective-permute-start | bytes 1228808 | tf_op jit(solution)/shard_map/ppermute | solution.py:35
  80.3 34.4 %collective-permute-start.11 = (bf16[320,640]{1,0:T(8,128)(2,1)}, bf16[320,640]{1,0:T(8,128)(2,1)}, u32[]{:S(2)}, u32[]{:S(2)}) collective-permute-start(bf16[320,640]{1,0:T(8,128)(2,1)} %copy-done.29), channel_id=1, source_target_pairs={{0,4},{4,0},{8,12},{12,8},{1,5},{5,1},{9,13},{13,9},{2,6},{6,2},{1... | collective-permute-start | bytes 1228808 | tf_op jit(solution)/shard_map/ppermute | solution.py:35
  128.5 193.1 %reduce-scatter.6.cloned.1.call-start = ((), (), s32[]{:S(2)}) async-start(), calls=%async_computation.5 | async-start | bytes 6553600 | tf_op jit(solution)/shard_map/reduce_scatter | solution.py:680
  148.8 51.1 %collective-permute-start.19 = (bf16[1728,640]{1,0:T(8,128)(2,1)}, bf16[1728,640]{1,0:T(8,128)(2,1)S(1)}, u32[]{:S(2)}, u32[]{:S(2)}) collective-permute-start(bf16[1728,640]{1,0:T(8,128)(2,1)} %bitcast.244), channel_id=1, source_target_pairs={{0,8},{4,12},{8,0},{12,4},{1,9},{5,13},{9,1},{13,5},{2,10},{6,14},... | collective-permute-start | bytes 6635528 | tf_op jit(solution)/shard_map/ppermute | solution.py:35
  167.9 32.1 %collective-permute-start.17 = (bf16[640,640]{1,0:T(8,128)(2,1)S(1)}, bf16[640,640]{1,0:T(8,128)(2,1)}, u32[]{:S(2)}, u32[]{:S(2)}) collective-permute-start(bf16[640,640]{1,0:T(8,128)(2,1)S(1)} %copy-done.20), channel_id=1, source_target_pairs={{0,4},{4,0},{8,12},{12,8},{1,5},{5,1},{9,13},{13,9},{2,6},{6,2},{1... | collective-permute-start | bytes 2457608 | tf_op jit(solution)/shard_map/ppermute | solution.py:35
  168.4 31.6 %collective-permute-start.18 = (bf16[640,640]{1,0:T(8,128)(2,1)}, bf16[640,640]{1,0:T(8,128)(2,1)}, u32[]{:S(2)}, u32[]{:S(2)}) collective-permute-start(bf16[640,640]{1,0:T(8,128)(2,1)} %collective-permute-done.16.refs_2_.refs_3_), channel_id=1, source_target_pairs={{0,4},{4,0},{8,12},{12,8},{1,5},{5,1},{9,13},{13,9},{2,6},{6,2},{1... | collective-permute-start | bytes 2457608 | tf_op jit(solution)/shard_map/ppermute | solution.py:35
  227.2 153.0 %all-gather.16.cloned.1.call-start = ((), (), s32[]{:S(2)}) async-start(), calls=%async_computation.12 | async-start | bytes 3276800 | tf_op jit(solution)/shard_map/all_gather | solution.py:676
  228.8 50.0 %collective-permute-start.25 = (bf16[1728,640]{1,0:T(8,128)(2,1)S(1)}, bf16[1728,640]{1,0:T(8,128)(2,1)S(1)}, u32[]{:S(2)}, u32[]{:S(2)}) collective-permute-start(bf16[1728,640]{1,0:T(8,128)(2,1)S(1)} %copy-done.3), channel_id=1, source_target_pairs={{0,8},{4,12},{8,0},{12,4},{1,9},{5,13},{9,1},{13,5},{2,10},{6,14},... | collective-permute-start | bytes 6635528 | tf_op jit(solution)/shard_map/ppermute | solution.py:35
  230.2 49.5 %collective-permute-start.24 = (bf16[1728,640]{1,0:T(8,128)(2,1)S(1)}, bf16[1728,640]{1,0:T(8,128)(2,1)S(1)}, u32[]{:S(2)}, u32[]{:S(2)}) collective-permute-start(bf16[1728,640]{1,0:T(8,128)(2,1)S(1)} %copy-done.3), channel_id=1, source_target_pairs={{0,4},{4,0},{8,12},{12,8},{1,5},{5,1},{9,13},{13,9},{2,6},{6,2},{1... | collective-permute-start | bytes 6635528 | tf_op jit(solution)/shard_map/ppermute | solution.py:35
  324.7 110.5 %all-gather.18.cloned.1.call-start = ((), (), s32[]{:S(2)}) async-start(), calls=%async_computation.13 | async-start | bytes 3276800 | tf_op jit(solution)/shard_map/all_gather | solution.py:676
  325.2 215.3 %reduce-scatter.8.cloned.1.call-start = ((), (), s32[]{:S(2)}) async-start(), calls=%async_computation.6 | async-start | bytes 3276800 | tf_op jit(solution)/shard_map/reduce_scatter | solution.py:680
  422.4 127.9 %reduce-scatter.10.cloned.1.call-start = ((), (), s32[]{:S(2)}) async-start(), calls=%async_computation.7 | async-start | bytes 3276800 | tf_op jit(solution)/shard_map/reduce_scatter | solution.py:680
  498.9 27.9 %collective-permute-start.30 = (bf16[1728,640]{1,0:T(8,128)(2,1)}, bf16[1728,640]{1,0:T(8,128)(2,1)}, u32[]{:S(2)}, u32[]{:S(2)}) collective-permute-start(bf16[1728,640]{1,0:T(8,128)(2,1)} %convolution_convert_fusion.4), channel_id=1, source_target_pairs={{0,4},{4,0},{8,12},{12,8},{1,5},{5,1},{9,13},{13,9},{2,6},{6,2},{1... | collective-permute-start | bytes 6635528 | tf_op jit(solution)/shard_map/ppermute | solution.py:35
  499.4 160.0 %all-gather.20.cloned.1.call-start = ((), (), s32[]{:S(2)}) async-start(), calls=%async_computation.14 | async-start | bytes 6553600 | tf_op jit(solution)/shard_map/all_gather | solution.py:676
  553.3 204.6 %reduce-scatter.12.cloned.1.call-start = ((), (), s32[]{:S(2)}) async-start(), calls=%async_computation.8 | async-start | bytes 6553600 | tf_op jit(solution)/shard_map/reduce_scatter | solution.py:680
  553.8 51.1 %collective-permute-start.33 = (bf16[1728,640]{1,0:T(8,128)(2,1)S(1)}, bf16[1728,640]{1,0:T(8,128)(2,1)S(1)}, u32[]{:S(2)}, u32[]{:S(2)}) collective-permute-start(bf16[1728,640]{1,0:T(8,128)(2,1)S(1)} %copy-done.44), channel_id=1, source_target_pairs={{0,8},{4,12},{8,0},{12,4},{1,9},{5,13},{9,1},{13,5},{2,10},{6,14},... | collective-permute-start | bytes 6635528 | tf_op jit(solution)/shard_map/ppermute | solution.py:35
  555.3 95.7 %collective-permute-start.35 = (bf16[1728,640]{1,0:T(8,128)(2,1)}, bf16[1728,640]{1,0:T(8,128)(2,1)}, u32[]{:S(2)}, u32[]{:S(2)}) collective-permute-start(bf16[1728,640]{1,0:T(8,128)(2,1)} %add_convert_fusion.5), channel_id=1, source_target_pairs={{0,8},{4,12},{8,0},{12,4},{1,9},{5,13},{9,1},{13,5},{2,10},{6,14},... | collective-permute-start | bytes 6635528 | tf_op jit(solution)/shard_map/ppermute | solution.py:35
  607.1 48.2 %collective-permute-start.34 = (bf16[1728,640]{1,0:T(8,128)(2,1)S(1)}, bf16[1728,640]{1,0:T(8,128)(2,1)}, u32[]{:S(2)}, u32[]{:S(2)}) collective-permute-start(bf16[1728,640]{1,0:T(8,128)(2,1)S(1)} %add_convert_fusion.2), channel_id=1, source_target_pairs={{0,16},{16,0},{1,17},{17,1},{2,18},{18,2},{3,19},{19,3},{4,20},{20... | collective-permute-start | bytes 6635528 | tf_op jit(solution)/shard_map/ppermute | solution.py:687
  659.4 195.2 %reduce-scatter.14.cloned.1.call-start = ((), (), s32[]{:S(2)}) async-start(), calls=%async_computation.9 | async-start | bytes 6553600 | tf_op jit(solution)/shard_map/reduce_scatter | solution.py:680
  661.0 53.4 %collective-permute-start.38 = (bf16[1728,640]{1,0:T(8,128)(2,1)S(1)}, bf16[1728,640]{1,0:T(8,128)(2,1)}, u32[]{:S(2)}, u32[]{:S(2)}) collective-permute-start(bf16[1728,640]{1,0:T(8,128)(2,1)S(1)} %copy-done.43), channel_id=1, source_target_pairs={{0,8},{4,12},{8,0},{12,4},{1,9},{5,13},{9,1},{13,5},{2,10},{6,14},... | collective-permute-start | bytes 6635528 | tf_op jit(solution)/shard_map/ppermute | solution.py:35
  662.5 54.2 %collective-permute-start.39 = (bf16[1728,640]{1,0:T(8,128)(2,1)}, bf16[1728,640]{1,0:T(8,128)(2,1)}, u32[]{:S(2)}, u32[]{:S(2)}) collective-permute-start(bf16[1728,640]{1,0:T(8,128)(2,1)} %add_convert_fusion.1), channel_id=1, source_target_pairs={{0,16},{16,0},{1,17},{17,1},{2,18},{18,2},{3,19},{19,3},{4,20},{20... | collective-permute-start | bytes 6635528 | tf_op jit(solution)/shard_map/ppermute | solution.py:687
  722.8 32.2 %collective-permute-start.40 = (bf16[960,640]{1,0:T(8,128)(2,1)}, bf16[960,640]{1,0:T(8,128)(2,1)}, u32[]{:S(2)}, u32[]{:S(2)}) collective-permute-start(bf16[960,640]{1,0:T(8,128)(2,1)} %slice.138), channel_id=1, source_target_pairs={{0,16},{16,0},{1,17},{17,1},{2,18},{18,2},{3,19},{19,3},{4,20},{20... | collective-permute-start | bytes 3686408 | tf_op jit(solution)/shard_map/ppermute | solution.py:687
  793.4 30.1 %collective-permute-start.52 = (bf16[640,640]{1,0:T(8,128)(2,1)S(1)}, bf16[640,640]{1,0:T(8,128)(2,1)S(1)}, u32[]{:S(2)}, u32[]{:S(2)}) collective-permute-start(bf16[640,640]{1,0:T(8,128)(2,1)S(1)} %add_convert_fusion.13), channel_id=1, source_target_pairs={{0,8},{4,12},{8,0},{12,4},{1,9},{5,13},{9,1},{13,5},{2,10},{6,14},... | collective-permute-start | bytes 2457608 | tf_op jit(solution)/shard_map/ppermute | solution.py:35
  794.4 29.0 %collective-permute-start.54 = (bf16[320,640]{1,0:T(8,128)(2,1)S(1)}, bf16[320,640]{1,0:T(8,128)(2,1)S(1)}, u32[]{:S(2)}, u32[]{:S(2)}) collective-permute-start(bf16[320,640]{1,0:T(8,128)(2,1)S(1)} %fusion.62), channel_id=1, source_target_pairs={{0,8},{4,12},{8,0},{12,4},{1,9},{5,13},{9,1},{13,5},{2,10},{6,14},... | collective-permute-start | bytes 1228808 | tf_op jit(solution)/shard_map/ppermute | solution.py:35
  795.7 40.2 %collective-permute-start.56 = (bf16[640,640]{1,0:T(8,128)(2,1)S(1)}, bf16[640,640]{1,0:T(8,128)(2,1)S(1)}, u32[]{:S(2)}, u32[]{:S(2)}) collective-permute-start(bf16[640,640]{1,0:T(8,128)(2,1)S(1)} %add_convert_fusion.11), channel_id=1, source_target_pairs={{0,16},{16,0},{1,17},{17,1},{2,18},{18,2},{3,19},{19,3},{4,20},{20... | collective-permute-start | bytes 2457608 | tf_op jit(solution)/shard_map/ppermute | solution.py:687
  824.8 28.5 %collective-permute-start.53 = (bf16[640,640]{1,0:T(8,128)(2,1)S(1)}, bf16[640,640]{1,0:T(8,128)(2,1)S(1)}, u32[]{:S(2)}, u32[]{:S(2)}) collective-permute-start(bf16[640,640]{1,0:T(8,128)(2,1)S(1)} %add_convert_fusion.12), channel_id=1, source_target_pairs={{0,16},{16,0},{1,17},{17,1},{2,18},{18,2},{3,19},{19,3},{4,20},{20... | collective-permute-start | bytes 2457608 | tf_op jit(solution)/shard_map/ppermute | solution.py:687
  (103 other events, 1470.1 us)
Sparse Core Ops, SparseCore 0:
  27.8 100.5 all-gather.11
  130.6 96.5 all-gather.13
  229.4 92.1 reduce-scatter.5
  324.8 55.3 all-gather.15
  381.5 53.5 all-gather.17
  437.9 50.8 reduce-scatter.7
  499.5 50.7 reduce-scatter.9
  553.4 97.7 all-gather.19
  659.5 93.6 reduce-scatter.11
  758.0 92.3 reduce-scatter.13

commit v11 on v10

--- a/solution.py
+++ b/solution.py
@@ -822,17 +822,29 @@
         shares.append(out[5])
         gain_share_two = gain_share_two + out[6]
     norm_two, grad_rows, act, dgate, dup = before
-    share_sums = [sum_cols(share) for share in shares]
+    if parts == 2 and cols == 4:
+        blocks = [
+            lax.dynamic_index_in_dim(shares[0], lax.axis_index("col") ^ m, 0, keepdims=False)
+            for m in range(cols)
+        ]
+        moved = exchange_blocks(blocks, "col")
+        norm_two, grad_rows, act, dgate, dup, moved = together(
+            norm_two, grad_rows, act, dgate, dup, moved
+        )
+        share_sums = [summed_up(moved), sum_cols(shares[1])]
+    else:
+        share_sums = [sum_cols(share) for share in shares]
+    share_sums = [total.astype(F32) for total in share_sums]
     down_grads = {k: dot(act, grad_rows[k], NT).astype(BF) for k in range(count)}
     gate_grads = {k: dot(dgate, norm_two[k], NT).astype(BF) for k in range(count)}
-    up_grads = {k: dot(dup, norm_two[k], NT).astype(BF) for k in range(count)}
     down_grads = fold(down_grads, "row", near)
     gate_grads = fold(gate_grads, "row", near)
+    *share_sums, down_grads, gate_grads, dup, norm_two = together(
+        *share_sums, down_grads, gate_grads, dup, norm_two
+    )
+    up_grads = {k: dot(dup, norm_two[k], NT).astype(BF) for k in range(count)}
     up_grads = fold(up_grads, "row", near)
-    *share_sums, down_grads, gate_grads, up_grads = together(
-        *share_sums, down_grads, gate_grads, up_grads
-    )
-    residual_grad_own = grad_own.astype(F32) + jnp.concatenate(share_sums, axis=2).astype(F32)
+    residual_grad_own = grad_own.astype(F32) + jnp.concatenate(share_sums, axis=2)
     down_total = fold(down_grads, "row", far)[0]
     gate_total = fold(gate_grads, "row", far)[0]
 

time: 891 us -> 899 us (level)
  other arithmetic: 46.5 us -> 56 us
    ppermute x59 -> x62, starting transfers between devices: 35.6 us -> 41.1 us  [swapped(): return lax.ppermute(value, axis, [(i, i ^ mask) for i in range(size)])]
    ppermute x59 -> x62, waiting for transfers between devices: 273 us -> 268 us  [swapped(): return lax.ppermute(value, axis, [(i, i ^ mask) for i in range(size)])]
    reduce_scatter x5 -> x4, waiting for transfers between devices: 35.4 us -> 38.5 us  [sum_cols(): return lax.psum_scatter(value, 'col', scatter_dimension=0, tiled=False)]
  transfers between devices with their start and end apart: 77 -> 79, of which waited for: 36 -> 37; matrix products, arithmetic and copies ran while one was open for 15% -> 15% of each run, Pallas kernels for 24% -> 24%
where the time goes in v11:
time: 899 us; the launch traced here: 891 us
  waiting for transfers between devices  418 us (46%)
  Pallas kernels  216 us (24%)
  matrix products  73.6 us (8%)
  other arithmetic  56 us (6%)
  starting transfers between devices  50.9 us (6%)
  blocking collectives  34.2 us (4%)
  local copies, waits for them, and re-layouts  26.8 us (3%)
  between operations  15.2 us (2%)
    ppermute x62, waiting for transfers between devices, swapped(): return lax.ppermute(value, axis, [(i, i ^ mask) for i in range(size)])  268 us
    all_gather x5, waiting for transfers between devices, spread_cols(): return lax.all_gather(value, 'col', axis=0, tiled=False)  88.5 us
    pallas_call x2, Pallas kernels, feed_forward(): pl.pallas_call(functools.partial(ff_kernel, count, bool(before)), out_sha...  84 us
    dot_general x24, matrix products, dot(): return lax.dot_general(left, right, dims, preferred_element_type=F32)  73.6 us
    ppermute x62, starting transfers between devices, swapped(): return lax.ppermute(value, axis, [(i, i ^ mask) for i in range(size)])  41.1 us
    reduce_scatter x4, waiting for transfers between devices, sum_cols(): return lax.psum_scatter(value, 'col', scatter_dimension=0, tiled=False)  38.5 us
    pallas_call x1, Pallas kernels, attend_back(): pl.pallas_call(functools.partial(attend_back_kernel, tile), out_shape=(sh...  37.7 us
    all_gather x1, blocking collectives, body(): lax.all_gather(jnp.stack([attn_gain, mlp_gain]), ('row', 'col'), axis=1,...  34.2 us
  transfers between devices with their start and end apart: 79, of which 37 were waited for; matrix products, arithmetic and copies ran while one was open for 15% of the time, Pallas kernels for 24%

profile of v11, /device:TPU:0, one launch (start us, length us, event | category | flops | bytes accessed | tf_op | source)
XLA Modules:
  0.0 890.8 jit_solution(13790824821681543114)
XLA Ops:
  11.9 8.5 collective-permute-done.1
  20.3 6.5 collective-permute-done.2
  30.4 8.7 collective-permute-done.4
  39.1 5.9 collective-permute-done.5
  48.3 27.9 %collective-permute-done.7.refs_6_ = bf16[320,640]{1,0:T(8,128)(2,1)S(1)} collective-permute-done((bf16[320,640]{1,0:T(8,128)(2,1)S(1)}, bf16[320,640]{1,0:T(8,128)(2,1)S(1)}, u32[]{:S(2)}, u32[]{:S(2)}) %collective-permute-start.7) | collective-permute-done | bytes 409632 | tf_op jit(solution)/shard_map/ppermute | solution.py:35
  79.9 34.2 %all-gather.5 = f32[16,160,2]{1,2,0:T(2,128)S(1)} all-gather(f32[1,160,2]{1,2,0:T(2,128)S(1)} %maximum_bitcast_fusion.1), channel_id=1, replica_groups=mesh['dp'=2,'row'=4,'col'=4] {'row','col'}, dimensions={0}, use_global_device_ids=true | all-gather | bytes 21760 | tf_op jit(solution)/shard_map/all_gather | solution.py:765
  119.0 7.5 collective-permute-done.12.refs_2_
  129.8 18.7 %collective-permute-done.16.refs_2_.refs_3_ = bf16[640,640]{1,0:T(8,128)(2,1)} collective-permute-done((bf16[640,640]{1,0:T(8,128)(2,1)S(1)}, bf16[640,640]{1,0:T(8,128)(2,1)}, u32[]{:S(2)}, u32[]{:S(2)}) %collective-permute-start.16) | collective-permute-done | bytes 819232 | tf_op jit(solution)/shard_map/ppermute | solution.py:35
  151.6 13.0 %qkv_project.1 = (bf16[4,640,1024]{2,1,0:T(8,128)(2,1)}, f32[1,1024]{1,0:T(1,128)}, bf16[2,480,1024]{2,1,0:T(8,128)(2,1)}) custom-call(bf16[4,4,160,1024]{3,2,1,0:T(8,128)(2,1)} %bitcast.249, f32[4,4,160,1]{3,2,1,0:T(8,128)} %copy.66.gain_ref, f32[40,1024]{1,0:T(8,128)} %get-tuple-element.170.cos_ref, f32[40,1024]{1,0:T(8,128)} %get-tuple-element.171.sin_ref, ...), custom_call_target="tpu_custom_call" | custom-call | flops 1200000000 | tf_op jit(solution)/shard_map/qkv_project/pallas_call | solution.py:157
  171.7 27.8 %attend.1 = (bf16[320,1024]{1,0:T(8,128)(2,1)}, bf16[320,1024]{1,0:T(8,128)(2,1)}, f32[2,4,1,1024]{3,2,1,0:T(1,128)}) custom-call(s32[1]{0:T(128)} %bitcast.parity_ref, bf16[480,1024]{1,0:T(8,128)(2,1)} %get-tuple-element.306.own_ref, bf16[480,1024]{1,0:T(8,128)(2,1)} %collective-permute-done.14.other_ref, s32[1,1024]{1,0:T(1,128)} %bitcast.289, ...), custom_call_target="tpu_custom_call" | custom-call | flops 2700000000 | tf_op jit(solution)/shard_map/attend/pallas_call | solution.py:249
  202.6 10.2 %mix_out.1 = bf16[4,4,160,1024]{3,2,1,0:T(8,128)(2,1)} custom-call(s32[1]{0:T(128)} %bitcast.parity_ref, bf16[320,1024]{1,0:T(8,128)(2,1)} %get-tuple-element.259.own_ref.own_out, bf16[320,1024]{1,0:T(8,128)(2,1)} %copy-done.26, bf16[640,640]{1,0:T(8,128)(2,1)} %refs_1_, bf16[640,640]{1,0:T(8,128)(2,1)} %collective-permute-done.17.refs_1_.refs_2_, ...), custom_call_target="tpu_custom_call" | custom-call | flops 1000000000 | tf_op jit(solution)/shard_map/mix_out/pallas_call | solution.py:424
  212.8 14.0 %all-gather.14.cloned.1.call-done = bf16[16,160,1024]{2,1,0:T(8,128)(2,1)} async-done(((bf16[4,160,1024]{2,1,0:T(8,128)(2,1)}), bf16[16,160,1024]{2,1,0:T(8,128)(2,1)}) %all-gather.14.cloned.1.call-update) | async-done | bytes 5242896 | tf_op jit(solution)/shard_map/all_gather | solution.py:676
  229.9 48.5 %collective-permute-done.25.refs_10_.refs_2_ = bf16[1728,640]{1,0:T(8,128)(2,1)S(1)} collective-permute-done((bf16[1728,640]{1,0:T(8,128)(2,1)S(1)}, bf16[1728,640]{1,0:T(8,128)(2,1)S(1)}, u32[]{:S(2)}, u32[]{:S(2)}) %collective-permute-start.25) | collective-permute-done | bytes 2211872 | tf_op jit(solution)/shard_map/ppermute | solution.py:35
  279.8 6.0 collective-permute-done.26.refs_11_.refs_3_
  295.6 25.7 %reduce-scatter.5.cloned.1.call-done = bf16[1,4,160,1024]{3,2,1,0:T(8,128)(2,1)} async-done(((bf16[4,4,160,1024]{3,2,1,0:T(8,128)(2,1)}), bf16[1,4,160,1024]{3,2,1,0:T(8,128)(2,1)}) %reduce-scatter.5.cloned.1.call-update) | async-done | bytes 1310736 | tf_op jit(solution)/shard_map/reduce_scatter | solution.py:680
  326.5 53.3 %all-gather.18.cloned.1.call-done = bf16[16,160,512]{2,1,0:T(8,128)(2,1)} async-done(((bf16[4,160,512]{2,1,0:T(8,128)(2,1)}), bf16[16,160,512]{2,1,0:T(8,128)(2,1)}) %all-gather.18.cloned.1.call-update) | async-done | bytes 2621456 | tf_op jit(solution)/shard_map/all_gather | solution.py:676
  379.8 42.2 %feed_forward.2 = (bf16[4,640,1024]{2,1,0:T(8,128)(2,1)}, bf16[4,640,1024]{2,1,0:T(8,128)(2,1)}, bf16[1728,1024]{1,0:T(8,128)(2,1)}, bf16[1728,1024]{1,0:T(8,128...) custom-call(bf16[4,4,160,512]{3,2,1,0:T(8,128)(2,1)} %bitcast.270, ...), custom_call_target="tpu_custom_call" | custom-call | flops 4200000000 | tf_op jit(solution)/shard_map/feed_forward/pallas_call | solution.py:563
  429.2 19.7 %all-gather.16.cloned.1.call-done = bf16[16,160,512]{2,1,0:T(8,128)(2,1)} async-done(((bf16[4,160,512]{2,1,0:T(8,128)(2,1)}), bf16[16,160,512]{2,1,0:T(8,128)(2,1)}) %all-gather.16.cloned.1.call-update) | async-done | bytes 2621456 | tf_op jit(solution)/shard_map/all_gather | solution.py:676
  448.9 41.8 %feed_forward.3 = (bf16[4,640,1024]{2,1,0:T(8,128)(2,1)}, bf16[4,640,1024]{2,1,0:T(8,128)(2,1)}, bf16[1728,1024]{1,0:T(8,128)(2,1)}, bf16[1728,1024]{1,0:T(8,128...) custom-call(bf16[4,4,160,512]{3,2,1,0:T(8,128)(2,1)} %bitcast.271, ...), custom_call_target="tpu_custom_call", output_to_operand_aliasing={{0}: (15, {}), {1}: (16, {}), {2}: (17, {}), {3}: (18, {}),... | custom-call | flops 4200000000 | tf_op jit(solution)/shard_map/feed_forward/pallas_call | solution.py:563
  530.9 12.9 %reduce-scatter.7.cloned.1.call-done = bf16[1,4,160,512]{3,2,1,0:T(8,128)(2,1)} async-done(((bf16[4,4,160,512]{3,2,1,0:T(8,128)(2,1)}), bf16[1,4,160,512]{3,2,1,0:T(8,128)(2,1)}) %reduce-scatter.7.cloned.1.call-update) | async-done | bytes 655376 | tf_op jit(solution)/shard_map/reduce_scatter | solution.py:680
  550.1 6.7 convolution_convert_fusion
  562.9 36.4 %collective-permute-done.34 = bf16[1728,640]{1,0:T(8,128)(2,1)S(1)} collective-permute-done((bf16[1728,640]{1,0:T(8,128)(2,1)}, bf16[1728,640]{1,0:T(8,128)(2,1)S(1)}, u32[]{:S(2)}, u32[]{:S(2)}) %collective-permute-start.34) | collective-permute-done | bytes 2211872 | tf_op jit(solution)/shard_map/ppermute | solution.py:35
  602.6 16.6 %fan_out.1 = bf16[4,4,160,1024]{3,2,1,0:T(8,128)(2,1)} custom-call(bf16[1728,1024]{1,0:T(8,128)(2,1)} %get-tuple-element.231.x_ref, bf16[1728,640]{1,0:T(8,128)(2,1)} %refs_0_.2, bf16[1728,640]{1,0:T(8,128)(2,1)} %copy-done.5, bf16[1728,640]{1,0:T(8,128)(2,1)} %copy-done.4, bf16[1728,640]{1,0:T(8,128)(2,1)} %copy-done.6), custom_call_target="tpu_custom_call" | custom-call | flops 1700000000 | tf_op jit(solution)/shard_map/fan_out/pallas_call | solution.py:485
  619.2 26.2 %collective-permute-done.36 = bf16[1728,640]{1,0:T(8,128)(2,1)} collective-permute-done((bf16[1728,640]{1,0:T(8,128)(2,1)}, bf16[1728,640]{1,0:T(8,128)(2,1)}, u32[]{:S(2)}, u32[]{:S(2)}) %collective-permute-start.36) | collective-permute-done | bytes 2211872 | tf_op jit(solution)/shard_map/ppermute | solution.py:35
  653.8 6.0 add_convert_fusion.2
  667.7 9.1 %mix_back.1 = (bf16[4,640,1024]{2,1,0:T(8,128)(2,1)}, bf16[320,1024]{1,0:T(8,128)(2,1)}, bf16[320,1024]{1,0:T(8,128)(2,1)}) custom-call(s32[1]{0:T(128)} %bitcast.parity_ref, bf16[4,4,160,1024]{3,2,1,0:T(8,128)(2,1)} %bitcast.261, bf16[640,640]{1,0:T(8,128)(2,1)} %refs_1_, bf16[640,640]{1,0:T(8,128)(2,1)} %collective-permute-done.17.refs_1_.refs_2_, ...), custom_call_target="tpu_custom_call" | custom-call | flops 900000000 | tf_op jit(solution)/shard_map/mix_back/pallas_call | solution.py:459
  680.0 37.7 %attend_back.1 = (bf16[480,1024]{1,0:T(8,128)(2,1)}, bf16[480,1024]{1,0:T(8,128)(2,1)}) custom-call(s32[1]{0:T(128)} %bitcast.parity_ref, bf16[480,1024]{1,0:T(8,128)(2,1)} %get-tuple-element.306.own_ref, bf16[480,1024]{1,0:T(8,128)(2,1)} %collective-permute-done.14.other_ref, bf16[320,1024]{1,0:T(8,128)(2,1)} %get-tuple-element.259.own_ref.own_out, ...), custom_call_target="tpu_custom_call" | custom-call | flops 3700000000 | tf_op jit(solution)/shard_map/attend_back/pallas_call | solution.py:361
  728.6 17.4 %qkv_back.1 = (bf16[640,1024]{1,0:T(8,128)(2,1)}, bf16[320,1024]{1,0:T(8,128)(2,1)}, bf16[4,4,160,1024]{3,2,1,0:T(8,128)(2,1)}, f32[4,4,160,1]{3,2,1,0:T(8,128)}) custom-call(s32[1]{0:T(128)} %bitcast.parity_ref, bf16[4,4,160,1024]{3,2,1,0:T(8,128)(2,1)} %bitcast.250, f32[4,4,160,1]{3,2,1,0:T(8,128)} %copy.66.gain_ref, ...), custom_call_target="tpu_custom_call" | custom-call | flops 1700000000 | tf_op jit(solution)/shard_map/qkv_back/pallas_call | solution.py:653
  785.3 11.5 %collective-permute-done.54 = bf16[640,640]{1,0:T(8,128)(2,1)S(1)} collective-permute-done((bf16[640,640]{1,0:T(8,128)(2,1)S(1)}, bf16[640,640]{1,0:T(8,128)(2,1)S(1)}, u32[]{:S(2)}, u32[]{:S(2)}) %collective-permute-start.54) | collective-permute-done | bytes 819232 | tf_op jit(solution)/shard_map/ppermute | solution.py:35
  816.1 13.8 %collective-permute-done.55 = bf16[640,640]{1,0:T(8,128)(2,1)S(1)} collective-permute-done((bf16[640,640]{1,0:T(8,128)(2,1)S(1)}, bf16[640,640]{1,0:T(8,128)(2,1)S(1)}, u32[]{:S(2)}, u32[]{:S(2)}) %collective-permute-start.55) | collective-permute-done | bytes 819232 | tf_op jit(solution)/shard_map/ppermute | solution.py:35
  845.7 16.1 %collective-permute-done.56 = bf16[640,640]{1,0:T(8,128)(2,1)S(1)} collective-permute-done((bf16[640,640]{1,0:T(8,128)(2,1)S(1)}, bf16[640,640]{1,0:T(8,128)(2,1)S(1)}, u32[]{:S(2)}, u32[]{:S(2)}) %collective-permute-start.56) | collective-permute-done | bytes 819232 | tf_op jit(solution)/shard_map/ppermute | solution.py:687
  869.3 7.1 collective-permute-done.68
  (374 shorter events, 238.1 us)
Async XLA Ops:
  7.2 120.9 %all-gather.12.cloned.1.call-start = ((), (), s32[]{:S(2)}) async-start(), calls=%async_computation.8 | async-start | bytes 6553600 | tf_op jit(solution)/shard_map/all_gather | solution.py:676
  28.1 198.7 %all-gather.14.cloned.1.call-start = ((), (), s32[]{:S(2)}) async-start(), calls=%async_computation.9 | async-start | bytes 6553600 | tf_op jit(solution)/shard_map/all_gather | solution.py:676
  46.2 29.9 %collective-permute-start.6 = (bf16[640,640]{1,0:T(8,128)(2,1)}, bf16[640,640]{1,0:T(8,128)(2,1)}, u32[]{:S(2)}, u32[]{:S(2)}) collective-permute-start(bf16[640,640]{1,0:T(8,128)(2,1)} %refs_0_.3), channel_id=1, source_target_pairs={{0,8},{4,12},{8,0},{12,4},{1,9},{5,13},{9,1},{13,5},{2,10},{6,14},... | collective-permute-start | bytes 2457608 | tf_op jit(solution)/shard_map/ppermute | solution.py:35
  76.2 50.4 %collective-permute-start.12 = (bf16[1728,640]{1,0:T(8,128)(2,1)S(1)}, bf16[1728,640]{1,0:T(8,128)(2,1)}, u32[]{:S(2)}, u32[]{:S(2)}) collective-permute-start(bf16[1728,640]{1,0:T(8,128)(2,1)S(1)} %bitcast.256), channel_id=1, source_target_pairs={{0,8},{4,12},{8,0},{12,4},{1,9},{5,13},{9,1},{13,5},{2,10},{6,14},... | collective-permute-start | bytes 6635528 | tf_op jit(solution)/shard_map/ppermute | solution.py:35
  77.8 41.2 %collective-permute-start.8 = (bf16[640,640]{1,0:T(8,128)(2,1)}, bf16[640,640]{1,0:T(8,128)(2,1)}, u32[]{:S(2)}, u32[]{:S(2)}) collective-permute-start(bf16[640,640]{1,0:T(8,128)(2,1)} %refs_0_.3), channel_id=1, source_target_pairs={{0,4},{4,0},{8,12},{12,8},{1,5},{5,1},{9,13},{13,9},{2,6},{6,2},{1... | collective-permute-start | bytes 2457608 | tf_op jit(solution)/shard_map/ppermute | solution.py:35
  78.4 40.7 %collective-permute-start.9 = (bf16[640,640]{1,0:T(8,128)(2,1)}, bf16[640,640]{1,0:T(8,128)(2,1)}, u32[]{:S(2)}, u32[]{:S(2)}) collective-permute-start(bf16[640,640]{1,0:T(8,128)(2,1)} %collective-permute-done.6.refs_2_), channel_id=1, source_target_pairs={{0,4},{4,0},{8,12},{12,8},{1,5},{5,1},{9,13},{13,9},{2,6},{6,2},{1... | collective-permute-start | bytes 2457608 | tf_op jit(solution)/shard_map/ppermute | solution.py:35
  128.1 193.1 %reduce-scatter.5.cloned.1.call-start = ((), (), s32[]{:S(2)}) async-start(), calls=%async_computation.4 | async-start | bytes 6553600 | tf_op jit(solution)/shard_map/reduce_scatter | solution.py:680
  148.5 51.2 %collective-permute-start.19 = (bf16[1728,640]{1,0:T(8,128)(2,1)}, bf16[1728,640]{1,0:T(8,128)(2,1)S(1)}, u32[]{:S(2)}, u32[]{:S(2)}) collective-permute-start(bf16[1728,640]{1,0:T(8,128)(2,1)} %bitcast.257), channel_id=1, source_target_pairs={{0,8},{4,12},{8,0},{12,4},{1,9},{5,13},{9,1},{13,5},{2,10},{6,14},... | collective-permute-start | bytes 6635528 | tf_op jit(solution)/shard_map/ppermute | solution.py:35
  167.6 32.1 %collective-permute-start.17 = (bf16[640,640]{1,0:T(8,128)(2,1)S(1)}, bf16[640,640]{1,0:T(8,128)(2,1)}, u32[]{:S(2)}, u32[]{:S(2)}) collective-permute-start(bf16[640,640]{1,0:T(8,128)(2,1)S(1)} %copy-done.25), channel_id=1, source_target_pairs={{0,4},{4,0},{8,12},{12,8},{1,5},{5,1},{9,13},{13,9},{2,6},{6,2},{1... | collective-permute-start | bytes 2457608 | tf_op jit(solution)/shard_map/ppermute | solution.py:35
  168.1 31.6 %collective-permute-start.18 = (bf16[640,640]{1,0:T(8,128)(2,1)}, bf16[640,640]{1,0:T(8,128)(2,1)}, u32[]{:S(2)}, u32[]{:S(2)}) collective-permute-start(bf16[640,640]{1,0:T(8,128)(2,1)} %collective-permute-done.16.refs_2_.refs_3_), channel_id=1, source_target_pairs={{0,4},{4,0},{8,12},{12,8},{1,5},{5,1},{9,13},{13,9},{2,6},{6,2},{1... | collective-permute-start | bytes 2457608 | tf_op jit(solution)/shard_map/ppermute | solution.py:35
  226.8 153.0 %all-gather.18.cloned.1.call-start = ((), (), s32[]{:S(2)}) async-start(), calls=%async_computation.11 | async-start | bytes 3276800 | tf_op jit(solution)/shard_map/all_gather | solution.py:676
  228.4 50.0 %collective-permute-start.25 = (bf16[1728,640]{1,0:T(8,128)(2,1)S(1)}, bf16[1728,640]{1,0:T(8,128)(2,1)S(1)}, u32[]{:S(2)}, u32[]{:S(2)}) collective-permute-start(bf16[1728,640]{1,0:T(8,128)(2,1)S(1)} %copy-done.3), channel_id=1, source_target_pairs={{0,8},{4,12},{8,0},{12,4},{1,9},{5,13},{9,1},{13,5},{2,10},{6,14},... | collective-permute-start | bytes 6635528 | tf_op jit(solution)/shard_map/ppermute | solution.py:35
  229.9 49.5 %collective-permute-start.24 = (bf16[1728,640]{1,0:T(8,128)(2,1)S(1)}, bf16[1728,640]{1,0:T(8,128)(2,1)S(1)}, u32[]{:S(2)}, u32[]{:S(2)}) collective-permute-start(bf16[1728,640]{1,0:T(8,128)(2,1)S(1)} %copy-done.3), channel_id=1, source_target_pairs={{0,4},{4,0},{8,12},{12,8},{1,5},{5,1},{9,13},{13,9},{2,6},{6,2},{1... | collective-permute-start | bytes 6635528 | tf_op jit(solution)/shard_map/ppermute | solution.py:35
  324.3 124.6 %all-gather.16.cloned.1.call-start = ((), (), s32[]{:S(2)}) async-start(), calls=%async_computation.10 | async-start | bytes 3276800 | tf_op jit(solution)/shard_map/all_gather | solution.py:676
  324.9 218.9 %reduce-scatter.7.cloned.1.call-start = ((), (), s32[]{:S(2)}) async-start(), calls=%async_computation.5 | async-start | bytes 3276800 | tf_op jit(solution)/shard_map/reduce_scatter | solution.py:680
  424.8 65.9 %collective-permute-start.27 = (bf16[4,160,512]{2,1,0:T(8,128)(2,1)}, bf16[4,160,512]{2,1,0:T(8,128)(2,1)}, u32[]{:S(2)}, u32[]{:S(2)}) collective-permute-start(bf16[4,160,512]{2,1,0:T(8,128)(2,1)} %get-tuple-element.303), channel_id=1, source_target_pairs={{0,1},{1,0},{2,3},{3,2},{4,5},{5,4},{6,7},{7,6},{8,9},{9,8},{10,11... | collective-permute-start | bytes 1966088 | tf_op jit(solution)/shard_map/ppermute | solution.py:35
  424.8 65.9 %collective-permute-start.28 = (bf16[4,160,512]{2,1,0:T(8,128)(2,1)S(1)}, bf16[4,160,512]{2,1,0:T(8,128)(2,1)}, u32[]{:S(2)}, u32[]{:S(2)}) collective-permute-start(bf16[4,160,512]{2,1,0:T(8,128)(2,1)S(1)} %get-tuple-element.302), channel_id=1, source_target_pairs={{0,2},{1,3},{2,0},{3,1},{4,6},{5,7},{6,4},{7,5},{8,10},{9,11},{10,... | collective-permute-start | bytes 1966088 | tf_op jit(solution)/shard_map/ppermute | solution.py:35
  426.2 64.6 %collective-permute-start.29 = (bf16[4,160,512]{2,1,0:T(8,128)(2,1)S(1)}, bf16[4,160,512]{2,1,0:T(8,128)(2,1)}, u32[]{:S(2)}, u32[]{:S(2)}) collective-permute-start(bf16[4,160,512]{2,1,0:T(8,128)(2,1)S(1)} %get-tuple-element.301), channel_id=1, source_target_pairs={{0,3},{1,2},{2,1},{3,0},{4,7},{5,6},{6,5},{7,4},{8,11},{9,10},{10,... | collective-permute-start | bytes 1966088 | tf_op jit(solution)/shard_map/ppermute | solution.py:35
  490.7 174.0 %all-gather.20.cloned.1.call-start = ((), (), s32[]{:S(2)}) async-start(), calls=%async_computation.12 | async-start | bytes 6553600 | tf_op jit(solution)/shard_map/all_gather | solution.py:676
  547.7 213.5 %reduce-scatter.9.cloned.1.call-start = ((), (), s32[]{:S(2)}) async-start(), calls=%async_computation.6 | async-start | bytes 6553600 | tf_op jit(solution)/shard_map/reduce_scatter | solution.py:680
  548.0 51.3 %collective-permute-start.34 = (bf16[1728,640]{1,0:T(8,128)(2,1)}, bf16[1728,640]{1,0:T(8,128)(2,1)S(1)}, u32[]{:S(2)}, u32[]{:S(2)}) collective-permute-start(bf16[1728,640]{1,0:T(8,128)(2,1)} %add_convert_fusion.7), channel_id=1, source_target_pairs={{0,8},{4,12},{8,0},{12,4},{1,9},{5,13},{9,1},{13,5},{2,10},{6,14},... | collective-permute-start | bytes 6635528 | tf_op jit(solution)/shard_map/ppermute | solution.py:35
  549.5 95.9 %collective-permute-start.36 = (bf16[1728,640]{1,0:T(8,128)(2,1)}, bf16[1728,640]{1,0:T(8,128)(2,1)}, u32[]{:S(2)}, u32[]{:S(2)}) collective-permute-start(bf16[1728,640]{1,0:T(8,128)(2,1)} %add_convert_fusion.5), channel_id=1, source_target_pairs={{0,8},{4,12},{8,0},{12,4},{1,9},{5,13},{9,1},{13,5},{2,10},{6,14},... | collective-permute-start | bytes 6635528 | tf_op jit(solution)/shard_map/ppermute | solution.py:35
  556.8 92.2 %collective-permute-start.38 = (bf16[1728,640]{1,0:T(8,128)(2,1)}, bf16[1728,640]{1,0:T(8,128)(2,1)}, u32[]{:S(2)}, u32[]{:S(2)}) collective-permute-start(bf16[1728,640]{1,0:T(8,128)(2,1)} %convolution_convert_fusion), channel_id=1, source_target_pairs={{0,4},{4,0},{8,12},{12,8},{1,5},{5,1},{9,13},{13,9},{2,6},{6,2},{1... | collective-permute-start | bytes 6635528 | tf_op jit(solution)/shard_map/ppermute | solution.py:35
  562.5 91.3 %collective-permute-start.37 = (bf16[1728,640]{1,0:T(8,128)(2,1)}, bf16[1728,640]{1,0:T(8,128)(2,1)}, u32[]{:S(2)}, u32[]{:S(2)}) collective-permute-start(bf16[1728,640]{1,0:T(8,128)(2,1)} %convolution_convert_fusion.2), channel_id=1, source_target_pairs={{0,4},{4,0},{8,12},{12,8},{1,5},{5,1},{9,13},{13,9},{2,6},{6,2},{1... | collective-permute-start | bytes 6635528 | tf_op jit(solution)/shard_map/ppermute | solution.py:35
  601.1 58.7 %collective-permute-start.35 = (bf16[1728,640]{1,0:T(8,128)(2,1)}, bf16[1728,640]{1,0:T(8,128)(2,1)}, u32[]{:S(2)}, u32[]{:S(2)}) collective-permute-start(bf16[1728,640]{1,0:T(8,128)(2,1)} %add_convert_fusion.4), channel_id=1, source_target_pairs={{0,16},{16,0},{1,17},{17,1},{2,18},{18,2},{3,19},{19,3},{4,20},{20... | collective-permute-start | bytes 6635528 | tf_op jit(solution)/shard_map/ppermute | solution.py:687
  664.7 198.5 %reduce-scatter.11.cloned.1.call-start = ((), (), s32[]{:S(2)}) async-start(), calls=%async_computation.7 | async-start | bytes 6553600 | tf_op jit(solution)/shard_map/reduce_scatter | solution.py:680
  664.7 53.3 %collective-permute-start.41 = (bf16[1728,640]{1,0:T(8,128)(2,1)S(1)}, bf16[1728,640]{1,0:T(8,128)(2,1)}, u32[]{:S(2)}, u32[]{:S(2)}) collective-permute-start(bf16[1728,640]{1,0:T(8,128)(2,1)S(1)} %add_convert_fusion.1), channel_id=1, source_target_pairs={{0,8},{4,12},{8,0},{12,4},{1,9},{5,13},{9,1},{13,5},{2,10},{6,14},... | collective-permute-start | bytes 6635528 | tf_op jit(solution)/shard_map/ppermute | solution.py:35
  666.3 54.0 %collective-permute-start.42 = (bf16[1728,640]{1,0:T(8,128)(2,1)}, bf16[1728,640]{1,0:T(8,128)(2,1)}, u32[]{:S(2)}, u32[]{:S(2)}) collective-permute-start(bf16[1728,640]{1,0:T(8,128)(2,1)} %add_convert_fusion.3), channel_id=1, source_target_pairs={{0,16},{16,0},{1,17},{17,1},{2,18},{18,2},{3,19},{19,3},{4,20},{20... | collective-permute-start | bytes 6635528 | tf_op jit(solution)/shard_map/ppermute | solution.py:687
  726.4 31.8 %collective-permute-start.43 = (bf16[960,640]{1,0:T(8,128)(2,1)}, bf16[960,640]{1,0:T(8,128)(2,1)}, u32[]{:S(2)}, u32[]{:S(2)}) collective-permute-start(bf16[960,640]{1,0:T(8,128)(2,1)} %slice.150), channel_id=1, source_target_pairs={{0,16},{16,0},{1,17},{17,1},{2,18},{18,2},{3,19},{19,3},{4,20},{20... | collective-permute-start | bytes 3686408 | tf_op jit(solution)/shard_map/ppermute | solution.py:687
  797.8 33.5 %collective-permute-start.64 = (bf16[160,1024]{1,0:T(8,128)(2,1)S(1)}, bf16[160,1024]{1,0:T(8,128)(2,1)S(1)}, u32[]{:S(2)}, u32[]{:S(2)}) collective-permute-start(bf16[160,1024]{1,0:T(8,128)(2,1)S(1)} %get-tuple-element.312), channel_id=1, source_target_pairs={{0,4},{4,0},{8,12},{12,8},{1,5},{5,1},{9,13},{13,9},{2,6},{6,2},{1... | collective-permute-start | bytes 983048 | tf_op jit(solution)/shard_map/ppermute | solution.py:35
  814.5 29.8 %collective-permute-start.59 = (bf16[640,640]{1,0:T(8,128)(2,1)S(1)}, bf16[640,640]{1,0:T(8,128)(2,1)S(1)}, u32[]{:S(2)}, u32[]{:S(2)}) collective-permute-start(bf16[640,640]{1,0:T(8,128)(2,1)S(1)} %add_convert_fusion.11), channel_id=1, source_target_pairs={{0,16},{16,0},{1,17},{17,1},{2,18},{18,2},{3,19},{19,3},{4,20},{20... | collective-permute-start | bytes 2457608 | tf_op jit(solution)/shard_map/ppermute | solution.py:687
  831.2 30.6 %collective-permute-start.56 = (bf16[640,640]{1,0:T(8,128)(2,1)S(1)}, bf16[640,640]{1,0:T(8,128)(2,1)S(1)}, u32[]{:S(2)}, u32[]{:S(2)}) collective-permute-start(bf16[640,640]{1,0:T(8,128)(2,1)S(1)} %add_convert_fusion.12), channel_id=1, source_target_pairs={{0,16},{16,0},{1,17},{17,1},{2,18},{18,2},{3,19},{19,3},{4,20},{20... | collective-permute-start | bytes 2457608 | tf_op jit(solution)/shard_map/ppermute | solution.py:687
  (106 other events, 1548.8 us)
Sparse Core Ops, SparseCore 0:
  28.2 99.8 all-gather.11
  130.2 96.5 all-gather.13
  229.1 92.1 reduce-scatter.4
  324.4 55.3 all-gather.17
  381.2 67.6 all-gather.15
  490.8 52.9 reduce-scatter.6
  547.8 97.7 all-gather.19
  664.8 93.6 reduce-scatter.8
  761.3 93.8 reduce-scatter.10

commit v12 on v10

--- a/solution.py
+++ b/solution.py
@@ -824,9 +824,10 @@
     norm_two, grad_rows, act, dgate, dup = before
     share_sums = [sum_cols(share) for share in shares]
     down_grads = {k: dot(act, grad_rows[k], NT).astype(BF) for k in range(count)}
+    down_grads = fold(down_grads, "row", near)
+    dgate, dup, norm_two, down_grads = together(dgate, dup, norm_two, down_grads)
     gate_grads = {k: dot(dgate, norm_two[k], NT).astype(BF) for k in range(count)}
     up_grads = {k: dot(dup, norm_two[k], NT).astype(BF) for k in range(count)}
-    down_grads = fold(down_grads, "row", near)
     gate_grads = fold(gate_grads, "row", near)
     up_grads = fold(up_grads, "row", near)
     *share_sums, down_grads, gate_grads, up_grads = together(

time: 891 us -> 883 us (level)
  transfers between devices with their start and end apart: 77 -> 77, of which waited for: 36 -> 36; matrix products, arithmetic and copies ran while one was open for 15% -> 14% of each run, Pallas kernels for 24% -> 25%
where the time goes in v12:
time: 883 us; the launch traced here: 874 us
  waiting for transfers between devices  419 us (47%)
  Pallas kernels  216 us (24%)
  matrix products  75.6 us (9%)
  other arithmetic  46.5 us (5%)
  starting transfers between devices  44.9 us (5%)
  blocking collectives  34 us (4%)
  local copies, waits for them, and re-layouts  23.2 us (3%)
  between operations  15.4 us (2%)
    ppermute x59, waiting for transfers between devices, swapped(): return lax.ppermute(value, axis, [(i, i ^ mask) for i in range(size)])  273 us
    pallas_call x2, Pallas kernels, feed_forward(): pl.pallas_call(functools.partial(ff_kernel, count, bool(before)), out_sha...  84 us
    all_gather x5, waiting for transfers between devices, spread_cols(): return lax.all_gather(value, 'col', axis=0, tiled=False)  82.5 us
    dot_general x24, matrix products, dot(): return lax.dot_general(left, right, dims, preferred_element_type=F32)  75.6 us
    pallas_call x1, Pallas kernels, attend_back(): pl.pallas_call(functools.partial(attend_back_kernel, tile), out_shape=(sh...  37.4 us
    ppermute x59, starting transfers between devices, swapped(): return lax.ppermute(value, axis, [(i, i ^ mask) for i in range(size)])  35.6 us
    reduce_scatter x5, waiting for transfers between devices, sum_cols(): return lax.psum_scatter(value, 'col', scatter_dimension=0, tiled=False)  35 us
    all_gather x1, blocking collectives, body(): lax.all_gather(jnp.stack([attn_gain, mlp_gain]), ('row', 'col'), axis=1,...  34 us
  transfers between devices with their start and end apart: 77, of which 36 were waited for; matrix products, arithmetic and copies ran while one was open for 14% of the time, Pallas kernels for 25%

profile of v12, /device:TPU:0, one launch (start us, length us, event | category | flops | bytes accessed | tf_op | source)
XLA Modules:
  0.0 874.5 jit_solution(18174279228473868394)
XLA Ops:
  11.8 7.4 collective-permute-done.2
  19.2 7.2 collective-permute-done.1
  30.5 7.6 collective-permute-done.5
  38.1 7.2 collective-permute-done.4
  48.6 27.3 %collective-permute-done.7.refs_6_ = bf16[320,640]{1,0:T(8,128)(2,1)S(1)} collective-permute-done((bf16[320,640]{1,0:T(8,128)(2,1)S(1)}, bf16[320,640]{1,0:T(8,128)(2,1)S(1)}, u32[]{:S(2)}, u32[]{:S(2)}) %collective-permute-start.7) | collective-permute-done | bytes 409632 | tf_op jit(solution)/shard_map/ppermute | solution.py:35
  80.4 34.0 %all-gather.5 = f32[16,160,2]{1,2,0:T(2,128)S(1)} all-gather(f32[1,160,2]{1,2,0:T(2,128)S(1)} %maximum_bitcast_fusion.1), channel_id=1, replica_groups=mesh['dp'=2,'row'=4,'col'=4] {'row','col'}, dimensions={0}, use_global_device_ids=true | all-gather | bytes 21760 | tf_op jit(solution)/shard_map/all_gather | solution.py:765
  114.7 11.0 %collective-permute-done.12.refs_2_ = bf16[1728,640]{1,0:T(8,128)(2,1)} collective-permute-done((bf16[1728,640]{1,0:T(8,128)(2,1)S(1)}, bf16[1728,640]{1,0:T(8,128)(2,1)}, u32[]{:S(2)}, u32[]{:S(2)}) %collective-permute-start.12) | collective-permute-done | bytes 2211872 | tf_op jit(solution)/shard_map/ppermute | solution.py:35
  130.1 18.7 %collective-permute-done.16.refs_2_.refs_3_ = bf16[640,640]{1,0:T(8,128)(2,1)} collective-permute-done((bf16[640,640]{1,0:T(8,128)(2,1)S(1)}, bf16[640,640]{1,0:T(8,128)(2,1)}, u32[]{:S(2)}, u32[]{:S(2)}) %collective-permute-start.16) | collective-permute-done | bytes 819232 | tf_op jit(solution)/shard_map/ppermute | solution.py:35
  151.9 13.1 %qkv_project.1 = (bf16[4,640,1024]{2,1,0:T(8,128)(2,1)}, f32[1,1024]{1,0:T(1,128)}, bf16[2,480,1024]{2,1,0:T(8,128)(2,1)}) custom-call(bf16[4,4,160,1024]{3,2,1,0:T(8,128)(2,1)} %bitcast.236, f32[4,4,160,1]{3,2,1,0:T(8,128)} %copy.66.gain_ref, f32[40,1024]{1,0:T(8,128)} %get-tuple-element.166.cos_ref, f32[40,1024]{1,0:T(8,128)} %get-tuple-element.167.sin_ref, ...), custom_call_target="tpu_custom_call" | custom-call | flops 1200000000 | tf_op jit(solution)/shard_map/qkv_project/pallas_call | solution.py:157
  172.0 27.8 %attend.1 = (bf16[320,1024]{1,0:T(8,128)(2,1)}, bf16[320,1024]{1,0:T(8,128)(2,1)}, f32[2,4,1,1024]{3,2,1,0:T(1,128)}) custom-call(s32[1]{0:T(128)} %bitcast.parity_ref, bf16[480,1024]{1,0:T(8,128)(2,1)} %get-tuple-element.294.own_ref, bf16[480,1024]{1,0:T(8,128)(2,1)} %collective-permute-done.14.other_ref, s32[1,1024]{1,0:T(1,128)} %bitcast.278, ...), custom_call_target="tpu_custom_call" | custom-call | flops 2700000000 | tf_op jit(solution)/shard_map/attend/pallas_call | solution.py:249
  203.0 10.2 %mix_out.1 = bf16[4,4,160,1024]{3,2,1,0:T(8,128)(2,1)} custom-call(s32[1]{0:T(128)} %bitcast.parity_ref, bf16[320,1024]{1,0:T(8,128)(2,1)} %get-tuple-element.251.own_ref.own_out, bf16[320,1024]{1,0:T(8,128)(2,1)} %copy-done.20, bf16[640,640]{1,0:T(8,128)(2,1)} %refs_1_, bf16[640,640]{1,0:T(8,128)(2,1)} %collective-permute-done.17.refs_1_.refs_2_, ...), custom_call_target="tpu_custom_call" | custom-call | flops 1000000000 | tf_op jit(solution)/shard_map/mix_out/pallas_call | solution.py:424
  213.2 13.9 %all-gather.14.cloned.1.call-done = bf16[16,160,1024]{2,1,0:T(8,128)(2,1)} async-done(((bf16[4,160,1024]{2,1,0:T(8,128)(2,1)}), bf16[16,160,1024]{2,1,0:T(8,128)(2,1)}) %all-gather.14.cloned.1.call-update) | async-done | bytes 5242896 | tf_op jit(solution)/shard_map/all_gather | solution.py:676
  230.2 48.5 %collective-permute-done.25.refs_10_.refs_2_ = bf16[1728,640]{1,0:T(8,128)(2,1)S(1)} collective-permute-done((bf16[1728,640]{1,0:T(8,128)(2,1)S(1)}, bf16[1728,640]{1,0:T(8,128)(2,1)S(1)}, u32[]{:S(2)}, u32[]{:S(2)}) %collective-permute-start.25) | collective-permute-done | bytes 2211872 | tf_op jit(solution)/shard_map/ppermute | solution.py:35
  295.9 25.7 %reduce-scatter.6.cloned.1.call-done = bf16[1,4,160,1024]{3,2,1,0:T(8,128)(2,1)} async-done(((bf16[4,4,160,1024]{3,2,1,0:T(8,128)(2,1)}), bf16[1,4,160,1024]{3,2,1,0:T(8,128)(2,1)}) %reduce-scatter.6.cloned.1.call-update) | async-done | bytes 1310736 | tf_op jit(solution)/shard_map/reduce_scatter | solution.py:680
  326.9 53.2 %all-gather.16.cloned.1.call-done = bf16[16,160,512]{2,1,0:T(8,128)(2,1)} async-done(((bf16[4,160,512]{2,1,0:T(8,128)(2,1)}), bf16[16,160,512]{2,1,0:T(8,128)(2,1)}) %all-gather.16.cloned.1.call-update) | async-done | bytes 2621456 | tf_op jit(solution)/shard_map/all_gather | solution.py:676
  380.1 42.2 %feed_forward.2 = (bf16[4,640,1024]{2,1,0:T(8,128)(2,1)}, bf16[4,640,1024]{2,1,0:T(8,128)(2,1)}, bf16[1728,1024]{1,0:T(8,128)(2,1)}, bf16[1728,1024]{1,0:T(8,128...) custom-call(bf16[4,4,160,512]{3,2,1,0:T(8,128)(2,1)} %bitcast.255, ...), custom_call_target="tpu_custom_call" | custom-call | flops 4200000000 | tf_op jit(solution)/shard_map/feed_forward/pallas_call | solution.py:563
  422.4 12.8 %all-gather.18.cloned.1.call-done = bf16[16,160,512]{2,1,0:T(8,128)(2,1)} async-done(((bf16[4,160,512]{2,1,0:T(8,128)(2,1)}), bf16[16,160,512]{2,1,0:T(8,128)(2,1)}) %all-gather.18.cloned.1.call-update) | async-done | bytes 2621456 | tf_op jit(solution)/shard_map/all_gather | solution.py:676
  435.1 41.8 %feed_forward.3 = (bf16[4,640,1024]{2,1,0:T(8,128)(2,1)}, bf16[4,640,1024]{2,1,0:T(8,128)(2,1)}, bf16[1728,1024]{1,0:T(8,128)(2,1)}, bf16[1728,1024]{1,0:T(8,128...) custom-call(bf16[4,4,160,512]{3,2,1,0:T(8,128)(2,1)} %bitcast.260, ...), custom_call_target="tpu_custom_call", output_to_operand_aliasing={{0}: (15, {}), {1}: (16, {}), {2}: (17, {}), {3}: (18, {}),... | custom-call | flops 4200000000 | tf_op jit(solution)/shard_map/feed_forward/pallas_call | solution.py:563
  477.0 6.9 convolution_convert_fusion.10
  490.0 6.2 add_convert_fusion.8
  496.2 6.2 add_convert_fusion.7
  533.6 9.4 %reduce-scatter.10.cloned.1.call-done = bf16[1,4,160,512]{3,2,1,0:T(8,128)(2,1)} async-done(((bf16[4,4,160,512]{3,2,1,0:T(8,128)(2,1)}), bf16[1,4,160,512]{3,2,1,0:T(8,128)(2,1)}) %reduce-scatter.10.cloned.1.call-update) | async-done | bytes 655376 | tf_op jit(solution)/shard_map/reduce_scatter | solution.py:680
  548.1 49.0 %collective-permute-done.33 = bf16[1728,640]{1,0:T(8,128)(2,1)S(1)} collective-permute-done((bf16[1728,640]{1,0:T(8,128)(2,1)S(1)}, bf16[1728,640]{1,0:T(8,128)(2,1)S(1)}, u32[]{:S(2)}, u32[]{:S(2)}) %collective-permute-start.33) | collective-permute-done | bytes 2211872 | tf_op jit(solution)/shard_map/ppermute | solution.py:35
  600.8 16.6 %fan_out.1 = bf16[4,4,160,1024]{3,2,1,0:T(8,128)(2,1)} custom-call(bf16[1728,1024]{1,0:T(8,128)(2,1)} %get-tuple-element.221.x_ref, bf16[1728,640]{1,0:T(8,128)(2,1)} %refs_0_.2, bf16[1728,640]{1,0:T(8,128)(2,1)} %copy-done.5, bf16[1728,640]{1,0:T(8,128)(2,1)} %copy-done.4, bf16[1728,640]{1,0:T(8,128)(2,1)} %copy-done.6), custom_call_target="tpu_custom_call" | custom-call | flops 1700000000 | tf_op jit(solution)/shard_map/fan_out/pallas_call | solution.py:485
  617.4 25.8 %collective-permute-done.35 = bf16[1728,640]{1,0:T(8,128)(2,1)} collective-permute-done((bf16[1728,640]{1,0:T(8,128)(2,1)}, bf16[1728,640]{1,0:T(8,128)(2,1)}, u32[]{:S(2)}, u32[]{:S(2)}) %collective-permute-start.35) | collective-permute-done | bytes 2211872 | tf_op jit(solution)/shard_map/ppermute | solution.py:35
  656.2 9.6 %mix_back.1 = (bf16[4,640,1024]{2,1,0:T(8,128)(2,1)}, bf16[320,1024]{1,0:T(8,128)(2,1)}, bf16[320,1024]{1,0:T(8,128)(2,1)}) custom-call(s32[1]{0:T(128)} %bitcast.parity_ref, bf16[4,4,160,1024]{3,2,1,0:T(8,128)(2,1)} %bitcast.248, bf16[640,640]{1,0:T(8,128)(2,1)} %refs_1_, bf16[640,640]{1,0:T(8,128)(2,1)} %collective-permute-done.17.refs_1_.refs_2_, ...), custom_call_target="tpu_custom_call" | custom-call | flops 900000000 | tf_op jit(solution)/shard_map/mix_back/pallas_call | solution.py:459
  668.9 37.4 %attend_back.1 = (bf16[480,1024]{1,0:T(8,128)(2,1)}, bf16[480,1024]{1,0:T(8,128)(2,1)}) custom-call(s32[1]{0:T(128)} %bitcast.parity_ref, bf16[480,1024]{1,0:T(8,128)(2,1)} %get-tuple-element.294.own_ref, bf16[480,1024]{1,0:T(8,128)(2,1)} %collective-permute-done.14.other_ref, bf16[320,1024]{1,0:T(8,128)(2,1)} %get-tuple-element.251.own_ref.own_out, ...), custom_call_target="tpu_custom_call" | custom-call | flops 3700000000 | tf_op jit(solution)/shard_map/attend_back/pallas_call | solution.py:361
  717.2 17.4 %qkv_back.1 = (bf16[640,1024]{1,0:T(8,128)(2,1)}, bf16[320,1024]{1,0:T(8,128)(2,1)}, bf16[4,4,160,1024]{3,2,1,0:T(8,128)(2,1)}, f32[4,4,160,1]{3,2,1,0:T(8,128)}) custom-call(s32[1]{0:T(128)} %bitcast.parity_ref, bf16[4,4,160,1024]{3,2,1,0:T(8,128)(2,1)} %bitcast.237, f32[4,4,160,1]{3,2,1,0:T(8,128)} %copy.66.gain_ref, ...), custom_call_target="tpu_custom_call" | custom-call | flops 1700000000 | tf_op jit(solution)/shard_map/qkv_back/pallas_call | solution.py:653
  774.3 11.4 %collective-permute-done.51 = bf16[640,640]{1,0:T(8,128)(2,1)S(1)} collective-permute-done((bf16[640,640]{1,0:T(8,128)(2,1)S(1)}, bf16[640,640]{1,0:T(8,128)(2,1)S(1)}, u32[]{:S(2)}, u32[]{:S(2)}) %collective-permute-start.51) | collective-permute-done | bytes 819232 | tf_op jit(solution)/shard_map/ppermute | solution.py:35
  807.9 7.6 collective-permute-done.54
  829.4 16.1 %collective-permute-done.53 = bf16[640,640]{1,0:T(8,128)(2,1)S(1)} collective-permute-done((bf16[640,640]{1,0:T(8,128)(2,1)S(1)}, bf16[640,640]{1,0:T(8,128)(2,1)S(1)}, u32[]{:S(2)}, u32[]{:S(2)}) %collective-permute-start.53) | collective-permute-done | bytes 819232 | tf_op jit(solution)/shard_map/ppermute | solution.py:687
  852.6 7.1 collective-permute-done.65
  (351 shorter events, 222.6 us)
Async XLA Ops:
  7.2 121.3 %all-gather.12.cloned.1.call-start = ((), (), s32[]{:S(2)}) async-start(), calls=%async_computation.10 | async-start | bytes 6553600 | tf_op jit(solution)/shard_map/all_gather | solution.py:676
  27.7 199.4 %all-gather.14.cloned.1.call-start = ((), (), s32[]{:S(2)}) async-start(), calls=%async_computation.11 | async-start | bytes 6553600 | tf_op jit(solution)/shard_map/all_gather | solution.py:676
  46.5 29.4 %collective-permute-start.6 = (bf16[640,640]{1,0:T(8,128)(2,1)}, bf16[640,640]{1,0:T(8,128)(2,1)}, u32[]{:S(2)}, u32[]{:S(2)}) collective-permute-start(bf16[640,640]{1,0:T(8,128)(2,1)} %refs_0_.3), channel_id=1, source_target_pairs={{0,8},{4,12},{8,0},{12,4},{1,9},{5,13},{9,1},{13,5},{2,10},{6,14},... | collective-permute-start | bytes 2457608 | tf_op jit(solution)/shard_map/ppermute | solution.py:35
  48.6 27.3 %collective-permute-start.7 = (bf16[320,640]{1,0:T(8,128)(2,1)S(1)}, bf16[320,640]{1,0:T(8,128)(2,1)S(1)}, u32[]{:S(2)}, u32[]{:S(2)}) collective-permute-start(bf16[320,640]{1,0:T(8,128)(2,1)S(1)} %pad_maximum_fusion.5.refs_4_), channel_id=1, source_target_pairs={{0,8},{4,12},{8,0},{12,4},{1,9},{5,13},{9,1},{13,5},{2,10},{6,14},... | collective-permute-start | bytes 1228808 | tf_op jit(solution)/shard_map/ppermute | solution.py:35
  75.9 49.8 %collective-permute-start.12 = (bf16[1728,640]{1,0:T(8,128)(2,1)S(1)}, bf16[1728,640]{1,0:T(8,128)(2,1)}, u32[]{:S(2)}, u32[]{:S(2)}) collective-permute-start(bf16[1728,640]{1,0:T(8,128)(2,1)S(1)} %bitcast.243), channel_id=1, source_target_pairs={{0,8},{4,12},{8,0},{12,4},{1,9},{5,13},{9,1},{13,5},{2,10},{6,14},... | collective-permute-start | bytes 6635528 | tf_op jit(solution)/shard_map/ppermute | solution.py:35
  77.8 36.9 %collective-permute-start.8 = (bf16[640,640]{1,0:T(8,128)(2,1)}, bf16[640,640]{1,0:T(8,128)(2,1)}, u32[]{:S(2)}, u32[]{:S(2)}) collective-permute-start(bf16[640,640]{1,0:T(8,128)(2,1)} %refs_0_.3), channel_id=1, source_target_pairs={{0,4},{4,0},{8,12},{12,8},{1,5},{5,1},{9,13},{13,9},{2,6},{6,2},{1... | collective-permute-start | bytes 2457608 | tf_op jit(solution)/shard_map/ppermute | solution.py:35
  78.3 36.4 %collective-permute-start.9 = (bf16[640,640]{1,0:T(8,128)(2,1)}, bf16[640,640]{1,0:T(8,128)(2,1)}, u32[]{:S(2)}, u32[]{:S(2)}) collective-permute-start(bf16[640,640]{1,0:T(8,128)(2,1)} %collective-permute-done.6.refs_2_), channel_id=1, source_target_pairs={{0,4},{4,0},{8,12},{12,8},{1,5},{5,1},{9,13},{13,9},{2,6},{6,2},{1... | collective-permute-start | bytes 2457608 | tf_op jit(solution)/shard_map/ppermute | solution.py:35
  79.8 34.9 %collective-permute-start.10 = (bf16[320,640]{1,0:T(8,128)(2,1)S(1)}, bf16[320,640]{1,0:T(8,128)(2,1)}, u32[]{:S(2)}, u32[]{:S(2)}) collective-permute-start(bf16[320,640]{1,0:T(8,128)(2,1)S(1)} %pad_maximum_fusion.5.refs_4_), channel_id=1, source_target_pairs={{0,4},{4,0},{8,12},{12,8},{1,5},{5,1},{9,13},{13,9},{2,6},{6,2},{1... | collective-permute-start | bytes 1228808 | tf_op jit(solution)/shard_map/ppermute | solution.py:35
  80.3 34.4 %collective-permute-start.11 = (bf16[320,640]{1,0:T(8,128)(2,1)}, bf16[320,640]{1,0:T(8,128)(2,1)}, u32[]{:S(2)}, u32[]{:S(2)}) collective-permute-start(bf16[320,640]{1,0:T(8,128)(2,1)} %copy-done.28), channel_id=1, source_target_pairs={{0,4},{4,0},{8,12},{12,8},{1,5},{5,1},{9,13},{13,9},{2,6},{6,2},{1... | collective-permute-start | bytes 1228808 | tf_op jit(solution)/shard_map/ppermute | solution.py:35
  128.5 193.1 %reduce-scatter.6.cloned.1.call-start = ((), (), s32[]{:S(2)}) async-start(), calls=%async_computation.5 | async-start | bytes 6553600 | tf_op jit(solution)/shard_map/reduce_scatter | solution.py:680
  148.8 51.1 %collective-permute-start.19 = (bf16[1728,640]{1,0:T(8,128)(2,1)}, bf16[1728,640]{1,0:T(8,128)(2,1)S(1)}, u32[]{:S(2)}, u32[]{:S(2)}) collective-permute-start(bf16[1728,640]{1,0:T(8,128)(2,1)} %bitcast.244), channel_id=1, source_target_pairs={{0,8},{4,12},{8,0},{12,4},{1,9},{5,13},{9,1},{13,5},{2,10},{6,14},... | collective-permute-start | bytes 6635528 | tf_op jit(solution)/shard_map/ppermute | solution.py:35
  167.9 32.1 %collective-permute-start.17 = (bf16[640,640]{1,0:T(8,128)(2,1)S(1)}, bf16[640,640]{1,0:T(8,128)(2,1)}, u32[]{:S(2)}, u32[]{:S(2)}) collective-permute-start(bf16[640,640]{1,0:T(8,128)(2,1)S(1)} %copy-done.19), channel_id=1, source_target_pairs={{0,4},{4,0},{8,12},{12,8},{1,5},{5,1},{9,13},{13,9},{2,6},{6,2},{1... | collective-permute-start | bytes 2457608 | tf_op jit(solution)/shard_map/ppermute | solution.py:35
  168.4 31.6 %collective-permute-start.18 = (bf16[640,640]{1,0:T(8,128)(2,1)}, bf16[640,640]{1,0:T(8,128)(2,1)}, u32[]{:S(2)}, u32[]{:S(2)}) collective-permute-start(bf16[640,640]{1,0:T(8,128)(2,1)} %collective-permute-done.16.refs_2_.refs_3_), channel_id=1, source_target_pairs={{0,4},{4,0},{8,12},{12,8},{1,5},{5,1},{9,13},{13,9},{2,6},{6,2},{1... | collective-permute-start | bytes 2457608 | tf_op jit(solution)/shard_map/ppermute | solution.py:35
  227.2 153.0 %all-gather.16.cloned.1.call-start = ((), (), s32[]{:S(2)}) async-start(), calls=%async_computation.12 | async-start | bytes 3276800 | tf_op jit(solution)/shard_map/all_gather | solution.py:676
  228.8 50.0 %collective-permute-start.25 = (bf16[1728,640]{1,0:T(8,128)(2,1)S(1)}, bf16[1728,640]{1,0:T(8,128)(2,1)S(1)}, u32[]{:S(2)}, u32[]{:S(2)}) collective-permute-start(bf16[1728,640]{1,0:T(8,128)(2,1)S(1)} %copy-done.3), channel_id=1, source_target_pairs={{0,8},{4,12},{8,0},{12,4},{1,9},{5,13},{9,1},{13,5},{2,10},{6,14},... | collective-permute-start | bytes 6635528 | tf_op jit(solution)/shard_map/ppermute | solution.py:35
  230.2 49.5 %collective-permute-start.24 = (bf16[1728,640]{1,0:T(8,128)(2,1)S(1)}, bf16[1728,640]{1,0:T(8,128)(2,1)S(1)}, u32[]{:S(2)}, u32[]{:S(2)}) collective-permute-start(bf16[1728,640]{1,0:T(8,128)(2,1)S(1)} %copy-done.3), channel_id=1, source_target_pairs={{0,4},{4,0},{8,12},{12,8},{1,5},{5,1},{9,13},{13,9},{2,6},{6,2},{1... | collective-permute-start | bytes 6635528 | tf_op jit(solution)/shard_map/ppermute | solution.py:35
  324.7 110.5 %all-gather.18.cloned.1.call-start = ((), (), s32[]{:S(2)}) async-start(), calls=%async_computation.13 | async-start | bytes 3276800 | tf_op jit(solution)/shard_map/all_gather | solution.py:676
  325.2 208.3 %reduce-scatter.8.cloned.1.call-start = ((), (), s32[]{:S(2)}) async-start(), calls=%async_computation.6 | async-start | bytes 3276800 | tf_op jit(solution)/shard_map/reduce_scatter | solution.py:680
  422.3 120.6 %reduce-scatter.10.cloned.1.call-start = ((), (), s32[]{:S(2)}) async-start(), calls=%async_computation.7 | async-start | bytes 3276800 | tf_op jit(solution)/shard_map/reduce_scatter | solution.py:680
  489.9 161.7 %all-gather.20.cloned.1.call-start = ((), (), s32[]{:S(2)}) async-start(), calls=%async_computation.14 | async-start | bytes 6553600 | tf_op jit(solution)/shard_map/all_gather | solution.py:676
  545.9 204.2 %reduce-scatter.12.cloned.1.call-start = ((), (), s32[]{:S(2)}) async-start(), calls=%async_computation.8 | async-start | bytes 6553600 | tf_op jit(solution)/shard_map/reduce_scatter | solution.py:680
  546.0 51.1 %collective-permute-start.33 = (bf16[1728,640]{1,0:T(8,128)(2,1)S(1)}, bf16[1728,640]{1,0:T(8,128)(2,1)S(1)}, u32[]{:S(2)}, u32[]{:S(2)}) collective-permute-start(bf16[1728,640]{1,0:T(8,128)(2,1)S(1)} %copy-done.43), channel_id=1, source_target_pairs={{0,8},{4,12},{8,0},{12,4},{1,9},{5,13},{9,1},{13,5},{2,10},{6,14},... | collective-permute-start | bytes 6635528 | tf_op jit(solution)/shard_map/ppermute | solution.py:35
  547.5 95.7 %collective-permute-start.35 = (bf16[1728,640]{1,0:T(8,128)(2,1)}, bf16[1728,640]{1,0:T(8,128)(2,1)}, u32[]{:S(2)}, u32[]{:S(2)}) collective-permute-start(bf16[1728,640]{1,0:T(8,128)(2,1)} %add_convert_fusion.5), channel_id=1, source_target_pairs={{0,8},{4,12},{8,0},{12,4},{1,9},{5,13},{9,1},{13,5},{2,10},{6,14},... | collective-permute-start | bytes 6635528 | tf_op jit(solution)/shard_map/ppermute | solution.py:35
  599.3 48.2 %collective-permute-start.34 = (bf16[1728,640]{1,0:T(8,128)(2,1)S(1)}, bf16[1728,640]{1,0:T(8,128)(2,1)}, u32[]{:S(2)}, u32[]{:S(2)}) collective-permute-start(bf16[1728,640]{1,0:T(8,128)(2,1)S(1)} %add_convert_fusion.2), channel_id=1, source_target_pairs={{0,16},{16,0},{1,17},{17,1},{2,18},{18,2},{3,19},{19,3},{4,20},{20... | collective-permute-start | bytes 6635528 | tf_op jit(solution)/shard_map/ppermute | solution.py:687
  651.6 195.2 %reduce-scatter.14.cloned.1.call-start = ((), (), s32[]{:S(2)}) async-start(), calls=%async_computation.9 | async-start | bytes 6553600 | tf_op jit(solution)/shard_map/reduce_scatter | solution.py:680
  653.2 53.4 %collective-permute-start.38 = (bf16[1728,640]{1,0:T(8,128)(2,1)S(1)}, bf16[1728,640]{1,0:T(8,128)(2,1)}, u32[]{:S(2)}, u32[]{:S(2)}) collective-permute-start(bf16[1728,640]{1,0:T(8,128)(2,1)S(1)} %copy-done.42), channel_id=1, source_target_pairs={{0,8},{4,12},{8,0},{12,4},{1,9},{5,13},{9,1},{13,5},{2,10},{6,14},... | collective-permute-start | bytes 6635528 | tf_op jit(solution)/shard_map/ppermute | solution.py:35
  654.7 54.2 %collective-permute-start.39 = (bf16[1728,640]{1,0:T(8,128)(2,1)}, bf16[1728,640]{1,0:T(8,128)(2,1)}, u32[]{:S(2)}, u32[]{:S(2)}) collective-permute-start(bf16[1728,640]{1,0:T(8,128)(2,1)} %add_convert_fusion.1), channel_id=1, source_target_pairs={{0,16},{16,0},{1,17},{17,1},{2,18},{18,2},{3,19},{19,3},{4,20},{20... | collective-permute-start | bytes 6635528 | tf_op jit(solution)/shard_map/ppermute | solution.py:687
  715.0 32.2 %collective-permute-start.40 = (bf16[960,640]{1,0:T(8,128)(2,1)}, bf16[960,640]{1,0:T(8,128)(2,1)}, u32[]{:S(2)}, u32[]{:S(2)}) collective-permute-start(bf16[960,640]{1,0:T(8,128)(2,1)} %slice.138), channel_id=1, source_target_pairs={{0,16},{16,0},{1,17},{17,1},{2,18},{18,2},{3,19},{19,3},{4,20},{20... | collective-permute-start | bytes 3686408 | tf_op jit(solution)/shard_map/ppermute | solution.py:687
  785.6 30.1 %collective-permute-start.52 = (bf16[640,640]{1,0:T(8,128)(2,1)S(1)}, bf16[640,640]{1,0:T(8,128)(2,1)S(1)}, u32[]{:S(2)}, u32[]{:S(2)}) collective-permute-start(bf16[640,640]{1,0:T(8,128)(2,1)S(1)} %add_convert_fusion.13), channel_id=1, source_target_pairs={{0,8},{4,12},{8,0},{12,4},{1,9},{5,13},{9,1},{13,5},{2,10},{6,14},... | collective-permute-start | bytes 2457608 | tf_op jit(solution)/shard_map/ppermute | solution.py:35
  786.6 29.0 %collective-permute-start.54 = (bf16[320,640]{1,0:T(8,128)(2,1)S(1)}, bf16[320,640]{1,0:T(8,128)(2,1)S(1)}, u32[]{:S(2)}, u32[]{:S(2)}) collective-permute-start(bf16[320,640]{1,0:T(8,128)(2,1)S(1)} %fusion.62), channel_id=1, source_target_pairs={{0,8},{4,12},{8,0},{12,4},{1,9},{5,13},{9,1},{13,5},{2,10},{6,14},... | collective-permute-start | bytes 1228808 | tf_op jit(solution)/shard_map/ppermute | solution.py:35
  787.9 40.2 %collective-permute-start.56 = (bf16[640,640]{1,0:T(8,128)(2,1)S(1)}, bf16[640,640]{1,0:T(8,128)(2,1)S(1)}, u32[]{:S(2)}, u32[]{:S(2)}) collective-permute-start(bf16[640,640]{1,0:T(8,128)(2,1)S(1)} %add_convert_fusion.11), channel_id=1, source_target_pairs={{0,16},{16,0},{1,17},{17,1},{2,18},{18,2},{3,19},{19,3},{4,20},{20... | collective-permute-start | bytes 2457608 | tf_op jit(solution)/shard_map/ppermute | solution.py:687
  817.0 28.5 %collective-permute-start.53 = (bf16[640,640]{1,0:T(8,128)(2,1)S(1)}, bf16[640,640]{1,0:T(8,128)(2,1)S(1)}, u32[]{:S(2)}, u32[]{:S(2)}) collective-permute-start(bf16[640,640]{1,0:T(8,128)(2,1)S(1)} %add_convert_fusion.12), channel_id=1, source_target_pairs={{0,16},{16,0},{1,17},{17,1},{2,18},{18,2},{3,19},{19,3},{4,20},{20... | collective-permute-start | bytes 2457608 | tf_op jit(solution)/shard_map/ppermute | solution.py:687
  (98 other events, 1337.9 us)
Sparse Core Ops, SparseCore 0:
  27.8 100.5 all-gather.11
  130.6 96.5 all-gather.13
  229.4 92.1 reduce-scatter.5
  324.8 55.3 all-gather.15
  381.5 53.5 all-gather.17
  437.9 50.8 reduce-scatter.7
  491.1 51.7 reduce-scatter.9
  546.1 97.7 all-gather.19
  651.7 93.6 reduce-scatter.11
  750.3 92.3 reduce-scatter.13

commit v13 on v12

--- a/solution.py
+++ b/solution.py
@@ -830,21 +830,27 @@
     up_grads = {k: dot(dup, norm_two[k], NT).astype(BF) for k in range(count)}
     gate_grads = fold(gate_grads, "row", near)
     up_grads = fold(up_grads, "row", near)
-    *share_sums, down_grads, gate_grads, up_grads = together(
-        *share_sums, down_grads, gate_grads, up_grads
+    cut = down_grads[0].shape[0] // 32 * 16
+    head = {k: v[:cut] for k, v in down_grads.items()}
+    tail = {k: v[cut:] for k, v in down_grads.items()}
+    head_moved = {k: swapped(head[k], "row", far_mask) for k in head if k & far_mask}
+    *share_sums, head, tail, head_moved, gate_grads, up_grads = together(
+        *share_sums, head, tail, head_moved, gate_grads, up_grads
     )
     residual_grad_own = grad_own.astype(F32) + jnp.concatenate(share_sums, axis=2).astype(F32)
-    down_total = fold(down_grads, "row", far)[0]
+    head = fold(fold_landed(head, head_moved, far_mask), "row", far[::-1][1:])[0]
+    tail = fold(tail, "row", far[::-1])[0]
+    tail, gate_grads = together(tail, gate_grads)
+    down_parts = sent_over_dp(jnp.concatenate([head, tail]))
     gate_total = fold(gate_grads, "row", far)[0]
 
     mix_cols = spread_cols(residual_grad_own.astype(BF))
     ff_part = fan_out(listed(down_blocks), act, cols)
-    down_total = over_dp(down_total)
-    mix_cols, ff_part, down_total, gate_total, up_grads = together(
-        mix_cols, ff_part, down_total, gate_total, up_grads
+    mix_cols, ff_part, down_parts, gate_total, up_grads = together(
+        mix_cols, ff_part, down_parts, gate_total, up_grads
     )
     up_total = fold(up_grads, "row", far)[0]
-    gate_total = over_dp(gate_total)
+    gate_parts = sent_over_dp(gate_total)
     mix_rows, grad_mine, grad_send = mix_back(own_core, [mix_cols], listed(mix_blocks))
     ff_sum = sum_cols(ff_part)
     grad_other = swapped(grad_send, "row", 1)
@@ -852,9 +858,7 @@
         own_core, own_set, other_set, attn_mine, attn_send, grad_mine, grad_other, lse, seg
     )
     back_other = swapped(back_send, "row", 1)
-    back_other, up_total, gate_total, down_total = together(
-        back_other, up_total, gate_total, down_total
-    )
+    back_other, up_total, gate_parts = together(back_other, up_total, gate_parts)
     cut = up_total.shape[0] * 5 // 9 // 16 * 16
     up_head, up_tail = over_dp(up_total[:cut]), sent_over_dp(up_total[cut:])
     dq, dkv, share, gain_share_one = qkv_back(
@@ -896,9 +900,12 @@
     ff_sum, gain_shares, q_near, kv_near, up_tail, mix_near, mix_moved = together(
         ff_sum, gain_shares, q_near, kv_near, up_tail, mix_near, mix_moved
     )
+    q_near, gate_parts, down_parts = together(q_near, gate_parts, down_parts)
+    gate_total, down_total = summed_up(gate_parts), summed_up(down_parts)
     mix_far = fold_landed(mix_near, mix_moved, far_mask)
     mix_total = over_dp(fold(mix_far, "row", far[::-1][1:])[0])
     q_far = fold(q_near, "row", far)[0]
+    q_far, kv_near = together(q_far, kv_near)
     kv_far = fold(kv_near, "row", far)[0]
     q_total, kv_total = over_dp(q_far), over_dp(kv_far)
     output_own = (residual_own + ff_sum.astype(F32)).astype(BF)

time: 883 us -> 872 us (0.988)
  waiting for transfers between devices: 419 us -> 400 us
    ppermute x59 -> x60, waiting for transfers between devices: 273 us -> 255 us  [swapped(): return lax.ppermute(value, axis, [(i, i ^ mask) for i in range(size)])]
    all_gather x5, waiting for transfers between devices: 82.5 us -> 98.6 us  [spread_cols(): return lax.all_gather(value, 'col', axis=0, tiled=False)]
    ppermute x8, waiting for transfers between devices: 26.9 us -> 13.1 us  [sent_over_dp(): lax.ppermute(low, 'dp', [(i, (i + step) % size) for i in range(size)])]
    ppermute x59 -> x60, starting transfers between devices: 35.6 us -> 41 us  [swapped(): return lax.ppermute(value, axis, [(i, i ^ mask) for i in range(size)])]
  transfers between devices with their start and end apart: 77 -> 78, of which waited for: 36 -> 37; matrix products, arithmetic and copies ran while one was open for 14% -> 15% of each run, Pallas kernels for 25% -> 25%
where the time goes in v13:
time: 872 us; the launch traced here: 863 us
  waiting for transfers between devices  400 us (46%)
  Pallas kernels  215 us (25%)
  matrix products  73.9 us (8%)
  starting transfers between devices  51.8 us (6%)
  other arithmetic  46.7 us (5%)
  blocking collectives  34 us (4%)
  local copies, waits for them, and re-layouts  26.6 us (3%)
  between operations  15.5 us (2%)
    ppermute x60, waiting for transfers between devices, swapped(): return lax.ppermute(value, axis, [(i, i ^ mask) for i in range(size)])  255 us
    all_gather x5, waiting for transfers between devices, spread_cols(): return lax.all_gather(value, 'col', axis=0, tiled=False)  98.6 us
    pallas_call x2, Pallas kernels, feed_forward(): pl.pallas_call(functools.partial(ff_kernel, count, bool(before)), out_sha...  84 us
    dot_general x24, matrix products, dot(): return lax.dot_general(left, right, dims, preferred_element_type=F32)  73.9 us
    ppermute x60, starting transfers between devices, swapped(): return lax.ppermute(value, axis, [(i, i ^ mask) for i in range(size)])  41 us
    pallas_call x1, Pallas kernels, attend_back(): pl.pallas_call(functools.partial(attend_back_kernel, tile), out_shape=(sh...  37.5 us
    all_gather x1, blocking collectives, body(): lax.all_gather(jnp.stack([attn_gain, mlp_gain]), ('row', 'col'), axis=1,...  34 us
    reduce_scatter x5, waiting for transfers between devices, sum_cols(): return lax.psum_scatter(value, 'col', scatter_dimension=0, tiled=False)  32.6 us
  transfers between devices with their start and end apart: 78, of which 37 were waited for; matrix products, arithmetic and copies ran while one was open for 15% of the time, Pallas kernels for 25%

profile of v13, /device:TPU:0, one launch (start us, length us, event | category | flops | bytes accessed | tf_op | source)
XLA Modules:
  0.0 863.4 jit_solution(16499087785992614791)
XLA Ops:
  11.8 7.4 collective-permute-done.2
  19.3 7.2 collective-permute-done.1
  31.4 6.7 collective-permute-done.5
  38.1 7.2 collective-permute-done.4
  48.6 27.3 %collective-permute-done.7.refs_6_ = bf16[320,640]{1,0:T(8,128)(2,1)S(1)} collective-permute-done((bf16[320,640]{1,0:T(8,128)(2,1)S(1)}, bf16[320,640]{1,0:T(8,128)(2,1)S(1)}, u32[]{:S(2)}, u32[]{:S(2)}) %collective-permute-start.7) | collective-permute-done | bytes 409632 | tf_op jit(solution)/shard_map/ppermute | solution.py:35
  80.4 34.0 %all-gather.5 = f32[16,160,2]{1,2,0:T(2,128)S(1)} all-gather(f32[1,160,2]{1,2,0:T(2,128)S(1)} %maximum_bitcast_fusion.1), channel_id=1, replica_groups=mesh['dp'=2,'row'=4,'col'=4] {'row','col'}, dimensions={0}, use_global_device_ids=true | all-gather | bytes 21760 | tf_op jit(solution)/shard_map/all_gather | solution.py:765
  114.7 11.0 %collective-permute-done.12.refs_2_ = bf16[1728,640]{1,0:T(8,128)(2,1)} collective-permute-done((bf16[1728,640]{1,0:T(8,128)(2,1)S(1)}, bf16[1728,640]{1,0:T(8,128)(2,1)}, u32[]{:S(2)}, u32[]{:S(2)}) %collective-permute-start.12) | collective-permute-done | bytes 2211872 | tf_op jit(solution)/shard_map/ppermute | solution.py:35
  130.1 18.7 %collective-permute-done.16.refs_2_.refs_3_ = bf16[640,640]{1,0:T(8,128)(2,1)} collective-permute-done((bf16[640,640]{1,0:T(8,128)(2,1)S(1)}, bf16[640,640]{1,0:T(8,128)(2,1)}, u32[]{:S(2)}, u32[]{:S(2)}) %collective-permute-start.16) | collective-permute-done | bytes 819232 | tf_op jit(solution)/shard_map/ppermute | solution.py:35
  151.9 13.1 %qkv_project.1 = (bf16[4,640,1024]{2,1,0:T(8,128)(2,1)}, f32[1,1024]{1,0:T(1,128)}, bf16[2,480,1024]{2,1,0:T(8,128)(2,1)}) custom-call(bf16[4,4,160,1024]{3,2,1,0:T(8,128)(2,1)} %bitcast.237, f32[4,4,160,1]{3,2,1,0:T(8,128)} %copy.66.gain_ref, f32[40,1024]{1,0:T(8,128)} %get-tuple-element.181.cos_ref, f32[40,1024]{1,0:T(8,128)} %get-tuple-element.182.sin_ref, ...), custom_call_target="tpu_custom_call" | custom-call | flops 1200000000 | tf_op jit(solution)/shard_map/qkv_project/pallas_call | solution.py:157
  172.1 27.8 %attend.1 = (bf16[320,1024]{1,0:T(8,128)(2,1)}, bf16[320,1024]{1,0:T(8,128)(2,1)}, f32[2,4,1,1024]{3,2,1,0:T(1,128)}) custom-call(s32[1]{0:T(128)} %bitcast.parity_ref, bf16[480,1024]{1,0:T(8,128)(2,1)} %get-tuple-element.328.own_ref, bf16[480,1024]{1,0:T(8,128)(2,1)} %collective-permute-done.14.other_ref, s32[1,1024]{1,0:T(1,128)} %bitcast.278, ...), custom_call_target="tpu_custom_call" | custom-call | flops 2700000000 | tf_op jit(solution)/shard_map/attend/pallas_call | solution.py:249
  203.0 10.2 %mix_out.1 = bf16[4,4,160,1024]{3,2,1,0:T(8,128)(2,1)} custom-call(s32[1]{0:T(128)} %bitcast.parity_ref, bf16[320,1024]{1,0:T(8,128)(2,1)} %get-tuple-element.270.own_ref.own_out, bf16[320,1024]{1,0:T(8,128)(2,1)} %copy-done.25, bf16[640,640]{1,0:T(8,128)(2,1)} %refs_1_, bf16[640,640]{1,0:T(8,128)(2,1)} %collective-permute-done.17.refs_1_.refs_2_, ...), custom_call_target="tpu_custom_call" | custom-call | flops 1000000000 | tf_op jit(solution)/shard_map/mix_out/pallas_call | solution.py:424
  213.3 13.9 %all-gather.14.cloned.1.call-done = bf16[16,160,1024]{2,1,0:T(8,128)(2,1)} async-done(((bf16[4,160,1024]{2,1,0:T(8,128)(2,1)}), bf16[16,160,1024]{2,1,0:T(8,128)(2,1)}) %all-gather.14.cloned.1.call-update) | async-done | bytes 5242896 | tf_op jit(solution)/shard_map/all_gather | solution.py:676
  230.2 48.5 %collective-permute-done.25.refs_10_.refs_2_ = bf16[1728,640]{1,0:T(8,128)(2,1)S(1)} collective-permute-done((bf16[1728,640]{1,0:T(8,128)(2,1)S(1)}, bf16[1728,640]{1,0:T(8,128)(2,1)S(1)}, u32[]{:S(2)}, u32[]{:S(2)}) %collective-permute-start.25) | collective-permute-done | bytes 2211872 | tf_op jit(solution)/shard_map/ppermute | solution.py:35
  295.9 25.7 %reduce-scatter.6.cloned.1.call-done = bf16[1,4,160,1024]{3,2,1,0:T(8,128)(2,1)} async-done(((bf16[4,4,160,1024]{3,2,1,0:T(8,128)(2,1)}), bf16[1,4,160,1024]{3,2,1,0:T(8,128)(2,1)}) %reduce-scatter.6.cloned.1.call-update) | async-done | bytes 1310736 | tf_op jit(solution)/shard_map/reduce_scatter | solution.py:680
  326.9 53.3 %all-gather.16.cloned.1.call-done = bf16[16,160,512]{2,1,0:T(8,128)(2,1)} async-done(((bf16[4,160,512]{2,1,0:T(8,128)(2,1)}), bf16[16,160,512]{2,1,0:T(8,128)(2,1)}) %all-gather.16.cloned.1.call-update) | async-done | bytes 2621456 | tf_op jit(solution)/shard_map/all_gather | solution.py:676
  380.1 42.2 %feed_forward.2 = (bf16[4,640,1024]{2,1,0:T(8,128)(2,1)}, bf16[4,640,1024]{2,1,0:T(8,128)(2,1)}, bf16[1728,1024]{1,0:T(8,128)(2,1)}, bf16[1728,1024]{1,0:T(8,128...) custom-call(bf16[4,4,160,512]{3,2,1,0:T(8,128)(2,1)} %bitcast.255, ...), custom_call_target="tpu_custom_call" | custom-call | flops 4200000000 | tf_op jit(solution)/shard_map/feed_forward/pallas_call | solution.py:563
  422.4 12.7 %all-gather.18.cloned.1.call-done = bf16[16,160,512]{2,1,0:T(8,128)(2,1)} async-done(((bf16[4,160,512]{2,1,0:T(8,128)(2,1)}), bf16[16,160,512]{2,1,0:T(8,128)(2,1)}) %all-gather.18.cloned.1.call-update) | async-done | bytes 2621456 | tf_op jit(solution)/shard_map/all_gather | solution.py:676
  435.2 41.8 %feed_forward.3 = (bf16[4,640,1024]{2,1,0:T(8,128)(2,1)}, bf16[4,640,1024]{2,1,0:T(8,128)(2,1)}, bf16[1728,1024]{1,0:T(8,128)(2,1)}, bf16[1728,1024]{1,0:T(8,128...) custom-call(bf16[4,4,160,512]{3,2,1,0:T(8,128)(2,1)} %bitcast.260, ...), custom_call_target="tpu_custom_call", output_to_operand_aliasing={{0}: (15, {}), {1}: (16, {}), {2}: (17, {}), {3}: (18, {}),... | custom-call | flops 4200000000 | tf_op jit(solution)/shard_map/feed_forward/pallas_call | solution.py:563
  476.9 6.9 convolution_convert_fusion.10
  536.8 7.8 collective-permute-done.29
  549.1 24.2 %collective-permute-done.34 = bf16[864,640]{1,0:T(8,128)(2,1)S(1)} collective-permute-done((bf16[864,640]{1,0:T(8,128)(2,1)}, bf16[864,640]{1,0:T(8,128)(2,1)S(1)}, u32[]{:S(2)}, u32[]{:S(2)}) %collective-permute-start.34) | collective-permute-done | bytes 1105952 | tf_op jit(solution)/shard_map/ppermute | solution.py:35
  581.2 16.6 %fan_out.1 = bf16[4,4,160,1024]{3,2,1,0:T(8,128)(2,1)} custom-call(bf16[1728,1024]{1,0:T(8,128)(2,1)} %get-tuple-element.236.x_ref, bf16[1728,640]{1,0:T(8,128)(2,1)} %refs_0_.2, bf16[1728,640]{1,0:T(8,128)(2,1)} %copy-done.4, bf16[1728,640]{1,0:T(8,128)(2,1)} %copy-done.3, bf16[1728,640]{1,0:T(8,128)(2,1)} %copy-done.5), custom_call_target="tpu_custom_call" | custom-call | flops 1700000000 | tf_op jit(solution)/shard_map/fan_out/pallas_call | solution.py:485
  597.8 26.0 %collective-permute-done.36 = bf16[1728,640]{1,0:T(8,128)(2,1)} collective-permute-done((bf16[1728,640]{1,0:T(8,128)(2,1)}, bf16[1728,640]{1,0:T(8,128)(2,1)}, u32[]{:S(2)}, u32[]{:S(2)}) %collective-permute-start.36) | collective-permute-done | bytes 2211872 | tf_op jit(solution)/shard_map/ppermute | solution.py:35
  628.1 16.1 %all-gather.20.cloned.1.call-done = bf16[16,160,1024]{2,1,0:T(8,128)(2,1)} async-done(((bf16[4,160,1024]{2,1,0:T(8,128)(2,1)}), bf16[16,160,1024]{2,1,0:T(8,128)(2,1)}) %all-gather.20.cloned.1.call-update) | async-done | bytes 5242896 | tf_op jit(solution)/shard_map/all_gather | solution.py:676
  647.4 8.7 %mix_back.1 = (bf16[4,640,1024]{2,1,0:T(8,128)(2,1)}, bf16[320,1024]{1,0:T(8,128)(2,1)}, bf16[320,1024]{1,0:T(8,128)(2,1)}) custom-call(s32[1]{0:T(128)} %bitcast.parity_ref, bf16[4,4,160,1024]{3,2,1,0:T(8,128)(2,1)} %bitcast.249, bf16[640,640]{1,0:T(8,128)(2,1)} %refs_1_, bf16[640,640]{1,0:T(8,128)(2,1)} %collective-permute-done.17.refs_1_.refs_2_, ...), custom_call_target="tpu_custom_call" | custom-call | flops 900000000 | tf_op jit(solution)/shard_map/mix_back/pallas_call | solution.py:459
  659.3 37.5 %attend_back.1 = (bf16[480,1024]{1,0:T(8,128)(2,1)}, bf16[480,1024]{1,0:T(8,128)(2,1)}) custom-call(s32[1]{0:T(128)} %bitcast.parity_ref, bf16[480,1024]{1,0:T(8,128)(2,1)} %get-tuple-element.328.own_ref, bf16[480,1024]{1,0:T(8,128)(2,1)} %collective-permute-done.14.other_ref, bf16[320,1024]{1,0:T(8,128)(2,1)} %get-tuple-element.270.own_ref.own_out, ...), custom_call_target="tpu_custom_call" | custom-call | flops 3700000000 | tf_op jit(solution)/shard_map/attend_back/pallas_call | solution.py:361
  702.4 17.5 %qkv_back.1 = (bf16[640,1024]{1,0:T(8,128)(2,1)}, bf16[320,1024]{1,0:T(8,128)(2,1)}, bf16[4,4,160,1024]{3,2,1,0:T(8,128)(2,1)}, f32[4,4,160,1]{3,2,1,0:T(8,128)}) custom-call(s32[1]{0:T(128)} %bitcast.parity_ref, bf16[4,4,160,1024]{3,2,1,0:T(8,128)(2,1)} %bitcast.238, f32[4,4,160,1]{3,2,1,0:T(8,128)} %copy.66.gain_ref, ...), custom_call_target="tpu_custom_call" | custom-call | flops 1700000000 | tf_op jit(solution)/shard_map/qkv_back/pallas_call | solution.py:653
  764.2 12.7 %collective-permute-done.52 = bf16[640,640]{1,0:T(8,128)(2,1)S(1)} collective-permute-done((bf16[640,640]{1,0:T(8,128)(2,1)S(1)}, bf16[640,640]{1,0:T(8,128)(2,1)S(1)}, u32[]{:S(2)}, u32[]{:S(2)}) %collective-permute-start.52) | collective-permute-done | bytes 819232 | tf_op jit(solution)/shard_map/ppermute | solution.py:35
  783.2 7.6 convert_add_fusion
  808.5 12.2 %collective-permute-done.55 = bf16[320,640]{1,0:T(8,128)(2,1)S(1)} collective-permute-done((bf16[320,640]{1,0:T(8,128)(2,1)S(1)}, bf16[320,640]{1,0:T(8,128)(2,1)S(1)}, u32[]{:S(2)}, u32[]{:S(2)}) %collective-permute-start.55) | collective-permute-done | bytes 409632 | tf_op jit(solution)/shard_map/ppermute | solution.py:35
  823.9 8.2 collective-permute-done.56
  841.4 7.0 collective-permute-done.66
  (356 shorter events, 230.3 us)
Async XLA Ops:
  7.2 121.3 %all-gather.12.cloned.1.call-start = ((), (), s32[]{:S(2)}) async-start(), calls=%async_computation.10 | async-start | bytes 6553600 | tf_op jit(solution)/shard_map/all_gather | solution.py:676
  27.7 199.4 %all-gather.14.cloned.1.call-start = ((), (), s32[]{:S(2)}) async-start(), calls=%async_computation.11 | async-start | bytes 6553600 | tf_op jit(solution)/shard_map/all_gather | solution.py:676
  46.5 29.4 %collective-permute-start.6 = (bf16[640,640]{1,0:T(8,128)(2,1)}, bf16[640,640]{1,0:T(8,128)(2,1)}, u32[]{:S(2)}, u32[]{:S(2)}) collective-permute-start(bf16[640,640]{1,0:T(8,128)(2,1)} %refs_0_.3), channel_id=1, source_target_pairs={{0,8},{4,12},{8,0},{12,4},{1,9},{5,13},{9,1},{13,5},{2,10},{6,14},... | collective-permute-start | bytes 2457608 | tf_op jit(solution)/shard_map/ppermute | solution.py:35
  48.6 27.3 %collective-permute-start.7 = (bf16[320,640]{1,0:T(8,128)(2,1)S(1)}, bf16[320,640]{1,0:T(8,128)(2,1)S(1)}, u32[]{:S(2)}, u32[]{:S(2)}) collective-permute-start(bf16[320,640]{1,0:T(8,128)(2,1)S(1)} %pad_maximum_fusion.6.refs_4_), channel_id=1, source_target_pairs={{0,8},{4,12},{8,0},{12,4},{1,9},{5,13},{9,1},{13,5},{2,10},{6,14},... | collective-permute-start | bytes 1228808 | tf_op jit(solution)/shard_map/ppermute | solution.py:35
  75.9 49.8 %collective-permute-start.12 = (bf16[1728,640]{1,0:T(8,128)(2,1)S(1)}, bf16[1728,640]{1,0:T(8,128)(2,1)}, u32[]{:S(2)}, u32[]{:S(2)}) collective-permute-start(bf16[1728,640]{1,0:T(8,128)(2,1)S(1)} %bitcast.244), channel_id=1, source_target_pairs={{0,8},{4,12},{8,0},{12,4},{1,9},{5,13},{9,1},{13,5},{2,10},{6,14},... | collective-permute-start | bytes 6635528 | tf_op jit(solution)/shard_map/ppermute | solution.py:35
  77.8 36.9 %collective-permute-start.8 = (bf16[640,640]{1,0:T(8,128)(2,1)}, bf16[640,640]{1,0:T(8,128)(2,1)}, u32[]{:S(2)}, u32[]{:S(2)}) collective-permute-start(bf16[640,640]{1,0:T(8,128)(2,1)} %refs_0_.3), channel_id=1, source_target_pairs={{0,4},{4,0},{8,12},{12,8},{1,5},{5,1},{9,13},{13,9},{2,6},{6,2},{1... | collective-permute-start | bytes 2457608 | tf_op jit(solution)/shard_map/ppermute | solution.py:35
  78.3 36.4 %collective-permute-start.9 = (bf16[640,640]{1,0:T(8,128)(2,1)}, bf16[640,640]{1,0:T(8,128)(2,1)}, u32[]{:S(2)}, u32[]{:S(2)}) collective-permute-start(bf16[640,640]{1,0:T(8,128)(2,1)} %collective-permute-done.6.refs_2_), channel_id=1, source_target_pairs={{0,4},{4,0},{8,12},{12,8},{1,5},{5,1},{9,13},{13,9},{2,6},{6,2},{1... | collective-permute-start | bytes 2457608 | tf_op jit(solution)/shard_map/ppermute | solution.py:35
  79.8 34.9 %collective-permute-start.10 = (bf16[320,640]{1,0:T(8,128)(2,1)S(1)}, bf16[320,640]{1,0:T(8,128)(2,1)}, u32[]{:S(2)}, u32[]{:S(2)}) collective-permute-start(bf16[320,640]{1,0:T(8,128)(2,1)S(1)} %pad_maximum_fusion.6.refs_4_), channel_id=1, source_target_pairs={{0,4},{4,0},{8,12},{12,8},{1,5},{5,1},{9,13},{13,9},{2,6},{6,2},{1... | collective-permute-start | bytes 1228808 | tf_op jit(solution)/shard_map/ppermute | solution.py:35
  80.3 34.4 %collective-permute-start.11 = (bf16[320,640]{1,0:T(8,128)(2,1)}, bf16[320,640]{1,0:T(8,128)(2,1)}, u32[]{:S(2)}, u32[]{:S(2)}) collective-permute-start(bf16[320,640]{1,0:T(8,128)(2,1)} %copy-done.31), channel_id=1, source_target_pairs={{0,4},{4,0},{8,12},{12,8},{1,5},{5,1},{9,13},{13,9},{2,6},{6,2},{1... | collective-permute-start | bytes 1228808 | tf_op jit(solution)/shard_map/ppermute | solution.py:35
  128.5 193.1 %reduce-scatter.6.cloned.1.call-start = ((), (), s32[]{:S(2)}) async-start(), calls=%async_computation.5 | async-start | bytes 6553600 | tf_op jit(solution)/shard_map/reduce_scatter | solution.py:680
  148.8 51.2 %collective-permute-start.19 = (bf16[1728,640]{1,0:T(8,128)(2,1)}, bf16[1728,640]{1,0:T(8,128)(2,1)S(1)}, u32[]{:S(2)}, u32[]{:S(2)}) collective-permute-start(bf16[1728,640]{1,0:T(8,128)(2,1)} %bitcast.245), channel_id=1, source_target_pairs={{0,8},{4,12},{8,0},{12,4},{1,9},{5,13},{9,1},{13,5},{2,10},{6,14},... | collective-permute-start | bytes 6635528 | tf_op jit(solution)/shard_map/ppermute | solution.py:35
  168.0 32.1 %collective-permute-start.17 = (bf16[640,640]{1,0:T(8,128)(2,1)S(1)}, bf16[640,640]{1,0:T(8,128)(2,1)}, u32[]{:S(2)}, u32[]{:S(2)}) collective-permute-start(bf16[640,640]{1,0:T(8,128)(2,1)S(1)} %copy-done.23), channel_id=1, source_target_pairs={{0,4},{4,0},{8,12},{12,8},{1,5},{5,1},{9,13},{13,9},{2,6},{6,2},{1... | collective-permute-start | bytes 2457608 | tf_op jit(solution)/shard_map/ppermute | solution.py:35
  168.5 31.6 %collective-permute-start.18 = (bf16[640,640]{1,0:T(8,128)(2,1)}, bf16[640,640]{1,0:T(8,128)(2,1)}, u32[]{:S(2)}, u32[]{:S(2)}) collective-permute-start(bf16[640,640]{1,0:T(8,128)(2,1)} %collective-permute-done.16.refs_2_.refs_3_), channel_id=1, source_target_pairs={{0,4},{4,0},{8,12},{12,8},{1,5},{5,1},{9,13},{13,9},{2,6},{6,2},{1... | collective-permute-start | bytes 2457608 | tf_op jit(solution)/shard_map/ppermute | solution.py:35
  227.2 153.0 %all-gather.16.cloned.1.call-start = ((), (), s32[]{:S(2)}) async-start(), calls=%async_computation.12 | async-start | bytes 3276800 | tf_op jit(solution)/shard_map/all_gather | solution.py:676
  228.8 50.0 %collective-permute-start.25 = (bf16[1728,640]{1,0:T(8,128)(2,1)S(1)}, bf16[1728,640]{1,0:T(8,128)(2,1)S(1)}, u32[]{:S(2)}, u32[]{:S(2)}) collective-permute-start(bf16[1728,640]{1,0:T(8,128)(2,1)S(1)} %copy-done.2), channel_id=1, source_target_pairs={{0,8},{4,12},{8,0},{12,4},{1,9},{5,13},{9,1},{13,5},{2,10},{6,14},... | collective-permute-start | bytes 6635528 | tf_op jit(solution)/shard_map/ppermute | solution.py:35
  230.2 49.5 %collective-permute-start.24 = (bf16[1728,640]{1,0:T(8,128)(2,1)S(1)}, bf16[1728,640]{1,0:T(8,128)(2,1)S(1)}, u32[]{:S(2)}, u32[]{:S(2)}) collective-permute-start(bf16[1728,640]{1,0:T(8,128)(2,1)S(1)} %copy-done.2), channel_id=1, source_target_pairs={{0,4},{4,0},{8,12},{12,8},{1,5},{5,1},{9,13},{13,9},{2,6},{6,2},{1... | collective-permute-start | bytes 6635528 | tf_op jit(solution)/shard_map/ppermute | solution.py:35
  324.7 110.5 %all-gather.18.cloned.1.call-start = ((), (), s32[]{:S(2)}) async-start(), calls=%async_computation.13 | async-start | bytes 3276800 | tf_op jit(solution)/shard_map/all_gather | solution.py:676
  325.2 219.3 %reduce-scatter.8.cloned.1.call-start = ((), (), s32[]{:S(2)}) async-start(), calls=%async_computation.6 | async-start | bytes 3276800 | tf_op jit(solution)/shard_map/reduce_scatter | solution.py:680
  422.4 122.2 %reduce-scatter.10.cloned.1.call-start = ((), (), s32[]{:S(2)}) async-start(), calls=%async_computation.7 | async-start | bytes 3276800 | tf_op jit(solution)/shard_map/reduce_scatter | solution.py:680
  489.9 154.3 %all-gather.20.cloned.1.call-start = ((), (), s32[]{:S(2)}) async-start(), calls=%async_computation.14 | async-start | bytes 6553600 | tf_op jit(solution)/shard_map/all_gather | solution.py:676
  518.1 26.5 %collective-permute-start.29 = (bf16[864,640]{1,0:T(8,128)(2,1)S(1)}, bf16[864,640]{1,0:T(8,128)(2,1)}, u32[]{:S(2)}, u32[]{:S(2)}) collective-permute-start(bf16[864,640]{1,0:T(8,128)(2,1)S(1)} %get-tuple-element.324), channel_id=1, source_target_pairs={{0,8},{4,12},{8,0},{12,4},{1,9},{5,13},{9,1},{13,5},{2,10},{6,14},... | collective-permute-start | bytes 3317768 | tf_op jit(solution)/shard_map/ppermute | solution.py:35
  547.5 191.2 %reduce-scatter.12.cloned.1.call-start = ((), (), s32[]{:S(2)}) async-start(), calls=%async_computation.8 | async-start | bytes 6553600 | tf_op jit(solution)/shard_map/reduce_scatter | solution.py:680
  547.5 25.9 %collective-permute-start.34 = (bf16[864,640]{1,0:T(8,128)(2,1)}, bf16[864,640]{1,0:T(8,128)(2,1)S(1)}, u32[]{:S(2)}, u32[]{:S(2)}) collective-permute-start(bf16[864,640]{1,0:T(8,128)(2,1)} %get-tuple-element.248), channel_id=1, source_target_pairs={{0,8},{4,12},{8,0},{12,4},{1,9},{5,13},{9,1},{13,5},{2,10},{6,14},... | collective-permute-start | bytes 3317768 | tf_op jit(solution)/shard_map/ppermute | solution.py:35
  574.9 48.8 %collective-permute-start.36 = (bf16[1728,640]{1,0:T(8,128)(2,1)}, bf16[1728,640]{1,0:T(8,128)(2,1)}, u32[]{:S(2)}, u32[]{:S(2)}) collective-permute-start(bf16[1728,640]{1,0:T(8,128)(2,1)} %add_convert_fusion.4), channel_id=1, source_target_pairs={{0,8},{4,12},{8,0},{12,4},{1,9},{5,13},{9,1},{13,5},{2,10},{6,14},... | collective-permute-start | bytes 6635528 | tf_op jit(solution)/shard_map/ppermute | solution.py:35
  579.7 48.4 %collective-permute-start.35 = (bf16[1728,640]{1,0:T(8,128)(2,1)}, bf16[1728,640]{1,0:T(8,128)(2,1)}, u32[]{:S(2)}, u32[]{:S(2)}) collective-permute-start(bf16[1728,640]{1,0:T(8,128)(2,1)} %pad_maximum_fusion.1), channel_id=1, source_target_pairs={{0,16},{16,0},{1,17},{17,1},{2,18},{18,2},{3,19},{19,3},{4,20},{20... | collective-permute-start | bytes 6635528 | tf_op jit(solution)/shard_map/ppermute | solution.py:687
  644.2 191.0 %reduce-scatter.14.cloned.1.call-start = ((), (), s32[]{:S(2)}) async-start(), calls=%async_computation.9 | async-start | bytes 6553600 | tf_op jit(solution)/shard_map/reduce_scatter | solution.py:680
  644.4 52.7 %collective-permute-start.39 = (bf16[1728,640]{1,0:T(8,128)(2,1)}, bf16[1728,640]{1,0:T(8,128)(2,1)}, u32[]{:S(2)}, u32[]{:S(2)}) collective-permute-start(bf16[1728,640]{1,0:T(8,128)(2,1)} %add_convert_fusion.2), channel_id=1, source_target_pairs={{0,8},{4,12},{8,0},{12,4},{1,9},{5,13},{9,1},{13,5},{2,10},{6,14},... | collective-permute-start | bytes 6635528 | tf_op jit(solution)/shard_map/ppermute | solution.py:35
  646.0 53.6 %collective-permute-start.40 = (bf16[1728,640]{1,0:T(8,128)(2,1)}, bf16[1728,640]{1,0:T(8,128)(2,1)}, u32[]{:S(2)}, u32[]{:S(2)}) collective-permute-start(bf16[1728,640]{1,0:T(8,128)(2,1)} %add_convert_fusion.1), channel_id=1, source_target_pairs={{0,16},{16,0},{1,17},{17,1},{2,18},{18,2},{3,19},{19,3},{4,20},{20... | collective-permute-start | bytes 6635528 | tf_op jit(solution)/shard_map/ppermute | solution.py:687
  700.7 29.8 %collective-permute-start.41 = (bf16[960,640]{1,0:T(8,128)(2,1)}, bf16[960,640]{1,0:T(8,128)(2,1)}, u32[]{:S(2)}, u32[]{:S(2)}) collective-permute-start(bf16[960,640]{1,0:T(8,128)(2,1)} %slice.154), channel_id=1, source_target_pairs={{0,16},{16,0},{1,17},{17,1},{2,18},{18,2},{3,19},{19,3},{4,20},{20... | collective-permute-start | bytes 3686408 | tf_op jit(solution)/shard_map/ppermute | solution.py:687
  777.9 44.4 %collective-permute-start.57 = (bf16[640,640]{1,0:T(8,128)(2,1)S(1)}, bf16[640,640]{1,0:T(8,128)(2,1)S(1)}, u32[]{:S(2)}, u32[]{:S(2)}) collective-permute-start(bf16[640,640]{1,0:T(8,128)(2,1)S(1)} %add_convert_fusion.12), channel_id=1, source_target_pairs={{0,16},{16,0},{1,17},{17,1},{2,18},{18,2},{3,19},{19,3},{4,20},{20... | collective-permute-start | bytes 2457608 | tf_op jit(solution)/shard_map/ppermute | solution.py:687
  797.6 24.7 %collective-permute-start.64 = (bf16[160,1024]{1,0:T(8,128)(2,1)S(1)}, bf16[160,1024]{1,0:T(8,128)(2,1)S(1)}, u32[]{:S(2)}, u32[]{:S(2)}) collective-permute-start(bf16[160,1024]{1,0:T(8,128)(2,1)S(1)} %get-tuple-element.332), channel_id=1, source_target_pairs={{0,12},{4,8},{8,4},{12,0},{1,13},{5,9},{9,5},{13,1},{2,14},{6,10},... | collective-permute-start | bytes 983048 | tf_op jit(solution)/shard_map/ppermute | solution.py:35
  807.0 25.2 %collective-permute-start.54 = (bf16[640,640]{1,0:T(8,128)(2,1)S(1)}, bf16[640,640]{1,0:T(8,128)(2,1)S(1)}, u32[]{:S(2)}, u32[]{:S(2)}) collective-permute-start(bf16[640,640]{1,0:T(8,128)(2,1)S(1)} %add_convert_fusion.13), channel_id=1, source_target_pairs={{0,16},{16,0},{1,17},{17,1},{2,18},{18,2},{3,19},{19,3},{4,20},{20... | collective-permute-start | bytes 2457608 | tf_op jit(solution)/shard_map/ppermute | solution.py:687
  (99 other events, 1436.1 us)
Sparse Core Ops, SparseCore 0:
  27.8 100.5 all-gather.11
  130.6 96.5 all-gather.13
  229.4 92.1 reduce-scatter.5
  324.8 55.3 all-gather.15
  381.5 53.5 all-gather.17
  437.9 50.8 reduce-scatter.7
  491.1 51.7 reduce-scatter.9
  547.6 96.5 all-gather.19
  646.5 92.1 reduce-scatter.11
  740.8 94.3 reduce-scatter.13

commit v14 on v13

--- a/solution.py
+++ b/solution.py
@@ -736,7 +736,7 @@
 
     def all_tokens(blocks):
         got = exchange_blocks([blocks[k] for k in range(count)], "row")
-        result = jnp.zeros((piece, count * rows), blocks.dtype)
+        result = jnp.zeros((piece, count * rows), BF)
         for k in range(count):
             result = lax.dynamic_update_slice(result, got[k], (0, (row ^ k) * rows))
         return result.T
@@ -860,7 +860,7 @@
     back_other = swapped(back_send, "row", 1)
     back_other, up_total, gate_parts = together(back_other, up_total, gate_parts)
     cut = up_total.shape[0] * 5 // 9 // 16 * 16
-    up_head, up_tail = over_dp(up_total[:cut]), sent_over_dp(up_total[cut:])
+    up_head, up_tail = over_dp(up_total[:cut]), up_total[cut:]
     dq, dkv, share, gain_share_one = qkv_back(
         own_core,
         source,
@@ -893,6 +893,8 @@
     share, dq, dkv, attn_low, mix_rows = together(share, dq, dkv, attn_low, mix_rows)
     mix_even = {k: dot(attn_low, mix_rows[k], NT).astype(BF) for k in range(0, count, 2)}
     mix_near = fold({**mix_even, **mix_odd}, "row", near)
+    mix_even, up_tail = together(mix_even, up_tail)
+    up_tail = sent_over_dp(up_tail)
     dq, dkv, mix_near = together(dq, dkv, mix_near)
     mix_moved = {k: swapped(mix_near[k], "row", far_mask) for k in mix_near if k & far_mask}
     q_near = fold({k: dot(norm_one[k], dq, NT).astype(BF) for k in range(count)}, "row", near)
@@ -920,7 +922,10 @@
         input_sum, q_total, kv_total, mix_total, gain_totals, layer_output, up_total
     )
 
-    input_grad = all_tokens((residual_grad_own + input_sum.astype(F32)).astype(BF)).astype(F32)
+    input_blocks = [
+        (residual_grad_own[k] + input_sum[k].astype(F32)).astype(BF) for k in range(count)
+    ]
+    input_grad = all_tokens(input_blocks).astype(F32)
     kv_rows = kv_total.shape[0] // 2
     return (
         layer_output,

time: 872 us -> 873 us (level)
  transfers between devices with their start and end apart: 78 -> 78, of which waited for: 37 -> 37; matrix products, arithmetic and copies ran while one was open for 15% -> 14% of each run, Pallas kernels for 25% -> 25%
where the time goes in v14:
time: 873 us; the launch traced here: 865 us
  waiting for transfers between devices  399 us (46%)
  Pallas kernels  216 us (25%)
  matrix products  73.6 us (8%)
  starting transfers between devices  50.6 us (6%)
  other arithmetic  49.3 us (6%)
  blocking collectives  34 us (4%)
  local copies, waits for them, and re-layouts  26.9 us (3%)
  between operations  15.5 us (2%)
    ppermute x60, waiting for transfers between devices, swapped(): return lax.ppermute(value, axis, [(i, i ^ mask) for i in range(size)])  248 us
    all_gather x5, waiting for transfers between devices, spread_cols(): return lax.all_gather(value, 'col', axis=0, tiled=False)  98.7 us
    pallas_call x2, Pallas kernels, feed_forward(): pl.pallas_call(functools.partial(ff_kernel, count, bool(before)), out_sha...  84 us
    dot_general x24, matrix products, dot(): return lax.dot_general(left, right, dims, preferred_element_type=F32)  73.6 us
    ppermute x60, starting transfers between devices, swapped(): return lax.ppermute(value, axis, [(i, i ^ mask) for i in range(size)])  40.2 us
    pallas_call x1, Pallas kernels, attend_back(): pl.pallas_call(functools.partial(attend_back_kernel, tile), out_shape=(sh...  37.5 us
    all_gather x1, blocking collectives, body(): lax.all_gather(jnp.stack([attn_gain, mlp_gain]), ('row', 'col'), axis=1,...  34 us
    reduce_scatter x5, waiting for transfers between devices, sum_cols(): return lax.psum_scatter(value, 'col', scatter_dimension=0, tiled=False)  29.9 us
  transfers between devices with their start and end apart: 78, of which 37 were waited for; matrix products, arithmetic and copies ran while one was open for 14% of the time, Pallas kernels for 25%

profile of v14, /device:TPU:0, one launch (start us, length us, event | category | flops | bytes accessed | tf_op | source)
XLA Modules:
  0.0 865.2 jit_solution(9986004132113535508)
XLA Ops:
  11.8 7.4 collective-permute-done.2
  19.3 7.2 collective-permute-done.1
  31.4 6.7 collective-permute-done.5
  38.1 7.2 collective-permute-done.4
  48.6 27.3 %collective-permute-done.7.refs_6_ = bf16[320,640]{1,0:T(8,128)(2,1)S(1)} collective-permute-done((bf16[320,640]{1,0:T(8,128)(2,1)S(1)}, bf16[320,640]{1,0:T(8,128)(2,1)S(1)}, u32[]{:S(2)}, u32[]{:S(2)}) %collective-permute-start.7) | collective-permute-done | bytes 409632 | tf_op jit(solution)/shard_map/ppermute | solution.py:35
  80.4 34.0 %all-gather.5 = f32[16,160,2]{1,2,0:T(2,128)S(1)} all-gather(f32[1,160,2]{1,2,0:T(2,128)S(1)} %maximum_bitcast_fusion.1), channel_id=1, replica_groups=mesh['dp'=2,'row'=4,'col'=4] {'row','col'}, dimensions={0}, use_global_device_ids=true | all-gather | bytes 21760 | tf_op jit(solution)/shard_map/all_gather | solution.py:765
  114.7 11.0 %collective-permute-done.12.refs_2_ = bf16[1728,640]{1,0:T(8,128)(2,1)} collective-permute-done((bf16[1728,640]{1,0:T(8,128)(2,1)S(1)}, bf16[1728,640]{1,0:T(8,128)(2,1)}, u32[]{:S(2)}, u32[]{:S(2)}) %collective-permute-start.12) | collective-permute-done | bytes 2211872 | tf_op jit(solution)/shard_map/ppermute | solution.py:35
  130.1 18.7 %collective-permute-done.16.refs_2_.refs_3_ = bf16[640,640]{1,0:T(8,128)(2,1)} collective-permute-done((bf16[640,640]{1,0:T(8,128)(2,1)S(1)}, bf16[640,640]{1,0:T(8,128)(2,1)}, u32[]{:S(2)}, u32[]{:S(2)}) %collective-permute-start.16) | collective-permute-done | bytes 819232 | tf_op jit(solution)/shard_map/ppermute | solution.py:35
  151.9 13.1 %qkv_project.1 = (bf16[4,640,1024]{2,1,0:T(8,128)(2,1)}, f32[1,1024]{1,0:T(1,128)}, bf16[2,480,1024]{2,1,0:T(8,128)(2,1)}) custom-call(bf16[4,4,160,1024]{3,2,1,0:T(8,128)(2,1)} %bitcast.237, f32[4,4,160,1]{3,2,1,0:T(8,128)} %copy.66.gain_ref, f32[40,1024]{1,0:T(8,128)} %get-tuple-element.182.cos_ref, f32[40,1024]{1,0:T(8,128)} %get-tuple-element.183.sin_ref, ...), custom_call_target="tpu_custom_call" | custom-call | flops 1200000000 | tf_op jit(solution)/shard_map/qkv_project/pallas_call | solution.py:157
  172.1 27.9 %attend.1 = (bf16[320,1024]{1,0:T(8,128)(2,1)}, bf16[320,1024]{1,0:T(8,128)(2,1)}, f32[2,4,1,1024]{3,2,1,0:T(1,128)}) custom-call(s32[1]{0:T(128)} %bitcast.parity_ref, bf16[480,1024]{1,0:T(8,128)(2,1)} %get-tuple-element.335.own_ref, bf16[480,1024]{1,0:T(8,128)(2,1)} %collective-permute-done.14.other_ref, s32[1,1024]{1,0:T(1,128)} %bitcast.277, ...), custom_call_target="tpu_custom_call" | custom-call | flops 2700000000 | tf_op jit(solution)/shard_map/attend/pallas_call | solution.py:249
  203.1 10.2 %mix_out.1 = bf16[4,4,160,1024]{3,2,1,0:T(8,128)(2,1)} custom-call(s32[1]{0:T(128)} %bitcast.parity_ref, bf16[320,1024]{1,0:T(8,128)(2,1)} %get-tuple-element.271.own_ref.own_out, bf16[320,1024]{1,0:T(8,128)(2,1)} %copy-done.23, bf16[640,640]{1,0:T(8,128)(2,1)} %refs_1_, bf16[640,640]{1,0:T(8,128)(2,1)} %collective-permute-done.17.refs_1_.refs_2_, ...), custom_call_target="tpu_custom_call" | custom-call | flops 1000000000 | tf_op jit(solution)/shard_map/mix_out/pallas_call | solution.py:424
  213.3 13.8 %all-gather.14.cloned.1.call-done = bf16[16,160,1024]{2,1,0:T(8,128)(2,1)} async-done(((bf16[4,160,1024]{2,1,0:T(8,128)(2,1)}), bf16[16,160,1024]{2,1,0:T(8,128)(2,1)}) %all-gather.14.cloned.1.call-update) | async-done | bytes 5242896 | tf_op jit(solution)/shard_map/all_gather | solution.py:676
  230.2 48.5 %collective-permute-done.25.refs_10_.refs_2_ = bf16[1728,640]{1,0:T(8,128)(2,1)S(1)} collective-permute-done((bf16[1728,640]{1,0:T(8,128)(2,1)S(1)}, bf16[1728,640]{1,0:T(8,128)(2,1)S(1)}, u32[]{:S(2)}, u32[]{:S(2)}) %collective-permute-start.25) | collective-permute-done | bytes 2211872 | tf_op jit(solution)/shard_map/ppermute | solution.py:35
  295.9 25.7 %reduce-scatter.6.cloned.1.call-done = bf16[1,4,160,1024]{3,2,1,0:T(8,128)(2,1)} async-done(((bf16[4,4,160,1024]{3,2,1,0:T(8,128)(2,1)}), bf16[1,4,160,1024]{3,2,1,0:T(8,128)(2,1)}) %reduce-scatter.6.cloned.1.call-update) | async-done | bytes 1310736 | tf_op jit(solution)/shard_map/reduce_scatter | solution.py:680
  326.9 53.3 %all-gather.16.cloned.1.call-done = bf16[16,160,512]{2,1,0:T(8,128)(2,1)} async-done(((bf16[4,160,512]{2,1,0:T(8,128)(2,1)}), bf16[16,160,512]{2,1,0:T(8,128)(2,1)}) %all-gather.16.cloned.1.call-update) | async-done | bytes 2621456 | tf_op jit(solution)/shard_map/all_gather | solution.py:676
  380.1 42.2 %feed_forward.2 = (bf16[4,640,1024]{2,1,0:T(8,128)(2,1)}, bf16[4,640,1024]{2,1,0:T(8,128)(2,1)}, bf16[1728,1024]{1,0:T(8,128)(2,1)}, bf16[1728,1024]{1,0:T(8,128...) custom-call(bf16[4,4,160,512]{3,2,1,0:T(8,128)(2,1)} %bitcast.255, ...), custom_call_target="tpu_custom_call" | custom-call | flops 4200000000 | tf_op jit(solution)/shard_map/feed_forward/pallas_call | solution.py:563
  422.4 12.7 %all-gather.18.cloned.1.call-done = bf16[16,160,512]{2,1,0:T(8,128)(2,1)} async-done(((bf16[4,160,512]{2,1,0:T(8,128)(2,1)}), bf16[16,160,512]{2,1,0:T(8,128)(2,1)}) %all-gather.18.cloned.1.call-update) | async-done | bytes 2621456 | tf_op jit(solution)/shard_map/all_gather | solution.py:676
  435.2 41.8 %feed_forward.3 = (bf16[4,640,1024]{2,1,0:T(8,128)(2,1)}, bf16[4,640,1024]{2,1,0:T(8,128)(2,1)}, bf16[1728,1024]{1,0:T(8,128)(2,1)}, bf16[1728,1024]{1,0:T(8,128...) custom-call(bf16[4,4,160,512]{3,2,1,0:T(8,128)(2,1)} %bitcast.256, ...), custom_call_target="tpu_custom_call", output_to_operand_aliasing={{0}: (15, {}), {1}: (16, {}), {2}: (17, {}), {3}: (18, {}),... | custom-call | flops 4200000000 | tf_op jit(solution)/shard_map/feed_forward/pallas_call | solution.py:563
  476.9 6.9 convolution_convert_fusion.10
  536.8 7.7 collective-permute-done.29
  550.0 24.2 %collective-permute-done.34 = bf16[864,640]{1,0:T(8,128)(2,1)S(1)} collective-permute-done((bf16[864,640]{1,0:T(8,128)(2,1)}, bf16[864,640]{1,0:T(8,128)(2,1)S(1)}, u32[]{:S(2)}, u32[]{:S(2)}) %collective-permute-start.34) | collective-permute-done | bytes 1105952 | tf_op jit(solution)/shard_map/ppermute | solution.py:35
  580.6 16.6 %fan_out.1 = bf16[4,4,160,1024]{3,2,1,0:T(8,128)(2,1)} custom-call(bf16[1728,1024]{1,0:T(8,128)(2,1)} %get-tuple-element.237.x_ref, bf16[1728,640]{1,0:T(8,128)(2,1)} %refs_0_.2, bf16[1728,640]{1,0:T(8,128)(2,1)} %copy-done.3, bf16[1728,640]{1,0:T(8,128)(2,1)} %copy-done.2, bf16[1728,640]{1,0:T(8,128)(2,1)} %copy-done.4), custom_call_target="tpu_custom_call" | custom-call | flops 1700000000 | tf_op jit(solution)/shard_map/fan_out/pallas_call | solution.py:485
  597.2 27.4 %collective-permute-done.36 = bf16[1728,640]{1,0:T(8,128)(2,1)} collective-permute-done((bf16[1728,640]{1,0:T(8,128)(2,1)}, bf16[1728,640]{1,0:T(8,128)(2,1)}, u32[]{:S(2)}, u32[]{:S(2)}) %collective-permute-start.36) | collective-permute-done | bytes 2211872 | tf_op jit(solution)/shard_map/ppermute | solution.py:35
  628.9 16.2 %all-gather.20.cloned.1.call-done = bf16[16,160,1024]{2,1,0:T(8,128)(2,1)} async-done(((bf16[4,160,1024]{2,1,0:T(8,128)(2,1)}), bf16[16,160,1024]{2,1,0:T(8,128)(2,1)}) %all-gather.20.cloned.1.call-update) | async-done | bytes 5242896 | tf_op jit(solution)/shard_map/all_gather | solution.py:676
  649.6 9.6 %mix_back.1 = (bf16[4,640,1024]{2,1,0:T(8,128)(2,1)}, bf16[320,1024]{1,0:T(8,128)(2,1)}, bf16[320,1024]{1,0:T(8,128)(2,1)}) custom-call(s32[1]{0:T(128)} %bitcast.parity_ref, bf16[4,4,160,1024]{3,2,1,0:T(8,128)(2,1)} %bitcast.249, bf16[640,640]{1,0:T(8,128)(2,1)} %refs_1_, bf16[640,640]{1,0:T(8,128)(2,1)} %collective-permute-done.17.refs_1_.refs_2_, ...), custom_call_target="tpu_custom_call" | custom-call | flops 900000000 | tf_op jit(solution)/shard_map/mix_back/pallas_call | solution.py:459
  662.4 37.5 %attend_back.1 = (bf16[480,1024]{1,0:T(8,128)(2,1)}, bf16[480,1024]{1,0:T(8,128)(2,1)}) custom-call(s32[1]{0:T(128)} %bitcast.parity_ref, bf16[480,1024]{1,0:T(8,128)(2,1)} %get-tuple-element.335.own_ref, bf16[480,1024]{1,0:T(8,128)(2,1)} %collective-permute-done.14.other_ref, bf16[320,1024]{1,0:T(8,128)(2,1)} %get-tuple-element.271.own_ref.own_out, ...), custom_call_target="tpu_custom_call" | custom-call | flops 3700000000 | tf_op jit(solution)/shard_map/attend_back/pallas_call | solution.py:361
  705.2 17.5 %qkv_back.1 = (bf16[640,1024]{1,0:T(8,128)(2,1)}, bf16[320,1024]{1,0:T(8,128)(2,1)}, bf16[4,4,160,1024]{3,2,1,0:T(8,128)(2,1)}, f32[4,4,160,1]{3,2,1,0:T(8,128)}) custom-call(s32[1]{0:T(128)} %bitcast.parity_ref, bf16[4,4,160,1024]{3,2,1,0:T(8,128)(2,1)} %bitcast.238, f32[4,4,160,1]{3,2,1,0:T(8,128)} %copy.66.gain_ref, ...), custom_call_target="tpu_custom_call" | custom-call | flops 1700000000 | tf_op jit(solution)/shard_map/qkv_back/pallas_call | solution.py:653
  761.3 11.1 %collective-permute-done.51 = bf16[768,640]{1,0:T(8,128)(2,1)S(1)} collective-permute-done((bf16[768,640]{1,0:T(8,128)(2,1)S(1)}, bf16[768,640]{1,0:T(8,128)(2,1)S(1)}, u32[]{:S(2)}, u32[]{:S(2)}) %collective-permute-start.51) | collective-permute-done | bytes 983072 | tf_op jit(solution)/shard_map/ppermute | solution.py:687
  783.2 7.6 convert_add_fusion
  808.4 12.3 %collective-permute-done.55 = bf16[320,640]{1,0:T(8,128)(2,1)S(1)} collective-permute-done((bf16[320,640]{1,0:T(8,128)(2,1)S(1)}, bf16[320,640]{1,0:T(8,128)(2,1)S(1)}, u32[]{:S(2)}, u32[]{:S(2)}) %collective-permute-start.55) | collective-permute-done | bytes 409632 | tf_op jit(solution)/shard_map/ppermute | solution.py:35
  823.8 8.5 collective-permute-done.56
  843.1 7.2 collective-permute-done.66
  (353 shorter events, 230.8 us)
Async XLA Ops:
  7.2 121.3 %all-gather.12.cloned.1.call-start = ((), (), s32[]{:S(2)}) async-start(), calls=%async_computation.10 | async-start | bytes 6553600 | tf_op jit(solution)/shard_map/all_gather | solution.py:676
  27.7 199.4 %all-gather.14.cloned.1.call-start = ((), (), s32[]{:S(2)}) async-start(), calls=%async_computation.11 | async-start | bytes 6553600 | tf_op jit(solution)/shard_map/all_gather | solution.py:676
  46.5 29.4 %collective-permute-start.6 = (bf16[640,640]{1,0:T(8,128)(2,1)}, bf16[640,640]{1,0:T(8,128)(2,1)}, u32[]{:S(2)}, u32[]{:S(2)}) collective-permute-start(bf16[640,640]{1,0:T(8,128)(2,1)} %refs_0_.3), channel_id=1, source_target_pairs={{0,8},{4,12},{8,0},{12,4},{1,9},{5,13},{9,1},{13,5},{2,10},{6,14},... | collective-permute-start | bytes 2457608 | tf_op jit(solution)/shard_map/ppermute | solution.py:35
  48.6 27.3 %collective-permute-start.7 = (bf16[320,640]{1,0:T(8,128)(2,1)S(1)}, bf16[320,640]{1,0:T(8,128)(2,1)S(1)}, u32[]{:S(2)}, u32[]{:S(2)}) collective-permute-start(bf16[320,640]{1,0:T(8,128)(2,1)S(1)} %pad_maximum_fusion.5.refs_4_), channel_id=1, source_target_pairs={{0,8},{4,12},{8,0},{12,4},{1,9},{5,13},{9,1},{13,5},{2,10},{6,14},... | collective-permute-start | bytes 1228808 | tf_op jit(solution)/shard_map/ppermute | solution.py:35
  75.9 49.8 %collective-permute-start.12 = (bf16[1728,640]{1,0:T(8,128)(2,1)S(1)}, bf16[1728,640]{1,0:T(8,128)(2,1)}, u32[]{:S(2)}, u32[]{:S(2)}) collective-permute-start(bf16[1728,640]{1,0:T(8,128)(2,1)S(1)} %bitcast.244), channel_id=1, source_target_pairs={{0,8},{4,12},{8,0},{12,4},{1,9},{5,13},{9,1},{13,5},{2,10},{6,14},... | collective-permute-start | bytes 6635528 | tf_op jit(solution)/shard_map/ppermute | solution.py:35
  77.8 36.9 %collective-permute-start.8 = (bf16[640,640]{1,0:T(8,128)(2,1)}, bf16[640,640]{1,0:T(8,128)(2,1)}, u32[]{:S(2)}, u32[]{:S(2)}) collective-permute-start(bf16[640,640]{1,0:T(8,128)(2,1)} %refs_0_.3), channel_id=1, source_target_pairs={{0,4},{4,0},{8,12},{12,8},{1,5},{5,1},{9,13},{13,9},{2,6},{6,2},{1... | collective-permute-start | bytes 2457608 | tf_op jit(solution)/shard_map/ppermute | solution.py:35
  78.3 36.4 %collective-permute-start.9 = (bf16[640,640]{1,0:T(8,128)(2,1)}, bf16[640,640]{1,0:T(8,128)(2,1)}, u32[]{:S(2)}, u32[]{:S(2)}) collective-permute-start(bf16[640,640]{1,0:T(8,128)(2,1)} %collective-permute-done.6.refs_2_), channel_id=1, source_target_pairs={{0,4},{4,0},{8,12},{12,8},{1,5},{5,1},{9,13},{13,9},{2,6},{6,2},{1... | collective-permute-start | bytes 2457608 | tf_op jit(solution)/shard_map/ppermute | solution.py:35
  79.8 34.9 %collective-permute-start.10 = (bf16[320,640]{1,0:T(8,128)(2,1)S(1)}, bf16[320,640]{1,0:T(8,128)(2,1)}, u32[]{:S(2)}, u32[]{:S(2)}) collective-permute-start(bf16[320,640]{1,0:T(8,128)(2,1)S(1)} %pad_maximum_fusion.5.refs_4_), channel_id=1, source_target_pairs={{0,4},{4,0},{8,12},{12,8},{1,5},{5,1},{9,13},{13,9},{2,6},{6,2},{1... | collective-permute-start | bytes 1228808 | tf_op jit(solution)/shard_map/ppermute | solution.py:35
  80.3 34.4 %collective-permute-start.11 = (bf16[320,640]{1,0:T(8,128)(2,1)}, bf16[320,640]{1,0:T(8,128)(2,1)}, u32[]{:S(2)}, u32[]{:S(2)}) collective-permute-start(bf16[320,640]{1,0:T(8,128)(2,1)} %copy-done.29), channel_id=1, source_target_pairs={{0,4},{4,0},{8,12},{12,8},{1,5},{5,1},{9,13},{13,9},{2,6},{6,2},{1... | collective-permute-start | bytes 1228808 | tf_op jit(solution)/shard_map/ppermute | solution.py:35
  128.5 193.1 %reduce-scatter.6.cloned.1.call-start = ((), (), s32[]{:S(2)}) async-start(), calls=%async_computation.5 | async-start | bytes 6553600 | tf_op jit(solution)/shard_map/reduce_scatter | solution.py:680
  148.8 51.3 %collective-permute-start.19 = (bf16[1728,640]{1,0:T(8,128)(2,1)}, bf16[1728,640]{1,0:T(8,128)(2,1)S(1)}, u32[]{:S(2)}, u32[]{:S(2)}) collective-permute-start(bf16[1728,640]{1,0:T(8,128)(2,1)} %bitcast.245), channel_id=1, source_target_pairs={{0,8},{4,12},{8,0},{12,4},{1,9},{5,13},{9,1},{13,5},{2,10},{6,14},... | collective-permute-start | bytes 6635528 | tf_op jit(solution)/shard_map/ppermute | solution.py:35
  168.0 32.1 %collective-permute-start.17 = (bf16[640,640]{1,0:T(8,128)(2,1)S(1)}, bf16[640,640]{1,0:T(8,128)(2,1)}, u32[]{:S(2)}, u32[]{:S(2)}) collective-permute-start(bf16[640,640]{1,0:T(8,128)(2,1)S(1)} %copy-done.22), channel_id=1, source_target_pairs={{0,4},{4,0},{8,12},{12,8},{1,5},{5,1},{9,13},{13,9},{2,6},{6,2},{1... | collective-permute-start | bytes 2457608 | tf_op jit(solution)/shard_map/ppermute | solution.py:35
  168.5 31.6 %collective-permute-start.18 = (bf16[640,640]{1,0:T(8,128)(2,1)}, bf16[640,640]{1,0:T(8,128)(2,1)}, u32[]{:S(2)}, u32[]{:S(2)}) collective-permute-start(bf16[640,640]{1,0:T(8,128)(2,1)} %collective-permute-done.16.refs_2_.refs_3_), channel_id=1, source_target_pairs={{0,4},{4,0},{8,12},{12,8},{1,5},{5,1},{9,13},{13,9},{2,6},{6,2},{1... | collective-permute-start | bytes 2457608 | tf_op jit(solution)/shard_map/ppermute | solution.py:35
  227.2 153.0 %all-gather.16.cloned.1.call-start = ((), (), s32[]{:S(2)}) async-start(), calls=%async_computation.12 | async-start | bytes 3276800 | tf_op jit(solution)/shard_map/all_gather | solution.py:676
  228.8 50.0 %collective-permute-start.25 = (bf16[1728,640]{1,0:T(8,128)(2,1)S(1)}, bf16[1728,640]{1,0:T(8,128)(2,1)S(1)}, u32[]{:S(2)}, u32[]{:S(2)}) collective-permute-start(bf16[1728,640]{1,0:T(8,128)(2,1)S(1)} %copy-done.1), channel_id=1, source_target_pairs={{0,8},{4,12},{8,0},{12,4},{1,9},{5,13},{9,1},{13,5},{2,10},{6,14},... | collective-permute-start | bytes 6635528 | tf_op jit(solution)/shard_map/ppermute | solution.py:35
  230.2 49.5 %collective-permute-start.24 = (bf16[1728,640]{1,0:T(8,128)(2,1)S(1)}, bf16[1728,640]{1,0:T(8,128)(2,1)S(1)}, u32[]{:S(2)}, u32[]{:S(2)}) collective-permute-start(bf16[1728,640]{1,0:T(8,128)(2,1)S(1)} %copy-done.1), channel_id=1, source_target_pairs={{0,4},{4,0},{8,12},{12,8},{1,5},{5,1},{9,13},{13,9},{2,6},{6,2},{1... | collective-permute-start | bytes 6635528 | tf_op jit(solution)/shard_map/ppermute | solution.py:35
  324.7 110.5 %all-gather.18.cloned.1.call-start = ((), (), s32[]{:S(2)}) async-start(), calls=%async_computation.13 | async-start | bytes 3276800 | tf_op jit(solution)/shard_map/all_gather | solution.py:676
  325.2 219.3 %reduce-scatter.8.cloned.1.call-start = ((), (), s32[]{:S(2)}) async-start(), calls=%async_computation.6 | async-start | bytes 3276800 | tf_op jit(solution)/shard_map/reduce_scatter | solution.py:680
  422.4 122.2 %reduce-scatter.10.cloned.1.call-start = ((), (), s32[]{:S(2)}) async-start(), calls=%async_computation.7 | async-start | bytes 3276800 | tf_op jit(solution)/shard_map/reduce_scatter | solution.py:680
  489.9 155.1 %all-gather.20.cloned.1.call-start = ((), (), s32[]{:S(2)}) async-start(), calls=%async_computation.14 | async-start | bytes 6553600 | tf_op jit(solution)/shard_map/all_gather | solution.py:676
  518.0 26.5 %collective-permute-start.29 = (bf16[864,640]{1,0:T(8,128)(2,1)S(1)}, bf16[864,640]{1,0:T(8,128)(2,1)}, u32[]{:S(2)}, u32[]{:S(2)}) collective-permute-start(bf16[864,640]{1,0:T(8,128)(2,1)S(1)} %get-tuple-element.331), channel_id=1, source_target_pairs={{0,8},{4,12},{8,0},{12,4},{1,9},{5,13},{9,1},{13,5},{2,10},{6,14},... | collective-permute-start | bytes 3317768 | tf_op jit(solution)/shard_map/ppermute | solution.py:35
  548.3 191.2 %reduce-scatter.12.cloned.1.call-start = ((), (), s32[]{:S(2)}) async-start(), calls=%async_computation.8 | async-start | bytes 6553600 | tf_op jit(solution)/shard_map/reduce_scatter | solution.py:680
  548.4 25.9 %collective-permute-start.34 = (bf16[864,640]{1,0:T(8,128)(2,1)}, bf16[864,640]{1,0:T(8,128)(2,1)S(1)}, u32[]{:S(2)}, u32[]{:S(2)}) collective-permute-start(bf16[864,640]{1,0:T(8,128)(2,1)} %get-tuple-element.249), channel_id=1, source_target_pairs={{0,8},{4,12},{8,0},{12,4},{1,9},{5,13},{9,1},{13,5},{2,10},{6,14},... | collective-permute-start | bytes 3317768 | tf_op jit(solution)/shard_map/ppermute | solution.py:35
  575.8 48.8 %collective-permute-start.36 = (bf16[1728,640]{1,0:T(8,128)(2,1)}, bf16[1728,640]{1,0:T(8,128)(2,1)}, u32[]{:S(2)}, u32[]{:S(2)}) collective-permute-start(bf16[1728,640]{1,0:T(8,128)(2,1)} %add_convert_fusion.4), channel_id=1, source_target_pairs={{0,8},{4,12},{8,0},{12,4},{1,9},{5,13},{9,1},{13,5},{2,10},{6,14},... | collective-permute-start | bytes 6635528 | tf_op jit(solution)/shard_map/ppermute | solution.py:35
  579.1 49.8 %collective-permute-start.35 = (bf16[1728,640]{1,0:T(8,128)(2,1)S(1)}, bf16[1728,640]{1,0:T(8,128)(2,1)}, u32[]{:S(2)}, u32[]{:S(2)}) collective-permute-start(bf16[1728,640]{1,0:T(8,128)(2,1)S(1)} %pad_maximum_fusion.1), channel_id=1, source_target_pairs={{0,16},{16,0},{1,17},{17,1},{2,18},{18,2},{3,19},{19,3},{4,20},{20... | collective-permute-start | bytes 6635528 | tf_op jit(solution)/shard_map/ppermute | solution.py:687
  645.1 191.0 %reduce-scatter.14.cloned.1.call-start = ((), (), s32[]{:S(2)}) async-start(), calls=%async_computation.9 | async-start | bytes 6553600 | tf_op jit(solution)/shard_map/reduce_scatter | solution.py:680
  646.7 53.4 %collective-permute-start.39 = (bf16[1728,640]{1,0:T(8,128)(2,1)S(1)}, bf16[1728,640]{1,0:T(8,128)(2,1)}, u32[]{:S(2)}, u32[]{:S(2)}) collective-permute-start(bf16[1728,640]{1,0:T(8,128)(2,1)S(1)} %copy-done.42), channel_id=1, source_target_pairs={{0,8},{4,12},{8,0},{12,4},{1,9},{5,13},{9,1},{13,5},{2,10},{6,14},... | collective-permute-start | bytes 6635528 | tf_op jit(solution)/shard_map/ppermute | solution.py:35
  648.2 54.5 %collective-permute-start.40 = (bf16[1728,640]{1,0:T(8,128)(2,1)}, bf16[1728,640]{1,0:T(8,128)(2,1)}, u32[]{:S(2)}, u32[]{:S(2)}) collective-permute-start(bf16[1728,640]{1,0:T(8,128)(2,1)} %add_convert_fusion.1), channel_id=1, source_target_pairs={{0,16},{16,0},{1,17},{17,1},{2,18},{18,2},{3,19},{19,3},{4,20},{20... | collective-permute-start | bytes 6635528 | tf_op jit(solution)/shard_map/ppermute | solution.py:687
  703.8 30.9 %collective-permute-start.41 = (bf16[960,640]{1,0:T(8,128)(2,1)}, bf16[960,640]{1,0:T(8,128)(2,1)}, u32[]{:S(2)}, u32[]{:S(2)}) collective-permute-start(bf16[960,640]{1,0:T(8,128)(2,1)} %slice.166), channel_id=1, source_target_pairs={{0,16},{16,0},{1,17},{17,1},{2,18},{18,2},{3,19},{19,3},{4,20},{20... | collective-permute-start | bytes 3686408 | tf_op jit(solution)/shard_map/ppermute | solution.py:687
  777.8 44.5 %collective-permute-start.57 = (bf16[640,640]{1,0:T(8,128)(2,1)S(1)}, bf16[640,640]{1,0:T(8,128)(2,1)S(1)}, u32[]{:S(2)}, u32[]{:S(2)}) collective-permute-start(bf16[640,640]{1,0:T(8,128)(2,1)S(1)} %add_convert_fusion.11), channel_id=1, source_target_pairs={{0,16},{16,0},{1,17},{17,1},{2,18},{18,2},{3,19},{19,3},{4,20},{20... | collective-permute-start | bytes 2457608 | tf_op jit(solution)/shard_map/ppermute | solution.py:687
  798.4 23.8 %collective-permute-start.64 = (bf16[160,1024]{1,0:T(8,128)(2,1)S(1)}, bf16[160,1024]{1,0:T(8,128)(2,1)S(1)}, u32[]{:S(2)}, u32[]{:S(2)}) collective-permute-start(bf16[160,1024]{1,0:T(8,128)(2,1)S(1)} %get-tuple-element.336), channel_id=1, source_target_pairs={{0,12},{4,8},{8,4},{12,0},{1,13},{5,9},{9,5},{13,1},{2,14},{6,10},... | collective-permute-start | bytes 983048 | tf_op jit(solution)/shard_map/ppermute | solution.py:35
  807.0 25.4 %collective-permute-start.54 = (bf16[640,640]{1,0:T(8,128)(2,1)S(1)}, bf16[640,640]{1,0:T(8,128)(2,1)S(1)}, u32[]{:S(2)}, u32[]{:S(2)}) collective-permute-start(bf16[640,640]{1,0:T(8,128)(2,1)S(1)} %add_convert_fusion.12), channel_id=1, source_target_pairs={{0,16},{16,0},{1,17},{17,1},{2,18},{18,2},{3,19},{19,3},{4,20},{20... | collective-permute-start | bytes 2457608 | tf_op jit(solution)/shard_map/ppermute | solution.py:687
  (98 other events, 1428.9 us)
Sparse Core Ops, SparseCore 0:
  27.8 100.5 all-gather.11
  130.6 96.5 all-gather.13
  229.4 92.1 reduce-scatter.5
  324.8 55.3 all-gather.15
  381.5 53.5 all-gather.17
  437.9 50.8 reduce-scatter.7
  491.1 51.7 reduce-scatter.9
  548.5 96.5 all-gather.19
  647.4 92.1 reduce-scatter.11
  741.7 94.3 reduce-scatter.13

commit v15 on v13

--- a/solution.py
+++ b/solution.py
@@ -734,11 +734,13 @@
         ]
         return jnp.stack(exchange_blocks(outgoing, "row"))
 
-    def all_tokens(blocks):
+    def all_tokens(blocks, dtype=BF):
         got = exchange_blocks([blocks[k] for k in range(count)], "row")
-        result = jnp.zeros((piece, count * rows), blocks.dtype)
+        result = jnp.zeros((piece, count * rows), dtype)
         for k in range(count):
-            result = lax.dynamic_update_slice(result, got[k], (0, (row ^ k) * rows))
+            result = lax.dynamic_update_slice(
+                result, got[k].astype(dtype), (0, (row ^ k) * rows)
+            )
         return result.T
 
     def listed(blocks):
@@ -802,8 +804,12 @@
     parts = 2 if rows % 256 == 0 else 1
     size = rows // parts
     spans = [slice(i * size, (i + 1) * size) for i in range(parts)]
-    residual_low = residual_own.astype(BF)
-    residual = [spread_cols(residual_low[..., span]) for span in spans]
+    lows = []
+    for span in spans:
+        low = source_own[..., span].astype(F32) + attn_sum[..., span].astype(F32)
+        lows.append(low.astype(BF))
+        attn_sum, *lows = together(attn_sum, *lows)
+    residual = [spread_cols(low) for low in lows]
     before, shares = (), []
     gain_share_two = 0.0
     for i in range(parts):
@@ -920,7 +926,8 @@
         input_sum, q_total, kv_total, mix_total, gain_totals, layer_output, up_total
     )
 
-    input_grad = all_tokens((residual_grad_own + input_sum.astype(F32)).astype(BF)).astype(F32)
+    input_low = (residual_grad_own + input_sum.astype(F32)).astype(BF)
+    input_grad = all_tokens(input_low, F32)
     kv_rows = kv_total.shape[0] // 2
     return (
         layer_output,

time: 872 us -> 873 us (level)
  no operation moved by 1% of the time
where the time goes in v15:
time: 873 us; the launch traced here: 864 us
  waiting for transfers between devices  399 us (46%)
  Pallas kernels  215 us (25%)
  matrix products  73.9 us (8%)
  starting transfers between devices  51.8 us (6%)
  other arithmetic  47.7 us (5%)
  blocking collectives  34 us (4%)
  local copies, waits for them, and re-layouts  27 us (3%)
  between operations  15.5 us (2%)
    ppermute x60, waiting for transfers between devices, swapped(): return lax.ppermute(value, axis, [(i, i ^ mask) for i in range(size)])  254 us
    all_gather x5, waiting for transfers between devices, spread_cols(): return lax.all_gather(value, 'col', axis=0, tiled=False)  98.6 us
    pallas_call x2, Pallas kernels, feed_forward(): pl.pallas_call(functools.partial(ff_kernel, count, bool(before)), out_sha...  84 us
    dot_general x24, matrix products, dot(): return lax.dot_general(left, right, dims, preferred_element_type=F32)  73.9 us
    ppermute x60, starting transfers between devices, swapped(): return lax.ppermute(value, axis, [(i, i ^ mask) for i in range(size)])  41 us
    pallas_call x1, Pallas kernels, attend_back(): pl.pallas_call(functools.partial(attend_back_kernel, tile), out_shape=(sh...  37.5 us
    all_gather x1, blocking collectives, body(): lax.all_gather(jnp.stack([attn_gain, mlp_gain]), ('row', 'col'), axis=1,...  34 us
    reduce_scatter x5, waiting for transfers between devices, sum_cols(): return lax.psum_scatter(value, 'col', scatter_dimension=0, tiled=False)  32.6 us
  transfers between devices with their start and end apart: 78, of which 37 were waited for; matrix products, arithmetic and copies ran while one was open for 15% of the time, Pallas kernels for 25%

profile of v15, /device:TPU:0, one launch (start us, length us, event | category | flops | bytes accessed | tf_op | source)
XLA Modules:
  0.0 864.4 jit_solution(9598530383209170178)
XLA Ops:
  11.8 7.4 collective-permute-done.2
  19.3 7.2 collective-permute-done.1
  31.4 6.7 collective-permute-done.5
  38.1 7.2 collective-permute-done.4
  48.6 27.3 %collective-permute-done.7.refs_6_ = bf16[320,640]{1,0:T(8,128)(2,1)S(1)} collective-permute-done((bf16[320,640]{1,0:T(8,128)(2,1)S(1)}, bf16[320,640]{1,0:T(8,128)(2,1)S(1)}, u32[]{:S(2)}, u32[]{:S(2)}) %collective-permute-start.7) | collective-permute-done | bytes 409632 | tf_op jit(solution)/shard_map/ppermute | solution.py:35
  80.4 34.0 %all-gather.5 = f32[16,160,2]{1,2,0:T(2,128)S(1)} all-gather(f32[1,160,2]{1,2,0:T(2,128)S(1)} %maximum_bitcast_fusion.1), channel_id=1, replica_groups=mesh['dp'=2,'row'=4,'col'=4] {'row','col'}, dimensions={0}, use_global_device_ids=true | all-gather | bytes 21760 | tf_op jit(solution)/shard_map/all_gather | solution.py:767
  114.7 11.0 %collective-permute-done.12.refs_2_ = bf16[1728,640]{1,0:T(8,128)(2,1)} collective-permute-done((bf16[1728,640]{1,0:T(8,128)(2,1)S(1)}, bf16[1728,640]{1,0:T(8,128)(2,1)}, u32[]{:S(2)}, u32[]{:S(2)}) %collective-permute-start.12) | collective-permute-done | bytes 2211872 | tf_op jit(solution)/shard_map/ppermute | solution.py:35
  130.1 18.7 %collective-permute-done.16.refs_2_.refs_3_ = bf16[640,640]{1,0:T(8,128)(2,1)} collective-permute-done((bf16[640,640]{1,0:T(8,128)(2,1)S(1)}, bf16[640,640]{1,0:T(8,128)(2,1)}, u32[]{:S(2)}, u32[]{:S(2)}) %collective-permute-start.16) | collective-permute-done | bytes 819232 | tf_op jit(solution)/shard_map/ppermute | solution.py:35
  151.9 13.1 %qkv_project.1 = (bf16[4,640,1024]{2,1,0:T(8,128)(2,1)}, f32[1,1024]{1,0:T(1,128)}, bf16[2,480,1024]{2,1,0:T(8,128)(2,1)}) custom-call(bf16[4,4,160,1024]{3,2,1,0:T(8,128)(2,1)} %bitcast.237, f32[4,4,160,1]{3,2,1,0:T(8,128)} %copy.66.gain_ref, f32[40,1024]{1,0:T(8,128)} %get-tuple-element.185.cos_ref, f32[40,1024]{1,0:T(8,128)} %get-tuple-element.186.sin_ref, ...), custom_call_target="tpu_custom_call" | custom-call | flops 1200000000 | tf_op jit(solution)/shard_map/qkv_project/pallas_call | solution.py:157
  172.1 27.8 %attend.1 = (bf16[320,1024]{1,0:T(8,128)(2,1)}, bf16[320,1024]{1,0:T(8,128)(2,1)}, f32[2,4,1,1024]{3,2,1,0:T(1,128)}) custom-call(s32[1]{0:T(128)} %bitcast.parity_ref, bf16[480,1024]{1,0:T(8,128)(2,1)} %get-tuple-element.336.own_ref, bf16[480,1024]{1,0:T(8,128)(2,1)} %collective-permute-done.14.other_ref, s32[1,1024]{1,0:T(1,128)} %bitcast.280, ...), custom_call_target="tpu_custom_call" | custom-call | flops 2700000000 | tf_op jit(solution)/shard_map/attend/pallas_call | solution.py:249
  203.0 10.2 %mix_out.1 = bf16[4,4,160,1024]{3,2,1,0:T(8,128)(2,1)} custom-call(s32[1]{0:T(128)} %bitcast.parity_ref, bf16[320,1024]{1,0:T(8,128)(2,1)} %get-tuple-element.278.own_ref.own_out, bf16[320,1024]{1,0:T(8,128)(2,1)} %copy-done.25, bf16[640,640]{1,0:T(8,128)(2,1)} %refs_1_, bf16[640,640]{1,0:T(8,128)(2,1)} %collective-permute-done.17.refs_1_.refs_2_, ...), custom_call_target="tpu_custom_call" | custom-call | flops 1000000000 | tf_op jit(solution)/shard_map/mix_out/pallas_call | solution.py:424
  213.3 13.9 %all-gather.14.cloned.1.call-done = bf16[16,160,1024]{2,1,0:T(8,128)(2,1)} async-done(((bf16[4,160,1024]{2,1,0:T(8,128)(2,1)}), bf16[16,160,1024]{2,1,0:T(8,128)(2,1)}) %all-gather.14.cloned.1.call-update) | async-done | bytes 5242896 | tf_op jit(solution)/shard_map/all_gather | solution.py:676
  230.2 48.5 %collective-permute-done.25.refs_10_.refs_2_ = bf16[1728,640]{1,0:T(8,128)(2,1)S(1)} collective-permute-done((bf16[1728,640]{1,0:T(8,128)(2,1)S(1)}, bf16[1728,640]{1,0:T(8,128)(2,1)S(1)}, u32[]{:S(2)}, u32[]{:S(2)}) %collective-permute-start.25) | collective-permute-done | bytes 2211872 | tf_op jit(solution)/shard_map/ppermute | solution.py:35
  295.9 25.7 %reduce-scatter.6.cloned.1.call-done = bf16[1,4,160,1024]{3,2,1,0:T(8,128)(2,1)} async-done(((bf16[4,4,160,1024]{3,2,1,0:T(8,128)(2,1)}), bf16[1,4,160,1024]{3,2,1,0:T(8,128)(2,1)}) %reduce-scatter.6.cloned.1.call-update) | async-done | bytes 1310736 | tf_op jit(solution)/shard_map/reduce_scatter | solution.py:680
  328.2 53.3 %all-gather.16.cloned.1.call-done = bf16[16,160,512]{2,1,0:T(8,128)(2,1)} async-done(((bf16[4,160,512]{2,1,0:T(8,128)(2,1)}), bf16[16,160,512]{2,1,0:T(8,128)(2,1)}) %all-gather.16.cloned.1.call-update) | async-done | bytes 2621456 | tf_op jit(solution)/shard_map/all_gather | solution.py:676
  381.4 42.2 %feed_forward.2 = (bf16[4,640,1024]{2,1,0:T(8,128)(2,1)}, bf16[4,640,1024]{2,1,0:T(8,128)(2,1)}, bf16[1728,1024]{1,0:T(8,128)(2,1)}, bf16[1728,1024]{1,0:T(8,128...) custom-call(bf16[4,4,160,512]{3,2,1,0:T(8,128)(2,1)} %bitcast.256, ...), custom_call_target="tpu_custom_call" | custom-call | flops 4200000000 | tf_op jit(solution)/shard_map/feed_forward/pallas_call | solution.py:563
  423.7 12.8 %all-gather.18.cloned.1.call-done = bf16[16,160,512]{2,1,0:T(8,128)(2,1)} async-done(((bf16[4,160,512]{2,1,0:T(8,128)(2,1)}), bf16[16,160,512]{2,1,0:T(8,128)(2,1)}) %all-gather.18.cloned.1.call-update) | async-done | bytes 2621456 | tf_op jit(solution)/shard_map/all_gather | solution.py:676
  436.5 41.8 %feed_forward.3 = (bf16[4,640,1024]{2,1,0:T(8,128)(2,1)}, bf16[4,640,1024]{2,1,0:T(8,128)(2,1)}, bf16[1728,1024]{1,0:T(8,128)(2,1)}, bf16[1728,1024]{1,0:T(8,128...) custom-call(bf16[4,4,160,512]{3,2,1,0:T(8,128)(2,1)} %bitcast.262, ...), custom_call_target="tpu_custom_call", output_to_operand_aliasing={{0}: (15, {}), {1}: (16, {}), {2}: (17, {}), {3}: (18, {}),... | custom-call | flops 4200000000 | tf_op jit(solution)/shard_map/feed_forward/pallas_call | solution.py:563
  478.3 6.9 convolution_convert_fusion.10
  538.1 7.8 collective-permute-done.29
  550.4 24.3 %collective-permute-done.34 = bf16[864,640]{1,0:T(8,128)(2,1)S(1)} collective-permute-done((bf16[864,640]{1,0:T(8,128)(2,1)}, bf16[864,640]{1,0:T(8,128)(2,1)S(1)}, u32[]{:S(2)}, u32[]{:S(2)}) %collective-permute-start.34) | collective-permute-done | bytes 1105952 | tf_op jit(solution)/shard_map/ppermute | solution.py:35
  582.5 16.6 %fan_out.1 = bf16[4,4,160,1024]{3,2,1,0:T(8,128)(2,1)} custom-call(bf16[1728,1024]{1,0:T(8,128)(2,1)} %get-tuple-element.244.x_ref, bf16[1728,640]{1,0:T(8,128)(2,1)} %refs_0_.2, bf16[1728,640]{1,0:T(8,128)(2,1)} %copy-done.4, bf16[1728,640]{1,0:T(8,128)(2,1)} %copy-done.3, bf16[1728,640]{1,0:T(8,128)(2,1)} %copy-done.5), custom_call_target="tpu_custom_call" | custom-call | flops 1700000000 | tf_op jit(solution)/shard_map/fan_out/pallas_call | solution.py:485
  599.1 26.0 %collective-permute-done.36 = bf16[1728,640]{1,0:T(8,128)(2,1)} collective-permute-done((bf16[1728,640]{1,0:T(8,128)(2,1)}, bf16[1728,640]{1,0:T(8,128)(2,1)}, u32[]{:S(2)}, u32[]{:S(2)}) %collective-permute-start.36) | collective-permute-done | bytes 2211872 | tf_op jit(solution)/shard_map/ppermute | solution.py:35
  629.4 16.1 %all-gather.20.cloned.1.call-done = bf16[16,160,1024]{2,1,0:T(8,128)(2,1)} async-done(((bf16[4,160,1024]{2,1,0:T(8,128)(2,1)}), bf16[16,160,1024]{2,1,0:T(8,128)(2,1)}) %all-gather.20.cloned.1.call-update) | async-done | bytes 5242896 | tf_op jit(solution)/shard_map/all_gather | solution.py:676
  648.7 8.7 %mix_back.1 = (bf16[4,640,1024]{2,1,0:T(8,128)(2,1)}, bf16[320,1024]{1,0:T(8,128)(2,1)}, bf16[320,1024]{1,0:T(8,128)(2,1)}) custom-call(s32[1]{0:T(128)} %bitcast.parity_ref, bf16[4,4,160,1024]{3,2,1,0:T(8,128)(2,1)} %bitcast.249, bf16[640,640]{1,0:T(8,128)(2,1)} %refs_1_, bf16[640,640]{1,0:T(8,128)(2,1)} %collective-permute-done.17.refs_1_.refs_2_, ...), custom_call_target="tpu_custom_call" | custom-call | flops 900000000 | tf_op jit(solution)/shard_map/mix_back/pallas_call | solution.py:459
  660.6 37.5 %attend_back.1 = (bf16[480,1024]{1,0:T(8,128)(2,1)}, bf16[480,1024]{1,0:T(8,128)(2,1)}) custom-call(s32[1]{0:T(128)} %bitcast.parity_ref, bf16[480,1024]{1,0:T(8,128)(2,1)} %get-tuple-element.336.own_ref, bf16[480,1024]{1,0:T(8,128)(2,1)} %collective-permute-done.14.other_ref, bf16[320,1024]{1,0:T(8,128)(2,1)} %get-tuple-element.278.own_ref.own_out, ...), custom_call_target="tpu_custom_call" | custom-call | flops 3700000000 | tf_op jit(solution)/shard_map/attend_back/pallas_call | solution.py:361
  703.7 17.5 %qkv_back.1 = (bf16[640,1024]{1,0:T(8,128)(2,1)}, bf16[320,1024]{1,0:T(8,128)(2,1)}, bf16[4,4,160,1024]{3,2,1,0:T(8,128)(2,1)}, f32[4,4,160,1]{3,2,1,0:T(8,128)}) custom-call(s32[1]{0:T(128)} %bitcast.parity_ref, bf16[4,4,160,1024]{3,2,1,0:T(8,128)(2,1)} %bitcast.238, f32[4,4,160,1]{3,2,1,0:T(8,128)} %copy.66.gain_ref, ...), custom_call_target="tpu_custom_call" | custom-call | flops 1700000000 | tf_op jit(solution)/shard_map/qkv_back/pallas_call | solution.py:653
  765.5 12.7 %collective-permute-done.52 = bf16[640,640]{1,0:T(8,128)(2,1)S(1)} collective-permute-done((bf16[640,640]{1,0:T(8,128)(2,1)S(1)}, bf16[640,640]{1,0:T(8,128)(2,1)S(1)}, u32[]{:S(2)}, u32[]{:S(2)}) %collective-permute-start.52) | collective-permute-done | bytes 819232 | tf_op jit(solution)/shard_map/ppermute | solution.py:35
  784.5 7.6 convert_add_fusion
  809.8 12.2 %collective-permute-done.55 = bf16[320,640]{1,0:T(8,128)(2,1)S(1)} collective-permute-done((bf16[320,640]{1,0:T(8,128)(2,1)S(1)}, bf16[320,640]{1,0:T(8,128)(2,1)S(1)}, u32[]{:S(2)}, u32[]{:S(2)}) %collective-permute-start.55) | collective-permute-done | bytes 409632 | tf_op jit(solution)/shard_map/ppermute | solution.py:35
  825.2 8.2 collective-permute-done.56
  843.0 6.8 collective-permute-done.66
  (357 shorter events, 231.5 us)
Async XLA Ops:
  7.2 121.3 %all-gather.12.cloned.1.call-start = ((), (), s32[]{:S(2)}) async-start(), calls=%async_computation.10 | async-start | bytes 6553600 | tf_op jit(solution)/shard_map/all_gather | solution.py:676
  27.7 199.4 %all-gather.14.cloned.1.call-start = ((), (), s32[]{:S(2)}) async-start(), calls=%async_computation.11 | async-start | bytes 6553600 | tf_op jit(solution)/shard_map/all_gather | solution.py:676
  46.5 29.4 %collective-permute-start.6 = (bf16[640,640]{1,0:T(8,128)(2,1)}, bf16[640,640]{1,0:T(8,128)(2,1)}, u32[]{:S(2)}, u32[]{:S(2)}) collective-permute-start(bf16[640,640]{1,0:T(8,128)(2,1)} %refs_0_.3), channel_id=1, source_target_pairs={{0,8},{4,12},{8,0},{12,4},{1,9},{5,13},{9,1},{13,5},{2,10},{6,14},... | collective-permute-start | bytes 2457608 | tf_op jit(solution)/shard_map/ppermute | solution.py:35
  48.6 27.3 %collective-permute-start.7 = (bf16[320,640]{1,0:T(8,128)(2,1)S(1)}, bf16[320,640]{1,0:T(8,128)(2,1)S(1)}, u32[]{:S(2)}, u32[]{:S(2)}) collective-permute-start(bf16[320,640]{1,0:T(8,128)(2,1)S(1)} %pad_maximum_fusion.6.refs_4_), channel_id=1, source_target_pairs={{0,8},{4,12},{8,0},{12,4},{1,9},{5,13},{9,1},{13,5},{2,10},{6,14},... | collective-permute-start | bytes 1228808 | tf_op jit(solution)/shard_map/ppermute | solution.py:35
  75.9 49.8 %collective-permute-start.12 = (bf16[1728,640]{1,0:T(8,128)(2,1)S(1)}, bf16[1728,640]{1,0:T(8,128)(2,1)}, u32[]{:S(2)}, u32[]{:S(2)}) collective-permute-start(bf16[1728,640]{1,0:T(8,128)(2,1)S(1)} %bitcast.244), channel_id=1, source_target_pairs={{0,8},{4,12},{8,0},{12,4},{1,9},{5,13},{9,1},{13,5},{2,10},{6,14},... | collective-permute-start | bytes 6635528 | tf_op jit(solution)/shard_map/ppermute | solution.py:35
  77.8 36.9 %collective-permute-start.8 = (bf16[640,640]{1,0:T(8,128)(2,1)}, bf16[640,640]{1,0:T(8,128)(2,1)}, u32[]{:S(2)}, u32[]{:S(2)}) collective-permute-start(bf16[640,640]{1,0:T(8,128)(2,1)} %refs_0_.3), channel_id=1, source_target_pairs={{0,4},{4,0},{8,12},{12,8},{1,5},{5,1},{9,13},{13,9},{2,6},{6,2},{1... | collective-permute-start | bytes 2457608 | tf_op jit(solution)/shard_map/ppermute | solution.py:35
  78.3 36.4 %collective-permute-start.9 = (bf16[640,640]{1,0:T(8,128)(2,1)}, bf16[640,640]{1,0:T(8,128)(2,1)}, u32[]{:S(2)}, u32[]{:S(2)}) collective-permute-start(bf16[640,640]{1,0:T(8,128)(2,1)} %collective-permute-done.6.refs_2_), channel_id=1, source_target_pairs={{0,4},{4,0},{8,12},{12,8},{1,5},{5,1},{9,13},{13,9},{2,6},{6,2},{1... | collective-permute-start | bytes 2457608 | tf_op jit(solution)/shard_map/ppermute | solution.py:35
  79.8 34.9 %collective-permute-start.10 = (bf16[320,640]{1,0:T(8,128)(2,1)S(1)}, bf16[320,640]{1,0:T(8,128)(2,1)}, u32[]{:S(2)}, u32[]{:S(2)}) collective-permute-start(bf16[320,640]{1,0:T(8,128)(2,1)S(1)} %pad_maximum_fusion.6.refs_4_), channel_id=1, source_target_pairs={{0,4},{4,0},{8,12},{12,8},{1,5},{5,1},{9,13},{13,9},{2,6},{6,2},{1... | collective-permute-start | bytes 1228808 | tf_op jit(solution)/shard_map/ppermute | solution.py:35
  80.3 34.4 %collective-permute-start.11 = (bf16[320,640]{1,0:T(8,128)(2,1)}, bf16[320,640]{1,0:T(8,128)(2,1)}, u32[]{:S(2)}, u32[]{:S(2)}) collective-permute-start(bf16[320,640]{1,0:T(8,128)(2,1)} %copy-done.32), channel_id=1, source_target_pairs={{0,4},{4,0},{8,12},{12,8},{1,5},{5,1},{9,13},{13,9},{2,6},{6,2},{1... | collective-permute-start | bytes 1228808 | tf_op jit(solution)/shard_map/ppermute | solution.py:35
  128.5 193.1 %reduce-scatter.6.cloned.1.call-start = ((), (), s32[]{:S(2)}) async-start(), calls=%async_computation.5 | async-start | bytes 6553600 | tf_op jit(solution)/shard_map/reduce_scatter | solution.py:680
  148.8 51.2 %collective-permute-start.19 = (bf16[1728,640]{1,0:T(8,128)(2,1)}, bf16[1728,640]{1,0:T(8,128)(2,1)S(1)}, u32[]{:S(2)}, u32[]{:S(2)}) collective-permute-start(bf16[1728,640]{1,0:T(8,128)(2,1)} %bitcast.245), channel_id=1, source_target_pairs={{0,8},{4,12},{8,0},{12,4},{1,9},{5,13},{9,1},{13,5},{2,10},{6,14},... | collective-permute-start | bytes 6635528 | tf_op jit(solution)/shard_map/ppermute | solution.py:35
  168.0 32.1 %collective-permute-start.17 = (bf16[640,640]{1,0:T(8,128)(2,1)S(1)}, bf16[640,640]{1,0:T(8,128)(2,1)}, u32[]{:S(2)}, u32[]{:S(2)}) collective-permute-start(bf16[640,640]{1,0:T(8,128)(2,1)S(1)} %copy-done.23), channel_id=1, source_target_pairs={{0,4},{4,0},{8,12},{12,8},{1,5},{5,1},{9,13},{13,9},{2,6},{6,2},{1... | collective-permute-start | bytes 2457608 | tf_op jit(solution)/shard_map/ppermute | solution.py:35
  168.5 31.6 %collective-permute-start.18 = (bf16[640,640]{1,0:T(8,128)(2,1)}, bf16[640,640]{1,0:T(8,128)(2,1)}, u32[]{:S(2)}, u32[]{:S(2)}) collective-permute-start(bf16[640,640]{1,0:T(8,128)(2,1)} %collective-permute-done.16.refs_2_.refs_3_), channel_id=1, source_target_pairs={{0,4},{4,0},{8,12},{12,8},{1,5},{5,1},{9,13},{13,9},{2,6},{6,2},{1... | collective-permute-start | bytes 2457608 | tf_op jit(solution)/shard_map/ppermute | solution.py:35
  227.2 154.3 %all-gather.16.cloned.1.call-start = ((), (), s32[]{:S(2)}) async-start(), calls=%async_computation.12 | async-start | bytes 3276800 | tf_op jit(solution)/shard_map/all_gather | solution.py:676
  228.8 50.0 %collective-permute-start.25 = (bf16[1728,640]{1,0:T(8,128)(2,1)S(1)}, bf16[1728,640]{1,0:T(8,128)(2,1)S(1)}, u32[]{:S(2)}, u32[]{:S(2)}) collective-permute-start(bf16[1728,640]{1,0:T(8,128)(2,1)S(1)} %copy-done.2), channel_id=1, source_target_pairs={{0,8},{4,12},{8,0},{12,4},{1,9},{5,13},{9,1},{13,5},{2,10},{6,14},... | collective-permute-start | bytes 6635528 | tf_op jit(solution)/shard_map/ppermute | solution.py:35
  230.2 49.5 %collective-permute-start.24 = (bf16[1728,640]{1,0:T(8,128)(2,1)S(1)}, bf16[1728,640]{1,0:T(8,128)(2,1)S(1)}, u32[]{:S(2)}, u32[]{:S(2)}) collective-permute-start(bf16[1728,640]{1,0:T(8,128)(2,1)S(1)} %copy-done.2), channel_id=1, source_target_pairs={{0,4},{4,0},{8,12},{12,8},{1,5},{5,1},{9,13},{13,9},{2,6},{6,2},{1... | collective-permute-start | bytes 6635528 | tf_op jit(solution)/shard_map/ppermute | solution.py:35
  326.0 110.5 %all-gather.18.cloned.1.call-start = ((), (), s32[]{:S(2)}) async-start(), calls=%async_computation.13 | async-start | bytes 3276800 | tf_op jit(solution)/shard_map/all_gather | solution.py:676
  326.6 219.3 %reduce-scatter.8.cloned.1.call-start = ((), (), s32[]{:S(2)}) async-start(), calls=%async_computation.6 | async-start | bytes 3276800 | tf_op jit(solution)/shard_map/reduce_scatter | solution.py:680
  423.7 122.2 %reduce-scatter.10.cloned.1.call-start = ((), (), s32[]{:S(2)}) async-start(), calls=%async_computation.7 | async-start | bytes 3276800 | tf_op jit(solution)/shard_map/reduce_scatter | solution.py:680
  491.2 154.3 %all-gather.20.cloned.1.call-start = ((), (), s32[]{:S(2)}) async-start(), calls=%async_computation.14 | async-start | bytes 6553600 | tf_op jit(solution)/shard_map/all_gather | solution.py:676
  519.4 26.5 %collective-permute-start.29 = (bf16[864,640]{1,0:T(8,128)(2,1)S(1)}, bf16[864,640]{1,0:T(8,128)(2,1)}, u32[]{:S(2)}, u32[]{:S(2)}) collective-permute-start(bf16[864,640]{1,0:T(8,128)(2,1)S(1)} %get-tuple-element.332), channel_id=1, source_target_pairs={{0,8},{4,12},{8,0},{12,4},{1,9},{5,13},{9,1},{13,5},{2,10},{6,14},... | collective-permute-start | bytes 3317768 | tf_op jit(solution)/shard_map/ppermute | solution.py:35
  548.8 191.2 %reduce-scatter.12.cloned.1.call-start = ((), (), s32[]{:S(2)}) async-start(), calls=%async_computation.8 | async-start | bytes 6553600 | tf_op jit(solution)/shard_map/reduce_scatter | solution.py:680
  548.8 25.9 %collective-permute-start.34 = (bf16[864,640]{1,0:T(8,128)(2,1)}, bf16[864,640]{1,0:T(8,128)(2,1)S(1)}, u32[]{:S(2)}, u32[]{:S(2)}) collective-permute-start(bf16[864,640]{1,0:T(8,128)(2,1)} %get-tuple-element.256), channel_id=1, source_target_pairs={{0,8},{4,12},{8,0},{12,4},{1,9},{5,13},{9,1},{13,5},{2,10},{6,14},... | collective-permute-start | bytes 3317768 | tf_op jit(solution)/shard_map/ppermute | solution.py:35
  576.3 48.9 %collective-permute-start.36 = (bf16[1728,640]{1,0:T(8,128)(2,1)}, bf16[1728,640]{1,0:T(8,128)(2,1)}, u32[]{:S(2)}, u32[]{:S(2)}) collective-permute-start(bf16[1728,640]{1,0:T(8,128)(2,1)} %add_convert_fusion.4), channel_id=1, source_target_pairs={{0,8},{4,12},{8,0},{12,4},{1,9},{5,13},{9,1},{13,5},{2,10},{6,14},... | collective-permute-start | bytes 6635528 | tf_op jit(solution)/shard_map/ppermute | solution.py:35
  581.0 48.4 %collective-permute-start.35 = (bf16[1728,640]{1,0:T(8,128)(2,1)}, bf16[1728,640]{1,0:T(8,128)(2,1)}, u32[]{:S(2)}, u32[]{:S(2)}) collective-permute-start(bf16[1728,640]{1,0:T(8,128)(2,1)} %pad_maximum_fusion.1), channel_id=1, source_target_pairs={{0,16},{16,0},{1,17},{17,1},{2,18},{18,2},{3,19},{19,3},{4,20},{20... | collective-permute-start | bytes 6635528 | tf_op jit(solution)/shard_map/ppermute | solution.py:687
  645.5 191.0 %reduce-scatter.14.cloned.1.call-start = ((), (), s32[]{:S(2)}) async-start(), calls=%async_computation.9 | async-start | bytes 6553600 | tf_op jit(solution)/shard_map/reduce_scatter | solution.py:680
  645.7 52.7 %collective-permute-start.39 = (bf16[1728,640]{1,0:T(8,128)(2,1)}, bf16[1728,640]{1,0:T(8,128)(2,1)}, u32[]{:S(2)}, u32[]{:S(2)}) collective-permute-start(bf16[1728,640]{1,0:T(8,128)(2,1)} %add_convert_fusion.2), channel_id=1, source_target_pairs={{0,8},{4,12},{8,0},{12,4},{1,9},{5,13},{9,1},{13,5},{2,10},{6,14},... | collective-permute-start | bytes 6635528 | tf_op jit(solution)/shard_map/ppermute | solution.py:35
  647.3 53.6 %collective-permute-start.40 = (bf16[1728,640]{1,0:T(8,128)(2,1)}, bf16[1728,640]{1,0:T(8,128)(2,1)}, u32[]{:S(2)}, u32[]{:S(2)}) collective-permute-start(bf16[1728,640]{1,0:T(8,128)(2,1)} %add_convert_fusion.1), channel_id=1, source_target_pairs={{0,16},{16,0},{1,17},{17,1},{2,18},{18,2},{3,19},{19,3},{4,20},{20... | collective-permute-start | bytes 6635528 | tf_op jit(solution)/shard_map/ppermute | solution.py:687
  702.0 29.8 %collective-permute-start.41 = (bf16[960,640]{1,0:T(8,128)(2,1)}, bf16[960,640]{1,0:T(8,128)(2,1)}, u32[]{:S(2)}, u32[]{:S(2)}) collective-permute-start(bf16[960,640]{1,0:T(8,128)(2,1)} %slice.162), channel_id=1, source_target_pairs={{0,16},{16,0},{1,17},{17,1},{2,18},{18,2},{3,19},{19,3},{4,20},{20... | collective-permute-start | bytes 3686408 | tf_op jit(solution)/shard_map/ppermute | solution.py:687
  779.2 44.4 %collective-permute-start.57 = (bf16[640,640]{1,0:T(8,128)(2,1)S(1)}, bf16[640,640]{1,0:T(8,128)(2,1)S(1)}, u32[]{:S(2)}, u32[]{:S(2)}) collective-permute-start(bf16[640,640]{1,0:T(8,128)(2,1)S(1)} %add_convert_fusion.12), channel_id=1, source_target_pairs={{0,16},{16,0},{1,17},{17,1},{2,18},{18,2},{3,19},{19,3},{4,20},{20... | collective-permute-start | bytes 2457608 | tf_op jit(solution)/shard_map/ppermute | solution.py:687
  798.9 24.7 %collective-permute-start.64 = (bf16[160,1024]{1,0:T(8,128)(2,1)S(1)}, bf16[160,1024]{1,0:T(8,128)(2,1)S(1)}, u32[]{:S(2)}, u32[]{:S(2)}) collective-permute-start(bf16[160,1024]{1,0:T(8,128)(2,1)S(1)} %get-tuple-element.340), channel_id=1, source_target_pairs={{0,12},{4,8},{8,4},{12,0},{1,13},{5,9},{9,5},{13,1},{2,14},{6,10},... | collective-permute-start | bytes 983048 | tf_op jit(solution)/shard_map/ppermute | solution.py:35
  808.3 25.2 %collective-permute-start.54 = (bf16[640,640]{1,0:T(8,128)(2,1)S(1)}, bf16[640,640]{1,0:T(8,128)(2,1)S(1)}, u32[]{:S(2)}, u32[]{:S(2)}) collective-permute-start(bf16[640,640]{1,0:T(8,128)(2,1)S(1)} %add_convert_fusion.13), channel_id=1, source_target_pairs={{0,16},{16,0},{1,17},{17,1},{2,18},{18,2},{3,19},{19,3},{4,20},{20... | collective-permute-start | bytes 2457608 | tf_op jit(solution)/shard_map/ppermute | solution.py:687
  (100 other events, 1439.1 us)
Sparse Core Ops, SparseCore 0:
  27.8 100.5 all-gather.11
  130.6 96.5 all-gather.13
  229.4 92.1 reduce-scatter.5
  326.1 55.3 all-gather.15
  382.8 53.5 all-gather.17
  439.2 50.8 reduce-scatter.7
  492.4 51.7 reduce-scatter.9
  548.9 96.5 all-gather.19
  647.8 92.1 reduce-scatter.11
  742.1 94.3 reduce-scatter.13
